TPU v7x, 32 devices: a whole 2x2x4 slice. The times are simulated.
32 devices in a mesh: page: 8 (over z, x), band: 4 (over y, core).
Axes of the slice: x: 2, y: 2, z: 4, core: 2. Of those that a mesh axis runs over, the one named last changes fastest.
Arguments:
- hidden: bfloat16 [16, 4, 128, 768], P('page', 'band'), may hold values from -6 to 6
- boxes: int32 [4, 16, 4, 128], P(None, 'page', 'band'), may hold values from 0 to 2599, as said below
- page_size: int32 [2, 16], P(None, 'page'), may hold values from 600 to 2599, as said below
- band_count: int32 [16, 4], P('page', 'band'), may hold values from 1 to 128, as said below
- layout_tables: bfloat16 [4, 1024, 768], P(None, ('page', 'band')), may hold values from -1.75 to 1.75
- attn_in: bfloat16 [2, 768, 2304], P(None, ('page', 'band')), may hold values from -0.21875 to 0.21875
- attn_bias: bfloat16 [2, 2, 768], P(None, None, ('page', 'band')), may hold values from -3 to 3
- attn_out: bfloat16 [2, 768, 768], P(None, ('page', 'band')), may hold values from -1.25 to 1.25
- out_bias: bfloat16 [2, 768], P(None, ('page', 'band')), may hold values from -1.75 to 1.75
- norm_gain: bfloat16 [2, 2, 768], P(None, None, ('page', 'band')), may hold values from 0.5 to 1.5
- norm_bias: bfloat16 [2, 2, 768], P(None, None, ('page', 'band')), may hold values from -1.75 to 1.75
- ffn_in: bfloat16 [2, 768, 3072], P(None, ('page', 'band')), may hold values from -0.21875 to 0.21875
- ffn_in_bias: bfloat16 [2, 3072], P(None, ('page', 'band')), may hold values from -3 to 3
- ffn_out: bfloat16 [2, 3072, 768], P(None, ('page', 'band')), may hold values from -0.109375 to 0.109375
- ffn_out_bias: bfloat16 [2, 768], P(None, ('page', 'band')), may hold values from -1.75 to 1.75
- out_grad: bfloat16 [16, 4, 128, 768], P('page', 'band'), may hold values from -6 to 6
Outputs:
- output: float32 [16, 4, 128, 768], P('page', 'band')
- input_grad: float32 [16, 4, 128, 768], P('page', 'band')
- grad_layout_tables: float32 [4, 1024, 768], P(None, ('page', 'band'))
- grad_attn_in: float32 [2, 768, 2304], P(None, ('page', 'band'))
- grad_attn_bias: float32 [2, 2, 768], P(None, None, ('page', 'band'))
- grad_attn_out: float32 [2, 768, 768], P(None, ('page', 'band'))
- grad_out_bias: float32 [2, 768], P(None, ('page', 'band'))
- grad_norm_gain: float32 [2, 2, 768], P(None, None, ('page', 'band'))
- grad_norm_bias: float32 [2, 2, 768], P(None, None, ('page', 'band'))
- grad_ffn_in: float32 [2, 768, 3072], P(None, ('page', 'band'))
- grad_ffn_in_bias: float32 [2, 3072], P(None, ('page', 'band'))
- grad_ffn_out: float32 [2, 3072, 768], P(None, ('page', 'band'))
- grad_ffn_out_bias: float32 [2, 768], P(None, ('page', 'band'))
Inputs may be any that keep to these rules, and one draw needn't show every extreme that they name: `band_count`: in every page one band holds 128 live tokens; live tokens fill the first slots of their band. `boxes`: left <= right <= the page's width and top <= bottom <= the page's height. `page_size`: widths from 600 to 1999, heights from 800 to 2599.
All inputs are finite; a program needn't handle non-finite values.
Results may differ from a plain program's by a relative error of at most 0.02.
Values may be sent and summed in bfloat16 or wider, within the bound.
No kernel may reach another device: no remote copies, remote signals or barrier semaphores. Data moves between devices by JAX's collectives and lax.ppermute only.
A program may use at most 256 MiB of HBM per device.

v0:
```python
import jax
import jax.numpy as jnp
from jax import lax
from jax.sharding import PartitionSpec as P

D = 768
HEADS = 12
HEAD_DIM = 64
POS = 1024
GRID = 1000
LAYERS = 2
MICRO = 2


norm_eps = 1e-12
table_pick = (0, 1, 0, 1, 2, 3)


def layer_norm(hidden_rows, gain_row, shift_row):
    row_mean = jnp.mean(hidden_rows, axis=-1, keepdims=True)
    centred = hidden_rows - row_mean
    row_var = jnp.mean(centred * centred, axis=-1, keepdims=True)
    return centred * lax.rsqrt(row_var + norm_eps) * gain_row + shift_row


def gelu_exact(values):
    return jax.nn.gelu(values, approximate=False)


def norm_backward(grad_rows, sum_rows, gain_row, shift_row):
    _, pull_back = jax.vjp(layer_norm, sum_rows, gain_row, shift_row)
    return pull_back(grad_rows)


def layout_index(boxes, page_size, band_count):
    widths = page_size[0][:, None]
    heights = page_size[1][:, None]
    box_left = boxes[0, :, 0] * GRID // widths
    box_top = boxes[1, :, 0] * GRID // heights
    box_right = boxes[2, :, 0] * GRID // widths
    box_bottom = boxes[3, :, 0] * GRID // heights
    box_index = jnp.stack(
        [box_left, box_top, box_right, box_bottom, box_bottom - box_top, box_right - box_left]
    )
    slot_index = lax.broadcasted_iota(jnp.int32, box_left.shape, 1)
    live_mask = slot_index < band_count
    return (box_index, live_mask)


def head_split(layer_rows):
    return layer_rows.reshape(layer_rows.shape[0], layer_rows.shape[1], HEADS, HEAD_DIM)


def page_scores(query_heads, page_keys, page_valid):
    scores = jnp.einsum(
        "pqhd,pkhd->phqk", query_heads, head_split(page_keys), preferred_element_type=jnp.float32
    ) * HEAD_DIM ** (-0.5)
    return jnp.where(page_valid[:, None, None, :] > 0, scores, -1000000000.0)


def owner_order(values):
    page_total = lax.axis_size("page")
    band_total = lax.axis_size("band")
    leading = values.shape[:-1]
    shard_width = values.shape[-1] // (page_total * band_total)
    grouped = values.reshape(leading + (page_total, band_total, shard_width))
    return jnp.swapaxes(grouped, -3, -2).reshape(leading + (-1,))


def matrix_terms(left_parts, right_parts):
    left_cols = (
        lax.all_to_all(owner_order(left_parts[0]), "band", split_axis=2, concat_axis=1, tiled=True),
        lax.all_to_all(owner_order(left_parts[1]), "band", split_axis=2, concat_axis=1, tiled=True),
        lax.all_to_all(owner_order(left_parts[2]), "band", split_axis=2, concat_axis=1, tiled=True),
        lax.all_to_all(owner_order(left_parts[3]), "band", split_axis=2, concat_axis=1, tiled=True),
    )
    right_page = (
        lax.all_gather(right_parts[0], "band", axis=1, tiled=True),
        lax.all_gather(right_parts[1], "band", axis=1, tiled=True),
        lax.all_gather(right_parts[2], "band", axis=1, tiled=True),
        lax.all_gather(right_parts[3], "band", axis=1, tiled=True),
    )
    return tuple(
        (
            jnp.einsum(
                "pcd,pce->de",
                left_cols[number],
                right_page[number],
                preferred_element_type=jnp.float32,
            )
            for number in range(4)
        )
    )


def layer_forward(layer_rows, valid_low, weights):
    (
        in_proj,
        in_bias,
        out_proj,
        out_shift,
        norm_gains,
        shifts,
        up_proj,
        up_shift,
        down_proj,
        down_shift,
    ) = weights
    rows_low = layer_rows.astype(jnp.bfloat16)
    joint_proj = jnp.einsum("pcd,de->pce", rows_low, in_proj, preferred_element_type=jnp.float32)
    query_low = (joint_proj[..., :D] + in_bias[0].astype(jnp.float32)).astype(jnp.bfloat16)
    key_low = joint_proj[..., D : 2 * D].astype(jnp.bfloat16)
    value_low = (joint_proj[..., 2 * D :] + in_bias[1].astype(jnp.float32)).astype(jnp.bfloat16)
    page_keys, page_values, page_valid = (
        lax.all_gather(key_low, "band", axis=1, tiled=True),
        lax.all_gather(value_low, "band", axis=1, tiled=True),
        lax.all_gather(valid_low, "band", axis=1, tiled=True),
    )
    scores = page_scores(head_split(query_low), page_keys, page_valid)
    row_peak = jnp.max(scores, axis=-1, keepdims=True)
    exponent = jnp.exp(scores - row_peak)
    denominator = jnp.sum(exponent, axis=-1, keepdims=True)
    probs_low = (exponent / denominator).astype(jnp.bfloat16)
    log_total = row_peak + jnp.log(denominator)
    attn_mixed = jnp.einsum(
        "phqk,pkhd->pqhd", probs_low, head_split(page_values), preferred_element_type=jnp.float32
    )
    mixed_low = attn_mixed.reshape(layer_rows.shape).astype(jnp.bfloat16)
    branch = jnp.einsum(
        "pce,ed->pcd", mixed_low, out_proj, preferred_element_type=jnp.float32
    ) + out_shift.astype(jnp.float32)
    first_sum = layer_rows + branch
    first_out = layer_norm(
        first_sum, norm_gains[0].astype(jnp.float32), shifts[0].astype(jnp.float32)
    )
    first_low = first_out.astype(jnp.bfloat16)
    up_rows = jnp.einsum(
        "pcd,df->pcf", first_low, up_proj, preferred_element_type=jnp.float32
    ) + up_shift.astype(jnp.float32)
    act_low = gelu_exact(up_rows).astype(jnp.bfloat16)
    down_rows = jnp.einsum(
        "pcf,fd->pcd", act_low, down_proj, preferred_element_type=jnp.float32
    ) + down_shift.astype(jnp.float32)
    second_sum = first_out + down_rows
    layer_out = layer_norm(
        second_sum, norm_gains[1].astype(jnp.float32), shifts[1].astype(jnp.float32)
    )
    saved_state = (
        rows_low,
        query_low,
        key_low,
        value_low,
        log_total,
        mixed_low,
        first_sum,
        first_low,
        up_rows,
        act_low,
        second_sum,
    )
    kept_pages = (page_keys, page_values, page_valid)
    return (layer_out, saved_state, kept_pages)


def layer_backward(grad_out, saved_state, kept_pages, weights):
    (
        in_proj,
        in_bias,
        out_proj,
        out_shift,
        norm_gains,
        shifts,
        up_proj,
        up_shift,
        down_proj,
        down_shift,
    ) = weights
    (
        rows_low,
        query_low,
        key_low,
        value_low,
        log_total,
        mixed_low,
        first_sum,
        first_low,
        up_rows,
        act_low,
        second_sum,
    ) = saved_state
    gains_f = norm_gains.astype(jnp.float32)
    shifts_f = shifts.astype(jnp.float32)
    grad_second, gain_two, shift_two = norm_backward(grad_out, second_sum, gains_f[1], shifts_f[1])
    down_low = grad_second.astype(jnp.bfloat16)
    grad_down_shift = jnp.sum(down_low, axis=(0, 1), dtype=jnp.float32)
    grad_act = jnp.einsum("pcd,fd->pcf", down_low, down_proj, preferred_element_type=jnp.float32)
    _, gelu_pull = jax.vjp(gelu_exact, up_rows)
    up_low = gelu_pull(grad_act)[0].astype(jnp.bfloat16)
    grad_up_shift = jnp.sum(up_low, axis=(0, 1), dtype=jnp.float32)
    grad_first = grad_second + jnp.einsum(
        "pcf,df->pcd", up_low, up_proj, preferred_element_type=jnp.float32
    )
    grad_attn_sum, gain_one, shift_one = norm_backward(
        grad_first, first_sum, gains_f[0], shifts_f[0]
    )
    branch_low = grad_attn_sum.astype(jnp.bfloat16)
    grad_out_shift = jnp.sum(branch_low, axis=(0, 1), dtype=jnp.float32)
    grad_mixed = head_split(
        jnp.einsum("pcd,ed->pce", branch_low, out_proj, preferred_element_type=jnp.float32).astype(
            jnp.bfloat16
        )
    )
    page_keys, page_values, page_valid = kept_pages
    query_heads = head_split(query_low)
    scores = page_scores(query_heads, page_keys, page_valid)
    attn_probs = jnp.exp(scores - log_total)
    grad_probs = jnp.einsum(
        "pqhd,pkhd->phqk", grad_mixed, head_split(page_values), preferred_element_type=jnp.float32
    )
    row_delta = jnp.sum(attn_probs * grad_probs, axis=-1, keepdims=True)
    grad_scores = attn_probs * (grad_probs - row_delta)
    scores_low = grad_scores.astype(jnp.bfloat16)
    score_scale = HEAD_DIM ** (-0.5)
    grad_query = (
        jnp.einsum(
            "phqk,pkhd->pqhd", scores_low, head_split(page_keys), preferred_element_type=jnp.float32
        )
        * score_scale
    )
    page_count = query_low.shape[0]
    probs_low = attn_probs.astype(jnp.bfloat16)
    value_part = jnp.einsum(
        "phqk,pqhd->pkhd", probs_low, grad_mixed, preferred_element_type=jnp.float32
    )
    key_part = (
        jnp.einsum("phqk,pqhd->pkhd", scores_low, query_heads, preferred_element_type=jnp.float32)
        * score_scale
    )
    key_grad, value_grad = (
        lax.psum_scatter(
            key_part.reshape(page_count, -1, D).astype(jnp.bfloat16),
            "band",
            scatter_dimension=1,
            tiled=True,
        ).astype(jnp.float32),
        lax.psum_scatter(
            value_part.reshape(page_count, -1, D).astype(jnp.bfloat16),
            "band",
            scatter_dimension=1,
            tiled=True,
        ).astype(jnp.float32),
    )
    joint_low = jnp.concatenate(
        [grad_query.reshape(key_grad.shape), key_grad, value_grad], axis=-1
    ).astype(jnp.bfloat16)
    column_sums = jnp.sum(joint_low, axis=(0, 1), dtype=jnp.float32)
    grad_in_bias = jnp.stack([column_sums[:D], column_sums[2 * D :]])
    grad_rows = grad_attn_sum + jnp.einsum(
        "pce,de->pcd", joint_low, in_proj, preferred_element_type=jnp.float32
    )
    grad_in_proj, grad_out_proj, grad_up_proj, grad_down_proj = matrix_terms(
        (rows_low, mixed_low, first_low, act_low), (joint_low, branch_low, up_low, down_low)
    )
    layer_grads = (
        grad_in_proj,
        grad_in_bias,
        grad_out_proj,
        grad_out_shift,
        jnp.stack([gain_one, gain_two]),
        jnp.stack([shift_one, shift_two]),
        grad_up_proj,
        grad_up_shift,
        grad_down_proj,
        grad_down_shift,
    )
    return (grad_rows, layer_grads)


def body(
    hidden,
    boxes,
    page_size,
    band_count,
    layout_tables,
    attn_in,
    attn_bias,
    attn_out,
    out_bias,
    norm_gain,
    norm_bias,
    ffn_in,
    ffn_in_bias,
    ffn_out,
    ffn_out_bias,
    out_grad,
):
    box_index, live_mask = layout_index(boxes, page_size, band_count)
    local_pages = hidden.shape[0]
    batch_pages = local_pages // MICRO
    live_low = live_mask.astype(jnp.bfloat16)
    live_float = live_mask.astype(jnp.float32)[..., None]
    pick_rows = jnp.array(table_pick, dtype=jnp.int32)[:, None, None] * POS
    grad_totals = None
    outputs = []
    input_grads = []
    for batch_number in range(MICRO):
        gathered = (
            lax.all_gather(layout_tables, ("page", "band"), axis=1, tiled=True),
            lax.all_gather(attn_in, ("page", "band"), axis=1, tiled=True),
            lax.all_gather(attn_bias, ("page", "band"), axis=2, tiled=True),
            lax.all_gather(attn_out, ("page", "band"), axis=1, tiled=True),
            lax.all_gather(out_bias, ("page", "band"), axis=1, tiled=True),
            lax.all_gather(norm_gain, ("page", "band"), axis=2, tiled=True),
            lax.all_gather(norm_bias, ("page", "band"), axis=2, tiled=True),
            lax.all_gather(ffn_in, ("page", "band"), axis=1, tiled=True),
            lax.all_gather(ffn_in_bias, ("page", "band"), axis=1, tiled=True),
            lax.all_gather(ffn_out, ("page", "band"), axis=1, tiled=True),
            lax.all_gather(ffn_out_bias, ("page", "band"), axis=1, tiled=True),
        )
        first_page = batch_number * batch_pages
        batch_rows = slice(first_page, first_page + batch_pages)
        tables = gathered[0]
        batch_index = box_index[:, batch_rows]
        batch_live = live_low[batch_rows]
        embedded = hidden[batch_rows, 0].astype(jnp.float32)
        for lookup_number in range(6):
            embedded = embedded + tables[table_pick[lookup_number]][
                batch_index[lookup_number]
            ].astype(jnp.float32)
        layer_rows = embedded
        stored_layers = []
        for layer_number in range(LAYERS):
            weights = tuple((member[layer_number] for member in gathered[1:]))
            layer_rows, saved_state, kept_pages = layer_forward(layer_rows, batch_live, weights)
            stored_layers.append((saved_state, kept_pages))
        outputs.append(layer_rows * live_float[batch_rows])
        grad_rows = out_grad[batch_rows, 0].astype(jnp.float32) * live_float[batch_rows]
        layer_grads = [None] * LAYERS
        for layer_number in reversed(range(LAYERS)):
            weights = tuple((member[layer_number] for member in gathered[1:]))
            saved_state, kept_pages = stored_layers[layer_number]
            grad_rows, layer_grads[layer_number] = layer_backward(
                grad_rows, saved_state, kept_pages, weights
            )
        input_grads.append(grad_rows)
        flat_index = (pick_rows + batch_index).reshape(-1)
        repeated = jnp.broadcast_to(grad_rows[None], (6,) + grad_rows.shape).reshape(-1, D)
        table_grad = (
            jnp.zeros((4 * POS, D), jnp.float32).at[flat_index].add(repeated).reshape(4, POS, D)
        )
        stacked = tuple(
            (
                jnp.stack([layer_grads[layer_number][member] for layer_number in range(LAYERS)])
                for member in range(10)
            )
        )
        batch_grads = (table_grad,) + stacked
        if grad_totals is None:
            grad_totals = batch_grads
        else:
            grad_totals = jax.tree.map(jnp.add, grad_totals, batch_grads)
    matrix_shards = (
        lax.psum_scatter(
            grad_totals[1].astype(jnp.bfloat16), "page", scatter_dimension=1, tiled=True
        ).astype(jnp.float32),
        lax.psum_scatter(
            grad_totals[3].astype(jnp.bfloat16), "page", scatter_dimension=1, tiled=True
        ).astype(jnp.float32),
        lax.psum_scatter(
            grad_totals[7].astype(jnp.bfloat16), "page", scatter_dimension=1, tiled=True
        ).astype(jnp.float32),
        lax.psum_scatter(
            grad_totals[9].astype(jnp.bfloat16), "page", scatter_dimension=1, tiled=True
        ).astype(jnp.float32),
    )
    small_shards = (
        lax.psum_scatter(grad_totals[0], ("page", "band"), scatter_dimension=1, tiled=True),
        lax.psum_scatter(grad_totals[2], ("page", "band"), scatter_dimension=2, tiled=True),
        lax.psum_scatter(grad_totals[4], ("page", "band"), scatter_dimension=1, tiled=True),
        lax.psum_scatter(grad_totals[5], ("page", "band"), scatter_dimension=2, tiled=True),
        lax.psum_scatter(grad_totals[6], ("page", "band"), scatter_dimension=2, tiled=True),
        lax.psum_scatter(grad_totals[8], ("page", "band"), scatter_dimension=1, tiled=True),
        lax.psum_scatter(grad_totals[10], ("page", "band"), scatter_dimension=1, tiled=True),
    )
    output = jnp.concatenate(outputs, axis=0)[:, None]
    input_grad = jnp.concatenate(input_grads, axis=0)[:, None]
    return (
        output,
        input_grad,
        small_shards[0],
        matrix_shards[0],
        small_shards[1],
        matrix_shards[1],
        small_shards[2],
        small_shards[3],
        small_shards[4],
        matrix_shards[2],
        small_shards[5],
        matrix_shards[3],
        small_shards[6],
    )


def solution(mesh):
    placed = (
        P("page", "band", None, None),
        P(None, "page", "band", None),
        P(None, "page"),
        P("page", "band"),
        P(None, ("page", "band"), None),
        P(None, ("page", "band"), None),
        P(None, None, ("page", "band")),
        P(None, ("page", "band"), None),
        P(None, ("page", "band")),
        P(None, None, ("page", "band")),
        P(None, None, ("page", "band")),
        P(None, ("page", "band"), None),
        P(None, ("page", "band")),
        P(None, ("page", "band"), None),
        P(None, ("page", "band")),
        P("page", "band", None, None),
    )
    return jax.shard_map(
        body,
        mesh=mesh,
        in_specs=placed,
        out_specs=(
            P("page", "band", None, None),
            P("page", "band", None, None),
            P(None, ("page", "band"), None),
            P(None, ("page", "band"), None),
            P(None, None, ("page", "band")),
            P(None, ("page", "band"), None),
            P(None, ("page", "band")),
            P(None, None, ("page", "band")),
            P(None, None, ("page", "band")),
            P(None, ("page", "band"), None),
            P(None, ("page", "band")),
            P(None, ("page", "band"), None),
            P(None, ("page", "band")),
        ),
        check_vma=False,
    )
```

profile of v0, /device:TPU:0, one launch (start us, length us, event | category | flops | bytes accessed | tf_op | source)
XLA Modules:
  0.0 1644.8 jit_solution(16691743001634958131)
XLA Ops:
  10.6 43.4 %all-gather.14 = bf16[32,24,2]{1,2,0:T(2,128)(2,1)S(1)} all-gather(bf16[1,24,2]{1,2,0:T(2,128)(2,1)} %bitcast.1310), channel_id=1, replica_groups=mesh['page'=8,'band'=4] {'page','band'}, dimensions={0}, use_global_device_ids=true | all-gather | bytes 3168 | tf_op jit(solution)/shard_map/all_gather | solution.py:318
  54.1 37.0 %all-gather.13 = bf16[32,96,2]{1,2,0:T(2,128)(2,1)S(1)} all-gather(bf16[1,96,2]{1,2,0:T(2,128)(2,1)} %bitcast.1311), channel_id=1, replica_groups=mesh['page'=8,'band'=4] {'page','band'}, dimensions={0}, use_global_device_ids=true | all-gather | bytes 12672 | tf_op jit(solution)/shard_map/all_gather | solution.py:316
  91.2 37.8 %all-gather.12 = bf16[32,24,2]{1,2,0:T(2,128)(2,1)S(1)} all-gather(bf16[1,24,2]{1,2,0:T(2,128)(2,1)} %bitcast.1312), channel_id=1, replica_groups=mesh['page'=8,'band'=4] {'page','band'}, dimensions={0}, use_global_device_ids=true | all-gather | bytes 3168 | tf_op jit(solution)/shard_map/all_gather | solution.py:312
  142.3 38.1 %all_gather.126 = bf16[2,2,768]{1,0,2:T(2,128)(2,1)S(1)} all-gather(bf16[2,2,24]{1,0,2:T(2,128)(2,1)S(1)} %copy.249), channel_id=1, replica_groups=mesh['page'=8,'band'=4] {'page','band'}, dimensions={2}, use_global_device_ids=true | all-gather | bytes 6336 | tf_op jit(solution)/shard_map/all_gather | solution.py:310
  180.4 39.3 %all_gather.133 = bf16[2,2,768]{1,0,2:T(2,128)(2,1)S(1)} all-gather(bf16[2,2,24]{1,0,2:T(2,128)(2,1)S(1)} %copy.255), channel_id=1, replica_groups=mesh['page'=8,'band'=4] {'page','band'}, dimensions={2}, use_global_device_ids=true | all-gather | bytes 6336 | tf_op jit(solution)/shard_map/all_gather | solution.py:314
  219.7 38.9 %all_gather.132 = bf16[2,2,768]{1,0,2:T(2,128)(2,1)S(1)} all-gather(bf16[2,2,24]{1,0,2:T(2,128)(2,1)S(1)} %copy.254), channel_id=1, replica_groups=mesh['page'=8,'band'=4] {'page','band'}, dimensions={2}, use_global_device_ids=true | all-gather | bytes 6336 | tf_op jit(solution)/shard_map/all_gather | solution.py:313
  272.4 9.8 fusion.160
  282.2 10.5 fusion.163
  292.8 10.0 fusion.159
  340.9 8.8 all_gather.127
  350.2 12.7 all_gather.129
  363.2 13.7 all_gather.140
  378.8 8.8 all_gather.142
  401.7 8.2 multiply_convert_fusion.11
  414.4 8.2 multiply_convert_fusion.9
  428.8 9.1 all_gather.138
  441.8 10.7 all_gather.139
  462.2 9.2 all_gather.143
  475.4 9.7 all_gather.144
  494.0 8.9 multiply_convert_fusion.10
  599.0 6.4 slice_reduce_fusion
  617.9 6.9 reduce-scatter.50.cloned.1.call-done
  628.5 22.3 %reduce-scatter.48.cloned.1.call-done = bf16[128,768]{1,0:T(8,128)(2,1)} async-done(((bf16[512,768]{1,0:T(8,128)(2,1)}), bf16[128,768]{1,0:T(8,128)(2,1)}) %reduce-scatter.48.cloned.1.call-update) | async-done | bytes 196624
  742.2 9.0 reduce-scatter.52.cloned.1.call-done
  754.5 22.4 %reduce-scatter.62.cloned.1.call-done = bf16[128,768]{1,0:T(8,128)(2,1)} async-done(((bf16[512,768]{1,0:T(8,128)(2,1)}), bf16[128,768]{1,0:T(8,128)(2,1)}) %reduce-scatter.62.cloned.1.call-update) | async-done | bytes 196624
  778.5 25.0 %reduce-scatter.60.cloned.1.call-done = bf16[128,768]{1,0:T(8,128)(2,1)} async-done(((bf16[512,768]{1,0:T(8,128)(2,1)}), bf16[128,768]{1,0:T(8,128)(2,1)}) %reduce-scatter.60.cloned.1.call-update) | async-done | bytes 196624
  845.9 12.6 copy.503
  858.5 17.0 %reduce.200 = bf16[3072,128]{1,0:T(8,128)(2,1)S(1)} reduce(bf16[3072,1,128]{2,1,0:T(2,128)(2,1)S(1)} %bitcast.1114, bf16[]{:T(256)} %broadcast.1689), dimensions={1}, to_apply=%bitcast.1074.reduce_sub_computation | reduce | bytes 1572866
  881.4 12.6 copy.504
  894.0 17.0 %reduce.201 = bf16[3072,128]{1,0:T(8,128)(2,1)S(1)} reduce(bf16[3072,1,128]{2,1,0:T(2,128)(2,1)S(1)} %bitcast.1115, bf16[]{:T(256)} %broadcast.1689), dimensions={1}, to_apply=%bitcast.1075.reduce_sub_computation | reduce | bytes 1572866
  918.6 12.6 copy.501
  931.2 17.0 %reduce.202 = bf16[3072,128]{1,0:T(8,128)(2,1)S(1)} reduce(bf16[3072,1,128]{2,1,0:T(2,128)(2,1)S(1)} %bitcast.1116, bf16[]{:T(256)} %broadcast.1689), dimensions={1}, to_apply=%bitcast.1072.reduce_sub_computation | reduce | bytes 1572866
  949.3 12.6 copy.502
  961.9 17.2 %reduce.203 = bf16[3072,128]{1,0:T(8,128)(2,1)S(1)} reduce(bf16[3072,1,128]{2,1,0:T(2,128)(2,1)S(1)} %bitcast.1117, bf16[]{:T(256)} %broadcast.1689), dimensions={1}, to_apply=%bitcast.1073.reduce_sub_computation | reduce | bytes 1572866
  980.1 9.2 all-gather.1
  993.8 25.0 %all-gather.3 = bf16[512,768]{1,0:T(8,128)(2,1)S(1)} all-gather(bf16[128,768]{1,0:T(8,128)(2,1)S(1)} %copy-done.166), channel_id=5, replica_groups=mesh['page'=8,'band'=4] {'band'}, dimensions={0}, use_global_device_ids=true | all-gather | bytes 983040 | tf_op jit(solution)/shard_map/all_gather | solution.py:79
  1018.8 9.3 all-gather.9
  1032.4 27.3 %all-gather.11 = bf16[512,768]{1,0:T(8,128)(2,1)} all-gather(bf16[128,768]{1,0:T(8,128)(2,1)S(1)} %copy-done.162), channel_id=13, replica_groups=mesh['page'=8,'band'=4] {'band'}, dimensions={0}, use_global_device_ids=true | all-gather | bytes 983040 | tf_op jit(solution)/shard_map/all_gather | solution.py:81
  1083.6 9.0 all-gather
  1092.9 8.7 all-gather.2
  1104.7 8.7 all-gather.8
  1114.3 8.7 all-gather.10
  1262.4 17.2 %scatter_custom_fusion = f32[4096,768]{1,0:T(8,128)} fusion(s32[1536]{0:T(1024)S(1)} %add_reduce_fusion, f32[]{:T(128)} %constant.39.clone.1, f32[768,768]{1,0:T(8,128)S(1)} %bitcast.1089, f32[]{:T(128)} %constant.38.clone.1, f32[768,768]{1,0:T(8,128)} %bitcast.1090), kind=kCustom, calls=%fused_computation.13 | custom fusion | flops 2359296 | bytes 17301512 | tf_op jit(solution)/shard_map/add | solution.py:361
  1285.7 40.2 %all-reduce.5 = (f32[2,2,768]{2,1,0:T(2,128)S(1)}, f32[2,768]{1,0:T(2,128)S(1)}, f32[2,2,768]{2,1,0:T(2,128)S(1)}, f32[2,2,768]{2,1,0:T(2,128)S(1)}, f32[2,768]{1,0:T(2,128)S(1)}) all-reduce(f32[2,2,768]{2,1,0:T(2,128)S(1)} %maximum_add_fusion.5, ...), channel_id=24, replica_groups=mesh['page'=8,'band'=4] {'page','band'}, use_global_device_ids=true, to_apply=%region_59.61.clone | all-reduce | flops 12288 | bytes 98304
  1330.1 6.2 reduce-scatter.46.cloned.1.call-done
  1338.1 67.4 %reduce-scatter.64.cloned.1.call-done = bf16[24,4608]{1,0:T(8,128)(2,1)} async-done(((bf16[192,4608]{1,0:T(8,128)(2,1)}), bf16[24,4608]{1,0:T(8,128)(2,1)}) %reduce-scatter.64.cloned.1.call-update) | async-done | bytes 221200
  1407.3 69.6 %reduce-scatter.68.cloned.1.call-done = bf16[24,6144]{1,0:T(8,128)(2,1)} async-done(((bf16[192,6144]{1,0:T(8,128)(2,1)}), bf16[24,6144]{1,0:T(8,128)(2,1)}) %reduce-scatter.68.cloned.1.call-update) | async-done | bytes 294928
  1478.9 158.9 %reduce-scatter.44.cloned.1.call-done = f32[4,32,768]{2,1,0:T(8,128)} async-done(((f32[4,1024,768]{2,1,0:T(8,128)}), f32[4,32,768]{2,1,0:T(8,128)}) %reduce-scatter.44.cloned.1.call-update) | async-done | bytes 393232 | tf_op jit(solution)/shard_map/reduce_scatter | solution.py:377
  (1234 shorter events, 576.4 us)
Async XLA Ops:
  7.2 251.3 %copy-start.276 = (s32[2,2]{1,0:T(2,128)S(1)}, s32[2,2]{1,0:T(2,128)}, u32[]{:S(2)}) copy-start(s32[2,2]{1,0:T(2,128)} %param.21) | copy-start | bytes 52
  7.2 251.4 %copy-start.277 = (s32[4,2,1,128]{3,2,1,0:T(1,128)S(1)}, s32[4,2,1,128]{3,2,1,0:T(1,128)}, u32[]{:S(2)}) copy-start(s32[4,2,1,128]{3,2,1,0:T(1,128)} %param.20) | copy-start | bytes 12292
  7.2 296.3 %all-gather.29.cloned.1.call-start = ((), (), s32[]{:S(2)}) async-start(), calls=%async_computation.30 | async-start | bytes 6488064 | tf_op jit(solution)/shard_map/all_gather | solution.py:308
  7.9 325.5 %all-gather.31.cloned.1.call-start = ((), (), s32[]{:S(2)}) async-start(), calls=%async_computation.31 | async-start | bytes 7299072 | tf_op jit(solution)/shard_map/all_gather | solution.py:309
  8.7 383.8 %all-gather.33.cloned.1.call-start = ((), (), s32[]{:S(2)}) async-start(), calls=%async_computation.32 | async-start | bytes 2433024 | tf_op jit(solution)/shard_map/all_gather | solution.py:311
  9.4 392.3 %all-gather.35.cloned.1.call-start = ((), (), s32[]{:S(2)}) async-start(), calls=%async_computation.33 | async-start | bytes 9732096 | tf_op jit(solution)/shard_map/all_gather | solution.py:315
  10.0 400.0 %all-gather.37.cloned.1.call-start = ((), (), s32[]{:S(2)}) async-start(), calls=%async_computation.34 | async-start | bytes 9732096 | tf_op jit(solution)/shard_map/all_gather | solution.py:317
  10.6 599.9 %reduce-scatter.58.cloned.1.call-start = ((), (), s32[]{:S(2)}) async-start(), calls=%async_computation.50 | async-start | bytes 983040
  265.3 127.2 %copy-start.194 = (f32[768]{0:T(1024)}, f32[768]{0:T(1024)S(1)}, u32[]{:S(2)}) copy-start(f32[768]{0:T(1024)S(1)} %get-tuple-element.111) | copy-start | bytes 9220
  282.2 142.1 %copy-start.185 = (f32[768]{0:T(1024)}, f32[768]{0:T(1024)S(1)}, u32[]{:S(2)}) copy-start(f32[768]{0:T(1024)S(1)} %get-tuple-element.98) | copy-start | bytes 9220
  302.8 121.5 %copy-start.188 = (f32[768]{0:T(1024)}, f32[768]{0:T(1024)S(1)}, u32[]{:S(2)}) copy-start(f32[768]{0:T(1024)S(1)} %get-tuple-element.102) | copy-start | bytes 9220
  552.2 62.0 %reduce-scatter.56.cloned.1.call-start = ((), (), s32[]{:S(2)}) async-start(), calls=%async_computation.49 | async-start | bytes 983040
  566.1 58.7 %reduce-scatter.50.cloned.1.call-start = ((), (), s32[]{:S(2)}) async-start(), calls=%async_computation.46 | async-start | bytes 983040
  584.6 66.2 %reduce-scatter.48.cloned.1.call-start = ((), (), s32[]{:S(2)}) async-start(), calls=%async_computation.45 | async-start | bytes 983040
  598.9 141.7 %reduce-scatter.54.cloned.1.call-start = ((), (), s32[]{:S(2)}) async-start(), calls=%async_computation.48 | async-start | bytes 983040
  701.8 49.4 %reduce-scatter.52.cloned.1.call-start = ((), (), s32[]{:S(2)}) async-start(), calls=%async_computation.47 | async-start | bytes 983040
  715.9 61.1 %reduce-scatter.62.cloned.1.call-start = ((), (), s32[]{:S(2)}) async-start(), calls=%async_computation.52 | async-start | bytes 983040
  729.0 74.5 %reduce-scatter.60.cloned.1.call-start = ((), (), s32[]{:S(2)}) async-start(), calls=%async_computation.51 | async-start | bytes 983040
  736.3 441.2 %all-gather.41.cloned.1.call-start = ((), (), s32[]{:S(2)}) async-start(), calls=%async_computation.37 | async-start | bytes 2949120 | tf_op jit(solution)/shard_map/all_gather | solution.py:78
  738.2 441.9 %all-gather.45.cloned.1.call-start = ((), (), s32[]{:S(2)}) async-start(), calls=%async_computation.39 | async-start | bytes 2949120 | tf_op jit(solution)/shard_map/all_gather | solution.py:78
  739.8 443.1 %all-gather.39.cloned.1.call-start = ((), (), s32[]{:S(2)}) async-start(), calls=%async_computation.36 | async-start | bytes 2949120 | tf_op jit(solution)/shard_map/all_gather | solution.py:78
  753.7 433.1 %all-gather.43.cloned.1.call-start = ((), (), s32[]{:S(2)}) async-start(), calls=%async_computation.38 | async-start | bytes 2949120 | tf_op jit(solution)/shard_map/all_gather | solution.py:78
  806.6 426.1 %all-gather.49.cloned.1.call-start = ((), (), s32[]{:S(2)}) async-start(), calls=%async_computation.42 | async-start | bytes 3932160 | tf_op jit(solution)/shard_map/all_gather | solution.py:80
  807.2 428.2 %all-gather.53.cloned.1.call-start = ((), (), s32[]{:S(2)}) async-start(), calls=%async_computation.44 | async-start | bytes 3932160 | tf_op jit(solution)/shard_map/all_gather | solution.py:80
  808.0 431.6 %all-gather.47.cloned.1.call-start = ((), (), s32[]{:S(2)}) async-start(), calls=%async_computation.41 | async-start | bytes 3932160 | tf_op jit(solution)/shard_map/all_gather | solution.py:80
  808.6 435.2 %all-gather.51.cloned.1.call-start = ((), (), s32[]{:S(2)}) async-start(), calls=%async_computation.43 | async-start | bytes 3932160 | tf_op jit(solution)/shard_map/all_gather | solution.py:80
  812.7 11.1 all-to-all-start.4
  823.8 8.9 all-to-all-start.6
  832.7 8.7 all-to-all-start.5
  842.1 34.4 %all-to-all-start.7 = ((bf16[4,2,12288]{2,1,0:T(2,128)(2,1)}), bf16[4,2,12288]{2,1,0:T(2,128)(2,1)S(1)}, u32[]{:S(2)}, u32[]{:S(2)}) async-start(bf16[4,2,12288]{2,1,0:T(2,128)(2,1)} %reshape.3886), calls=%async_computation.8 | async-start | bytes 393216 | tf_op jit(solution)/shard_map/all_to_all | solution.py:73
  877.1 34.8 %all-to-all-start.13 = ((bf16[4,2,49152]{2,1,0:T(2,128)(2,1)}), bf16[4,2,49152]{2,1,0:T(2,128)(2,1)S(1)}, u32[]{:S(2)}, u32[]{:S(2)}) async-start(bf16[4,2,49152]{2,1,0:T(2,128)(2,1)} %reshape.3898), calls=%async_computation.14 | async-start | bytes 1572864 | tf_op jit(solution)/shard_map/all_to_all | solution.py:75
  911.9 77.4 %all-to-all-start.12 = ((bf16[4,2,49152]{2,1,0:T(2,128)(2,1)}), bf16[4,2,49152]{2,1,0:T(2,128)(2,1)}, u32[]{:S(2)}, u32[]{:S(2)}) async-start(bf16[4,2,49152]{2,1,0:T(2,128)(2,1)} %reshape.3900), calls=%async_computation.13 | async-start | bytes 1572864 | tf_op jit(solution)/shard_map/all_to_all | solution.py:75
  989.3 38.8 %all-to-all-start.15 = ((bf16[4,2,49152]{2,1,0:T(2,128)(2,1)}), bf16[4,2,49152]{2,1,0:T(2,128)(2,1)S(1)}, u32[]{:S(2)}, u32[]{:S(2)}) async-start(bf16[4,2,49152]{2,1,0:T(2,128)(2,1)} %reshape.3902), calls=%async_computation.16 | async-start | bytes 1572864 | tf_op jit(solution)/shard_map/all_to_all | solution.py:75
  1028.1 44.1 %all-to-all-start.14 = ((bf16[4,2,49152]{2,1,0:T(2,128)(2,1)}), bf16[4,2,49152]{2,1,0:T(2,128)(2,1)}, u32[]{:S(2)}, u32[]{:S(2)}) async-start(bf16[4,2,49152]{2,1,0:T(2,128)(2,1)} %reshape.3904), calls=%async_computation.15 | async-start | bytes 1572864 | tf_op jit(solution)/shard_map/all_to_all | solution.py:75
  1032.3 250.2 %reduce-scatter.70.cloned.1.call-start = ((), (), s32[]{:S(2)}) async-start(), calls=%async_computation.56 | async-start | bytes 1622016
  1102.0 182.0 %reduce-scatter.66.cloned.1.call-start = ((), (), s32[]{:S(2)}) async-start(), calls=%async_computation.54 | async-start | bytes 663552
  1104.6 231.7 %reduce-scatter.46.cloned.1.call-start = ((), (), s32[]{:S(2)}) async-start(), calls=%async_computation.40 | async-start | bytes 2654208 | tf_op jit(solution)/shard_map/reduce_scatter | solution.py:372
  1141.4 8.7 all-to-all-start
  1150.0 8.7 all-to-all-start.2
  1158.7 9.1 all-to-all-start.1
  1167.8 8.7 all-to-all-start.3
  1171.1 234.3 %reduce-scatter.64.cloned.1.call-start = ((), (), s32[]{:S(2)}) async-start(), calls=%async_computation.53 | async-start | bytes 1990656
  1197.3 8.8 all-to-all-start.8
  1206.1 8.8 all-to-all-start.10
  1214.9 8.7 all-to-all-start.9
  1223.6 8.7 all-to-all-start.11
  1227.0 249.9 %reduce-scatter.68.cloned.1.call-start = ((), (), s32[]{:S(2)}) async-start(), calls=%async_computation.55 | async-start | bytes 2654208
  1252.6 385.1 %reduce-scatter.44.cloned.1.call-start = ((), (), s32[]{:S(2)}) async-start(), calls=%async_computation.35 | async-start | bytes 12976128 | tf_op jit(solution)/shard_map/reduce_scatter | solution.py:377
  (324 other events, 1613.1 us)
Sparse Core Ops, SparseCore 0:
  11.0 72.3 all-gather.28
  86.2 73.6 all-gather.30
  162.7 55.2 all-gather.32
  220.7 81.5 all-gather.34
  304.9 89.6 all-gather.36
  552.4 20.5 reduce-scatter.57
  575.6 23.2 reduce-scatter.55
  601.5 23.2 reduce-scatter.49
  627.5 23.2 reduce-scatter.47
  701.9 23.2 reduce-scatter.53
  727.9 23.2 reduce-scatter.51
  753.6 23.2 reduce-scatter.61
  780.2 23.2 reduce-scatter.59
  805.5 26.4 all-gather.40
  833.4 26.4 all-gather.44
  861.9 24.6 all-gather.38
  888.0 24.6 all-gather.42
  914.2 32.4 all-gather.48
  948.2 28.5 all-gather.52
  978.2 36.4 all-gather.46
  1016.3 41.2 all-gather.50
  1102.1 97.1 reduce-scatter.69
  1203.2 61.1 reduce-scatter.65
  1268.1 68.1 reduce-scatter.45
  1340.1 65.2 reduce-scatter.63
  1408.8 67.9 reduce-scatter.67
  1483.3 154.4 reduce-scatter.43
where the time goes:
time: 1650 us; the launch traced here: 1640 us
  blocking collectives  473 us (29%)
  waiting for transfers between devices  423 us (26%)
  local copies, waits for them, and re-layouts  284 us (17%)
  other arithmetic  192 us (12%)
  matrix products  192 us (12%)
  starting transfers between devices  60.1 us (4%)
  between operations  19.9 us (1%)
    unnamed x39, waiting for transfers between devices  228 us
    reduce_scatter x1, waiting for transfers between devices, body(): lax.psum_scatter(grad_totals[0], ('page', 'band'), scatter_dimension=1, t...  159 us
    unnamed x761, local copies, waits for them, and re-layouts  144 us
    unnamed x27, other arithmetic  92.4 us
    all_gather x4, blocking collectives, matrix_terms(): lax.all_gather(right_parts[3], 'band', axis=1, tiled=True)  54 us
    reshape x16, local copies, waits for them, and re-layouts, owner_order(): return jnp.swapaxes(grouped, -3, -2).reshape(leading + (-1,))  54 us
    all_gather x4, blocking collectives, matrix_terms(): lax.all_gather(right_parts[1], 'band', axis=1, tiled=True)  52 us
    all_gather x1, blocking collectives, body(): lax.all_gather(ffn_out_bias, ('page', 'band'), axis=1, tiled=True)  43.4 us
  transfers between devices with their start and end apart: 43, of which 20 were waited for; matrix products, arithmetic and copies ran while one was open for 30% of the time, Pallas kernels for 0%

commit v1 on v0

v1 whole, which is shorter than its diff:
```python
import functools

import jax
import jax.numpy as jnp
from jax import lax
from jax.experimental import pallas as pl
from jax.experimental.pallas import tpu as pltpu
from jax.sharding import PartitionSpec as P

D = 768
HEADS = 12
HEAD_DIM = 64
HALF = D // 2
PAIRS = HEADS // 4
FF = 3072
POS = 1024
GRID = 1000
LAYERS = 2
CORES = 2
LANES = 128
EPS = 1e-12
DEAD = -1000000000.0
SCALE = HEAD_DIM ** (-0.5)
VMEM = 40 * 1024 * 1024
F32 = jnp.float32
BF16 = jnp.bfloat16

ROW_ATTN, ROW_OUT, ROW_GAIN, ROW_SHIFT, ROW_DOWN = 0, 4, 6, 10, 14
SMALL_ROWS = 16


def dot(a, b, dims=((1,), (0,))):
    return lax.dot_general(a, b, (dims, ((), ())), preferred_element_type=F32)


NT = ((1,), (1,))
TN = ((0,), (0,))


def sds(shape, dtype):
    return jax.ShapeDtypeStruct(shape, dtype)


def whole(shape):
    return pl.BlockSpec(shape, lambda *_: (0,) * len(shape))


def cost(flops, nbytes, trans=0):
    return pl.CostEstimate(flops=flops, bytes_accessed=nbytes, transcendentals=trans)


def params():
    return pltpu.CompilerParams(vmem_limit_bytes=VMEM)


def embed_kernel(idx, t0, t1, t2, t3, out):
    rows = t0.shape[0]
    place = lax.broadcasted_iota(jnp.int32, (idx.shape[0], rows), 1)

    def hot(*cols):
        total = None
        for col in cols:
            one = jnp.where(place == idx[:, col : col + 1], 1.0, 0.0)
            total = one if total is None else total + one
        return total.astype(BF16)

    out[...] = (
        dot(hot(0, 2), t0[...])
        + dot(hot(1, 3), t1[...])
        + dot(hot(4), t2[...])
        + dot(hot(5), t3[...])
    )


def embed(idx, tables):
    tokens = idx.shape[0]
    block = 128
    rows = tables[0].shape[0]
    return pl.pallas_call(
        embed_kernel,
        name="embed",
        out_shape=sds((tokens, D), F32),
        grid=(tokens // block,),
        in_specs=[pl.BlockSpec((block, 8), lambda i: (i, 0))] + [whole((rows, D))] * 4,
        out_specs=pl.BlockSpec((block, D), lambda i: (i, 0)),
        compiler_params=params(),
        cost_estimate=cost(8 * tokens * rows * D, 8 * rows * D + 4 * tokens * D),
    )(idx, *tables)


def table_kernel(idx, own, sib, o0, o1, o2, o3):
    half = own.shape[0]
    block = o0.shape[0]
    first = pl.program_id(0) * block
    place = lax.broadcasted_iota(jnp.int32, (block, 2 * half), 0) + first

    def hot(*rows):
        total = None
        for row in rows:
            one = jnp.where(place == idx[row : row + 1, :], 1.0, 0.0)
            total = one if total is None else total + one
        return total.astype(BF16)

    for out, rows in ((o0, (0, 2)), (o1, (1, 3)), (o2, (4,)), (o3, (5,))):
        mark = hot(*rows)
        out[...] = (dot(mark[:, :half], own[...]) + dot(mark[:, half:], sib[...])).astype(BF16)


def table_grads(idx, own, sib, rows):
    half = own.shape[0]
    block = 256
    return pl.pallas_call(
        table_kernel,
        name="table_grads",
        out_shape=[sds((rows, D), BF16)] * 4,
        grid=(rows // block,),
        in_specs=[whole((8, 2 * half)), whole((half, D)), whole((half, D))],
        out_specs=[pl.BlockSpec((block, D), lambda i: (i, 0))] * 4,
        compiler_params=params(),
        cost_estimate=cost(16 * half * rows * D, 8 * rows * D),
    )(idx, own, sib)


def attn_fwd_kernel(core, xo, xs, wq, wk, wv, small, mask, q, k, v, mo, ms, *, layer):
    half = xo.shape[0]
    for first, rows in ((0, xo), (half, xs)):
        x = rows[...]
        q[first : first + half, :] = (
            dot(x, wq[...]) + small[ROW_ATTN + 2 * layer : ROW_ATTN + 2 * layer + 1, :]
        ).astype(BF16)
        k[first : first + half, :] = dot(x, wk[...]).astype(BF16)
        v[first : first + half, :] = (
            dot(x, wv[...]) + small[ROW_ATTN + 2 * layer + 1 : ROW_ATTN + 2 * layer + 2, :]
        ).astype(BF16)
    keys, values = k[...], v[...]
    low_lanes = lax.broadcasted_iota(jnp.int32, (1, LANES), 1) < HEAD_DIM
    for first, out in ((0, mo), (half, ms)):
        queries = q[first : first + half, :].astype(F32) * SCALE
        parts = []
        for head in range(2):
            lanes = low_lanes if head == 0 else jnp.logical_not(low_lanes)
            one = jnp.where(lanes, queries, 0.0).astype(BF16)
            scores = dot(one, keys, NT) + mask[...]
            expo = jnp.exp(scores - jnp.max(scores, axis=-1, keepdims=True))
            total = jnp.sum(expo, axis=-1, keepdims=True)
            parts.append(dot(expo.astype(BF16), values) / total)
        out[...] = jnp.where(low_lanes, parts[0], parts[1]).astype(BF16)


def attn_fwd(core, xo, xs, wq, wk, wv, small, mask, layer):
    half = xo.shape[0]
    tokens = 2 * half
    col = lambda p, core: (0, p)
    weight = pl.BlockSpec((D, LANES), col)
    rows = pl.BlockSpec((tokens, LANES), col)
    return pl.pallas_call(
        functools.partial(attn_fwd_kernel, layer=layer),
        name="attn_fwd",
        out_shape=[sds((tokens, HALF), BF16)] * 3 + [sds((half, HALF), BF16)] * 2,
        grid_spec=pltpu.PrefetchScalarGridSpec(
            num_scalar_prefetch=1,
            grid=(PAIRS,),
            in_specs=[
                whole((half, D)),
                whole((half, D)),
                weight,
                weight,
                weight,
                pl.BlockSpec((SMALL_ROWS, LANES), lambda p, core: (0, core[0] * PAIRS + p)),
                whole((1, tokens)),
            ],
            out_specs=[rows] * 3 + [pl.BlockSpec((half, LANES), col)] * 2,
        ),
        compiler_params=params(),
        cost_estimate=cost(
            2 * tokens * D * 3 * HALF + 4 * PAIRS * 2 * tokens * tokens * LANES,
            2 * (tokens * D + 3 * D * HALF + 4 * tokens * HALF),
            PAIRS * 2 * tokens * tokens,
        ),
    )(core, xo, xs, wq, wk, wv, small, mask)


def attn_bwd_kernel(
    core, dao, das, wo, q, k, v, mo, ms, xo, xs, wq, wk, wv, mask,
    dwq, dwk, dwv, dwo, sums, dxo, dxs, acc, dq_s, dk_s, dv_s,
):
    half = xo.shape[0]
    step = pl.program_id(0)
    keys, values = k[...], v[...]
    low_lanes = lax.broadcasted_iota(jnp.int32, (1, LANES), 1) < HEAD_DIM
    grad_keys = [None, None]
    grad_values = [None, None]
    for part, da in ((0, dao), (1, das)):
        first = part * half
        span = slice(first, first + half)
        grad_mix = dot(da[...], wo[...], NT)
        queries = q[span, :].astype(F32) * SCALE
        grad_queries = []
        for head in range(2):
            lanes = low_lanes if head == 0 else jnp.logical_not(low_lanes)
            one = jnp.where(lanes, queries, 0.0).astype(BF16)
            scores = dot(one, keys, NT) + mask[...]
            expo = jnp.exp(scores - jnp.max(scores, axis=-1, keepdims=True))
            probs = expo * (1.0 / jnp.sum(expo, axis=-1, keepdims=True))
            grad_one = jnp.where(lanes, grad_mix, 0.0).astype(BF16)
            grad_probs = dot(grad_one, values, NT)
            weighted = probs * grad_probs
            delta = jnp.sum(weighted, axis=-1, keepdims=True)
            grad_scores = (weighted - probs * delta).astype(BF16)
            grad_queries.append(dot(grad_scores, keys))
            key_part = dot(grad_scores, one, TN)
            value_part = dot(probs.astype(BF16), grad_one, TN)
            if part == 0:
                grad_keys[head], grad_values[head] = key_part, value_part
            else:
                grad_keys[head] = grad_keys[head] + key_part
                grad_values[head] = grad_values[head] + value_part
        dq_s[span, :] = (jnp.where(low_lanes, grad_queries[0], grad_queries[1]) * SCALE).astype(BF16)
    dk_s[...] = (grad_keys[0] + grad_keys[1]).astype(BF16)
    dv_s[...] = (grad_values[0] + grad_values[1]).astype(BF16)
    sums[...] = jnp.zeros_like(sums)
    sums[0:1, :] = jnp.sum(dq_s[...].astype(F32), axis=0, keepdims=True)
    sums[1:2, :] = jnp.sum(dv_s[...].astype(F32), axis=0, keepdims=True)
    for out, grad in ((dwq, dq_s), (dwk, dk_s), (dwv, dv_s)):
        out[...] = (dot(xo[...], grad[:half, :], TN) + dot(xs[...], grad[half:, :], TN)).astype(BF16)
    out_rows = dot(mo[...], dao[...], TN) + dot(ms[...], das[...], TN)
    dwo[0] = out_rows[:, :HALF].astype(BF16)
    dwo[1] = out_rows[:, HALF:].astype(BF16)
    total = dot(dq_s[...], wq[...], NT) + dot(dk_s[...], wk[...], NT) + dot(dv_s[...], wv[...], NT)

    @pl.when(step == 0)
    def _():
        acc[...] = total

    @pl.when(step > 0)
    def _():
        acc[...] += total

    @pl.when(step == PAIRS - 1)
    def _():
        dxo[...] = acc[:half, :]
        dxs[...] = acc[half:, :].astype(BF16)


def attn_bwd(core, dao, das, wo, q, k, v, mo, ms, xo, xs, wq, wk, wv, mask):
    half = xo.shape[0]
    tokens = 2 * half
    col = lambda p, core: (0, p)
    weight = pl.BlockSpec((D, LANES), col)
    rows = pl.BlockSpec((tokens, LANES), col)
    part = pl.BlockSpec((half, LANES), col)
    return pl.pallas_call(
        attn_bwd_kernel,
        name="attn_bwd",
        out_shape=[sds((D, HALF), BF16)] * 3
        + [
            sds((CORES, HALF, HALF), BF16),
            sds((8, HALF), F32),
            sds((half, D), F32),
            sds((half, D), BF16),
        ],
        grid_spec=pltpu.PrefetchScalarGridSpec(
            num_scalar_prefetch=1,
            grid=(PAIRS,),
            in_specs=[
                whole((half, D)),
                whole((half, D)),
                pl.BlockSpec((LANES, D), lambda p, core: (core[0] * PAIRS + p, 0)),
                rows,
                rows,
                rows,
                part,
                part,
                whole((half, D)),
                whole((half, D)),
                weight,
                weight,
                weight,
                whole((1, tokens)),
            ],
            out_specs=[weight] * 3
            + [
                pl.BlockSpec((CORES, LANES, HALF), lambda p, core: (0, p, 0)),
                pl.BlockSpec((8, LANES), col),
                whole((half, D)),
                whole((half, D)),
            ],
            scratch_shapes=[pltpu.VMEM((tokens, D), F32)] + [pltpu.VMEM((tokens, LANES), BF16)] * 3,
        ),
        compiler_params=params(),
        cost_estimate=cost(
            8 * tokens * D * 3 * HALF // 2 + 10 * PAIRS * 2 * tokens * tokens * LANES,
            2 * (4 * tokens * D + 8 * D * HALF + 4 * tokens * HALF),
            PAIRS * 2 * tokens * tokens,
        ),
    )(core, dao, das, wo, q, k, v, mo, ms, xo, xs, wq, wk, wv, mask)


def norm_rows(h, gain, shift, y, yb, n, rstd):
    mean = jnp.mean(h, axis=-1, keepdims=True)
    centred = h - mean
    scale = lax.rsqrt(jnp.mean(centred * centred, axis=-1, keepdims=True) + EPS)
    normal = centred * scale
    out = normal * gain + shift
    y[...] = out
    yb[...] = out.astype(BF16)
    n[...] = normal
    rstd[...] = scale


def norm_outs(half):
    return [sds((half, D), F32), sds((half, D), BF16), sds((half, D), F32), sds((half, 1), F32)]


def out_norm_kernel(core, mine, theirs, wo, base, small, y, yb, n, rstd, *, layer):
    first = core[0] * HALF
    mine_rows = pl.ds(pl.multiple_of(first, HALF), HALF)
    their_rows = pl.ds(pl.multiple_of(HALF - first, HALF), HALF)
    h = (
        base[...]
        + dot(mine[...], wo[mine_rows, :])
        + dot(theirs[...], wo[their_rows, :])
        + small[ROW_OUT + layer : ROW_OUT + layer + 1, :]
    )
    row = 2 * layer
    norm_rows(
        h, small[ROW_GAIN + row : ROW_GAIN + row + 1, :], small[ROW_SHIFT + row : ROW_SHIFT + row + 1, :],
        y, yb, n, rstd,
    )


def out_norm(core, mine, theirs, wo, base, small, layer):
    half = base.shape[0]
    return pl.pallas_call(
        functools.partial(out_norm_kernel, layer=layer),
        name="out_norm",
        out_shape=norm_outs(half),
        in_specs=[pl.BlockSpec(memory_space=pltpu.SMEM)] + [pl.BlockSpec(memory_space=pltpu.VMEM)] * 5,
        out_specs=[pl.BlockSpec(memory_space=pltpu.VMEM)] * 4,
        compiler_params=params(),
        cost_estimate=cost(2 * half * D * D, 2 * D * D + 16 * half * D),
    )(core, mine, theirs, wo, base, small)


def add_norm_kernel(base, part, recv, small, y, yb, n, rstd, *, layer):
    h = base[...] + part[...] + recv[...].astype(F32) + small[ROW_DOWN + layer : ROW_DOWN + layer + 1, :]
    row = 2 * layer + 1
    norm_rows(
        h, small[ROW_GAIN + row : ROW_GAIN + row + 1, :], small[ROW_SHIFT + row : ROW_SHIFT + row + 1, :],
        y, yb, n, rstd,
    )


def add_norm(base, part, recv, small, layer):
    half = base.shape[0]
    return pl.pallas_call(
        functools.partial(add_norm_kernel, layer=layer),
        name="add_norm",
        out_shape=norm_outs(half),
        in_specs=[pl.BlockSpec(memory_space=pltpu.VMEM)] * 4,
        out_specs=[pl.BlockSpec(memory_space=pltpu.VMEM)] * 4,
        compiler_params=params(),
        cost_estimate=cost(20 * half * D, 20 * half * D),
    )(base, part, recv, small)


def norm_bwd_kernel(*refs, row, summed):
    if summed:
        base, part, recv, n, rstd, small, gh, ghb, sums = refs
        gz = base[...] + part[...] + recv[...].astype(F32)
    else:
        base, live, n, rstd, small, gh, ghb, sums = refs
        gz = base[...].astype(F32) * live[...]
    normal = n[...]
    e = gz * small[ROW_GAIN + row : ROW_GAIN + row + 1, :]
    mean = jnp.mean(e, axis=-1, keepdims=True)
    slope = jnp.mean(e * normal, axis=-1, keepdims=True)
    grad = (e - mean - normal * slope) * rstd[...]
    low = grad.astype(BF16)
    gh[...] = grad
    ghb[...] = low
    sums[...] = jnp.zeros_like(sums)
    sums[0:1, :] = jnp.sum(gz * normal, axis=0, keepdims=True)
    sums[1:2, :] = jnp.sum(gz, axis=0, keepdims=True)
    sums[2:3, :] = jnp.sum(low.astype(F32), axis=0, keepdims=True)


def norm_bwd(sources, n, rstd, small, row):
    half = n.shape[0]
    operands = tuple(sources) + (n, rstd, small)
    return pl.pallas_call(
        functools.partial(norm_bwd_kernel, row=row, summed=len(sources) == 3),
        name="norm_bwd",
        out_shape=[sds((half, D), F32), sds((half, D), BF16), sds((8, D), F32)],
        in_specs=[pl.BlockSpec(memory_space=pltpu.VMEM)] * len(operands),
        out_specs=[pl.BlockSpec(memory_space=pltpu.VMEM)] * 3,
        compiler_params=params(),
        cost_estimate=cost(20 * half * D, 20 * half * D),
    )(*operands)


FF_BLOCK = 256
FF_STEPS = FF // CORES // FF_BLOCK
UNIT_STEPS = FF_STEPS // 2


def first_unit(j):
    return jnp.minimum(j, UNIT_STEPS - 1)


def second_unit(j):
    return jnp.maximum(j - UNIT_STEPS, 0)


def ffn_fwd_kernel(yo, ys, w1a, w1b, bias, w2a, w2b, act, slope, po, ps, acc, *, layer):
    half = yo.shape[0]
    j = pl.program_id(0)
    early = j < UNIT_STEPS
    w1 = jnp.where(early, w1a[...], w1b[...])
    w2 = jnp.where(early, w2a[...], w2b[...])
    for first, rows in ((0, yo), (half, ys)):
        span = slice(first, first + half)
        up = dot(rows[...], w1) + bias[layer : layer + 1, :]
        cdf = 0.5 * (1.0 + lax.erf(up * (2.0**-0.5)))
        low = (up * cdf).astype(BF16)
        act[span, :] = low
        slope[span, :] = (cdf + up * (jnp.exp(-0.5 * up * up) * 0.3989422804014327)).astype(BF16)
        total = dot(low, w2)

        @pl.when(j == 0)
        def _():
            acc[span, :] = total

        @pl.when(j > 0)
        def _():
            acc[span, :] += total

    @pl.when(j == FF_STEPS - 1)
    def _():
        po[...] = acc[:half, :]
        ps[...] = acc[half:, :].astype(BF16)


def ffn_fwd(yo, ys, w1a, w1b, bias, w2a, w2b, layer):
    half = yo.shape[0]
    tokens = 2 * half
    width = FF // CORES
    return pl.pallas_call(
        functools.partial(ffn_fwd_kernel, layer=layer),
        name="ffn_fwd",
        out_shape=[sds((tokens, width), BF16)] * 2 + [sds((half, D), F32), sds((half, D), BF16)],
        grid=(FF_STEPS,),
        in_specs=[
            whole((half, D)),
            whole((half, D)),
            pl.BlockSpec((D, FF_BLOCK), lambda j: (0, first_unit(j))),
            pl.BlockSpec((D, FF_BLOCK), lambda j: (0, second_unit(j))),
            pl.BlockSpec((LAYERS, FF_BLOCK), lambda j: (0, j)),
            pl.BlockSpec((FF_BLOCK, D), lambda j: (first_unit(j), 0)),
            pl.BlockSpec((FF_BLOCK, D), lambda j: (second_unit(j), 0)),
        ],
        out_specs=[pl.BlockSpec((tokens, FF_BLOCK), lambda j: (0, j))] * 2 + [whole((half, D))] * 2,
        scratch_shapes=[pltpu.VMEM((tokens, D), F32)],
        compiler_params=params(),
        cost_estimate=cost(4 * tokens * D * width, 4 * D * width + 4 * tokens * width, tokens * width),
    )(yo, ys, w1a, w1b, bias, w2a, w2b)


def ffn_bwd_kernel(
    dfo, dfs, w1a, w1b, w2a, w2b, act, slope, yo, ys, dw1a, dw1b, dw2a, dw2b, sums, po, ps, acc, du
):
    half = yo.shape[0]
    j = pl.program_id(0)
    early = j < UNIT_STEPS
    w1 = jnp.where(early, w1a[...], w1b[...])
    w2 = jnp.where(early, w2a[...], w2b[...])
    for first, rows in ((0, dfo), (half, dfs)):
        span = slice(first, first + half)
        low = (slope[span, :].astype(F32) * dot(rows[...], w2, NT)).astype(BF16)
        du[span, :] = low
        total = dot(low, w1, NT)

        @pl.when(j == 0)
        def _():
            acc[span, :] = total

        @pl.when(j > 0)
        def _():
            acc[span, :] += total

    sums[...] = jnp.zeros_like(sums)
    sums[0:1, :] = jnp.sum(du[...].astype(F32), axis=0, keepdims=True)
    grad1 = (dot(yo[...], du[:half, :], TN) + dot(ys[...], du[half:, :], TN)).astype(BF16)
    grad2 = (dot(act[:half, :], dfo[...], TN) + dot(act[half:, :], dfs[...], TN)).astype(BF16)

    @pl.when(early)
    def _():
        dw1a[...] = grad1
        dw2a[...] = grad2

    @pl.when(jnp.logical_not(early))
    def _():
        dw1b[...] = grad1
        dw2b[...] = grad2

    @pl.when(j == FF_STEPS - 1)
    def _():
        po[...] = acc[:half, :]
        ps[...] = acc[half:, :].astype(BF16)


def ffn_bwd(dfo, dfs, w1a, w1b, w2a, w2b, act, slope, yo, ys):
    half = yo.shape[0]
    tokens = 2 * half
    width = FF // CORES
    col_a = pl.BlockSpec((D, FF_BLOCK), lambda j: (0, first_unit(j)))
    col_b = pl.BlockSpec((D, FF_BLOCK), lambda j: (0, second_unit(j)))
    row_a = pl.BlockSpec((FF_BLOCK, D), lambda j: (first_unit(j), 0))
    row_b = pl.BlockSpec((FF_BLOCK, D), lambda j: (second_unit(j), 0))
    rows = pl.BlockSpec((tokens, FF_BLOCK), lambda j: (0, j))
    return pl.pallas_call(
        ffn_bwd_kernel,
        name="ffn_bwd",
        out_shape=[sds((D, width // 2), BF16)] * 2
        + [sds((width // 2, D), BF16)] * 2
        + [sds((8, width), F32), sds((half, D), F32), sds((half, D), BF16)],
        grid=(FF_STEPS,),
        in_specs=[whole((half, D))] * 2 + [col_a, col_b, row_a, row_b, rows, rows] + [whole((half, D))] * 2,
        out_specs=[col_a, col_b, row_a, row_b, pl.BlockSpec((8, FF_BLOCK), lambda j: (0, j))]
        + [whole((half, D))] * 2,
        scratch_shapes=[pltpu.VMEM((tokens, D), F32), pltpu.VMEM((tokens, FF_BLOCK), BF16)],
        compiler_params=params(),
        cost_estimate=cost(8 * tokens * D * width, 8 * D * width + 4 * tokens * width),
    )(dfo, dfs, w1a, w1b, w2a, w2b, act, slope, yo, ys)


def shuffle_kernel(table, *refs, moves, count, placed):
    for out, to, source, at in moves:
        if placed:
            refs[count + out][table[to]] = refs[source][at]
        else:
            refs[count + out][to] = refs[source][table[at]]


def shuffle(table, sources, shapes, moves, placed):
    nbytes = sum(4 * source.size for source in sources)
    return pl.pallas_call(
        functools.partial(shuffle_kernel, moves=moves, count=len(sources), placed=placed),
        name="shuffle",
        out_shape=shapes,
        in_specs=[pl.BlockSpec(memory_space=pltpu.SMEM)]
        + [pl.BlockSpec(memory_space=pltpu.VMEM)] * len(sources),
        out_specs=[pl.BlockSpec(memory_space=pltpu.VMEM)] * len(shapes),
        compiler_params=params(),
        cost_estimate=cost(0, nbytes),
    )(table, *sources)


class Places:
    def __init__(self, pages, bands):
        self.ny = bands // CORES
        self.nx = self.ny if pages % self.ny == 0 else 1
        self.nz = pages // self.nx
        self.chips = pages * self.ny
        page, band = lax.axis_index("page"), lax.axis_index("band")
        self.z, self.x = page // self.nx, page % self.nx
        self.y, self.core = band // CORES, band % CORES
        self.sizes = (self.nz, self.nx, self.ny, CORES)

    def shift(self, value, axis, steps):
        pairs = []
        nz, nx, ny, nc = self.sizes
        for device in range(nz * nx * ny * nc):
            place = [device // (nx * ny * nc), device // (ny * nc) % nx, device // nc % ny, device % nc]
            place[axis] = (place[axis] + steps) % self.sizes[axis]
            pairs.append((device, ((place[0] * nx + place[1]) * ny + place[2]) * nc + place[3]))
        return lax.ppermute(value, ("page", "band"), pairs)

    def swap(self, value):
        return self.shift(value, 3, 1)

    def spread(self, value, axis):
        return [value] + [self.shift(value, axis, k) for k in range(1, self.sizes[axis])]

    def chip_of(self, kz, kx, ky):
        z, x, y = (self.z - kz) % self.nz, (self.x - kx) % self.nx, (self.y - ky) % self.ny
        return (z * self.nx + x) * self.ny + y

    def gather(self, first, second):
        count = len(first)
        local = jnp.stack(list(first) + list(second))
        rows, cols = local.shape[1:]
        along_z = self.spread(local, 0)
        sources, moves, table = [], [], []
        for axes, start, stop in (((1, 2), 0, count), ((2, 1), count, local.shape[0])):
            part = jnp.stack([piece[start:stop] for piece in along_z])
            part = jnp.stack(self.spread(part, axes[0]))
            for far, piece in enumerate(self.spread(part, axes[1])):
                number = 0
                for near in range(self.sizes[axes[0]]):
                    kx, ky = (near, far) if axes[0] == 1 else (far, near)
                    for kz in range(self.nz):
                        for unit in range(start, stop):
                            moves.append((unit, len(table), len(sources), number))
                            number += 1
                        table.append(self.chip_of(kz, kx, ky))
                sources.append(piece.reshape((-1, rows, cols)))
        outs = shuffle(
            jnp.stack(table), sources, [sds((self.chips, rows, cols), BF16)] * local.shape[0], moves, True
        )
        return [out.reshape(-1, cols) for out in outs]

    def reduce(self, first, second, turns=None):
        turns = turns or {}
        units = list(first) + list(second)
        cols = units[0].shape[-1]
        rows = units[0].shape[0] // self.chips
        count = len(first)
        shapes, moves, table = [], [], []
        for axes, start, stop in (((2, 1), 0, count), ((1, 2), count, len(units))):
            inner = self.sizes[axes[1]]
            for far in range(self.sizes[axes[0]]):
                number = 0
                for near in range(inner):
                    kx, ky = (near, far) if axes[0] == 2 else (far, near)
                    for kz in range(self.nz):
                        chip = self.chip_of(kz, kx, ky)
                        for unit in range(start, stop):
                            moves.append((len(shapes), number, unit, len(table)))
                            table.append((chip + turns[unit]) % self.chips if unit in turns else chip)
                            number += 1
                shapes.append(sds((number, rows, cols), BF16))
        terms = shuffle(
            jnp.stack(table), [unit.reshape(self.chips, rows, cols) for unit in units], shapes, moves, False
        )
        lows = []
        for axes, start, stop in (((2, 1), 0, count), ((1, 2), count, len(units))):
            outer, inner = self.sizes[axes[0]], self.sizes[axes[1]]
            mine, terms = terms[:outer], terms[outer:]
            total = mine[0].astype(F32)
            for k in range(1, outer):
                total = total + self.shift(mine[k], axes[0], -k).astype(F32)
            low = total.astype(BF16).reshape(inner, self.nz, stop - start, rows, cols)
            total = low[0].astype(F32)
            for k in range(1, inner):
                total = total + self.shift(low[k], axes[1], -k).astype(F32)
            lows.append(total.astype(BF16))
        low = jnp.concatenate(lows, axis=1)
        total = low[0].astype(F32)
        for k in range(1, self.nz):
            total = total + self.shift(low[k], 0, -k).astype(F32)
        return total


def pick(stacked, index, axis=0):
    return lax.dynamic_index_in_dim(stacked, index, axis, keepdims=False)


def by_core(core, mine, theirs, axis):
    return jnp.where(core == 0, jnp.stack([mine, theirs], axis), jnp.stack([theirs, mine], axis))


def body(
    hidden,
    boxes,
    page_size,
    band_count,
    layout_tables,
    attn_in,
    attn_bias,
    attn_out,
    out_bias,
    norm_gain,
    norm_bias,
    ffn_in,
    ffn_in_bias,
    ffn_out,
    ffn_out_bias,
    out_grad,
    *,
    pages,
    bands,
):
    at = Places(pages, bands)
    core = at.core
    core_id = core.astype(jnp.int32).reshape(1)
    devices = pages * bands
    ny, chips = at.ny, at.chips
    cap = hidden.shape[2]
    rows_dev = attn_in.shape[1]
    table_rows = layout_tables.shape[1]
    ff_dev = ffn_out.shape[1]

    def to_chip(stacked):
        own = [pick(stacked, at.y)]
        for k in range(1, ny):
            own.append(at.shift(pick(stacked, (at.y + k) % ny), 2, k))
        return own

    def from_chip(rows):
        parts = rows.reshape((ny, cap) + rows.shape[1:])
        back = [parts[0]]
        for k in range(1, ny):
            back.append(at.shift(parts[k].astype(BF16), 2, -k).astype(F32))
        back = jnp.stack(back)
        return jnp.stack([pick(back, (page - at.y) % ny) for page in range(ny)])[:, None]

    widths, heights = page_size[0][:, None], page_size[1][:, None]
    left = boxes[0, :, 0] * GRID // widths
    top = boxes[1, :, 0] * GRID // heights
    right = boxes[2, :, 0] * GRID // widths
    bottom = boxes[3, :, 0] * GRID // heights
    live = (lax.broadcasted_iota(jnp.int32, left.shape, 1) < band_count).astype(jnp.int32)
    facts = jnp.stack([left, top, right, bottom, bottom - top, right - left, live, live], axis=1)
    facts_own = jnp.concatenate(to_chip(facts), axis=-1)
    facts_all = jnp.concatenate([facts_own, at.swap(facts_own)], axis=-1)
    owner = facts_all // table_rows
    index = jnp.where(
        owner % CORES == core, owner // CORES * table_rows + facts_all % table_rows, -1
    )
    mask = jnp.where(facts_all[6:7] > 0, 0.0, DEAD).astype(F32)
    live_own = facts_own[6].astype(F32)[:, None]
    hidden_own = jnp.concatenate(to_chip(hidden[:, 0]), axis=0)
    grad_own = jnp.concatenate(to_chip(out_grad[:, 0]), axis=0)

    segment = jnp.concatenate(
        [
            attn_bias.reshape(-1),
            out_bias.reshape(-1),
            norm_gain.reshape(-1),
            norm_bias.reshape(-1),
            ffn_out_bias.reshape(-1),
            ffn_in_bias.reshape(-1),
        ]
    )
    split = SMALL_ROWS * rows_dev
    smalls = lax.all_to_all(
        jnp.broadcast_to(segment, (devices, segment.shape[0])), ("page", "band"), 0, 0, tiled=True
    ).astype(F32)
    small = smalls[:, :split].reshape(devices, SMALL_ROWS, rows_dev).swapaxes(0, 1).reshape(SMALL_ROWS, D)
    up_bias = pick(smalls[:, split:].reshape(chips, CORES, LAYERS, 2, ff_dev // 2), core, 1)
    up_bias = up_bias.transpose(1, 2, 0, 3).reshape(LAYERS, FF // CORES)

    tables = at.gather(layout_tables[:2], layout_tables[2:])
    columns = jnp.concatenate(
        [
            attn_in.reshape(LAYERS, rows_dev, 3, CORES, HALF),
            attn_out.reshape(LAYERS, rows_dev, 1, CORES, HALF),
        ],
        axis=2,
    ).transpose(3, 0, 2, 1, 4)
    ups = ffn_in.reshape(LAYERS, rows_dev, chips, CORES, 2, ff_dev // 2).transpose(3, 0, 4, 1, 2, 5)
    ups = ups.reshape(CORES, LAYERS, 2, rows_dev, D)

    def chip_rows(by_columns):
        both = by_core(core, pick(by_columns, core), at.swap(pick(by_columns, 1 - core)), 2)
        return both.reshape(both.shape[:2] + (CORES * rows_dev, both.shape[-1]))

    columns = chip_rows(columns)
    ups = chip_rows(ups)
    downs = ffn_out.reshape(LAYERS, 2, ff_dev // 2, D)
    weights = []
    for layer in range(LAYERS):
        wq, wk, wv, wo_mine = at.gather(columns[layer, :2], columns[layer, 2:])
        w1a, w2a, w1b, w2b = at.gather(
            (ups[layer, 0], downs[layer, 0]), (ups[layer, 1], downs[layer, 1])
        )
        wo = by_core(core, wo_mine, at.swap(wo_mine), 1).reshape(D, D)
        weights.append((wq, wk, wv, wo, w1a, w1b, w2a, w2b))

    half = ny * cap
    looked_up = embed(index.T, tables)
    x = hidden_own.astype(F32) + looked_up[:half] + at.swap(looked_up[half:].astype(BF16)).astype(F32)
    x_low = x.astype(BF16)
    saved = []
    for layer in range(LAYERS):
        wq, wk, wv, wo, w1a, w1b, w2a, w2b = weights[layer]
        x_other = at.swap(x_low)
        q, k, v, mix_own, mix_other = attn_fwd(core_id, x_low, x_other, wq, wk, wv, small, mask, layer)
        y1, y1_low, n1, r1 = out_norm(core_id, mix_own, at.swap(mix_other), wo, x, small, layer)
        y1_other = at.swap(y1_low)
        act, slope, part, part_other = ffn_fwd(y1_low, y1_other, w1a, w1b, up_bias, w2a, w2b, layer)
        saved.append(
            (x_low, x_other, q, k, v, mix_own, mix_other, n1, r1, y1_low, y1_other, act, slope)
        )
        x, x_low, n2, r2 = add_norm(y1, part, at.swap(part_other), small, layer)
        saved[layer] += (n2, r2)
    output = from_chip(x * live_own)

    sources = (grad_own, live_own)
    small_grads = [None] * LAYERS
    results = [None] * LAYERS
    for layer in reversed(range(LAYERS)):
        wq, wk, wv, wo, w1a, w1b, w2a, w2b = weights[layer]
        x_low, x_other, q, k, v, mix_own, mix_other, n1, r1, y1_low, y1_other, act, slope, n2, r2 = saved[layer]
        gh2, df, sums2 = norm_bwd(sources, n2, r2, small, 2 * layer + 1)
        df_other = at.swap(df)
        dw1a, dw1b, dw2a, dw2b, up_sums, part, part_other = ffn_bwd(
            df, df_other, w1a, w1b, w2a, w2b, act, slope, y1_low, y1_other
        )
        ffn_result = at.reduce((dw1a, dw2a), (dw1b, dw2b))
        gh1, da, sums1 = norm_bwd((gh2, part, at.swap(part_other)), n1, r1, small, 2 * layer)
        da_other = at.swap(da)
        dwq, dwk, dwv, dwo, attn_sums, part, part_other = attn_bwd(
            core_id, da, da_other, wo, q, k, v, mix_own, mix_other, x_low, x_other, wq, wk, wv, mask
        )
        sources = (gh1, part, at.swap(part_other))
        dwo = jnp.concatenate([pick(dwo, core), at.swap(pick(dwo, 1 - core))])
        attn_result = at.reduce((dwq, dwk), (dwv, dwo), {3: core * (chips // 2)})
        results[layer] = (attn_result, ffn_result)
        small_grads[layer] = (sums1, sums2, attn_sums, up_sums)
    grad_x = sources[0] + sources[1] + sources[2].astype(F32)
    input_grad = from_chip(grad_x)
    grad_low = grad_x.astype(BF16)
    table_parts = table_grads(index, grad_low, at.swap(grad_low), chips * table_rows)
    grad_tables = at.reduce(table_parts[:2], table_parts[2:])

    zeros = jnp.zeros((2, HALF), F32)
    vectors = []
    for layer in range(LAYERS):
        mine = small_grads[layer][2][:2]
        vectors.append(by_core(core, mine, zeros, 1).reshape(2, D))
    vectors.append(jnp.stack([small_grads[layer][0][2] for layer in range(LAYERS)]))
    for row in range(2):
        for layer in range(LAYERS):
            vectors.append(jnp.stack([small_grads[layer][norm][row] for norm in range(2)]))
    vectors.append(jnp.stack([small_grads[layer][1][2] for layer in range(LAYERS)]))
    vectors = jnp.concatenate(vectors).reshape(SMALL_ROWS, devices, rows_dev).swapaxes(0, 1)
    ups_grad = jnp.stack([small_grads[layer][3][0] for layer in range(LAYERS)])
    ups_grad = ups_grad.reshape(LAYERS, 2, chips, ff_dev // 2).transpose(2, 0, 1, 3)
    ups_grad = by_core(core, ups_grad, jnp.zeros_like(ups_grad), 1)
    segments = jnp.concatenate(
        [vectors.reshape(devices, split), ups_grad.reshape(devices, LAYERS * ff_dev)], axis=1
    )
    segment = jnp.sum(lax.all_to_all(segments, ("page", "band"), 0, 0, tiled=True), axis=0)
    rows = segment[:split].reshape(SMALL_ROWS, rows_dev)

    grads = [[], [], [], []]
    for layer in range(LAYERS):
        attn_result, ffn_result = results[layer]

        def my_rows(result):
            units, cols = result.shape[0], result.shape[-1]
            by_owner = result.reshape(units, CORES, rows_dev, cols)
            return by_core(core, pick(by_owner, core, 1), at.swap(pick(by_owner, 1 - core, 1)), 2)

        both = my_rows(attn_result).swapaxes(0, 1)
        grads[0].append(both[:, :3].reshape(rows_dev, 3 * D))
        grads[1].append(both[:, 3].reshape(rows_dev, D))
        both = my_rows(jnp.stack([ffn_result[0], ffn_result[2]]))
        both = both.reshape(2, rows_dev, CORES, chips, ff_dev // 2).transpose(1, 3, 2, 0, 4)
        grads[2].append(both.reshape(rows_dev, FF))
        grads[3].append(jnp.concatenate([ffn_result[1], ffn_result[3]]))
    grads = [jnp.stack(pair) for pair in grads]

    return (
        output,
        input_grad,
        grad_tables,
        grads[0],
        rows[ROW_ATTN:ROW_OUT].reshape(LAYERS, 2, rows_dev),
        grads[1],
        rows[ROW_OUT:ROW_GAIN],
        rows[ROW_GAIN:ROW_SHIFT].reshape(LAYERS, 2, rows_dev),
        rows[ROW_SHIFT:ROW_DOWN].reshape(LAYERS, 2, rows_dev),
        grads[2],
        segment[split:].reshape(LAYERS, ff_dev),
        grads[3],
        rows[ROW_DOWN:SMALL_ROWS],
    )


def solution(mesh):
    both = ("page", "band")
    tokens = P("page", "band", None, None)
    middle = P(None, both, None)
    last = P(None, both)
    third = P(None, None, both)
    return jax.shard_map(
        functools.partial(body, pages=mesh.shape["page"], bands=mesh.shape["band"]),
        mesh=mesh,
        in_specs=(
            tokens,
            P(None, "page", "band", None),
            P(None, "page"),
            P("page", "band"),
            middle,
            middle,
            third,
            middle,
            last,
            third,
            third,
            middle,
            last,
            middle,
            last,
            tokens,
        ),
        out_specs=(
            tokens,
            tokens,
            middle,
            middle,
            third,
            middle,
            last,
            third,
            third,
            middle,
            last,
            middle,
            last,
        ),
        check_vma=False,
    )
```

time: 1650 us -> 704 us (0.43)
  blocking collectives: 473 us -> 0 us
  waiting for transfers between devices: 423 us -> 216 us
  matrix products: 192 us -> 0 us
  other arithmetic: 192 us -> 54.2 us
  local copies, waits for them, and re-layouts: 284 us -> 154 us
  Pallas kernels: 0 us -> 126 us
  starting transfers between devices: 60.1 us -> 137 us
    all_gather x24 -> x0, blocking collectives: 433 us -> none  [the longest x4 54 us: matrix_terms(): lax.all_gather(right_parts[3], 'band', axis=1, tiled=True)]
    unnamed x39 -> x0, waiting for transfers between devices: 228 us -> none
    ppermute x0 -> x104, waiting for transfers between devices: none -> 211 us  [shift(): return lax.ppermute(value, ('page', 'band'), pairs)]
    dot_general x72 -> x0, matrix products: 192 us -> none  [the longest x16 37.4 us: matrix_terms(): jnp.einsum('pcd,pce->de', left_cols[number], right_page[number], preferre...]
    reduce_scatter x2 -> x0, waiting for transfers between devices: 165 us -> none  [the longest x1 159 us: body(): lax.psum_scatter(grad_totals[0], ('page', 'band'), scatter_dimension=1, t...]
    ppermute x0 -> x104, starting transfers between devices: none -> 127 us  [shift(): return lax.ppermute(value, ('page', 'band'), pairs)]
    pallas_call x0 -> x28, Pallas kernels: none -> 126 us  [the longest x2 33.7 us: attn_bwd(): pl.pallas_call(attn_bwd_kernel, name='attn_bwd', out_shape=[sds((D, HALF)...]
    unnamed x27 -> x11, other arithmetic: 92.4 us -> 7.6 us
  transfers between devices with their start and end apart: 43 -> 106, of which waited for: 20 -> 35; matrix products, arithmetic and copies ran while one was open for 30% -> 18% of each run, Pallas kernels for 0% -> 14%
where the time goes in v1:
time: 704 us; the launch traced here: 690 us
  waiting for transfers between devices  216 us (31%)
  local copies, waits for them, and re-layouts  154 us (22%)
  starting transfers between devices  137 us (19%)
  Pallas kernels  126 us (18%)
  other arithmetic  54.2 us (8%)
    ppermute x104, waiting for transfers between devices, shift(): return lax.ppermute(value, ('page', 'band'), pairs)  211 us
    ppermute x104, starting transfers between devices, shift(): return lax.ppermute(value, ('page', 'band'), pairs)  127 us
    unnamed x386, local copies, waits for them, and re-layouts  88.2 us
    pallas_call x2, Pallas kernels, attn_bwd(): pl.pallas_call(attn_bwd_kernel, name='attn_bwd', out_shape=[sds((D, HALF)...  33.7 us
    pallas_call x2, Pallas kernels, ffn_bwd(): pl.pallas_call(ffn_bwd_kernel, name='ffn_bwd', out_shape=[sds((D, width /...  30.9 us
    pallas_call x2, Pallas kernels, ffn_fwd(): pl.pallas_call(functools.partial(ffn_fwd_kernel, layer=layer), name='ffn_...  20.2 us
  transfers between devices with their start and end apart: 106, of which 35 were waited for; matrix products, arithmetic and copies ran while one was open for 18% of the time, Pallas kernels for 14%

profile of v1, /device:TPU:0, one launch (start us, length us, event | category | flops | bytes accessed | tf_op | source)
XLA Modules:
  0.0 690.4 jit_solution(2518339158448286717)
XLA Ops:
  0.7 5.1 collective-permute-start.5
  25.7 5.1 all-to-all-start
  45.5 3.3 collective-permute-start.26
  49.9 2.6 collective-permute-start.25
  52.5 4.2 collective-permute-done.14
  57.0 17.4 %collective-permute-start.34 = (bf16[4,48,384]{2,1,0:T(8,128)(2,1)S(1)}, bf16[4,48,384]{2,1,0:T(8,128)(2,1)S(1)}, u32[]{:S(2)}, u32[]{:S(2)}) collective-permute-start(bf16[4,48,384]{2,1,0:T(8,128)(2,1)S(1)} %pad_maximum_fusion.37), channel_id=1, source_target_pairs={{0,16},{1,17},{2,18},{3,19},{4,20},{5,21},{6,22},{7,23},{8,24},{9,... | collective-permute-start | bytes 442376 | tf_op jit(solution)/shard_map/ppermute | solution.py:577
  74.4 11.4 %collective-permute-start.33 = (bf16[4,48,384]{2,1,0:T(8,128)(2,1)S(1)}, bf16[4,48,384]{2,1,0:T(8,128)(2,1)S(1)}, u32[]{:S(2)}, u32[]{:S(2)}) collective-permute-start(bf16[4,48,384]{2,1,0:T(8,128)(2,1)S(1)} %pad_maximum_fusion.37), channel_id=1, source_target_pairs={{0,8},{1,9},{2,10},{3,11},{4,12},{5,13},{6,14},{7,15},{8,16},{9,17... | collective-permute-start | bytes 442376 | tf_op jit(solution)/shard_map/ppermute | solution.py:577
  90.3 7.8 %collective-permute-done.6 = bf16[4,2,32,768]{3,2,1,0:T(8,128)(2,1)S(1)} collective-permute-done((bf16[4,2,32,768]{3,2,1,0:T(8,128)(2,1)S(1)}, bf16[4,2,32,768]{3,2,1,0:T(8,128)(2,1)S(1)}, u32[]{:S(2)}, u32[]{:S(2)}) %collective-permute-start.6) | collective-permute-done | bytes 393248 | tf_op jit(solution)/shard_map/ppermute | solution.py:577
  102.6 4.7 collective-permute-done.24
  108.6 10.7 %collective-permute-done.7 = bf16[2,4,2,32,768]{4,3,2,1,0:T(8,128)(2,1)S(1)} collective-permute-done((bf16[2,4,2,32,768]{4,3,2,1,0:T(8,128)(2,1)S(1)}, bf16[2,4,2,32,768]{4,3,2,1,0:T(8,128)(2,1)S(1)}, u32[]{:S(2)}, u32[]{:S(2)}) %collective-permute-start.7) | collective-permute-done | bytes 786464 | tf_op jit(solution)/shard_map/ppermute | solution.py:577
  119.3 3.3 collective-permute-start.45
  124.3 2.8 embed.1
  133.1 6.8 collective-permute-done.27
  140.0 3.5 collective-permute-done.29
  144.0 11.8 %collective-permute-done.17 = bf16[2,4,2,48,384]{4,3,2,1,0:T(8,128)(2,1)S(1)} collective-permute-done((bf16[2,4,2,48,384]{4,3,2,1,0:T(8,128)(2,1)S(1)}, bf16[2,4,2,48,384]{4,3,2,1,0:T(8,128)(2,1)S(1)}, u32[]{:S(2)}, u32[]{:S(2)}) %collective-permute-start.17) | collective-permute-done | bytes 589856 | tf_op jit(solution)/shard_map/ppermute | solution.py:577
  160.3 6.8 attn_fwd.2
  169.9 21.0 %collective-permute-done.36 = bf16[4,2,48,384]{3,2,1,0:T(8,128)(2,1)S(1)} collective-permute-done((bf16[4,2,48,384]{3,2,1,0:T(8,128)(2,1)S(1)}, bf16[4,2,48,384]{3,2,1,0:T(8,128)(2,1)S(1)}, u32[]{:S(2)}, u32[]{:S(2)}) %collective-permute-start.36) | collective-permute-done | bytes 294944 | tf_op jit(solution)/shard_map/ppermute | solution.py:577
  196.3 9.6 %ffn_fwd.2 = (bf16[512,1536]{1,0:T(8,128)(2,1)S(1)}, bf16[512,1536]{1,0:T(8,128)(2,1)S(1)}, f32[256,768]{1,0:T(8,128)S(1)}, bf16[256,768]{1,0:T(8,128)(2,1)S(1)}) custom-call(bf16[256,768]{1,0:T(8,128)(2,1)S(1)} %get-tuple-element.142.yo, bf16[256,768]{1,0:T(8,128)(2,1)S(1)} %collective-permute-done.22.ys, bf16[768,768]{1,0:T(8,128)(2,1)S(1)} %bitcast.579, ...), custom_call_target="tpu_custom_call" | custom-call | flops 2415919104 | bytes 7864320 | tf_op jit(solution)/shard_map/ffn_fwd/pallas_call | solution.py:448
  211.6 9.0 %collective-permute-done.37 = bf16[2,4,2,48,384]{4,3,2,1,0:T(8,128)(2,1)S(1)} collective-permute-done((bf16[2,4,2,48,384]{4,3,2,1,0:T(8,128)(2,1)S(1)}, bf16[2,4,2,48,384]{4,3,2,1,0:T(8,128)(2,1)S(1)}, u32[]{:S(2)}, u32[]{:S(2)}) %collective-permute-start.37) | collective-permute-done | bytes 589856 | tf_op jit(solution)/shard_map/ppermute | solution.py:577
  221.5 6.8 attn_fwd.3
  231.4 11.7 %collective-permute-done.47 = bf16[2,4,2,48,768]{4,3,2,1,0:T(8,128)(2,1)S(1)} collective-permute-done((bf16[2,4,2,48,768]{4,3,2,1,0:T(8,128)(2,1)S(1)}, bf16[2,4,2,48,768]{4,3,2,1,0:T(8,128)(2,1)S(1)}, u32[]{:S(2)}, u32[]{:S(2)}) %collective-permute-start.47) | collective-permute-done | bytes 1179680 | tf_op jit(solution)/shard_map/ppermute | solution.py:577
  244.1 10.7 %ffn_fwd.3 = (bf16[512,1536]{1,0:T(8,128)(2,1)S(1)}, bf16[512,1536]{1,0:T(8,128)(2,1)S(1)}, f32[256,768]{1,0:T(8,128)S(1)}, bf16[256,768]{1,0:T(8,128)(2,1)}) custom-call(bf16[256,768]{1,0:T(8,128)(2,1)S(1)} %get-tuple-element.158.yo, bf16[256,768]{1,0:T(8,128)(2,1)S(1)} %collective-permute-done.42.ys, bf16[768,768]{1,0:T(8,128)(2,1)S(1)} %bitcast.587, ...), custom_call_target="tpu_custom_call" | custom-call | flops 2415919104 | bytes 7864320 | tf_op jit(solution)/shard_map/ffn_fwd/pallas_call | solution.py:448
  260.0 6.4 collective-permute-done.52
  285.0 15.5 %ffn_bwd.2 = (bf16[768,768]{1,0:T(8,128)(2,1)S(1)}, bf16[768,768]{1,0:T(8,128)(2,1)S(1)}, bf16[768,768]{1,0:T(8,128)(2,1)S(1)}, bf16[768,768]{1,0:T(8,128)(2,1)S...) custom-call(bf16[256,768]{1,0:T(8,128)(2,1)} %get-tuple-element.169.dfo, ...), custom_call_target="tpu_custom_call" | custom-call | flops 4831838208 | bytes 12582912 | tf_op jit(solution)/shard_map/ffn_bwd/pallas_call | solution.py:521
  315.8 2.5 norm_bwd.5
  319.9 2.3 shuffle.19
  340.5 17.4 %attn_bwd.2 = (bf16[768,384]{1,0:T(8,128)(2,1)S(1)}, bf16[768,384]{1,0:T(8,128)(2,1)S(1)}, bf16[768,384]{1,0:T(8,128)(2,1)S(1)}, bf16[2,384,384]{2,1,0:T(8,128)(...) custom-call(s32[1]{0:T(128)} %bitcast.core, ...), custom_call_target="tpu_custom_call" | custom-call | flops 3825205248 | bytes 9437184 | tf_op jit(solution)/shard_map/attn_bwd/pallas_call | solution.py:252
  390.9 15.4 %ffn_bwd.3 = (bf16[768,768]{1,0:T(8,128)(2,1)S(1)}, bf16[768,768]{1,0:T(8,128)(2,1)S(1)}, bf16[768,768]{1,0:T(8,128)(2,1)S(1)}, bf16[768,768]{1,0:T(8,128)(2,1)S...) custom-call(bf16[256,768]{1,0:T(8,128)(2,1)} %get-tuple-element.186.dfo, ...), custom_call_target="tpu_custom_call" | custom-call | flops 4831838208 | bytes 12582912 | tf_op jit(solution)/shard_map/ffn_bwd/pallas_call | solution.py:521
  432.2 22.3 %collective-permute-done.83 = bf16[4,2,48,384]{3,2,1,0:T(8,128)(2,1)S(1)} collective-permute-done((bf16[4,2,48,384]{3,2,1,0:T(8,128)(2,1)S(1)}, bf16[4,2,48,384]{3,2,1,0:T(8,128)(2,1)S(1)}, u32[]{:S(2)}, u32[]{:S(2)}) %collective-permute-start.83) | collective-permute-done | bytes 294944 | tf_op jit(solution)/shard_map/ppermute | solution.py:577
  454.5 2.5 collective-permute-start.100
  464.8 3.3 collective-permute-start.84
  470.3 2.7 collective-permute-done.86
  473.1 4.6 collective-permute-done.85
  488.0 3.0 stack_reshape.25
  504.6 16.3 %attn_bwd.3 = (bf16[768,384]{1,0:T(8,128)(2,1)S(1)}, bf16[768,384]{1,0:T(8,128)(2,1)S(1)}, bf16[768,384]{1,0:T(8,128)(2,1)S(1)}, bf16[2,384,384]{2,1,0:T(8,128)(...) custom-call(s32[1]{0:T(128)} %bitcast.core, bf16[256,768]{1,0:T(8,128)(2,1)S(1)} %copy-done.121, ...), custom_call_target="tpu_custom_call" | custom-call | flops 3825205248 | bytes 9437184 | tf_op jit(solution)/shard_map/attn_bwd/pallas_call | solution.py:252
  529.8 4.7 all-to-all-start.1
  539.1 3.0 all-to-all-done.1
  558.8 22.5 %collective-permute-done.61 = bf16[128,768]{1,0:T(8,128)(2,1)S(1)} collective-permute-done((bf16[128,768]{1,0:T(8,128)(2,1)S(1)}, bf16[128,768]{1,0:T(8,128)(2,1)S(1)}, u32[]{:S(2)}, u32[]{:S(2)}) %collective-permute-start.61) | collective-permute-done | bytes 196640 | tf_op jit(solution)/shard_map/ppermute | solution.py:577
  590.9 20.9 %collective-permute-done.72 = bf16[4,2,48,384]{3,2,1,0:T(8,128)(2,1)S(1)} collective-permute-done((bf16[4,2,48,384]{3,2,1,0:T(8,128)(2,1)S(1)}, bf16[4,2,48,384]{3,2,1,0:T(8,128)(2,1)S(1)}, u32[]{:S(2)}, u32[]{:S(2)}) %collective-permute-start.72) | collective-permute-done | bytes 294944 | tf_op jit(solution)/shard_map/ppermute | solution.py:577
  616.6 12.2 %collective-permute-done.93 = bf16[4,48,768]{2,1,0:T(8,128)(2,1)S(1)} collective-permute-done((bf16[4,48,768]{2,1,0:T(8,128)(2,1)S(1)}, bf16[4,48,768]{2,1,0:T(8,128)(2,1)S(1)}, u32[]{:S(2)}, u32[]{:S(2)}) %collective-permute-start.93) | collective-permute-done | bytes 294944 | tf_op jit(solution)/shard_map/ppermute | solution.py:577
  628.7 9.7 %collective-permute-start.75 = (bf16[4,48,384]{2,1,0:T(8,128)(2,1)}, bf16[4,48,384]{2,1,0:T(8,128)(2,1)}, u32[]{:S(2)}, u32[]{:S(2)}) collective-permute-start(bf16[4,48,384]{2,1,0:T(8,128)(2,1)} %get-tuple-element.362), channel_id=1, source_target_pairs={{0,24},{1,25},{2,26},{3,27},{4,28},{5,29},{6,30},{7,31},{8,0},{9,1... | collective-permute-start | bytes 442376 | tf_op jit(solution)/shard_map/ppermute | solution.py:577
  651.9 2.3 stack_reshape.24
  662.5 4.2 collective-permute-done.64
  666.8 3.5 collective-permute-done.66
  671.6 2.5 collective-permute-start.69
  674.1 2.6 collective-permute-start.68
  678.6 3.5 collective-permute-done.69
  682.0 7.1 %collective-permute-done.68 = bf16[4,32,768]{2,1,0:T(8,128)(2,1)S(1)} collective-permute-done((bf16[4,32,768]{2,1,0:T(8,128)(2,1)S(1)}, bf16[4,32,768]{2,1,0:T(8,128)(2,1)S(1)}, u32[]{:S(2)}, u32[]{:S(2)}) %collective-permute-start.68) | collective-permute-done | bytes 196640 | tf_op jit(solution)/shard_map/ppermute | solution.py:577
  (827 shorter events, 297.4 us)
Async XLA Ops:
  0.7 41.5 %collective-permute-start.5 = (bf16[4,32,768]{2,1,0:T(8,128)(2,1)}, bf16[4,32,768]{2,1,0:T(8,128)(2,1)}, u32[]{:S(2)}, u32[]{:S(2)}) collective-permute-start(bf16[4,32,768]{2,1,0:T(8,128)(2,1)} %param.22), channel_id=1, source_target_pairs={{0,24},{1,25},{2,26},{3,27},{4,28},{5,29},{6,30},{7,31},{8,0},{9,1... | collective-permute-start | bytes 589832 | tf_op jit(solution)/shard_map/ppermute | solution.py:577
  5.8 38.1 %collective-permute-start.4 = (bf16[4,32,768]{2,1,0:T(8,128)(2,1)}, bf16[4,32,768]{2,1,0:T(8,128)(2,1)}, u32[]{:S(2)}, u32[]{:S(2)}) collective-permute-start(bf16[4,32,768]{2,1,0:T(8,128)(2,1)} %param.22), channel_id=1, source_target_pairs={{0,16},{1,17},{2,18},{3,19},{4,20},{5,21},{6,22},{7,23},{8,24},{9,... | collective-permute-start | bytes 589832 | tf_op jit(solution)/shard_map/ppermute | solution.py:577
  5.8 39.7 %collective-permute-start.3 = (bf16[4,32,768]{2,1,0:T(8,128)(2,1)}, bf16[4,32,768]{2,1,0:T(8,128)(2,1)}, u32[]{:S(2)}, u32[]{:S(2)}) collective-permute-start(bf16[4,32,768]{2,1,0:T(8,128)(2,1)} %param.22), channel_id=1, source_target_pairs={{0,8},{1,9},{2,10},{3,11},{4,12},{5,13},{6,14},{7,15},{8,16},{9,17... | collective-permute-start | bytes 589832 | tf_op jit(solution)/shard_map/ppermute | solution.py:577
  18.4 110.6 %collective-permute-start = (bf16[128,768]{1,0:T(8,128)(2,1)}, bf16[128,768]{1,0:T(8,128)(2,1)}, u32[]{:S(2)}, u32[]{:S(2)}) collective-permute-start(bf16[128,768]{1,0:T(8,128)(2,1)} %get-tuple-element.391), channel_id=1, source_target_pairs={{0,2},{1,3},{2,0},{3,1},{4,6},{5,7},{6,4},{7,5},{8,10},{9,11},{10,... | collective-permute-start | bytes 589832 | tf_op jit(solution)/shard_map/ppermute | solution.py:577
  45.5 54.8 %collective-permute-start.26 = (bf16[4,48,768]{2,1,0:T(8,128)(2,1)S(1)}, bf16[4,48,768]{2,1,0:T(8,128)(2,1)S(1)}, u32[]{:S(2)}, u32[]{:S(2)}) collective-permute-start(bf16[4,48,768]{2,1,0:T(8,128)(2,1)S(1)} %pad_maximum_fusion.27), channel_id=1, source_target_pairs={{0,24},{1,25},{2,26},{3,27},{4,28},{5,29},{6,30},{7,31},{8,0},{9,1... | collective-permute-start | bytes 884744 | tf_op jit(solution)/shard_map/ppermute | solution.py:577
  49.9 51.1 %collective-permute-start.25 = (bf16[4,48,768]{2,1,0:T(8,128)(2,1)S(1)}, bf16[4,48,768]{2,1,0:T(8,128)(2,1)S(1)}, u32[]{:S(2)}, u32[]{:S(2)}) collective-permute-start(bf16[4,48,768]{2,1,0:T(8,128)(2,1)S(1)} %pad_maximum_fusion.27), channel_id=1, source_target_pairs={{0,16},{1,17},{2,18},{3,19},{4,20},{5,21},{6,22},{7,23},{8,24},{9,... | collective-permute-start | bytes 884744 | tf_op jit(solution)/shard_map/ppermute | solution.py:577
  57.0 30.7 %collective-permute-start.34 = (bf16[4,48,384]{2,1,0:T(8,128)(2,1)S(1)}, bf16[4,48,384]{2,1,0:T(8,128)(2,1)S(1)}, u32[]{:S(2)}, u32[]{:S(2)}) collective-permute-start(bf16[4,48,384]{2,1,0:T(8,128)(2,1)S(1)} %pad_maximum_fusion.37), channel_id=1, source_target_pairs={{0,16},{1,17},{2,18},{3,19},{4,20},{5,21},{6,22},{7,23},{8,24},{9,... | collective-permute-start | bytes 442376 | tf_op jit(solution)/shard_map/ppermute | solution.py:577
  98.8 20.5 %collective-permute-start.7 = (bf16[2,4,2,32,768]{4,3,2,1,0:T(8,128)(2,1)S(1)}, bf16[2,4,2,32,768]{4,3,2,1,0:T(8,128)(2,1)S(1)}, u32[]{:S(2)}, u32[]{:S(2)}) collective-permute-start(bf16[2,4,2,32,768]{4,3,2,1,0:T(8,128)(2,1)S(1)} %pad_maximum_fusion.4), channel_id=1, source_target_pairs={{0,2},{1,3},{2,0},{3,1},{4,6},{5,7},{6,4},{7,5},{8,10},{9,11},{10,... | collective-permute-start | bytes 2359304 | tf_op jit(solution)/shard_map/ppermute | solution.py:577
  100.4 22.2 %collective-permute-start.9 = (bf16[2,4,2,32,768]{4,3,2,1,0:T(8,128)(2,1)S(1)}, bf16[2,4,2,32,768]{4,3,2,1,0:T(8,128)(2,1)S(1)}, u32[]{:S(2)}, u32[]{:S(2)}) collective-permute-start(bf16[2,4,2,32,768]{4,3,2,1,0:T(8,128)(2,1)S(1)} %pad_maximum_fusion.5), channel_id=1, source_target_pairs={{0,4},{1,5},{2,6},{3,7},{4,0},{5,1},{6,2},{7,3},{8,12},{9,13},{10,... | collective-permute-start | bytes 2359304 | tf_op jit(solution)/shard_map/ppermute | solution.py:577
  101.0 26.2 %collective-permute-start.16 = (bf16[4,2,48,384]{3,2,1,0:T(8,128)(2,1)S(1)}, bf16[4,2,48,384]{3,2,1,0:T(8,128)(2,1)S(1)}, u32[]{:S(2)}, u32[]{:S(2)}) collective-permute-start(bf16[4,2,48,384]{3,2,1,0:T(8,128)(2,1)S(1)} %get-tuple-element.442), channel_id=1, source_target_pairs={{0,4},{1,5},{2,6},{3,7},{4,0},{5,1},{6,2},{7,3},{8,12},{9,13},{10,... | collective-permute-start | bytes 884744 | tf_op jit(solution)/shard_map/ppermute | solution.py:577
  107.3 20.0 %collective-permute-start.18 = (bf16[4,2,48,384]{3,2,1,0:T(8,128)(2,1)S(1)}, bf16[4,2,48,384]{3,2,1,0:T(8,128)(2,1)S(1)}, u32[]{:S(2)}, u32[]{:S(2)}) collective-permute-start(bf16[4,2,48,384]{3,2,1,0:T(8,128)(2,1)S(1)} %get-tuple-element.440), channel_id=1, source_target_pairs={{0,2},{1,3},{2,0},{3,1},{4,6},{5,7},{6,4},{7,5},{8,10},{9,11},{10,... | collective-permute-start | bytes 884744 | tf_op jit(solution)/shard_map/ppermute | solution.py:577
  129.0 26.8 %collective-permute-start.17 = (bf16[2,4,2,48,384]{4,3,2,1,0:T(8,128)(2,1)S(1)}, bf16[2,4,2,48,384]{4,3,2,1,0:T(8,128)(2,1)S(1)}, u32[]{:S(2)}, u32[]{:S(2)}) collective-permute-start(bf16[2,4,2,48,384]{4,3,2,1,0:T(8,128)(2,1)S(1)} %pad_maximum_fusion.6), channel_id=1, source_target_pairs={{0,2},{1,3},{2,0},{3,1},{4,6},{5,7},{6,4},{7,5},{8,10},{9,11},{10,... | collective-permute-start | bytes 1769480 | tf_op jit(solution)/shard_map/ppermute | solution.py:577
  129.6 27.7 %collective-permute-start.19 = (bf16[2,4,2,48,384]{4,3,2,1,0:T(8,128)(2,1)S(1)}, bf16[2,4,2,48,384]{4,3,2,1,0:T(8,128)(2,1)S(1)}, u32[]{:S(2)}, u32[]{:S(2)}) collective-permute-start(bf16[2,4,2,48,384]{4,3,2,1,0:T(8,128)(2,1)S(1)} %pad_maximum_fusion.7), channel_id=1, source_target_pairs={{0,4},{1,5},{2,6},{3,7},{4,0},{5,1},{6,2},{7,3},{8,12},{9,13},{10,... | collective-permute-start | bytes 1769480 | tf_op jit(solution)/shard_map/ppermute | solution.py:577
  130.7 27.9 %collective-permute-start.44 = (bf16[4,48,768]{2,1,0:T(8,128)(2,1)S(1)}, bf16[4,48,768]{2,1,0:T(8,128)(2,1)S(1)}, u32[]{:S(2)}, u32[]{:S(2)}) collective-permute-start(bf16[4,48,768]{2,1,0:T(8,128)(2,1)S(1)} %pad_maximum_fusion.30), channel_id=1, source_target_pairs={{0,16},{1,17},{2,18},{3,19},{4,20},{5,21},{6,22},{7,23},{8,24},{9,... | collective-permute-start | bytes 884744 | tf_op jit(solution)/shard_map/ppermute | solution.py:577
  143.5 23.7 %collective-permute-start.43 = (bf16[4,48,768]{2,1,0:T(8,128)(2,1)S(1)}, bf16[4,48,768]{2,1,0:T(8,128)(2,1)S(1)}, u32[]{:S(2)}, u32[]{:S(2)}) collective-permute-start(bf16[4,48,768]{2,1,0:T(8,128)(2,1)S(1)} %pad_maximum_fusion.30), channel_id=1, source_target_pairs={{0,8},{1,9},{2,10},{3,11},{4,12},{5,13},{6,14},{7,15},{8,16},{9,17... | collective-permute-start | bytes 884744 | tf_op jit(solution)/shard_map/ppermute | solution.py:577
  155.8 37.1 %collective-permute-start.28 = (bf16[2,4,2,48,768]{4,3,2,1,0:T(8,128)(2,1)S(1)}, bf16[2,4,2,48,768]{4,3,2,1,0:T(8,128)(2,1)S(1)}, u32[]{:S(2)}, u32[]{:S(2)}) collective-permute-start(bf16[2,4,2,48,768]{4,3,2,1,0:T(8,128)(2,1)S(1)} %pad_maximum_fusion), channel_id=1, source_target_pairs={{0,2},{1,3},{2,0},{3,1},{4,6},{5,7},{6,4},{7,5},{8,10},{9,11},{10,... | collective-permute-start | bytes 3538952 | tf_op jit(solution)/shard_map/ppermute | solution.py:577
  157.3 36.6 %collective-permute-start.30 = (bf16[2,4,2,48,768]{4,3,2,1,0:T(8,128)(2,1)S(1)}, bf16[2,4,2,48,768]{4,3,2,1,0:T(8,128)(2,1)S(1)}, u32[]{:S(2)}, u32[]{:S(2)}) collective-permute-start(bf16[2,4,2,48,768]{4,3,2,1,0:T(8,128)(2,1)S(1)} %pad_maximum_fusion.1), channel_id=1, source_target_pairs={{0,4},{1,5},{2,6},{3,7},{4,0},{5,1},{6,2},{7,3},{8,12},{9,13},{10,... | collective-permute-start | bytes 3538952 | tf_op jit(solution)/shard_map/ppermute | solution.py:577
  158.7 32.2 %collective-permute-start.36 = (bf16[4,2,48,384]{3,2,1,0:T(8,128)(2,1)S(1)}, bf16[4,2,48,384]{3,2,1,0:T(8,128)(2,1)S(1)}, u32[]{:S(2)}, u32[]{:S(2)}) collective-permute-start(bf16[4,2,48,384]{3,2,1,0:T(8,128)(2,1)S(1)} %get-tuple-element.421), channel_id=1, source_target_pairs={{0,4},{1,5},{2,6},{3,7},{4,0},{5,1},{6,2},{7,3},{8,12},{9,13},{10,... | collective-permute-start | bytes 884744 | tf_op jit(solution)/shard_map/ppermute | solution.py:577
  167.5 24.1 %collective-permute-start.38 = (bf16[4,2,48,384]{3,2,1,0:T(8,128)(2,1)S(1)}, bf16[4,2,48,384]{3,2,1,0:T(8,128)(2,1)S(1)}, u32[]{:S(2)}, u32[]{:S(2)}) collective-permute-start(bf16[4,2,48,384]{3,2,1,0:T(8,128)(2,1)S(1)} %get-tuple-element.419), channel_id=1, source_target_pairs={{0,2},{1,3},{2,0},{3,1},{4,6},{5,7},{6,4},{7,5},{8,10},{9,11},{10,... | collective-permute-start | bytes 884744 | tf_op jit(solution)/shard_map/ppermute | solution.py:577
  169.6 26.7 %collective-permute-start.22 = (bf16[256,768]{1,0:T(8,128)(2,1)S(1)}, bf16[256,768]{1,0:T(8,128)(2,1)S(1)}, u32[]{:S(2)}, u32[]{:S(2)}) collective-permute-start(bf16[256,768]{1,0:T(8,128)(2,1)S(1)} %get-tuple-element.142.yo), channel_id=1, source_target_pairs={{0,1},{1,0},{2,3},{3,2},{4,5},{5,4},{6,7},{7,6},{8,9},{9,8},{10,11... | collective-permute-start | bytes 1179656 | tf_op jit(solution)/shard_map/ppermute | solution.py:577
  192.8 27.8 %collective-permute-start.37 = (bf16[2,4,2,48,384]{4,3,2,1,0:T(8,128)(2,1)S(1)}, bf16[2,4,2,48,384]{4,3,2,1,0:T(8,128)(2,1)S(1)}, u32[]{:S(2)}, u32[]{:S(2)}) collective-permute-start(bf16[2,4,2,48,384]{4,3,2,1,0:T(8,128)(2,1)S(1)} %pad_maximum_fusion.10), channel_id=1, source_target_pairs={{0,2},{1,3},{2,0},{3,1},{4,6},{5,7},{6,4},{7,5},{8,10},{9,11},{10,... | collective-permute-start | bytes 1769480 | tf_op jit(solution)/shard_map/ppermute | solution.py:577
  193.9 26.7 %collective-permute-start.39 = (bf16[2,4,2,48,384]{4,3,2,1,0:T(8,128)(2,1)S(1)}, bf16[2,4,2,48,384]{4,3,2,1,0:T(8,128)(2,1)S(1)}, u32[]{:S(2)}, u32[]{:S(2)}) collective-permute-start(bf16[2,4,2,48,384]{4,3,2,1,0:T(8,128)(2,1)S(1)} %pad_maximum_fusion.11), channel_id=1, source_target_pairs={{0,4},{1,5},{2,6},{3,7},{4,0},{5,1},{6,2},{7,3},{8,12},{9,13},{10,... | collective-permute-start | bytes 1769480 | tf_op jit(solution)/shard_map/ppermute | solution.py:577
  208.5 34.6 %collective-permute-start.47 = (bf16[2,4,2,48,768]{4,3,2,1,0:T(8,128)(2,1)S(1)}, bf16[2,4,2,48,768]{4,3,2,1,0:T(8,128)(2,1)S(1)}, u32[]{:S(2)}, u32[]{:S(2)}) collective-permute-start(bf16[2,4,2,48,768]{4,3,2,1,0:T(8,128)(2,1)S(1)} %pad_maximum_fusion.2), channel_id=1, source_target_pairs={{0,2},{1,3},{2,0},{3,1},{4,6},{5,7},{6,4},{7,5},{8,10},{9,11},{10,... | collective-permute-start | bytes 3538952 | tf_op jit(solution)/shard_map/ppermute | solution.py:577
  209.2 33.9 %collective-permute-start.49 = (bf16[2,4,2,48,768]{4,3,2,1,0:T(8,128)(2,1)S(1)}, bf16[2,4,2,48,768]{4,3,2,1,0:T(8,128)(2,1)S(1)}, u32[]{:S(2)}, u32[]{:S(2)}) collective-permute-start(bf16[2,4,2,48,768]{4,3,2,1,0:T(8,128)(2,1)S(1)} %pad_maximum_fusion.3), channel_id=1, source_target_pairs={{0,4},{1,5},{2,6},{3,7},{4,0},{5,1},{6,2},{7,3},{8,12},{9,13},{10,... | collective-permute-start | bytes 3538952 | tf_op jit(solution)/shard_map/ppermute | solution.py:577
  324.2 47.8 %collective-permute-start.96 = (bf16[16,48,768]{2,1,0:T(8,128)(2,1)}, bf16[16,48,768]{2,1,0:T(8,128)(2,1)}, u32[]{:S(2)}, u32[]{:S(2)}) collective-permute-start(bf16[16,48,768]{2,1,0:T(8,128)(2,1)} %get-tuple-element.245), channel_id=1, source_target_pairs={{0,2},{1,3},{2,0},{3,1},{4,6},{5,7},{6,4},{7,5},{8,10},{9,11},{10,... | collective-permute-start | bytes 3538952 | tf_op jit(solution)/shard_map/ppermute | solution.py:577
  326.9 50.2 %collective-permute-start.98 = (bf16[16,48,768]{2,1,0:T(8,128)(2,1)}, bf16[16,48,768]{2,1,0:T(8,128)(2,1)}, u32[]{:S(2)}, u32[]{:S(2)}) collective-permute-start(bf16[16,48,768]{2,1,0:T(8,128)(2,1)} %get-tuple-element.247), channel_id=1, source_target_pairs={{0,4},{1,5},{2,6},{3,7},{4,0},{5,1},{6,2},{7,3},{8,12},{9,13},{10,... | collective-permute-start | bytes 3538952 | tf_op jit(solution)/shard_map/ppermute | solution.py:577
  370.4 49.1 %collective-permute-start.80 = (bf16[16,48,384]{2,1,0:T(8,128)(2,1)}, bf16[16,48,384]{2,1,0:T(8,128)(2,1)}, u32[]{:S(2)}, u32[]{:S(2)}) collective-permute-start(bf16[16,48,384]{2,1,0:T(8,128)(2,1)} %get-tuple-element.221), channel_id=1, source_target_pairs={{0,2},{1,3},{2,0},{3,1},{4,6},{5,7},{6,4},{7,5},{8,10},{9,11},{10,... | collective-permute-start | bytes 1769480 | tf_op jit(solution)/shard_map/ppermute | solution.py:577
  370.9 50.5 %collective-permute-start.82 = (bf16[16,48,384]{2,1,0:T(8,128)(2,1)}, bf16[16,48,384]{2,1,0:T(8,128)(2,1)}, u32[]{:S(2)}, u32[]{:S(2)}) collective-permute-start(bf16[16,48,384]{2,1,0:T(8,128)(2,1)} %get-tuple-element.223), channel_id=1, source_target_pairs={{0,4},{1,5},{2,6},{3,7},{4,0},{5,1},{6,2},{7,3},{8,12},{9,13},{10,... | collective-permute-start | bytes 1769480 | tf_op jit(solution)/shard_map/ppermute | solution.py:577
  374.8 49.2 %collective-permute-start.97 = (bf16[4,2,48,768]{3,2,1,0:T(8,128)(2,1)}, bf16[4,2,48,768]{3,2,1,0:T(8,128)(2,1)}, u32[]{:S(2)}, u32[]{:S(2)}) collective-permute-start(bf16[4,2,48,768]{3,2,1,0:T(8,128)(2,1)} %bitcast.280), channel_id=1, source_target_pairs={{0,4},{1,5},{2,6},{3,7},{4,0},{5,1},{6,2},{7,3},{8,12},{9,13},{10,... | collective-permute-start | bytes 1769480 | tf_op jit(solution)/shard_map/ppermute | solution.py:577
  380.1 46.4 %collective-permute-start.99 = (bf16[4,2,48,768]{3,2,1,0:T(8,128)(2,1)}, bf16[4,2,48,768]{3,2,1,0:T(8,128)(2,1)}, u32[]{:S(2)}, u32[]{:S(2)}) collective-permute-start(bf16[4,2,48,768]{3,2,1,0:T(8,128)(2,1)} %bitcast.282), channel_id=1, source_target_pairs={{0,2},{1,3},{2,0},{3,1},{4,6},{5,7},{6,4},{7,5},{8,10},{9,11},{10,... | collective-permute-start | bytes 1769480 | tf_op jit(solution)/shard_map/ppermute | solution.py:577
  411.3 46.6 %collective-permute-start.58 = (bf16[256,768]{1,0:T(8,128)(2,1)}, bf16[256,768]{1,0:T(8,128)(2,1)}, u32[]{:S(2)}, u32[]{:S(2)}) collective-permute-start(bf16[256,768]{1,0:T(8,128)(2,1)} %get-tuple-element.190), channel_id=1, source_target_pairs={{0,1},{1,0},{2,3},{3,2},{4,5},{5,4},{6,7},{7,6},{8,9},{9,8},{10,11... | collective-permute-start | bytes 1179656 | tf_op jit(solution)/shard_map/ppermute | solution.py:577
  419.5 130.9 %collective-permute-start.88 = (bf16[16,48,768]{2,1,0:T(8,128)(2,1)}, bf16[16,48,768]{2,1,0:T(8,128)(2,1)}, u32[]{:S(2)}, u32[]{:S(2)}) collective-permute-start(bf16[16,48,768]{2,1,0:T(8,128)(2,1)} %get-tuple-element.237), channel_id=1, source_target_pairs={{0,2},{1,3},{2,0},{3,1},{4,6},{5,7},{6,4},{7,5},{8,10},{9,11},{10,... | collective-permute-start | bytes 3538952 | tf_op jit(solution)/shard_map/ppermute | solution.py:577
  423.9 30.5 %collective-permute-start.83 = (bf16[4,2,48,384]{3,2,1,0:T(8,128)(2,1)S(1)}, bf16[4,2,48,384]{3,2,1,0:T(8,128)(2,1)S(1)}, u32[]{:S(2)}, u32[]{:S(2)}) collective-permute-start(bf16[4,2,48,384]{3,2,1,0:T(8,128)(2,1)S(1)} %bitcast.654), channel_id=1, source_target_pairs={{0,2},{1,3},{2,0},{3,1},{4,6},{5,7},{6,4},{7,5},{8,10},{9,11},{10,... | collective-permute-start | bytes 884744 | tf_op jit(solution)/shard_map/ppermute | solution.py:577
  429.0 35.2 %collective-permute-start.102 = (bf16[4,48,768]{2,1,0:T(8,128)(2,1)}, bf16[4,48,768]{2,1,0:T(8,128)(2,1)}, u32[]{:S(2)}, u32[]{:S(2)}) collective-permute-start(bf16[4,48,768]{2,1,0:T(8,128)(2,1)} %get-tuple-element.337), channel_id=1, source_target_pairs={{0,8},{1,9},{2,10},{3,11},{4,12},{5,13},{6,14},{7,15},{8,16},{9,17... | collective-permute-start | bytes 884744 | tf_op jit(solution)/shard_map/ppermute | solution.py:577
  430.8 33.5 %collective-permute-start.101 = (bf16[4,48,768]{2,1,0:T(8,128)(2,1)}, bf16[4,48,768]{2,1,0:T(8,128)(2,1)}, u32[]{:S(2)}, u32[]{:S(2)}) collective-permute-start(bf16[4,48,768]{2,1,0:T(8,128)(2,1)} %get-tuple-element.338), channel_id=1, source_target_pairs={{0,16},{1,17},{2,18},{3,19},{4,20},{5,21},{6,22},{7,23},{8,24},{9,... | collective-permute-start | bytes 884744 | tf_op jit(solution)/shard_map/ppermute | solution.py:577
  457.9 95.3 %collective-permute-start.90 = (bf16[16,48,768]{2,1,0:T(8,128)(2,1)}, bf16[16,48,768]{2,1,0:T(8,128)(2,1)}, u32[]{:S(2)}, u32[]{:S(2)}) collective-permute-start(bf16[16,48,768]{2,1,0:T(8,128)(2,1)} %get-tuple-element.239), channel_id=1, source_target_pairs={{0,4},{1,5},{2,6},{3,7},{4,0},{5,1},{6,2},{7,3},{8,12},{9,13},{10,... | collective-permute-start | bytes 3538952 | tf_op jit(solution)/shard_map/ppermute | solution.py:577
  536.6 19.9 %collective-permute-start.60 = (bf16[256,768]{1,0:T(8,128)(2,1)}, bf16[256,768]{1,0:T(8,128)(2,1)}, u32[]{:S(2)}, u32[]{:S(2)}) collective-permute-start(bf16[256,768]{1,0:T(8,128)(2,1)} %get-tuple-element.199), channel_id=1, source_target_pairs={{0,1},{1,0},{2,3},{3,2},{4,5},{5,4},{6,7},{7,6},{8,9},{9,8},{10,11... | collective-permute-start | bytes 1179656 | tf_op jit(solution)/shard_map/ppermute | solution.py:577
  549.0 37.2 %collective-permute-start.71 = (bf16[16,48,384]{2,1,0:T(8,128)(2,1)S(1)}, bf16[16,48,384]{2,1,0:T(8,128)(2,1)S(1)}, u32[]{:S(2)}, u32[]{:S(2)}) collective-permute-start(bf16[16,48,384]{2,1,0:T(8,128)(2,1)S(1)} %get-tuple-element.213), channel_id=1, source_target_pairs={{0,2},{1,3},{2,0},{3,1},{4,6},{5,7},{6,4},{7,5},{8,10},{9,11},{10,... | collective-permute-start | bytes 1769480 | tf_op jit(solution)/shard_map/ppermute | solution.py:577
  549.5 37.7 %collective-permute-start.73 = (bf16[16,48,384]{2,1,0:T(8,128)(2,1)S(1)}, bf16[16,48,384]{2,1,0:T(8,128)(2,1)S(1)}, u32[]{:S(2)}, u32[]{:S(2)}) collective-permute-start(bf16[16,48,384]{2,1,0:T(8,128)(2,1)S(1)} %get-tuple-element.215), channel_id=1, source_target_pairs={{0,4},{1,5},{2,6},{3,7},{4,0},{5,1},{6,2},{7,3},{8,12},{9,13},{10,... | collective-permute-start | bytes 1769480 | tf_op jit(solution)/shard_map/ppermute | solution.py:577
  552.0 36.7 %collective-permute-start.89 = (bf16[4,2,48,768]{3,2,1,0:T(8,128)(2,1)S(1)}, bf16[4,2,48,768]{3,2,1,0:T(8,128)(2,1)S(1)}, u32[]{:S(2)}, u32[]{:S(2)}) collective-permute-start(bf16[4,2,48,768]{3,2,1,0:T(8,128)(2,1)S(1)} %bitcast.632), channel_id=1, source_target_pairs={{0,4},{1,5},{2,6},{3,7},{4,0},{5,1},{6,2},{7,3},{8,12},{9,13},{10,... | collective-permute-start | bytes 1769480 | tf_op jit(solution)/shard_map/ppermute | solution.py:577
  554.9 35.8 %collective-permute-start.91 = (bf16[4,2,48,768]{3,2,1,0:T(8,128)(2,1)S(1)}, bf16[4,2,48,768]{3,2,1,0:T(8,128)(2,1)S(1)}, u32[]{:S(2)}, u32[]{:S(2)}) collective-permute-start(bf16[4,2,48,768]{3,2,1,0:T(8,128)(2,1)S(1)} %bitcast.633), channel_id=1, source_target_pairs={{0,2},{1,3},{2,0},{3,1},{4,6},{5,7},{6,4},{7,5},{8,10},{9,11},{10,... | collective-permute-start | bytes 1769480 | tf_op jit(solution)/shard_map/ppermute | solution.py:577
  557.7 23.6 %collective-permute-start.61 = (bf16[128,768]{1,0:T(8,128)(2,1)S(1)}, bf16[128,768]{1,0:T(8,128)(2,1)S(1)}, u32[]{:S(2)}, u32[]{:S(2)}) collective-permute-start(bf16[128,768]{1,0:T(8,128)(2,1)S(1)} %slice.726), channel_id=1, source_target_pairs={{0,2},{1,3},{2,0},{3,1},{4,6},{5,7},{6,4},{7,5},{8,10},{9,11},{10,... | collective-permute-start | bytes 589832 | tf_op jit(solution)/shard_map/ppermute | solution.py:577
  585.8 68.4 %collective-permute-start.63 = (bf16[16,32,768]{2,1,0:T(8,128)(2,1)S(1)}, bf16[16,32,768]{2,1,0:T(8,128)(2,1)}, u32[]{:S(2)}, u32[]{:S(2)}) collective-permute-start(bf16[16,32,768]{2,1,0:T(8,128)(2,1)S(1)} %get-tuple-element.205), channel_id=1, source_target_pairs={{0,2},{1,3},{2,0},{3,1},{4,6},{5,7},{6,4},{7,5},{8,10},{9,11},{10,... | collective-permute-start | bytes 2359304 | tf_op jit(solution)/shard_map/ppermute | solution.py:577
  586.2 70.9 %collective-permute-start.65 = (bf16[16,32,768]{2,1,0:T(8,128)(2,1)S(1)}, bf16[16,32,768]{2,1,0:T(8,128)(2,1)}, u32[]{:S(2)}, u32[]{:S(2)}) collective-permute-start(bf16[16,32,768]{2,1,0:T(8,128)(2,1)S(1)} %get-tuple-element.207), channel_id=1, source_target_pairs={{0,4},{1,5},{2,6},{3,7},{4,0},{5,1},{6,2},{7,3},{8,12},{9,13},{10,... | collective-permute-start | bytes 2359304 | tf_op jit(solution)/shard_map/ppermute | solution.py:577
  587.2 24.6 %collective-permute-start.72 = (bf16[4,2,48,384]{3,2,1,0:T(8,128)(2,1)S(1)}, bf16[4,2,48,384]{3,2,1,0:T(8,128)(2,1)S(1)}, u32[]{:S(2)}, u32[]{:S(2)}) collective-permute-start(bf16[4,2,48,384]{3,2,1,0:T(8,128)(2,1)S(1)} %bitcast.653), channel_id=1, source_target_pairs={{0,4},{1,5},{2,6},{3,7},{4,0},{5,1},{6,2},{7,3},{8,12},{9,13},{10,... | collective-permute-start | bytes 884744 | tf_op jit(solution)/shard_map/ppermute | solution.py:577
  588.8 24.1 %collective-permute-start.74 = (bf16[4,2,48,384]{3,2,1,0:T(8,128)(2,1)S(1)}, bf16[4,2,48,384]{3,2,1,0:T(8,128)(2,1)S(1)}, u32[]{:S(2)}, u32[]{:S(2)}) collective-permute-start(bf16[4,2,48,384]{3,2,1,0:T(8,128)(2,1)S(1)} %bitcast.655), channel_id=1, source_target_pairs={{0,2},{1,3},{2,0},{3,1},{4,6},{5,7},{6,4},{7,5},{8,10},{9,11},{10,... | collective-permute-start | bytes 884744 | tf_op jit(solution)/shard_map/ppermute | solution.py:577
  590.9 25.7 %collective-permute-start.94 = (bf16[4,48,768]{2,1,0:T(8,128)(2,1)S(1)}, bf16[4,48,768]{2,1,0:T(8,128)(2,1)S(1)}, u32[]{:S(2)}, u32[]{:S(2)}) collective-permute-start(bf16[4,48,768]{2,1,0:T(8,128)(2,1)S(1)} %get-tuple-element.330), channel_id=1, source_target_pairs={{0,8},{1,9},{2,10},{3,11},{4,12},{5,13},{6,14},{7,15},{8,16},{9,17... | collective-permute-start | bytes 884744 | tf_op jit(solution)/shard_map/ppermute | solution.py:577
  616.6 27.3 %collective-permute-start.77 = (bf16[4,48,384]{2,1,0:T(8,128)(2,1)}, bf16[4,48,384]{2,1,0:T(8,128)(2,1)}, u32[]{:S(2)}, u32[]{:S(2)}) collective-permute-start(bf16[4,48,384]{2,1,0:T(8,128)(2,1)} %get-tuple-element.363), channel_id=1, source_target_pairs={{0,8},{1,9},{2,10},{3,11},{4,12},{5,13},{6,14},{7,15},{8,16},{9,17... | collective-permute-start | bytes 442376 | tf_op jit(solution)/shard_map/ppermute | solution.py:577
  (242 other events, 1943.4 us)

commit v2 on v1

v2 whole, which is shorter than its diff:
```python
import functools

import jax
import jax.numpy as jnp
from jax import lax
from jax.experimental import pallas as pl
from jax.experimental.pallas import tpu as pltpu
from jax.sharding import PartitionSpec as P

D = 768
HEADS = 12
HEAD_DIM = 64
HALF = D // 2
PAIRS = HEADS // 4
FF = 3072
POS = 1024
GRID = 1000
LAYERS = 2
CORES = 2
LANES = 128
EPS = 1e-12
DEAD = -1000000000.0
SCALE = HEAD_DIM ** (-0.5)
VMEM = 60 * 1024 * 1024
F32 = jnp.float32
BF16 = jnp.bfloat16

ROW_ATTN, ROW_OUT, ROW_GAIN, ROW_SHIFT, ROW_DOWN = 0, 4, 6, 10, 14
SMALL_ROWS = 16


def dot(a, b, dims=((1,), (0,))):
    return lax.dot_general(a, b, (dims, ((), ())), preferred_element_type=F32)


def halves(core):
    first = core[0] * HALF
    return pl.ds(pl.multiple_of(first, LANES), HALF), pl.ds(pl.multiple_of(HALF - first, LANES), HALF)


NT = ((1,), (1,))
TN = ((0,), (0,))


def sds(shape, dtype):
    return jax.ShapeDtypeStruct(shape, dtype)


def whole(shape):
    return pl.BlockSpec(shape, lambda *_: (0,) * len(shape))


def cost(flops, nbytes, trans=0):
    return pl.CostEstimate(flops=flops, bytes_accessed=nbytes, transcendentals=trans)


def params():
    return pltpu.CompilerParams(vmem_limit_bytes=VMEM)


def embed_kernel(idx, t0, t1, t2, t3, out):
    rows = t0.shape[0]
    place = lax.broadcasted_iota(jnp.int32, (idx.shape[0], rows), 1)

    def hot(*cols):
        total = None
        for col in cols:
            one = jnp.where(place == idx[:, col : col + 1], 1.0, 0.0)
            total = one if total is None else total + one
        return total.astype(BF16)

    out[...] = (
        dot(hot(0, 2), t0[...])
        + dot(hot(1, 3), t1[...])
        + dot(hot(4), t2[...])
        + dot(hot(5), t3[...])
    )


def embed(idx, tables):
    tokens = idx.shape[0]
    block = 128
    rows = tables[0].shape[0]
    return pl.pallas_call(
        embed_kernel,
        name="embed",
        out_shape=sds((tokens, D), F32),
        grid=(tokens // block,),
        in_specs=[pl.BlockSpec((block, 8), lambda i: (i, 0))] + [whole((rows, D))] * 4,
        out_specs=pl.BlockSpec((block, D), lambda i: (i, 0)),
        compiler_params=params(),
        cost_estimate=cost(8 * tokens * rows * D, 8 * rows * D + 4 * tokens * D),
    )(idx, *tables)


def table_kernel(idx, own, sib, o0, o1, o2, o3):
    half = own.shape[0]
    block = o0.shape[0]
    first = pl.program_id(0) * block
    place = lax.broadcasted_iota(jnp.int32, (block, 2 * half), 0) + first

    def hot(*rows):
        total = None
        for row in rows:
            one = jnp.where(place == idx[row : row + 1, :], 1.0, 0.0)
            total = one if total is None else total + one
        return total.astype(BF16)

    for out, rows in ((o0, (0, 2)), (o1, (1, 3)), (o2, (4,)), (o3, (5,))):
        mark = hot(*rows)
        out[...] = (dot(mark[:, :half], own[...]) + dot(mark[:, half:], sib[...])).astype(BF16)


def table_grads(idx, own, sib, rows):
    half = own.shape[0]
    block = 256
    return pl.pallas_call(
        table_kernel,
        name="table_grads",
        out_shape=[sds((rows, D), BF16)] * 4,
        grid=(rows // block,),
        in_specs=[whole((8, 2 * half)), whole((half, D)), whole((half, D))],
        out_specs=[pl.BlockSpec((block, D), lambda i: (i, 0))] * 4,
        compiler_params=params(),
        cost_estimate=cost(16 * half * rows * D, 8 * rows * D),
    )(idx, own, sib)


def attn_fwd_kernel(core, xo, xs, wq, wk, wv, small, mask, q, k, v, mo, ms, *, layer):
    half = xo.shape[0]
    for first, rows in ((0, xo), (half, xs)):
        x = rows[...]
        q[first : first + half, :] = (
            dot(x, wq[...]) + small[ROW_ATTN + 2 * layer : ROW_ATTN + 2 * layer + 1, :]
        ).astype(BF16)
        k[first : first + half, :] = dot(x, wk[...]).astype(BF16)
        v[first : first + half, :] = (
            dot(x, wv[...]) + small[ROW_ATTN + 2 * layer + 1 : ROW_ATTN + 2 * layer + 2, :]
        ).astype(BF16)
    keys, values = k[...], v[...]
    low_lanes = lax.broadcasted_iota(jnp.int32, (1, LANES), 1) < HEAD_DIM
    for first, out in ((0, mo), (half, ms)):
        queries = q[first : first + half, :].astype(F32) * SCALE
        parts = []
        for head in range(2):
            lanes = low_lanes if head == 0 else jnp.logical_not(low_lanes)
            one = jnp.where(lanes, queries, 0.0).astype(BF16)
            scores = dot(one, keys, NT) + mask[...]
            expo = jnp.exp(scores - jnp.max(scores, axis=-1, keepdims=True))
            total = jnp.sum(expo, axis=-1, keepdims=True)
            parts.append(dot(expo.astype(BF16), values) / total)
        out[...] = jnp.where(low_lanes, parts[0], parts[1]).astype(BF16)


def weight_block(part):
    return pl.BlockSpec((D, LANES), lambda p, core: (0, part * PAIRS + p))


def attn_fwd(core, xo, xs, wa, small, mask, layer):
    half = xo.shape[0]
    tokens = 2 * half
    col = lambda p, core: (0, p)
    rows = pl.BlockSpec((tokens, LANES), col)
    return pl.pallas_call(
        functools.partial(attn_fwd_kernel, layer=layer),
        name="attn_fwd",
        out_shape=[sds((tokens, HALF), BF16)] * 3 + [sds((half, HALF), BF16)] * 2,
        grid_spec=pltpu.PrefetchScalarGridSpec(
            num_scalar_prefetch=1,
            grid=(PAIRS,),
            in_specs=[
                whole((half, D)),
                whole((half, D)),
                weight_block(0),
                weight_block(1),
                weight_block(2),
                pl.BlockSpec((SMALL_ROWS, LANES), lambda p, core: (0, core[0] * PAIRS + p)),
                whole((1, tokens)),
            ],
            out_specs=[rows] * 3 + [pl.BlockSpec((half, LANES), col)] * 2,
        ),
        compiler_params=params(),
        cost_estimate=cost(
            2 * tokens * D * 3 * HALF + 4 * PAIRS * 2 * tokens * tokens * LANES,
            2 * (tokens * D + 3 * D * HALF + 4 * tokens * HALF),
            PAIRS * 2 * tokens * tokens,
        ),
    )(core, xo, xs, wa, wa, wa, small, mask)


def attn_bwd_kernel(
    core, dao, das, wom, wot, q, k, v, mo, ms, xo, xs, wq, wk, wv, mask,
    dwq, dwk, dwv, dwo, sums, dxo, dxs, acc, all_s, turned,
):
    half = xo.shape[0]
    step = pl.program_id(0)
    mine_cols, their_cols = halves(core)
    dq_s, dk_s, dv_s = [all_s.at[:, part * LANES : (part + 1) * LANES] for part in range(3)]

    @pl.when(step == 0)
    def _():
        turned[:, :half] = xo[...].T
        turned[:, half:] = xs[...].T

    keys, values = k[...], v[...]
    low_lanes = lax.broadcasted_iota(jnp.int32, (1, LANES), 1) < HEAD_DIM
    grad_keys = [None, None]
    grad_values = [None, None]
    for part, da in ((0, dao), (1, das)):
        first = part * half
        span = slice(first, first + half)
        grad_mix = dot(da[:, mine_cols], wom[...], NT) + dot(da[:, their_cols], wot[...], NT)
        queries = q[span, :].astype(F32) * SCALE
        grad_queries = []
        for head in range(2):
            lanes = low_lanes if head == 0 else jnp.logical_not(low_lanes)
            one = jnp.where(lanes, queries, 0.0).astype(BF16)
            scores = dot(one, keys, NT) + mask[...]
            expo = jnp.exp(scores - jnp.max(scores, axis=-1, keepdims=True))
            probs = expo * (1.0 / jnp.sum(expo, axis=-1, keepdims=True))
            grad_one = jnp.where(lanes, grad_mix, 0.0).astype(BF16)
            grad_probs = dot(grad_one, values, NT)
            weighted = probs * grad_probs
            delta = jnp.sum(weighted, axis=-1, keepdims=True)
            grad_scores = (weighted - probs * delta).astype(BF16)
            grad_queries.append(dot(grad_scores, keys))
            key_part = dot(grad_scores, one, TN)
            value_part = dot(probs.astype(BF16), grad_one, TN)
            if part == 0:
                grad_keys[head], grad_values[head] = key_part, value_part
            else:
                grad_keys[head] = grad_keys[head] + key_part
                grad_values[head] = grad_values[head] + value_part
        dq_s[span, :] = (jnp.where(low_lanes, grad_queries[0], grad_queries[1]) * SCALE).astype(BF16)
    dk_s[...] = (grad_keys[0] + grad_keys[1]).astype(BF16)
    dv_s[...] = (grad_values[0] + grad_values[1]).astype(BF16)
    sums[...] = jnp.zeros_like(sums)
    sums[0:1, :] = jnp.sum(dq_s[...].astype(F32), axis=0, keepdims=True)
    sums[1:2, :] = jnp.sum(dv_s[...].astype(F32), axis=0, keepdims=True)
    for part, out in enumerate((dwq, dwk, dwv)):
        out[...] = dot(turned[...], all_s[:, part * LANES : (part + 1) * LANES]).astype(BF16)
    out_rows = dot(mo[...], dao[...], TN) + dot(ms[...], das[...], TN)
    dwo[0] = out_rows[:, :HALF].astype(BF16)
    dwo[1] = out_rows[:, HALF:].astype(BF16)
    total = dot(dq_s[...], wq[...], NT) + dot(dk_s[...], wk[...], NT) + dot(dv_s[...], wv[...], NT)

    @pl.when(step == 0)
    def _():
        acc[...] = total

    @pl.when(step > 0)
    def _():
        acc[...] += total

    @pl.when(step == PAIRS - 1)
    def _():
        dxo[...] = acc[:half, :]
        dxs[...] = acc[half:, :].astype(BF16)


def attn_bwd(core, dao, das, wom, wot, q, k, v, mo, ms, xo, xs, wa, mask):
    half = xo.shape[0]
    tokens = 2 * half
    col = lambda p, core: (0, p)
    weight = pl.BlockSpec((D, LANES), col)
    rows = pl.BlockSpec((tokens, LANES), col)
    part = pl.BlockSpec((half, LANES), col)
    out_rows = pl.BlockSpec((LANES, HALF), lambda p, core: (core[0] * PAIRS + p, 0))
    return pl.pallas_call(
        attn_bwd_kernel,
        name="attn_bwd",
        out_shape=[sds((D, HALF), BF16)] * 3
        + [
            sds((CORES, HALF, HALF), BF16),
            sds((8, HALF), F32),
            sds((half, D), F32),
            sds((half, D), BF16),
        ],
        grid_spec=pltpu.PrefetchScalarGridSpec(
            num_scalar_prefetch=1,
            grid=(PAIRS,),
            in_specs=[
                whole((half, D)),
                whole((half, D)),
                out_rows,
                out_rows,
                rows,
                rows,
                rows,
                part,
                part,
                whole((half, D)),
                whole((half, D)),
                weight_block(0),
                weight_block(1),
                weight_block(2),
                whole((1, tokens)),
            ],
            out_specs=[weight] * 3
            + [
                pl.BlockSpec((CORES, LANES, HALF), lambda p, core: (0, p, 0)),
                pl.BlockSpec((8, LANES), col),
                whole((half, D)),
                whole((half, D)),
            ],
            scratch_shapes=[
                pltpu.VMEM((tokens, D), F32),
                pltpu.VMEM((tokens, 3 * LANES), BF16),
                pltpu.VMEM((D, tokens), BF16),
            ],
        ),
        compiler_params=params(),
        cost_estimate=cost(
            8 * tokens * D * 3 * HALF // 2 + 10 * PAIRS * 2 * tokens * tokens * LANES,
            2 * (4 * tokens * D + 8 * D * HALF + 4 * tokens * HALF),
            PAIRS * 2 * tokens * tokens,
        ),
    )(core, dao, das, wom, wot, q, k, v, mo, ms, xo, xs, wa, wa, wa, mask)


def norm_rows(h, gain, shift, y, yb, n, rstd):
    mean = jnp.mean(h, axis=-1, keepdims=True)
    centred = h - mean
    scale = lax.rsqrt(jnp.mean(centred * centred, axis=-1, keepdims=True) + EPS)
    normal = centred * scale
    out = normal * gain + shift
    y[...] = out
    yb[...] = out.astype(BF16)
    n[...] = normal
    rstd[...] = scale


def norm_outs(half):
    return [sds((half, D), F32), sds((half, D), BF16), sds((half, D), F32), sds((half, 1), F32)]


def out_norm_kernel(core, mine, theirs, wom, wot, base, small, y, yb, n, rstd, *, layer):
    mine_rows, their_rows = halves(core)
    near = dot(mine[...], wom[mine_rows, :]) + dot(theirs[...], wom[their_rows, :])
    far = dot(mine[...], wot[mine_rows, :]) + dot(theirs[...], wot[their_rows, :])
    first = core[0] == 0
    mixed = jnp.concatenate([jnp.where(first, near, far), jnp.where(first, far, near)], axis=1)
    h = base[...] + mixed + small[ROW_OUT + layer : ROW_OUT + layer + 1, :]
    row = 2 * layer
    norm_rows(
        h, small[ROW_GAIN + row : ROW_GAIN + row + 1, :], small[ROW_SHIFT + row : ROW_SHIFT + row + 1, :],
        y, yb, n, rstd,
    )


def out_norm(core, mine, theirs, wom, wot, base, small, layer):
    half = base.shape[0]
    return pl.pallas_call(
        functools.partial(out_norm_kernel, layer=layer),
        name="out_norm",
        out_shape=norm_outs(half),
        in_specs=[pl.BlockSpec(memory_space=pltpu.SMEM)] + [pl.BlockSpec(memory_space=pltpu.VMEM)] * 6,
        out_specs=[pl.BlockSpec(memory_space=pltpu.VMEM)] * 4,
        compiler_params=params(),
        cost_estimate=cost(2 * half * D * D, 2 * D * D + 16 * half * D),
    )(core, mine, theirs, wom, wot, base, small)


def add_norm_kernel(base, part, recv, small, y, yb, n, rstd, *, layer):
    h = base[...] + part[...] + recv[...].astype(F32) + small[ROW_DOWN + layer : ROW_DOWN + layer + 1, :]
    row = 2 * layer + 1
    norm_rows(
        h, small[ROW_GAIN + row : ROW_GAIN + row + 1, :], small[ROW_SHIFT + row : ROW_SHIFT + row + 1, :],
        y, yb, n, rstd,
    )


def add_norm(base, part, recv, small, layer):
    half = base.shape[0]
    return pl.pallas_call(
        functools.partial(add_norm_kernel, layer=layer),
        name="add_norm",
        out_shape=norm_outs(half),
        in_specs=[pl.BlockSpec(memory_space=pltpu.VMEM)] * 4,
        out_specs=[pl.BlockSpec(memory_space=pltpu.VMEM)] * 4,
        compiler_params=params(),
        cost_estimate=cost(20 * half * D, 20 * half * D),
    )(base, part, recv, small)


def norm_bwd_kernel(*refs, row, summed):
    if summed:
        base, part, recv, n, rstd, small, gh, ghb, sums = refs
        gz = base[...] + part[...] + recv[...].astype(F32)
    else:
        base, live, n, rstd, small, gh, ghb, sums = refs
        gz = base[...].astype(F32) * live[...]
    normal = n[...]
    e = gz * small[ROW_GAIN + row : ROW_GAIN + row + 1, :]
    mean = jnp.mean(e, axis=-1, keepdims=True)
    slope = jnp.mean(e * normal, axis=-1, keepdims=True)
    grad = (e - mean - normal * slope) * rstd[...]
    low = grad.astype(BF16)
    gh[...] = grad
    ghb[...] = low
    sums[...] = jnp.zeros_like(sums)
    sums[0:1, :] = jnp.sum(gz * normal, axis=0, keepdims=True)
    sums[1:2, :] = jnp.sum(gz, axis=0, keepdims=True)
    sums[2:3, :] = jnp.sum(low.astype(F32), axis=0, keepdims=True)


def norm_bwd(sources, n, rstd, small, row):
    half = n.shape[0]
    operands = tuple(sources) + (n, rstd, small)
    return pl.pallas_call(
        functools.partial(norm_bwd_kernel, row=row, summed=len(sources) == 3),
        name="norm_bwd",
        out_shape=[sds((half, D), F32), sds((half, D), BF16), sds((8, D), F32)],
        in_specs=[pl.BlockSpec(memory_space=pltpu.VMEM)] * len(operands),
        out_specs=[pl.BlockSpec(memory_space=pltpu.VMEM)] * 3,
        compiler_params=params(),
        cost_estimate=cost(20 * half * D, 20 * half * D),
    )(*operands)


FF_BLOCK = 256
FF_STEPS = FF // CORES // FF_BLOCK


def ffn_fwd_kernel(yo, ys, w1, bias, w2, act, slope, po, ps, acc, *, layer):
    half = yo.shape[0]
    j = pl.program_id(0)
    for first, rows in ((0, yo), (half, ys)):
        span = slice(first, first + half)
        up = dot(rows[...], w1[...]) + bias[layer : layer + 1, :]
        cdf = 0.5 * (1.0 + lax.erf(up * (2.0**-0.5)))
        low = (up * cdf).astype(BF16)
        act[span, :] = low
        slope[span, :] = (cdf + up * (jnp.exp(-0.5 * up * up) * 0.3989422804014327)).astype(BF16)
        total = dot(low, w2[...])

        @pl.when(j == 0)
        def _():
            acc[span, :] = total

        @pl.when(j > 0)
        def _():
            acc[span, :] += total

    @pl.when(j == FF_STEPS - 1)
    def _():
        po[...] = acc[:half, :]
        ps[...] = acc[half:, :].astype(BF16)


DOWN_STEPS = D // FF_BLOCK


def ffn_specs(tokens, col):
    return (
        pl.BlockSpec((D, FF_BLOCK), lambda j: (0, col // FF_BLOCK + j)),
        pl.BlockSpec((FF_BLOCK, D), lambda j: (j % DOWN_STEPS, col // D + 2 + j // DOWN_STEPS)),
        pl.BlockSpec((tokens, FF_BLOCK), lambda j: (0, j)),
    )


def ffn_fwd(yo, ys, wf, col, bias, layer):
    half = yo.shape[0]
    tokens = 2 * half
    width = FF // CORES
    cols, down, rows = ffn_specs(tokens, col)
    return pl.pallas_call(
        functools.partial(ffn_fwd_kernel, layer=layer),
        name="ffn_fwd",
        out_shape=[sds((tokens, width), BF16)] * 2 + [sds((half, D), F32), sds((half, D), BF16)],
        grid=(FF_STEPS,),
        in_specs=[
            whole((half, D)),
            whole((half, D)),
            cols,
            pl.BlockSpec((LAYERS, FF_BLOCK), lambda j: (0, j)),
            down,
        ],
        out_specs=[rows] * 2 + [whole((half, D))] * 2,
        scratch_shapes=[pltpu.VMEM((tokens, D), F32)],
        compiler_params=params(),
        cost_estimate=cost(4 * tokens * D * width, 4 * D * width + 4 * tokens * width, tokens * width),
    )(yo, ys, wf, bias, wf)


def ffn_bwd_kernel(dfo, dfs, w1, w2, act, slope, yo, ys, dw1, dw2, sums, po, ps, acc, du, turned):
    half = yo.shape[0]
    j = pl.program_id(0)

    @pl.when(j == 0)
    def _():
        turned[:, :half] = yo[...].T
        turned[:, half:] = ys[...].T

    for first, rows in ((0, dfo), (half, dfs)):
        span = slice(first, first + half)
        low = (slope[span, :].astype(F32) * dot(rows[...], w2[...], NT)).astype(BF16)
        du[span, :] = low
        total = dot(low, w1[...], NT)

        @pl.when(j == 0)
        def _():
            acc[span, :] = total

        @pl.when(j > 0)
        def _():
            acc[span, :] += total

    sums[...] = jnp.zeros_like(sums)
    sums[0:1, :] = jnp.sum(du[...].astype(F32), axis=0, keepdims=True)
    dw1[...] = dot(turned[...], du[...]).astype(BF16)
    dw2[...] = (dot(act[:half, :], dfo[...], TN) + dot(act[half:, :], dfs[...], TN)).astype(BF16)

    @pl.when(j == FF_STEPS - 1)
    def _():
        po[...] = acc[:half, :]
        ps[...] = acc[half:, :].astype(BF16)


def ffn_bwd(dfo, dfs, wf, col, act, slope, yo, ys):
    half = yo.shape[0]
    tokens = 2 * half
    width = FF // CORES
    cols, down, rows = ffn_specs(tokens, col)
    return pl.pallas_call(
        ffn_bwd_kernel,
        name="ffn_bwd",
        out_shape=[
            sds((2, D, D), BF16),
            sds((2, D, D), BF16),
            sds((8, width), F32),
            sds((half, D), F32),
            sds((half, D), BF16),
        ],
        grid=(FF_STEPS,),
        in_specs=[whole((half, D))] * 2 + [cols, down, rows, rows] + [whole((half, D))] * 2,
        out_specs=[
            pl.BlockSpec((None, D, FF_BLOCK), lambda j: (j // DOWN_STEPS, 0, j % DOWN_STEPS)),
            pl.BlockSpec((None, FF_BLOCK, D), lambda j: (j // DOWN_STEPS, j % DOWN_STEPS, 0)),
            pl.BlockSpec((8, FF_BLOCK), lambda j: (0, j)),
        ]
        + [whole((half, D))] * 2,
        scratch_shapes=[
            pltpu.VMEM((tokens, D), F32),
            pltpu.VMEM((tokens, FF_BLOCK), BF16),
            pltpu.VMEM((D, tokens), BF16),
        ],
        compiler_params=params(),
        cost_estimate=cost(8 * tokens * D * width, 8 * D * width + 4 * tokens * width),
    )(dfo, dfs, wf, wf, act, slope, yo, ys)


def shuffle_kernel(table, *refs, moves, count):
    for out, to, to_col, source, at, at_col, width in moves:
        to = table[to[0]] if isinstance(to, list) else to
        at = table[at[0]] if isinstance(at, list) else at
        refs[count + out][to, :, to_col : to_col + width] = refs[source][at, :, at_col : at_col + width]


def shuffle(table, sources, shapes, moves):
    nbytes = sum(4 * source.size for source in sources)
    return pl.pallas_call(
        functools.partial(shuffle_kernel, moves=moves, count=len(sources)),
        name="shuffle",
        out_shape=shapes,
        in_specs=[pl.BlockSpec(memory_space=pltpu.SMEM)]
        + [pl.BlockSpec(memory_space=pltpu.VMEM)] * len(sources),
        out_specs=[pl.BlockSpec(memory_space=pltpu.VMEM)] * len(shapes),
        compiler_params=params(),
        cost_estimate=cost(0, nbytes),
    )(table, *sources)


def pack_kernel(core, qkv, out, up, mine, send):
    chips = FF // (2 * CORES * FF_CHUNK)
    ups = up[0].astype(F32)
    parts = []
    for parity in range(CORES):
        starts = [
            ((chip * CORES + parity) * 2 + part) * FF_CHUNK for part in range(2) for chip in range(chips)
        ]
        parts.append(jnp.concatenate([ups[:, start : start + FF_CHUNK] for start in starts], axis=1))
    even = core[0] == 0
    for ref, cols, ff in (
        (mine, halves(core)[0], jnp.where(even, parts[0], parts[1])),
        (send, halves(core)[1], jnp.where(even, parts[1], parts[0])),
    ):
        for part in range(3):
            whole_part = qkv.at[0, :, part * D : (part + 1) * D]
            ref[:, part * HALF : (part + 1) * HALF] = whole_part[:, cols]
        ref[:, 3 * HALF : 4 * HALF] = out.at[0][:, cols]
        ref[:, 4 * HALF :] = ff.astype(BF16)


FF_CHUNK = 48
PACKED = 4 * HALF + FF // CORES


def layer_block(shape, layer):
    return pl.BlockSpec((1,) + shape, lambda *_: (layer, 0, 0))


def pack(core, attn_in, attn_out, ffn_in, layer):
    rows = attn_in.shape[1]
    return pl.pallas_call(
        pack_kernel,
        name="pack",
        out_shape=[sds((rows, PACKED), BF16)] * 2,
        grid=(1,),
        in_specs=[
            pl.BlockSpec(memory_space=pltpu.SMEM),
            layer_block((rows, 3 * D), layer),
            layer_block((rows, D), layer),
            layer_block((rows, FF), layer),
        ],
        out_specs=[whole((rows, PACKED))] * 2,
        compiler_params=params(),
        cost_estimate=cost(0, 8 * rows * PACKED),
    )(core, attn_in, attn_out, ffn_in)


def join_kernel(core, mine, recv, down, *outs):
    rows = mine.shape[0]
    even = core[0] == 0
    near, far = mine[...].astype(F32), recv[...].astype(F32)
    both = jnp.concatenate([jnp.where(even, near, far), jnp.where(even, far, near)], axis=0).astype(BF16)
    downs = [down[0, part * CORES * rows : (part + 1) * CORES * rows, :] for part in range(2)]
    attn, ffn = outs
    for unit in range(2):
        attn[unit] = both[:, unit * D : (unit + 1) * D]
        ffn[2 * unit] = both[:, (2 + unit) * D : (3 + unit) * D]
        ffn[2 * unit + 1] = downs[unit]


def join(core, mine, recv, ffn_out, layer, shapes):
    rows = mine.shape[0]
    down = ffn_out.shape[1]
    return pl.pallas_call(
        join_kernel,
        name="join",
        out_shape=[sds(shape, BF16) for shape in shapes],
        grid=(1,),
        in_specs=[
            pl.BlockSpec(memory_space=pltpu.SMEM),
            whole((rows, PACKED)),
            whole((rows, PACKED)),
            layer_block((down, D), layer),
        ],
        out_specs=[whole(shape) for shape in shapes],
        compiler_params=params(),
        cost_estimate=cost(0, 8 * rows * PACKED),
    )(core, mine, recv, ffn_out)


def split_kernel(core, *refs):
    mine, send = refs[-2:]
    rows = mine.shape[0]
    even = core[0] == 0
    for part, block in enumerate(refs[:-2]):
        top, bottom = block[:rows, :], block[rows:, :]
        mine[:, part * D : (part + 1) * D] = jnp.where(even, top, bottom)
        send[:, part * D : (part + 1) * D] = jnp.where(even, bottom, top)


def split(core, units):
    rows = units[0].shape[0] // CORES
    return pl.pallas_call(
        split_kernel,
        name="split",
        out_shape=[sds((rows, PACKED), F32)] * 2,
        in_specs=[pl.BlockSpec(memory_space=pltpu.SMEM)] + [pl.BlockSpec(memory_space=pltpu.VMEM)] * len(units),
        out_specs=[pl.BlockSpec(memory_space=pltpu.VMEM)] * 2,
        compiler_params=params(),
        cost_estimate=cost(0, 16 * rows * PACKED),
    )(core, *units)


def merge_kernel(core, *refs):
    qkv, out, up, down = refs[4 * LAYERS :]
    chips = FF // (2 * CORES * FF_CHUNK)
    even = core[0] == 0
    for layer in range(LAYERS):
        mine, recv, first_down, second_down = refs[4 * layer : 4 * layer + 4]
        near, far = mine[...], recv[...]
        first, second = jnp.where(even, near, far), jnp.where(even, far, near)
        for part in range(3):
            span = slice(part * HALF, (part + 1) * HALF)
            qkv[layer, :, part * D : part * D + HALF] = first[:, span]
            qkv[layer, :, part * D + HALF : (part + 1) * D] = second[:, span]
        out[layer, :, :HALF] = first[:, 3 * HALF : 4 * HALF]
        out[layer, :, HALF:] = second[:, 3 * HALF : 4 * HALF]
        chunks = []
        for chip in range(chips):
            for source in (first, second):
                for part in range(2):
                    start = 4 * HALF + part * D + chip * FF_CHUNK
                    chunks.append(source[:, start : start + FF_CHUNK])
        up[layer] = jnp.concatenate(chunks, axis=1)
        rows = first_down.shape[0]
        down[layer, :rows, :] = first_down[...]
        down[layer, rows:, :] = second_down[...]


def merge(core, parts):
    rows = parts[0].shape[0]
    down = 2 * parts[2].shape[0]
    return pl.pallas_call(
        merge_kernel,
        name="merge",
        out_shape=[
            sds((LAYERS, rows, 3 * D), F32),
            sds((LAYERS, rows, D), F32),
            sds((LAYERS, rows, FF), F32),
            sds((LAYERS, down, D), F32),
        ],
        in_specs=[pl.BlockSpec(memory_space=pltpu.SMEM)] + [pl.BlockSpec(memory_space=pltpu.VMEM)] * len(parts),
        out_specs=[pl.BlockSpec(memory_space=pltpu.VMEM)] * 4,
        compiler_params=params(),
        cost_estimate=cost(0, 32 * rows * PACKED),
    )(core, *parts)


class Places:
    def __init__(self, pages, bands):
        self.ny = bands // CORES
        self.nx = self.ny if pages % self.ny == 0 else 1
        self.nz = pages // self.nx
        self.chips = pages * self.ny
        page, band = lax.axis_index("page"), lax.axis_index("band")
        self.z, self.x = page // self.nx, page % self.nx
        self.y, self.core = band // CORES, band % CORES
        self.sizes = (self.nz, self.nx, self.ny, CORES)

    def move(self, value, axis, step, flip=False):
        pairs = []
        nz, nx, ny, nc = self.sizes
        for device in range(nz * nx * ny * nc):
            place = [device // (nx * ny * nc), device // (ny * nc) % nx, device // nc % ny, device % nc]
            place[axis] = place[axis] ^ step if flip else (place[axis] + step) % self.sizes[axis]
            pairs.append((device, ((place[0] * nx + place[1]) * ny + place[2]) * nc + place[3]))
        return lax.ppermute(value, ("page", "band"), pairs)

    def exchange(self, wants):
        keys = []
        for axis, step, _ in wants:
            key = (axis, step if axis == 0 else step % self.sizes[axis])
            keys.append(key)
        got = [None] * len(wants)
        for key in dict.fromkeys(keys):
            numbers = [i for i, other in enumerate(keys) if other == key]
            flat = [wants[i][2].reshape(-1, wants[i][2].shape[-1]) for i in numbers]
            moved = self.move(jnp.concatenate(flat) if len(flat) > 1 else flat[0], *key, flip=key[0] == 0)
            first = 0
            for i, part in zip(numbers, flat):
                got[i] = moved[first : first + part.shape[0]].reshape(wants[i][2].shape)
                first += part.shape[0]
        return got

    def swap(self, value):
        return self.move(value, 3, 1)

    def chip_of(self, kz, kx, ky):
        z, x, y = self.z ^ kz, (self.x - kx) % self.nx, (self.y - ky) % self.ny
        return (z * self.nx + x) * self.ny + y

    def flips(self):
        return [1 << bit for bit in reversed(range(self.nz.bit_length() - 1))]


def tie(values, *others):
    return lax.optimization_barrier((values, others))[0]


class Gather:
    def __init__(self, at, local, shapes, place):
        self.at, self.local = at, local
        self.half = local.shape[0] // 2
        self.shapes, self.place = shapes, place
        self.stages = [functools.partial(self.flip, step) for step in at.flips()]
        self.stages += [self.first, self.second]
        self.held = local[None]
        self.spots = [0]

    def flip(self, step, got):
        if got:
            self.held = jnp.concatenate([self.held] + list(got))
        self.spots = self.spots + [spot ^ step for spot in self.spots]
        return [(0, step, self.held)]

    def near(self, axis, part):
        return [(axis, k, part) for k in range(1, self.at.sizes[axis])]

    def first(self, got):
        held = jnp.concatenate([self.held] + list(got))
        self.sent = [held[:, : self.half], held[:, self.half :]]
        return self.near(1, self.sent[0]) + self.near(2, self.sent[1])

    def second(self, got):
        cut = self.at.nx - 1
        self.sent = [jnp.stack([part] + got) for part, got in zip(self.sent, (got[:cut], got[cut:]))]
        return self.near(2, self.sent[0]) + self.near(1, self.sent[1])

    def finish(self, got):
        at = self.at
        rows, cols = self.local.shape[1:]
        sources, moves, table = [], [], []
        cut = at.ny - 1
        for axes, part, other, start in (
            ((1, 2), self.sent[0], got[:cut], 0),
            ((2, 1), self.sent[1], got[cut:], self.half),
        ):
            for far, piece in enumerate([part] + list(other)):
                number = 0
                for near in range(at.sizes[axes[0]]):
                    kx, ky = (near, far) if axes[0] == 1 else (far, near)
                    for kz in self.spots:
                        chip = at.chip_of(kz, kx, ky)
                        for unit in range(start, start + self.half):
                            for out, step, offset, to_col, at_col, width in self.place[unit]:
                                moves.append(
                                    (out, [len(table)], to_col, len(sources), number, at_col, width)
                                )
                                table.append(chip * step + offset)
                            number += 1
                sources.append(piece.reshape((-1, rows, cols)))
        outs = shuffle(jnp.stack(table), sources, [sds(shape, BF16) for shape in self.shapes], moves)
        return [out.reshape(-1, out.shape[-1]) for out in outs]


class Reduce:
    def __init__(self, at, first, second):
        self.at, self.halves = at, (first, second)
        self.stages = [self.first, self.second]
        self.stages += [functools.partial(self.flip, number) for number in range(len(at.flips()))]

    def picked(self, groups, axis, index):
        at = self.at
        rows = []
        for group in groups:
            parts = []
            for part in group:
                blocks = part.reshape(at.nz, at.nx, at.ny, part.shape[0] // at.chips, part.shape[1])
                parts.append(pick(blocks, index, axis))
            rows.append(jnp.concatenate(parts, axis=-1) if len(parts) > 1 else parts[0])
        return jnp.concatenate(rows, axis=2) if len(rows) > 1 else rows[0]

    def first(self, got):
        at = self.at
        wants = [(2, -k, self.picked(self.halves[0], 2, (at.y - k) % at.ny)) for k in range(1, at.ny)]
        return wants + [
            (1, -k, self.picked(self.halves[1], 1, (at.x - k) % at.nx)) for k in range(1, at.nx)
        ]

    def second(self, got):
        at = self.at
        cut = at.ny - 1
        self.lows = []
        for mine, other in (
            (self.picked(self.halves[0], 2, at.y), got[:cut]),
            (self.picked(self.halves[1], 1, at.x), got[cut:]),
        ):
            self.lows.append(self.total(mine, other).astype(BF16))
        wants = [(1, -k, pick(self.lows[0], (at.x - k) % at.nx, 1)) for k in range(1, at.nx)]
        return wants + [(2, -k, pick(self.lows[1], (at.y - k) % at.ny, 1)) for k in range(1, at.ny)]

    def total(self, mine, other):
        mine = mine.astype(F32)
        for term in other:
            mine = mine + term.astype(F32)
        return mine

    def flip(self, number, got):
        at = self.at
        bit = 1 << number
        if number == 0:
            cut = at.nx - 1
            first = self.total(pick(self.lows[0], at.x, 1), got[:cut])
            second = self.total(pick(self.lows[1], at.y, 1), got[cut:])
            self.cut = first.shape[1]
            low = jnp.concatenate([first, second], axis=1).astype(BF16)
        else:
            low = self.total(self.low, got).astype(BF16)
        low = low.reshape((low.shape[0] // 2, 2) + low.shape[1:])
        side = at.z // bit % 2
        self.low = pick(low, side, 1)
        return [(0, bit, pick(low, 1 - side, 1))]

    def finish(self, got):
        total = self.total(self.low, got)[0]
        return total[: self.cut], total[self.cut :]


class Line:
    def __init__(self, at):
        self.at, self.chunks, self.age, self.got = at, [], [], []

    def add(self, chunk):
        self.chunks.append(chunk)
        self.age.append(0)
        self.got.append([])

    def step(self, *others, extra=None):
        wants, spans = [], []
        for number, chunk in enumerate(self.chunks):
            if self.age[number] < len(chunk.stages):
                new = chunk.stages[self.age[number]](self.got[number])
                spans.append((number, len(wants), len(wants) + len(new)))
                wants += new
                self.age[number] += 1
        values, others = lax.optimization_barrier(([want[2] for want in wants], others))
        wants = [want[:2] + (value,) for want, value in zip(wants, values)]
        self.spans, self.moved = spans, self.at.exchange(wants)
        return others

    def close(self, *others):
        self.moved, others = lax.optimization_barrier((self.moved, others))
        for number, start, stop in self.spans:
            self.got[number] = self.moved[start:stop]
        return others

    def busy(self):
        return not all(self.done(chunk) for chunk in self.chunks)

    def done(self, chunk):
        number = self.chunks.index(chunk)
        return self.age[number] == len(chunk.stages)

    def fresh(self, chunk):
        return self.done(chunk) and any(span[0] == self.chunks.index(chunk) for span in self.spans)

    def result(self, chunk):
        return chunk.finish(self.got[self.chunks.index(chunk)])


def blocks_kernel(scalars, *refs, count, jobs):
    def rows(place, height):
        start, slopes = place
        for number, slope in slopes:
            start = start + scalars[number] * slope
        return pl.ds(pl.multiple_of(start, 16) if slopes else start, height)

    for out, to, height, terms in jobs:
        total = None
        for parts, place in terms:
            values = [refs[ref][rows(place, height), :] for ref in parts]
            value = values[0] if len(values) == 1 else jnp.concatenate(values, axis=1)
            if len(terms) > 1:
                value = value.astype(F32)
            total = value if total is None else total + value
        ref = refs[count + out]
        ref[to : to + height, :] = total.astype(ref.dtype)


class Stream:
    def __init__(self, parts, first_y, rows, base=0):
        self.parts, self.first_y, self.rows, self.base = parts, first_y, rows, base
        self.age = 0
        self.keep = self.recv = self.total = None


class Pipe:
    def __init__(self, at):
        self.at, self.groups = at, []
        self.bits = at.nz.bit_length() - 1
        self.last = 2 + self.bits
        scalars = [at.x, at.y] + [at.z // (1 << bit) % 2 for bit in range(self.bits)]
        self.scalars = jnp.stack(scalars).astype(jnp.int32)

    def add(self, streams):
        self.groups.append(streams)

    def pieces(self, stream, rows):
        nz = self.at.nz
        first = 1 if stream.first_y else 0
        strides = (2, 1)

        def chip(z, coords):
            start, slopes = stream.base + 4 * z * rows, []
            for axis, (fixed, slope) in enumerate(coords):
                start += fixed * strides[axis] * rows
                if slope:
                    slopes.append((axis, slope * strides[axis] * rows))
            return start, slopes

        def spot(fixed, number, slope, scale, base=0):
            return (base + fixed * scale, [(number, slope * scale)])

        other, same = (1, -1), (0, 1)
        sent, kept = [], []
        if stream.age == 0:
            for z in range(nz):
                for far in range(2):
                    coords = [None, None]
                    coords[first], coords[1 - first] = other, (far, 0)
                    sent.append([(stream.parts, chip(z, coords))])
        elif stream.age == 1:
            ref, base = stream.recv
            for out, side in ((sent, other), (kept, same)):
                for z in range(nz):
                    coords = [None, None]
                    coords[first], coords[1 - first] = same, side
                    place = spot(2 * z + side[0], 1 - first, side[1], rows, base)
                    out.append([(stream.parts, chip(z, coords)), ([ref], place)])
        elif stream.age < self.last:
            bit = stream.age - 2
            ref, base = stream.recv
            for out, side in ((sent, other), (kept, same)):
                for high in range(nz >> (bit + 1)):
                    fixed = 2 * high + side[0]
                    keep = spot(fixed, 2 + bit, side[1], rows)
                    out.append([([stream.keep], keep), ([ref], spot(fixed, 2 + bit, side[1], rows, base))])
        else:
            ref, base = stream.recv
            kept.append([([stream.keep], (0, [])), ([ref], (base, []))])
        return sent, kept

    def step(self, *others, extra=None):
        arrays, shapes, jobs = [], [], []
        heights, keeps, self.sent = {}, [], []

        def number(array):
            for i, known in enumerate(arrays):
                if known is array:
                    return i
            arrays.append(array)
            return len(arrays) - 1

        todo = []
        for streams in self.groups:
            for stream in streams:
                if stream.age > self.last:
                    continue
                rows = stream.rows
                sent, kept = self.pieces(stream, rows)
                axis = (2, 1) if stream.first_y else (1, 2)
                key = axis[stream.age] if stream.age < 2 else -stream.age
                start = heights.get(key, 0)
                if sent:
                    heights[key] = start + len(sent) * rows
                    self.sent.append((stream, key, start))
                todo.append((stream, key, start, sent, kept, rows))
        if extra is not None:
            span = (heights.get(2, 0), extra.shape[0])
            heights[2] = sum(span)
        order = list(heights)
        shapes = [sds((heights[key], D), BF16) for key in order]
        if extra is not None:
            jobs.append((order.index(2), span[0], span[1], [([number(extra)], (0, []))]))
        for stream, key, start, sent, kept, rows in todo:
            for block, terms in enumerate(sent):
                terms = [([number(part) for part in parts], place) for parts, place in terms]
                jobs.append((order.index(key), start + block * rows, rows, terms))
            if kept:
                last = stream.age == self.last
                keeps.append((stream, len(shapes)))
                for block, terms in enumerate(kept):
                    terms = [([number(part) for part in parts], place) for parts, place in terms]
                    jobs.append((len(shapes), block * rows, rows, terms))
                shapes.append(sds((len(kept) * rows, D), F32 if last else BF16))
        outs = pl.pallas_call(
            functools.partial(blocks_kernel, count=len(arrays), jobs=jobs),
            name="blocks",
            out_shape=shapes,
            in_specs=[pl.BlockSpec(memory_space=pltpu.SMEM)]
            + [pl.BlockSpec(memory_space=pltpu.VMEM)] * len(arrays),
            out_specs=[pl.BlockSpec(memory_space=pltpu.VMEM)] * len(shapes),
            compiler_params=params(),
            cost_estimate=cost(0, sum(3 * array.size for array in arrays)),
        )(self.scalars, *arrays)
        for stream, out in keeps:
            stream.keep = outs[out]
            if stream.age == self.last:
                stream.total = outs[out]
        for stream, *_ in todo:
            stream.age += 1
        payloads, others = lax.optimization_barrier((outs[: len(order)], others))
        self.moved = {}
        self.span = None if extra is None else span
        for key, payload in zip(order, payloads):
            if key > 0:
                self.moved[key] = self.at.move(payload, key, 1)
            else:
                self.moved[key] = self.at.move(payload, 0, 1 << (-key - 2), flip=True)
        return others

    def close(self, *others):
        self.moved, others = lax.optimization_barrier((self.moved, others))
        for stream, key, start in self.sent:
            stream.recv = (self.moved[key], start)
        if self.span is not None:
            self.extra = [self.moved[2][self.span[0] : sum(self.span)]]
        return others

    def busy(self):
        return any(stream.age <= self.last for streams in self.groups for stream in streams)


def pick(stacked, index, axis=0):
    return lax.dynamic_index_in_dim(stacked, index, axis, keepdims=False)


def by_core(core, mine, theirs, axis):
    return jnp.where(core == 0, jnp.stack([mine, theirs], axis), jnp.stack([theirs, mine], axis))


def body(
    hidden,
    boxes,
    page_size,
    band_count,
    layout_tables,
    attn_in,
    attn_bias,
    attn_out,
    out_bias,
    norm_gain,
    norm_bias,
    ffn_in,
    ffn_in_bias,
    ffn_out,
    ffn_out_bias,
    out_grad,
    *,
    pages,
    bands,
):
    at = Places(pages, bands)
    core = at.core
    core_id = core.astype(jnp.int32).reshape(1)
    devices = pages * bands
    ny, chips = at.ny, at.chips
    cap = hidden.shape[2]
    rows_dev = attn_in.shape[1]
    table_rows = layout_tables.shape[1]
    ff_dev = ffn_out.shape[1]
    chip_rows = CORES * rows_dev
    tiled = rows_dev % 8 == 0 and ff_dev == 2 * FF_CHUNK and at.nx == ny == 2

    def local_weights(layer):
        if tiled:
            mine, send = pack(core_id, attn_in, attn_out, ffn_in, layer)
            shapes = ((2, chip_rows, D), (4, chip_rows, D))
            return join(core_id, mine, at.swap(send), ffn_out, layer, shapes)
        columns = jnp.concatenate(
            [attn_in[layer].reshape(rows_dev, 3, CORES, HALF), attn_out[layer].reshape(rows_dev, 1, CORES, HALF)],
            axis=1,
        ).transpose(2, 0, 1, 3)
        ups = ffn_in[layer].reshape(rows_dev, chips, CORES, 2, ff_dev // 2).transpose(2, 0, 3, 1, 4)
        packed = jnp.concatenate(
            [columns.reshape(CORES, rows_dev, 4 * HALF), ups.reshape(CORES, rows_dev, FF // CORES)], axis=2
        )
        both = by_core(core, pick(packed, core), at.swap(pick(packed, 1 - core)), 0)
        both = both.reshape(chip_rows, PACKED)
        down = ffn_out[layer].reshape(2, chip_rows, D)
        both = both.reshape(chip_rows, 4, D).swapaxes(0, 1)
        return both[:2], jnp.stack([both[2], down[0], both[3], down[1]])

    attn_place = ([(0, 1, 0, 0, 0, D)], [(0, 1, 0, D, 0, D), (1, 1, 0, 0, HALF, HALF)])
    attn_shapes = ((chips, chip_rows, 2 * D), (chips, chip_rows, HALF))
    ffn_place = [[(0, 1, 0, col * D, 0, D)] for col in (0, 2, 1, 3)]
    ffn_shapes = ((chips, chip_rows, 4 * D),)
    table_place = [[(table, 1, 0, 0, 0, D)] for table in range(4)]
    table_shapes = ((chips, table_rows, D),) * 4

    def to_chip(stacked):
        own = [pick(stacked, at.y)]
        for k in range(1, ny):
            own.append(at.move(pick(stacked, (at.y + k) % ny), 2, k))
        return own

    def send_back(rows):
        parts = rows.reshape((ny, cap) + rows.shape[1:])
        return [at.move(parts[k].astype(BF16), 2, -k) for k in range(1, ny)]

    def from_chip(rows, back):
        back = [rows[:cap]] + [part.astype(F32) for part in back]
        back = jnp.stack(back)
        return jnp.stack([pick(back, (page - at.y) % ny) for page in range(ny)])[:, None]

    def token_facts(hidden, boxes, page_size, band_count):
        widths, heights = page_size[0][:, None], page_size[1][:, None]
        left = boxes[0, :, 0] * GRID // widths
        top = boxes[1, :, 0] * GRID // heights
        right = boxes[2, :, 0] * GRID // widths
        bottom = boxes[3, :, 0] * GRID // heights
        live = (lax.broadcasted_iota(jnp.int32, left.shape, 1) < band_count).astype(jnp.int32)
        facts = jnp.stack([left, top, right, bottom, bottom - top, right - left, live, live], axis=1)
        facts_own = jnp.concatenate(to_chip(facts), axis=-1)
        facts_all = jnp.concatenate([facts_own, at.swap(facts_own)], axis=-1)
        owner = facts_all // table_rows
        index = jnp.where(
            owner % CORES == core, owner // CORES * table_rows + facts_all % table_rows, -1
        )
        mask = jnp.where(facts_all[6:7] > 0, 0.0, DEAD).astype(F32)
        live_own = facts_own[6].astype(F32)[:, None]
        hidden_own = jnp.concatenate(to_chip(hidden[:, 0]), axis=0)
        return index, mask, live_own, hidden_own

    cut = SMALL_ROWS * rows_dev

    def small_params(attn_bias, out_bias, norm_gain, norm_bias, ffn_out_bias, ffn_in_bias):
        segment = jnp.concatenate(
            [
                attn_bias.reshape(-1),
                out_bias.reshape(-1),
                norm_gain.reshape(-1),
                norm_bias.reshape(-1),
                ffn_out_bias.reshape(-1),
                ffn_in_bias.reshape(-1),
            ]
        )
        smalls = lax.all_to_all(
            jnp.broadcast_to(segment, (devices, segment.shape[0])), ("page", "band"), 0, 0, tiled=True
        ).astype(F32)
        small = smalls[:, :cut].reshape(devices, SMALL_ROWS, rows_dev).swapaxes(0, 1).reshape(SMALL_ROWS, D)
        up_bias = pick(smalls[:, cut:].reshape(chips, CORES, LAYERS, 2, ff_dev // 2), core, 1)
        up_bias = up_bias.transpose(1, 2, 0, 3).reshape(LAYERS, FF // CORES)
        return small, up_bias

    saved = [[], []]
    weights = [[], []]

    def look_up(state):
        tables = line.result(chunks[0])
        looked_up = embed(index.T, tables)
        mine = hidden_own.astype(F32) + looked_up[:half]
        x = mine + at.swap(looked_up[half:].astype(BF16)).astype(F32)
        return x, x.astype(BF16)

    def attend(layer, state):
        x, x_low = state
        wa, wom = line.result(chunks[1 + 2 * layer])
        wot, x_other = at.swap(wom), at.swap(x_low)
        weights[layer] += [wa, wom, wot]
        q, k, v, mix_own, mix_other = attn_fwd(core_id, x_low, x_other, wa, small, mask, layer)
        y1, y1_low, n1, r1 = out_norm(core_id, mix_own, at.swap(mix_other), wom, wot, x, small, layer)
        saved[layer] += [x_low, x_other, q, k, v, mix_own, mix_other, n1, r1]
        return y1, y1_low

    def feed(layer, state):
        y1, y1_low = state
        (wf,) = line.result(chunks[2 + 2 * layer])
        y1_other = at.swap(y1_low)
        weights[layer] += [wf, 0]
        act, slope, part, part_other = ffn_fwd(y1_low, y1_other, wf, 0, up_bias, layer)
        x, x_low, n2, r2 = add_norm(y1, part, at.swap(part_other), small, layer)
        saved[layer] += [y1_low, y1_other, act, slope, n2, r2]
        return x, x_low

    half = ny * cap
    line = Line(at)
    chunks = [Gather(at, layout_tables, table_shapes, table_place)]
    parts = [look_up]
    line.add(chunks[0])
    line.step()
    locals0 = local_weights(0)
    token_args = (hidden, boxes, page_size, band_count)
    small_args = (attn_bias, out_bias, norm_gain, norm_bias, ffn_out_bias, ffn_in_bias)
    locals0, token_args = line.close(locals0, token_args)
    state = ()
    running = None
    waiting = []
    for layer in range(LAYERS):
        waiting += [(layer, 0), (layer, 1)]
        parts += [functools.partial(attend, layer), functools.partial(feed, layer)]
    local = locals0
    while waiting or running is not None or not line.done(chunks[-1]):
        if waiting:
            layer, number = waiting.pop(0)
            if layer > 0 and number == 0:
                local = local_weights(layer)
            chunks.append(
                Gather(at, local[number], (attn_shapes, ffn_shapes)[number], (attn_place, ffn_place)[number])
            )
            line.add(chunks[-1])
        if all(line.done(chunk) for chunk in chunks):
            state = running(state)
            break
        state = line.step(*state)
        if running is not None:
            state = running(state)
        if len(chunks) == 2:
            tokens, small_args, late = line.close(
                token_facts(*token_args), small_args, (attn_in, attn_out, ffn_in)
            )
            index, mask, live_own, hidden_own = tokens
            attn_in, attn_out, ffn_in = late
        elif len(chunks) == 3:
            small, up_bias = line.close(*small_params(*small_args))
        else:
            state = line.close(*state)
        ready = [number for number, chunk in enumerate(chunks) if line.fresh(chunk)]
        running = parts[ready[0]] if ready else None
    x = state[0]

    small_grads = [None] * LAYERS

    def backward_ffn(layer, sources):
        wf, col = weights[layer][3:]
        y1_low, y1_other, act, slope, n2, r2 = saved[layer][9:]
        gh2, df, sums2 = norm_bwd(sources, n2, r2, small, 2 * layer + 1)
        dw1, dw2, up_sums, part, part_other = ffn_bwd(df, at.swap(df), wf, col, act, slope, y1_low, y1_other)
        small_grads[layer] = [sums2, up_sums]
        return (gh2, part, at.swap(part_other)), dw1, dw2

    def backward_attn(layer, sources):
        wa, wom, wot = weights[layer][:3]
        x_low, x_other, q, k, v, mix_own, mix_other, n1, r1 = saved[layer][:9]
        gh1, da, sums1 = norm_bwd(sources, n1, r1, small, 2 * layer)
        dwq, dwk, dwv, dwo, attn_sums, part, part_other = attn_bwd(
            core_id, da, at.swap(da), wom, wot, q, k, v, mix_own, mix_other, x_low, x_other, wa, mask
        )
        small_grads[layer] = [sums1] + small_grads[layer] + [attn_sums]
        return (gh1, part, at.swap(part_other)), (dwq, dwk, dwv), (pick(dwo, core), at.swap(pick(dwo, 1 - core)))

    def attn_groups(dqkv, dwo):
        dwq, dwk, dwv = dqkv
        return [dwq, dwk], [dwv, by_core(core, *dwo, 0).reshape(D, HALF)]

    grad_own = jnp.concatenate(to_chip(tie(out_grad[:, 0], saved[0][0])), axis=0)
    line = Pipe(at) if tiled else Line(at)

    def ffn_chunk(dw1, dw2):
        if tiled:
            flat = [dw.reshape(2 * D, D) for dw in (dw1, dw2)]
            streams = [Stream([unit], part == 0, chip_rows, part * D) for part in range(2) for unit in flat]
            line.add(streams)
            return streams
        chunk = Reduce(at, [[dw1[0]], [dw2[0]]], [[dw1[1]], [dw2[1]]])
        line.add(chunk)
        return chunk

    def attn_chunk(dqkv, dwo):
        first, second = attn_groups(dqkv, dwo)
        if tiled:
            streams = [Stream(first, True, chip_rows), Stream(second, False, chip_rows)]
            line.add(streams)
            return streams
        chunk = Reduce(at, [first], [second])
        line.add(chunk)
        return chunk

    def table_chunk(tables):
        if tiled:
            streams = [Stream([table], number < 2, table_rows) for number, table in enumerate(tables)]
            line.add(streams)
            return streams
        chunk = Reduce(at, [[table] for table in tables[:2]], [[table] for table in tables[2:]])
        line.add(chunk)
        return chunk

    sources, dw1, dw2 = backward_ffn(1, (grad_own, live_own))
    ffn1 = ffn_chunk(dw1, dw2)
    output = x * live_own
    sources = line.step(*sources, extra=output[cap:] if tiled else None)
    sources, dqkv, dwo = backward_attn(1, sources)
    sources = line.close(*sources)
    output = from_chip(output, line.extra if tiled else send_back(output))
    att1 = attn_chunk(dqkv, dwo)
    sources = line.step(*sources)
    sources, dw1, dw2 = backward_ffn(0, sources)
    sources = line.close(*sources)
    ffn0 = ffn_chunk(dw1, dw2)
    sources = line.step(*sources)
    sources, dqkv, dwo = backward_attn(0, sources)
    sources = line.close(*sources)
    att0 = attn_chunk(dqkv, dwo)
    sources = line.step(*sources)
    grad_x = sources[0] + sources[1] + sources[2].astype(F32)
    grad_low = grad_x.astype(BF16)
    table_parts = table_grads(index, grad_low, at.swap(grad_low), chips * table_rows)
    table_parts = line.close(*table_parts)
    tab = table_chunk(table_parts)
    line.step(extra=grad_x[cap:] if tiled else None)
    line.close()
    input_grad = from_chip(grad_x, line.extra if tiled else send_back(grad_x))
    zeros = jnp.zeros((2, HALF), F32)
    vectors = []
    for layer in range(LAYERS):
        mine = small_grads[layer][3][:2]
        vectors.append(by_core(core, mine, zeros, 1).reshape(2, D))
    vectors.append(jnp.stack([small_grads[layer][0][2] for layer in range(LAYERS)]))
    for row in range(2):
        for layer in range(LAYERS):
            vectors.append(jnp.stack([small_grads[layer][norm][row] for norm in range(2)]))
    vectors.append(jnp.stack([small_grads[layer][1][2] for layer in range(LAYERS)]))
    vectors = lax.optimization_barrier(jnp.concatenate(vectors)).reshape(SMALL_ROWS, devices, rows_dev).swapaxes(0, 1)
    ups_grad = jnp.stack([small_grads[layer][2][0] for layer in range(LAYERS)])
    ups_grad = ups_grad.reshape(LAYERS, 2, chips, ff_dev // 2).transpose(2, 0, 1, 3)
    ups_grad = by_core(core, ups_grad, jnp.zeros_like(ups_grad), 1)
    segments = jnp.concatenate(
        [vectors.reshape(devices, cut), ups_grad.reshape(devices, LAYERS * ff_dev)], axis=1
    )
    segments = lax.all_to_all(segments, ("page", "band"), 0, 0, tiled=True)

    while line.busy():
        line.step()
        line.close()
    segments = tie(segments, tab[0].total if tiled else line.moved)
    segment = jnp.sum(segments, axis=0)
    rows = segment[:cut].reshape(SMALL_ROWS, rows_dev)
    if tiled:
        grad_tables = jnp.stack([stream.total for stream in tab])
        results = [
            [stream.total for stream in attn[:2] + ffn] for attn, ffn in ((att0, ffn0), (att1, ffn1))
        ]
    else:
        sums = [line.result(chunk) for chunk in (att0, ffn0, att1, ffn1)]
        grad_tables = jnp.stack(line.result(tab)).reshape(4, table_rows, D)
        results = []
        for attn_sum, ffn_sum in ((sums[0], sums[1]), (sums[2], sums[3])):
            attn = jnp.stack(attn_sum)
            ffn = jnp.stack(ffn_sum).reshape(4, chip_rows, D)
            results.append((attn, ffn, ffn))

    if tiled:
        parts = []
        for layer in range(LAYERS):
            qk, vo, up_a, down_a, up_b, down_b = results[layer]
            mine, send = split(core_id, (qk, vo, up_a, up_b))
            parts += [mine, at.swap(send), down_a, down_b]
        grads = merge(core_id, parts)
    else:
        grads = [[], [], [], []]
        for layer in range(LAYERS):
            attn_sum, up_sum, down_sum = results[layer]
            both = jnp.stack([attn_sum[0], attn_sum[1], up_sum[0], up_sum[2]])
            by_owner = both.reshape(4, CORES, rows_dev, D)
            mine, theirs = pick(by_owner, core, 1), at.swap(pick(by_owner, 1 - core, 1))
            both = by_core(core, mine, theirs, 0).transpose(2, 0, 1, 3)
            attn = both[:, :, :2].reshape(rows_dev, CORES, 4, HALF).swapaxes(1, 2)
            grads[0].append(attn[:, :3].reshape(rows_dev, 3 * D))
            grads[1].append(attn[:, 3].reshape(rows_dev, D))
            ups = both[:, :, 2:].reshape(rows_dev, CORES, 2, chips, ff_dev // 2).transpose(0, 3, 1, 2, 4)
            grads[2].append(ups.reshape(rows_dev, FF))
            grads[3].append(jnp.concatenate([down_sum[1], down_sum[3]]))
        grads = [jnp.stack(pair) for pair in grads]

    return (
        output,
        input_grad,
        grad_tables,
        grads[0],
        rows[ROW_ATTN:ROW_OUT].reshape(LAYERS, 2, rows_dev),
        grads[1],
        rows[ROW_OUT:ROW_GAIN],
        rows[ROW_GAIN:ROW_SHIFT].reshape(LAYERS, 2, rows_dev),
        rows[ROW_SHIFT:ROW_DOWN].reshape(LAYERS, 2, rows_dev),
        grads[2],
        segment[cut:].reshape(LAYERS, ff_dev),
        grads[3],
        rows[ROW_DOWN:SMALL_ROWS],
    )


def solution(mesh):
    both = ("page", "band")
    tokens = P("page", "band", None, None)
    middle = P(None, both, None)
    last = P(None, both)
    third = P(None, None, both)
    return jax.shard_map(
        functools.partial(body, pages=mesh.shape["page"], bands=mesh.shape["band"]),
        mesh=mesh,
        in_specs=(
            tokens,
            P(None, "page", "band", None),
            P(None, "page"),
            P("page", "band"),
            middle,
            middle,
            third,
            middle,
            last,
            third,
            third,
            middle,
            last,
            middle,
            last,
            tokens,
        ),
        out_specs=(
            tokens,
            tokens,
            middle,
            middle,
            third,
            middle,
            last,
            third,
            third,
            middle,
            last,
            middle,
            last,
        ),
        check_vma=False,
    )
```

time: 704 us -> 547 us (0.78); the launches traced: 690 us -> 542 us
  Pallas kernels: 126 us -> 226 us
  local copies, waits for them, and re-layouts: 154 us -> 64.6 us
  waiting for transfers between devices: 216 us -> 137 us
  starting transfers between devices: 137 us -> 78.3 us
  other arithmetic: 54.2 us -> 33.7 us
    ppermute x104 -> x74, waiting for transfers between devices: 211 us -> 131 us  [move(): return lax.ppermute(value, ('page', 'band'), pairs)]
    unnamed x386 -> x174, local copies, waits for them, and re-layouts: 88.2 us -> 19 us
    pallas_call x2 -> x18, Pallas kernels: 30.9 us -> 90.7 us  [the longest x9 44 us: step(): pl.pallas_call(functools.partial(blocks_kernel, count=len(arrays), jobs=j...]
    ppermute x104 -> x74, starting transfers between devices: 127 us -> 72.8 us  [move(): return lax.ppermute(value, ('page', 'band'), pairs)]
    convert_element_type x22 -> x3, other arithmetic: 17.5 us -> 4.23 us  [the longest x1 2.13 us: look_up(): return (x, x.astype(BF16))]
    another operation x11 -> x2, local copies, waits for them, and re-layouts: 12.5 us -> 1.42 us  [by_core(): jnp.stack([mine, theirs], axis)]
    concatenate x5 -> x22, other arithmetic: 3.2 us -> 14.1 us  [the longest x8 7.47 us: exchange(): jnp.concatenate(flat)]
    slice x26 -> x23, local copies, waits for them, and re-layouts: 6.48 us -> 16.9 us  [the longest x15 12.5 us: exchange(): got[i] = moved[first:first + part.shape[0]].reshape(wants[i][2].shape)]
  transfers between devices with their start and end apart: 106 -> 76, of which waited for: 35 -> 43; matrix products, arithmetic and copies ran while one was open for 18% -> 12% of each run, Pallas kernels for 14% -> 28%
where the time goes in v2:
time: 547 us; the launch traced here: 542 us
  Pallas kernels  226 us (41%)
  waiting for transfers between devices  137 us (25%)
  starting transfers between devices  78.3 us (14%)
  local copies, waits for them, and re-layouts  64.6 us (12%)
  other arithmetic  33.7 us (6%)
    ppermute x74, waiting for transfers between devices, move(): return lax.ppermute(value, ('page', 'band'), pairs)  131 us
    ppermute x74, starting transfers between devices, move(): return lax.ppermute(value, ('page', 'band'), pairs)  72.8 us
    pallas_call x9, Pallas kernels, step(): pl.pallas_call(functools.partial(blocks_kernel, count=len(arrays), jobs=j...  44 us
    pallas_call x2, Pallas kernels, attn_bwd(): pl.pallas_call(attn_bwd_kernel, name='attn_bwd', out_shape=[sds((D, HALF)...  37.5 us
    pallas_call x2, Pallas kernels, ffn_bwd(): pl.pallas_call(ffn_bwd_kernel, name='ffn_bwd', out_shape=[sds((2, D, D),...  32.2 us
    pallas_call x2, Pallas kernels, ffn_fwd(): pl.pallas_call(functools.partial(ffn_fwd_kernel, layer=layer), name='ffn_...  24.1 us
    pallas_call x5, Pallas kernels, shuffle(): pl.pallas_call(functools.partial(shuffle_kernel, moves=moves, count=len(s...  20.3 us
    unnamed x174, local copies, waits for them, and re-layouts  19 us
  transfers between devices with their start and end apart: 76, of which 43 were waited for; matrix products, arithmetic and copies ran while one was open for 12% of the time, Pallas kernels for 28%

profile of v2, /device:TPU:0, one launch (start us, length us, event | category | flops | bytes accessed | tf_op | source)
XLA Modules:
  0.0 542.0 jit_solution(17563081470898868639)
XLA Ops:
  0.7 4.1 collective-permute-start
  10.8 3.4 collective-permute-done
  17.9 4.1 collective-permute-start.2
  26.4 5.6 %collective-permute-done.2 = bf16[256,768]{1,0:T(8,128)(2,1)S(1)} collective-permute-done((bf16[256,768]{1,0:T(8,128)(2,1)S(1)}, bf16[256,768]{1,0:T(8,128)(2,1)S(1)}, u32[]{:S(2)}, u32[]{:S(2)}) %collective-permute-start.2) | collective-permute-done | bytes 393248 | tf_op jit(solution)/shard_map/ppermute | solution.py:741
  37.1 3.4 collective-permute-start.11
  48.3 6.0 %all-to-all-done = bf16[32,2,288]{2,1,0:T(2,128)(2,1)S(1)} async-done(((bf16[32,2,288]{2,1,0:T(2,128)(2,1)}), bf16[32,2,288]{2,1,0:T(2,128)(2,1)S(1)}, u32[]{:S(2)}, u32[]{:S(2)}) %all-to-all-start) | async-done | bytes 36896 | tf_op jit(solution)/shard_map/all_to_all | solution.py:1212
  67.4 20.0 %collective-permute-done.13 = bf16[704,768]{1,0:T(8,128)(2,1)S(1)} collective-permute-done((bf16[704,768]{1,0:T(8,128)(2,1)S(1)}, bf16[704,768]{1,0:T(8,128)(2,1)S(1)}, u32[]{:S(2)}, u32[]{:S(2)}) %collective-permute-start.13) | collective-permute-done | bytes 1081376 | tf_op jit(solution)/shard_map/ppermute | solution.py:741
  99.2 3.8 shuffle.5
  103.0 5.8 %embed.1 = f32[512,768]{1,0:T(8,128)} custom-call(s32[512,8]{1,0:T(8,128)} %copy.69.idx, bf16[512,768]{1,0:T(8,128)(2,1)} %bitcast.425, bf16[512,768]{1,0:T(8,128)(2,1)} %bitcast.426, bf16[512,768]{1,0:T(8,128)(2,1)} %bitcast.427, bf16[512,768]{1,0:T(8,128)(2,1)} %bitcast.428), custom_call_target="tpu_custom_call" | custom-call | flops 1610612736 | bytes 4718592 | tf_op jit(solution)/shard_map/embed/pallas_call | solution.py:84
  115.5 5.9 %collective-permute-done.17 = bf16[768,768]{1,0:T(8,128)(2,1)} collective-permute-done((bf16[768,768]{1,0:T(8,128)(2,1)}, bf16[768,768]{1,0:T(8,128)(2,1)}, u32[]{:S(2)}, u32[]{:S(2)}) %collective-permute-start.17) | collective-permute-done | bytes 1179680 | tf_op jit(solution)/shard_map/ppermute | solution.py:741
  135.1 3.5 shuffle.6
  139.5 8.5 %attn_fwd.2 = (bf16[512,384]{1,0:T(8,128)(2,1)}, bf16[512,384]{1,0:T(8,128)(2,1)}, bf16[512,384]{1,0:T(8,128)(2,1)}, bf16[256,384]{1,0:T(8,128)(2,1)}, bf16[256,384]{1,0:T(8,128)(2,1)}) custom-call(s32[1]{0:T(128)} %bitcast.core, bf16[256,768]{1,0:T(8,128)(2,1)} %copy-done.13, bf16[256,768]{1,0:T(8,128)(2,1)} %collective-permute-done.24.xs, ...), custom_call_target="tpu_custom_call" | custom-call | flops 1711276032 | bytes 4128768 | tf_op jit(solution)/shard_map/attn_fwd/pallas_call | solution.py:164
  150.3 3.9 out_norm.2
  154.2 10.4 %collective-permute-done.22 = bf16[960,768]{1,0:T(8,128)(2,1)} collective-permute-done((bf16[960,768]{1,0:T(8,128)(2,1)}, bf16[960,768]{1,0:T(8,128)(2,1)}, u32[]{:S(2)}, u32[]{:S(2)}) %collective-permute-start.22) | collective-permute-done | bytes 1474592 | tf_op jit(solution)/shard_map/ppermute | solution.py:741
  175.9 4.8 shuffle.7
  180.7 12.1 %ffn_fwd.2 = (bf16[512,1536]{1,0:T(8,128)(2,1)}, bf16[512,1536]{1,0:T(8,128)(2,1)}, f32[256,768]{1,0:T(8,128)}, bf16[256,768]{1,0:T(8,128)(2,1)}) custom-call(bf16[256,768]{1,0:T(8,128)(2,1)} %get-tuple-element.453.yo, bf16[256,768]{1,0:T(8,128)(2,1)} %collective-permute-done.29.ys, bf16[768,3072]{1,0:T(8,128)(2,1)} %bitcast.279, f32[2,1536]{1,0:T(2,128)} %reshape.526.bias, ...), custom_call_target="tpu_custom_call" | custom-call | flops 2415919104 | bytes 7864320 | tf_op jit(solution)/shard_map/ffn_fwd/pallas_call | solution.py:467
  195.6 3.2 add_norm.2
  199.7 3.9 collective-permute-done.27
  206.9 3.4 shuffle.8
  210.8 8.5 %attn_fwd.3 = (bf16[512,384]{1,0:T(8,128)(2,1)}, bf16[512,384]{1,0:T(8,128)(2,1)}, bf16[512,384]{1,0:T(8,128)(2,1)}, bf16[256,384]{1,0:T(8,128)(2,1)}, bf16[256,384]{1,0:T(8,128)(2,1)}) custom-call(s32[1]{0:T(128)} %bitcast.core, bf16[256,768]{1,0:T(8,128)(2,1)} %get-tuple-element.467.xo, bf16[256,768]{1,0:T(8,128)(2,1)} %collective-permute-done.33.xs, ...), custom_call_target="tpu_custom_call" | custom-call | flops 1711276032 | bytes 4128768 | tf_op jit(solution)/shard_map/attn_fwd/pallas_call | solution.py:164
  221.1 3.9 out_norm.3
  225.0 7.5 %collective-permute-done.32 = bf16[768,768]{1,0:T(8,128)(2,1)S(1)} collective-permute-done((bf16[768,768]{1,0:T(8,128)(2,1)S(1)}, bf16[768,768]{1,0:T(8,128)(2,1)S(1)}, u32[]{:S(2)}, u32[]{:S(2)}) %collective-permute-start.32) | collective-permute-done | bytes 1179680 | tf_op jit(solution)/shard_map/ppermute | solution.py:741
  233.6 4.8 shuffle.9
  239.2 12.0 %ffn_fwd.3 = (bf16[512,1536]{1,0:T(8,128)(2,1)}, bf16[512,1536]{1,0:T(8,128)(2,1)}, f32[256,768]{1,0:T(8,128)}, bf16[256,768]{1,0:T(8,128)(2,1)}) custom-call(bf16[256,768]{1,0:T(8,128)(2,1)} %get-tuple-element.478.yo, bf16[256,768]{1,0:T(8,128)(2,1)} %copy-done.39, bf16[768,3072]{1,0:T(8,128)(2,1)} %bitcast.283, f32[2,1536]{1,0:T(2,128)} %reshape.526.bias, ...), custom_call_target="tpu_custom_call" | custom-call | flops 2415919104 | bytes 7864320 | tf_op jit(solution)/shard_map/ffn_fwd/pallas_call | solution.py:467
  253.4 5.3 collective-permute-done.38
  260.2 3.1 add_norm.3
  269.0 16.2 %ffn_bwd.2 = (bf16[2,768,768]{2,1,0:T(8,128)(2,1)}, bf16[2,768,768]{2,1,0:T(8,128)(2,1)}, f32[8,1536]{1,0:T(8,128)}, f32[256,768]{1,0:T(8,128)}, bf16[256,768]{1,0:T(8,128)(2,1)}) custom-call(bf16[256,768]{1,0:T(8,128)(2,1)} %get-tuple-element.488.dfo, bf16[256,768]{1,0:T(8,128)(2,1)} %copy-done.71, bf16[768,3072]{1,0:T(8,128)(2,1)} %bitcast.285, ...), custom_call_target="tpu_custom_call" | custom-call | flops 4831838208 | bytes 12582912 | tf_op jit(solution)/shard_map/ffn_bwd/pallas_call | solution.py:525
  286.3 4.2 blocks.9
  291.3 3.3 norm_bwd.5
  296.7 18.9 %attn_bwd.2 = (bf16[768,384]{1,0:T(8,128)(2,1)}, bf16[768,384]{1,0:T(8,128)(2,1)}, bf16[768,384]{1,0:T(8,128)(2,1)}, bf16[2,384,384]{2,1,0:T(8,128)(2,1)}, f32[8...) custom-call(s32[1]{0:T(128)} %bitcast.core, bf16[256,768]{1,0:T(8,128)(2,1)} %get-tuple-element.506.dao, ...), custom_call_target="tpu_custom_call" | custom-call | flops 3825205248 | bytes 9437184 | tf_op jit(solution)/shard_map/attn_bwd/pallas_call | solution.py:269
  324.7 6.0 %blocks.10 = (bf16[768,768]{1,0:T(8,128)(2,1)}, bf16[768,768]{1,0:T(8,128)(2,1)}, bf16[192,768]{1,0:T(8,128)(2,1)}, bf16[192,768]{1,0:T(8,128)(2,1)}, bf16[192,7...) custom-call(s32[4]{0:T(128)} %pad_add_fusion.2.scalars, bf16[1536,768]{1,0:T(8,128)(2,1)} %bitcast.308, ...), custom_call_target="tpu_custom_call" | custom-call | bytes 14450688 | tf_op jit(solution)/shard_map/blocks/pallas_call | solution.py:1060
  330.7 3.3 norm_bwd.6
  337.3 16.1 %ffn_bwd.3 = (bf16[2,768,768]{2,1,0:T(8,128)(2,1)}, bf16[2,768,768]{2,1,0:T(8,128)(2,1)}, f32[8,1536]{1,0:T(8,128)}, f32[256,768]{1,0:T(8,128)}, bf16[256,768]{1,0:T(8,128)(2,1)}) custom-call(bf16[256,768]{1,0:T(8,128)(2,1)} %get-tuple-element.532.dfo, bf16[256,768]{1,0:T(8,128)(2,1)} %copy-done.75, bf16[768,3072]{1,0:T(8,128)(2,1)} %bitcast.281, ...), custom_call_target="tpu_custom_call" | custom-call | flops 4831838208 | bytes 12582912 | tf_op jit(solution)/shard_map/ffn_bwd/pallas_call | solution.py:525
  355.4 7.3 %collective-permute-done.46.refs_1_ = bf16[768,768]{1,0:T(8,128)(2,1)S(1)} collective-permute-done((bf16[768,768]{1,0:T(8,128)(2,1)}, bf16[768,768]{1,0:T(8,128)(2,1)S(1)}, u32[]{:S(2)}, u32[]{:S(2)}) %collective-permute-start.46) | collective-permute-done | bytes 1179680 | tf_op jit(solution)/shard_map/ppermute | solution.py:741
  364.6 7.0 %blocks.11 = (bf16[384,768]{1,0:T(8,128)(2,1)}, bf16[960,768]{1,0:T(8,128)(2,1)}, bf16[960,768]{1,0:T(8,128)(2,1)}, bf16[96,768]{1,0:T(8,128)(2,1)}, bf16[96,768...) custom-call(s32[4]{0:T(128)} %pad_add_fusion.2.scalars, ...), custom_call_target="tpu_custom_call" | custom-call | bytes 15925248 | tf_op jit(solution)/shard_map/blocks/pallas_call | solution.py:1060
  373.7 3.3 norm_bwd.7
  379.8 18.6 %attn_bwd.3 = (bf16[768,384]{1,0:T(8,128)(2,1)}, bf16[768,384]{1,0:T(8,128)(2,1)}, bf16[768,384]{1,0:T(8,128)(2,1)}, bf16[2,384,384]{2,1,0:T(8,128)(2,1)}, f32[8...) custom-call(s32[1]{0:T(128)} %bitcast.core, bf16[256,768]{1,0:T(8,128)(2,1)} %get-tuple-element.560.dao, ...), custom_call_target="tpu_custom_call" | custom-call | flops 3825205248 | bytes 9437184 | tf_op jit(solution)/shard_map/attn_bwd/pallas_call | solution.py:269
  402.1 3.3 collective-permute-done.51.refs_6_
  407.3 7.4 %blocks.12 = (bf16[192,768]{1,0:T(8,128)(2,1)}, bf16[192,768]{1,0:T(8,128)(2,1)}, bf16[768,768]{1,0:T(8,128)(2,1)}, bf16[768,768]{1,0:T(8,128)(2,1)}, bf16[48,76...) custom-call(s32[4]{0:T(128)} %pad_add_fusion.2.scalars, ...), custom_call_target="tpu_custom_call" | custom-call | bytes 17694720 | tf_op jit(solution)/shard_map/blocks/pallas_call | solution.py:1060
  428.1 3.9 table_grads.1
  432.0 7.2 %collective-permute-done.56.refs_2_ = bf16[192,768]{1,0:T(8,128)(2,1)S(1)} collective-permute-done((bf16[192,768]{1,0:T(8,128)(2,1)}, bf16[192,768]{1,0:T(8,128)(2,1)S(1)}, u32[]{:S(2)}, u32[]{:S(2)}) %collective-permute-start.56) | collective-permute-done | bytes 294944 | tf_op jit(solution)/shard_map/ppermute | solution.py:741
  442.3 7.1 %blocks.13 = (bf16[96,768]{1,0:T(8,128)(2,1)}, bf16[384,768]{1,0:T(8,128)(2,1)}, bf16[704,768]{1,0:T(8,128)(2,1)}, bf16[832,768]{1,0:T(8,128)(2,1)}, f32[48,768]...) custom-call(s32[4]{0:T(128)} %pad_add_fusion.2.scalars, ...), custom_call_target="tpu_custom_call" | custom-call | bytes 15630336 | tf_op jit(solution)/shard_map/blocks/pallas_call | solution.py:1060
  465.8 3.5 collective-permute-done.61.refs_1_
  470.0 4.7 collective-permute-done.63.refs_9_
  478.7 5.5 %blocks.14 = (bf16[192,768]{1,0:T(8,128)(2,1)}, bf16[192,768]{1,0:T(8,128)(2,1)}, bf16[256,768]{1,0:T(8,128)(2,1)}, bf16[256,768]{1,0:T(8,128)(2,1)}, f32[48,768...) custom-call(s32[4]{0:T(128)} %pad_add_fusion.2.scalars, ...), custom_call_target="tpu_custom_call" | custom-call | bytes 11354112 | tf_op jit(solution)/shard_map/blocks/pallas_call | solution.py:1060
  509.3 5.4 %collective-permute-done.69.refs_1_ = bf16[96,768]{1,0:T(8,128)(2,1)S(1)} collective-permute-done((bf16[96,768]{1,0:T(8,128)(2,1)S(1)}, bf16[96,768]{1,0:T(8,128)(2,1)S(1)}, u32[]{:S(2)}, u32[]{:S(2)}) %collective-permute-start.69) | collective-permute-done | bytes 147488 | tf_op jit(solution)/shard_map/ppermute | solution.py:741
  524.2 5.4 collective-permute-done.71.refs_1_
  538.7 3.1 merge.1
  (457 shorter events, 218.8 us)
Async XLA Ops:
  0.7 13.4 %collective-permute-start = (bf16[128,768]{1,0:T(8,128)(2,1)}, bf16[128,768]{1,0:T(8,128)(2,1)S(1)}, u32[]{:S(2)}, u32[]{:S(2)}) collective-permute-start(bf16[128,768]{1,0:T(8,128)(2,1)} %bitcast.368), channel_id=1, source_target_pairs={{0,16},{1,17},{2,18},{3,19},{4,20},{5,21},{6,22},{7,23},{8,24},{9,... | collective-permute-start | bytes 589832 | tf_op jit(solution)/shard_map/ppermute | solution.py:741
  17.2 9.2 %collective-permute-start.3 = (bf16[96,768]{1,0:T(8,128)(2,1)}, bf16[96,768]{1,0:T(8,128)(2,1)S(1)}, u32[]{:S(2)}, u32[]{:S(2)}) collective-permute-start(bf16[96,768]{1,0:T(8,128)(2,1)} %bitcast.378), channel_id=1, source_target_pairs={{0,16},{1,17},{2,18},{3,19},{4,20},{5,21},{6,22},{7,23},{8,24},{9,... | collective-permute-start | bytes 442376 | tf_op jit(solution)/shard_map/ppermute | solution.py:741
  17.9 14.1 %collective-permute-start.2 = (bf16[256,768]{1,0:T(8,128)(2,1)S(1)}, bf16[256,768]{1,0:T(8,128)(2,1)S(1)}, u32[]{:S(2)}, u32[]{:S(2)}) collective-permute-start(bf16[256,768]{1,0:T(8,128)(2,1)S(1)} %bitcast.395), channel_id=1, source_target_pairs={{0,8},{1,9},{2,10},{3,11},{4,12},{5,13},{6,14},{7,15},{8,0},{9,1},... | collective-permute-start | bytes 1179656 | tf_op jit(solution)/shard_map/ppermute | solution.py:741
  34.0 24.9 %collective-permute-start.9 = (bf16[256,768]{1,0:T(8,128)(2,1)}, bf16[256,768]{1,0:T(8,128)(2,1)S(1)}, u32[]{:S(2)}, u32[]{:S(2)}) collective-permute-start(bf16[256,768]{1,0:T(8,128)(2,1)} %bitcast.37), channel_id=1, source_target_pairs={{0,2},{1,3},{2,0},{3,1},{4,6},{5,7},{6,4},{7,5},{8,10},{9,11},{10,... | collective-permute-start | bytes 1179656 | tf_op jit(solution)/shard_map/ppermute | solution.py:741
  35.4 23.5 %collective-permute-start.8 = (bf16[256,768]{1,0:T(8,128)(2,1)}, bf16[256,768]{1,0:T(8,128)(2,1)S(1)}, u32[]{:S(2)}, u32[]{:S(2)}) collective-permute-start(bf16[256,768]{1,0:T(8,128)(2,1)} %bitcast.35), channel_id=1, source_target_pairs={{0,4},{1,5},{2,6},{3,7},{4,0},{5,1},{6,2},{7,3},{8,12},{9,13},{10,... | collective-permute-start | bytes 1179656 | tf_op jit(solution)/shard_map/ppermute | solution.py:741
  36.9 22.0 %collective-permute-start.10 = (bf16[192,768]{1,0:T(8,128)(2,1)}, bf16[192,768]{1,0:T(8,128)(2,1)}, u32[]{:S(2)}, u32[]{:S(2)}) collective-permute-start(bf16[192,768]{1,0:T(8,128)(2,1)} %bitcast.39), channel_id=1, source_target_pairs={{0,8},{1,9},{2,10},{3,11},{4,12},{5,13},{6,14},{7,15},{8,0},{9,1},... | collective-permute-start | bytes 884744 | tf_op jit(solution)/shard_map/ppermute | solution.py:741
  37.1 21.7 %collective-permute-start.11 = (bf16[192,768]{1,0:T(8,128)(2,1)S(1)}, bf16[192,768]{1,0:T(8,128)(2,1)S(1)}, u32[]{:S(2)}, u32[]{:S(2)}) collective-permute-start(bf16[192,768]{1,0:T(8,128)(2,1)S(1)} %bitcast.354), channel_id=1, source_target_pairs={{0,16},{1,17},{2,18},{3,19},{4,20},{5,21},{6,22},{7,23},{8,24},{9,... | collective-permute-start | bytes 884744 | tf_op jit(solution)/shard_map/ppermute | solution.py:741
  43.4 10.9 %all-to-all-start = ((bf16[32,2,288]{2,1,0:T(2,128)(2,1)}), bf16[32,2,288]{2,1,0:T(2,128)(2,1)S(1)}, u32[]{:S(2)}, u32[]{:S(2)}) async-start(bf16[32,2,288]{2,1,0:T(2,128)(2,1)} %reshape.617), calls=%async_computation | async-start | bytes 98304 | tf_op jit(solution)/shard_map/all_to_all | solution.py:1212
  61.5 25.9 %collective-permute-start.13 = (bf16[704,768]{1,0:T(8,128)(2,1)S(1)}, bf16[704,768]{1,0:T(8,128)(2,1)S(1)}, u32[]{:S(2)}, u32[]{:S(2)}) collective-permute-start(bf16[704,768]{1,0:T(8,128)(2,1)S(1)} %pad_maximum_fusion.13), channel_id=1, source_target_pairs={{0,4},{1,5},{2,6},{3,7},{4,0},{5,1},{6,2},{7,3},{8,12},{9,13},{10,... | collective-permute-start | bytes 3244040 | tf_op jit(solution)/shard_map/ppermute | solution.py:741
  62.9 25.7 %collective-permute-start.12 = (bf16[704,768]{1,0:T(8,128)(2,1)S(1)}, bf16[704,768]{1,0:T(8,128)(2,1)S(1)}, u32[]{:S(2)}, u32[]{:S(2)}) collective-permute-start(bf16[704,768]{1,0:T(8,128)(2,1)S(1)} %pad_maximum_fusion.12), channel_id=1, source_target_pairs={{0,2},{1,3},{2,0},{3,1},{4,6},{5,7},{6,4},{7,5},{8,10},{9,11},{10,... | collective-permute-start | bytes 3244040 | tf_op jit(solution)/shard_map/ppermute | solution.py:741
  64.7 25.1 %collective-permute-start.14 = (bf16[384,768]{1,0:T(8,128)(2,1)S(1)}, bf16[384,768]{1,0:T(8,128)(2,1)S(1)}, u32[]{:S(2)}, u32[]{:S(2)}) collective-permute-start(bf16[384,768]{1,0:T(8,128)(2,1)S(1)} %bitcast.384), channel_id=1, source_target_pairs={{0,8},{1,9},{2,10},{3,11},{4,12},{5,13},{6,14},{7,15},{8,0},{9,1},... | collective-permute-start | bytes 1769480 | tf_op jit(solution)/shard_map/ppermute | solution.py:741
  64.9 24.9 %collective-permute-start.15 = (bf16[96,768]{1,0:T(8,128)(2,1)S(1)}, bf16[96,768]{1,0:T(8,128)(2,1)S(1)}, u32[]{:S(2)}, u32[]{:S(2)}) collective-permute-start(bf16[96,768]{1,0:T(8,128)(2,1)S(1)} %bitcast.373), channel_id=1, source_target_pairs={{0,16},{1,17},{2,18},{3,19},{4,20},{5,21},{6,22},{7,23},{8,24},{9,... | collective-permute-start | bytes 442376 | tf_op jit(solution)/shard_map/ppermute | solution.py:741
  94.1 27.4 %collective-permute-start.17 = (bf16[768,768]{1,0:T(8,128)(2,1)}, bf16[768,768]{1,0:T(8,128)(2,1)}, u32[]{:S(2)}, u32[]{:S(2)}) collective-permute-start(bf16[768,768]{1,0:T(8,128)(2,1)} %pad_maximum_fusion.4), channel_id=1, source_target_pairs={{0,4},{1,5},{2,6},{3,7},{4,0},{5,1},{6,2},{7,3},{8,12},{9,13},{10,... | collective-permute-start | bytes 3538952 | tf_op jit(solution)/shard_map/ppermute | solution.py:741
  96.4 27.2 %collective-permute-start.16 = (bf16[768,768]{1,0:T(8,128)(2,1)}, bf16[768,768]{1,0:T(8,128)(2,1)S(1)}, u32[]{:S(2)}, u32[]{:S(2)}) collective-permute-start(bf16[768,768]{1,0:T(8,128)(2,1)} %pad_maximum_fusion.3), channel_id=1, source_target_pairs={{0,2},{1,3},{2,0},{3,1},{4,6},{5,7},{6,4},{7,5},{8,10},{9,11},{10,... | collective-permute-start | bytes 3538952 | tf_op jit(solution)/shard_map/ppermute | solution.py:741
  110.1 15.7 %collective-permute-start.18 = (bf16[192,768]{1,0:T(8,128)(2,1)S(1)}, bf16[192,768]{1,0:T(8,128)(2,1)S(1)}, u32[]{:S(2)}, u32[]{:S(2)}) collective-permute-start(bf16[192,768]{1,0:T(8,128)(2,1)S(1)} %bitcast.400), channel_id=1, source_target_pairs={{0,8},{1,9},{2,10},{3,11},{4,12},{5,13},{6,14},{7,15},{8,0},{9,1},... | collective-permute-start | bytes 884744 | tf_op jit(solution)/shard_map/ppermute | solution.py:741
  110.8 16.3 %collective-permute-start.19 = (bf16[192,768]{1,0:T(8,128)(2,1)S(1)}, bf16[192,768]{1,0:T(8,128)(2,1)S(1)}, u32[]{:S(2)}, u32[]{:S(2)}) collective-permute-start(bf16[192,768]{1,0:T(8,128)(2,1)S(1)} %bitcast.351), channel_id=1, source_target_pairs={{0,16},{1,17},{2,18},{3,19},{4,20},{5,21},{6,22},{7,23},{8,24},{9,... | collective-permute-start | bytes 884744 | tf_op jit(solution)/shard_map/ppermute | solution.py:741
  131.8 32.8 %collective-permute-start.22 = (bf16[960,768]{1,0:T(8,128)(2,1)}, bf16[960,768]{1,0:T(8,128)(2,1)}, u32[]{:S(2)}, u32[]{:S(2)}) collective-permute-start(bf16[960,768]{1,0:T(8,128)(2,1)} %pad_maximum_fusion.1), channel_id=1, source_target_pairs={{0,4},{1,5},{2,6},{3,7},{4,0},{5,1},{6,2},{7,3},{8,12},{9,13},{10,... | collective-permute-start | bytes 4423688 | tf_op jit(solution)/shard_map/ppermute | solution.py:741
  133.9 34.1 %collective-permute-start.21 = (bf16[960,768]{1,0:T(8,128)(2,1)}, bf16[960,768]{1,0:T(8,128)(2,1)S(1)}, u32[]{:S(2)}, u32[]{:S(2)}) collective-permute-start(bf16[960,768]{1,0:T(8,128)(2,1)} %pad_maximum_fusion), channel_id=1, source_target_pairs={{0,2},{1,3},{2,0},{3,1},{4,6},{5,7},{6,4},{7,5},{8,10},{9,11},{10,... | collective-permute-start | bytes 4423688 | tf_op jit(solution)/shard_map/ppermute | solution.py:741
  138.5 9.4 %collective-permute-start.26 = (bf16[768,384]{1,0:T(8,128)(2,1)}, bf16[768,384]{1,0:T(8,128)(2,1)}, u32[]{:S(2)}, u32[]{:S(2)}) collective-permute-start(bf16[768,384]{1,0:T(8,128)(2,1)} %bitcast.385), channel_id=1, source_target_pairs={{0,1},{1,0},{2,3},{3,2},{4,5},{5,4},{6,7},{7,6},{8,9},{9,8},{10,11... | collective-permute-start | bytes 1769480 | tf_op jit(solution)/shard_map/ppermute | solution.py:741
  139.0 30.4 %collective-permute-start.23 = (bf16[384,768]{1,0:T(8,128)(2,1)S(1)}, bf16[384,768]{1,0:T(8,128)(2,1)}, u32[]{:S(2)}, u32[]{:S(2)}) collective-permute-start(bf16[384,768]{1,0:T(8,128)(2,1)S(1)} %bitcast.383), channel_id=1, source_target_pairs={{0,8},{1,9},{2,10},{3,11},{4,12},{5,13},{6,14},{7,15},{8,0},{9,1},... | collective-permute-start | bytes 1769480 | tf_op jit(solution)/shard_map/ppermute | solution.py:741
  173.2 25.6 %collective-permute-start.28 = (bf16[768,768]{1,0:T(8,128)(2,1)}, bf16[768,768]{1,0:T(8,128)(2,1)S(1)}, u32[]{:S(2)}, u32[]{:S(2)}) collective-permute-start(bf16[768,768]{1,0:T(8,128)(2,1)} %pad_maximum_fusion.9), channel_id=1, source_target_pairs={{0,4},{1,5},{2,6},{3,7},{4,0},{5,1},{6,2},{7,3},{8,12},{9,13},{10,... | collective-permute-start | bytes 3538952 | tf_op jit(solution)/shard_map/ppermute | solution.py:741
  175.1 28.6 %collective-permute-start.27 = (bf16[768,768]{1,0:T(8,128)(2,1)}, bf16[768,768]{1,0:T(8,128)(2,1)S(1)}, u32[]{:S(2)}, u32[]{:S(2)}) collective-permute-start(bf16[768,768]{1,0:T(8,128)(2,1)} %pad_maximum_fusion.8), channel_id=1, source_target_pairs={{0,2},{1,3},{2,0},{3,1},{4,6},{5,7},{6,4},{7,5},{8,10},{9,11},{10,... | collective-permute-start | bytes 3538952 | tf_op jit(solution)/shard_map/ppermute | solution.py:741
  204.8 27.7 %collective-permute-start.32 = (bf16[768,768]{1,0:T(8,128)(2,1)S(1)}, bf16[768,768]{1,0:T(8,128)(2,1)S(1)}, u32[]{:S(2)}, u32[]{:S(2)}) collective-permute-start(bf16[768,768]{1,0:T(8,128)(2,1)S(1)} %bitcast.329), channel_id=1, source_target_pairs={{0,4},{1,5},{2,6},{3,7},{4,0},{5,1},{6,2},{7,3},{8,12},{9,13},{10,... | collective-permute-start | bytes 3538952 | tf_op jit(solution)/shard_map/ppermute | solution.py:741
  206.2 27.4 %collective-permute-start.31 = (bf16[768,768]{1,0:T(8,128)(2,1)S(1)}, bf16[768,768]{1,0:T(8,128)(2,1)}, u32[]{:S(2)}, u32[]{:S(2)}) collective-permute-start(bf16[768,768]{1,0:T(8,128)(2,1)S(1)} %bitcast.327), channel_id=1, source_target_pairs={{0,2},{1,3},{2,0},{3,1},{4,6},{5,7},{6,4},{7,5},{8,10},{9,11},{10,... | collective-permute-start | bytes 3538952 | tf_op jit(solution)/shard_map/ppermute | solution.py:741
  210.3 9.0 %collective-permute-start.35 = (bf16[768,384]{1,0:T(8,128)(2,1)}, bf16[768,384]{1,0:T(8,128)(2,1)S(1)}, u32[]{:S(2)}, u32[]{:S(2)}) collective-permute-start(bf16[768,384]{1,0:T(8,128)(2,1)} %bitcast.388), channel_id=1, source_target_pairs={{0,1},{1,0},{2,3},{3,2},{4,5},{5,4},{6,7},{7,6},{8,9},{9,8},{10,11... | collective-permute-start | bytes 1769480 | tf_op jit(solution)/shard_map/ppermute | solution.py:741
  290.6 32.7 %collective-permute-start.42 = (bf16[896,768]{1,0:T(8,128)(2,1)}, bf16[896,768]{1,0:T(8,128)(2,1)S(1)}, u32[]{:S(2)}, u32[]{:S(2)}) collective-permute-start(bf16[896,768]{1,0:T(8,128)(2,1)} %get-tuple-element.499), channel_id=1, source_target_pairs={{0,2},{1,3},{2,0},{3,1},{4,6},{5,7},{6,4},{7,5},{8,10},{9,11},{10,... | collective-permute-start | bytes 4128776 | tf_op jit(solution)/shard_map/ppermute | solution.py:741
  295.0 28.2 %collective-permute-start.41 = (bf16[768,768]{1,0:T(8,128)(2,1)}, bf16[768,768]{1,0:T(8,128)(2,1)S(1)}, u32[]{:S(2)}, u32[]{:S(2)}) collective-permute-start(bf16[768,768]{1,0:T(8,128)(2,1)} %get-tuple-element.498), channel_id=1, source_target_pairs={{0,4},{1,5},{2,6},{3,7},{4,0},{5,1},{6,2},{7,3},{8,12},{9,13},{10,... | collective-permute-start | bytes 3538952 | tf_op jit(solution)/shard_map/ppermute | solution.py:741
  334.0 28.6 %collective-permute-start.46 = (bf16[768,768]{1,0:T(8,128)(2,1)}, bf16[768,768]{1,0:T(8,128)(2,1)S(1)}, u32[]{:S(2)}, u32[]{:S(2)}) collective-permute-start(bf16[768,768]{1,0:T(8,128)(2,1)} %get-tuple-element.524), channel_id=1, source_target_pairs={{0,4},{1,5},{2,6},{3,7},{4,0},{5,1},{6,2},{7,3},{8,12},{9,13},{10,... | collective-permute-start | bytes 3538952 | tf_op jit(solution)/shard_map/ppermute | solution.py:741
  335.2 28.3 %collective-permute-start.47 = (bf16[768,768]{1,0:T(8,128)(2,1)}, bf16[768,768]{1,0:T(8,128)(2,1)S(1)}, u32[]{:S(2)}, u32[]{:S(2)}) collective-permute-start(bf16[768,768]{1,0:T(8,128)(2,1)} %get-tuple-element.525), channel_id=1, source_target_pairs={{0,2},{1,3},{2,0},{3,1},{4,6},{5,7},{6,4},{7,5},{8,10},{9,11},{10,... | collective-permute-start | bytes 3538952 | tf_op jit(solution)/shard_map/ppermute | solution.py:741
  371.5 33.9 %collective-permute-start.51 = (bf16[960,768]{1,0:T(8,128)(2,1)}, bf16[960,768]{1,0:T(8,128)(2,1)S(1)}, u32[]{:S(2)}, u32[]{:S(2)}) collective-permute-start(bf16[960,768]{1,0:T(8,128)(2,1)} %get-tuple-element.552), channel_id=1, source_target_pairs={{0,4},{1,5},{2,6},{3,7},{4,0},{5,1},{6,2},{7,3},{8,12},{9,13},{10,... | collective-permute-start | bytes 4423688 | tf_op jit(solution)/shard_map/ppermute | solution.py:741
  372.4 33.7 %collective-permute-start.52 = (bf16[960,768]{1,0:T(8,128)(2,1)}, bf16[960,768]{1,0:T(8,128)(2,1)S(1)}, u32[]{:S(2)}, u32[]{:S(2)}) collective-permute-start(bf16[960,768]{1,0:T(8,128)(2,1)} %get-tuple-element.553), channel_id=1, source_target_pairs={{0,2},{1,3},{2,0},{3,1},{4,6},{5,7},{6,4},{7,5},{8,10},{9,11},{10,... | collective-permute-start | bytes 4423688 | tf_op jit(solution)/shard_map/ppermute | solution.py:741
  377.1 25.1 %collective-permute-start.50 = (bf16[384,768]{1,0:T(8,128)(2,1)}, bf16[384,768]{1,0:T(8,128)(2,1)}, u32[]{:S(2)}, u32[]{:S(2)}) collective-permute-start(bf16[384,768]{1,0:T(8,128)(2,1)} %get-tuple-element.551), channel_id=1, source_target_pairs={{0,8},{1,9},{2,10},{3,11},{4,12},{5,13},{6,14},{7,15},{8,0},{9,1},... | collective-permute-start | bytes 1769480 | tf_op jit(solution)/shard_map/ppermute | solution.py:741
  414.6 26.5 %collective-permute-start.58 = (bf16[768,768]{1,0:T(8,128)(2,1)}, bf16[768,768]{1,0:T(8,128)(2,1)S(1)}, u32[]{:S(2)}, u32[]{:S(2)}) collective-permute-start(bf16[768,768]{1,0:T(8,128)(2,1)} %get-tuple-element.591), channel_id=1, source_target_pairs={{0,4},{1,5},{2,6},{3,7},{4,0},{5,1},{6,2},{7,3},{8,12},{9,13},{10,... | collective-permute-start | bytes 3538952 | tf_op jit(solution)/shard_map/ppermute | solution.py:741
  415.7 26.3 %collective-permute-start.59 = (bf16[768,768]{1,0:T(8,128)(2,1)}, bf16[768,768]{1,0:T(8,128)(2,1)}, u32[]{:S(2)}, u32[]{:S(2)}) collective-permute-start(bf16[768,768]{1,0:T(8,128)(2,1)} %get-tuple-element.592), channel_id=1, source_target_pairs={{0,2},{1,3},{2,0},{3,1},{4,6},{5,7},{6,4},{7,5},{8,10},{9,11},{10,... | collective-permute-start | bytes 3538952 | tf_op jit(solution)/shard_map/ppermute | solution.py:741
  422.4 16.8 %collective-permute-start.56 = (bf16[192,768]{1,0:T(8,128)(2,1)}, bf16[192,768]{1,0:T(8,128)(2,1)S(1)}, u32[]{:S(2)}, u32[]{:S(2)}) collective-permute-start(bf16[192,768]{1,0:T(8,128)(2,1)} %get-tuple-element.589), channel_id=1, source_target_pairs={{0,16},{1,17},{2,18},{3,19},{4,20},{5,21},{6,22},{7,23},{8,24},{9,... | collective-permute-start | bytes 884744 | tf_op jit(solution)/shard_map/ppermute | solution.py:741
  424.1 15.2 %collective-permute-start.57 = (bf16[192,768]{1,0:T(8,128)(2,1)S(1)}, bf16[192,768]{1,0:T(8,128)(2,1)S(1)}, u32[]{:S(2)}, u32[]{:S(2)}) collective-permute-start(bf16[192,768]{1,0:T(8,128)(2,1)S(1)} %copy-done.76), channel_id=1, source_target_pairs={{0,8},{1,9},{2,10},{3,11},{4,12},{5,13},{6,14},{7,15},{8,0},{9,1},... | collective-permute-start | bytes 884744 | tf_op jit(solution)/shard_map/ppermute | solution.py:741
  449.4 28.2 %collective-permute-start.64 = (bf16[832,768]{1,0:T(8,128)(2,1)}, bf16[832,768]{1,0:T(8,128)(2,1)S(1)}, u32[]{:S(2)}, u32[]{:S(2)}) collective-permute-start(bf16[832,768]{1,0:T(8,128)(2,1)} %get-tuple-element.621), channel_id=1, source_target_pairs={{0,2},{1,3},{2,0},{3,1},{4,6},{5,7},{6,4},{7,5},{8,10},{9,11},{10,... | collective-permute-start | bytes 3833864 | tf_op jit(solution)/shard_map/ppermute | solution.py:741
  451.5 23.3 %collective-permute-start.63 = (bf16[704,768]{1,0:T(8,128)(2,1)}, bf16[704,768]{1,0:T(8,128)(2,1)S(1)}, u32[]{:S(2)}, u32[]{:S(2)}) collective-permute-start(bf16[704,768]{1,0:T(8,128)(2,1)} %get-tuple-element.620), channel_id=1, source_target_pairs={{0,4},{1,5},{2,6},{3,7},{4,0},{5,1},{6,2},{7,3},{8,12},{9,13},{10,... | collective-permute-start | bytes 3244040 | tf_op jit(solution)/shard_map/ppermute | solution.py:741
  454.1 15.9 %collective-permute-start.62 = (bf16[384,768]{1,0:T(8,128)(2,1)}, bf16[384,768]{1,0:T(8,128)(2,1)}, u32[]{:S(2)}, u32[]{:S(2)}) collective-permute-start(bf16[384,768]{1,0:T(8,128)(2,1)} %get-tuple-element.619), channel_id=1, source_target_pairs={{0,8},{1,9},{2,10},{3,11},{4,12},{5,13},{6,14},{7,15},{8,0},{9,1},... | collective-permute-start | bytes 1769480 | tf_op jit(solution)/shard_map/ppermute | solution.py:741
  484.2 13.6 %collective-permute-start.65 = (bf16[192,768]{1,0:T(8,128)(2,1)}, bf16[192,768]{1,0:T(8,128)(2,1)S(1)}, u32[]{:S(2)}, u32[]{:S(2)}) collective-permute-start(bf16[192,768]{1,0:T(8,128)(2,1)} %get-tuple-element.639), channel_id=1, source_target_pairs={{0,16},{1,17},{2,18},{3,19},{4,20},{5,21},{6,22},{7,23},{8,24},{9,... | collective-permute-start | bytes 884744 | tf_op jit(solution)/shard_map/ppermute | solution.py:741
  486.1 11.9 %collective-permute-start.66 = (bf16[192,768]{1,0:T(8,128)(2,1)}, bf16[192,768]{1,0:T(8,128)(2,1)S(1)}, u32[]{:S(2)}, u32[]{:S(2)}) collective-permute-start(bf16[192,768]{1,0:T(8,128)(2,1)} %get-tuple-element.640), channel_id=1, source_target_pairs={{0,8},{1,9},{2,10},{3,11},{4,12},{5,13},{6,14},{7,15},{8,0},{9,1},... | collective-permute-start | bytes 884744 | tf_op jit(solution)/shard_map/ppermute | solution.py:741
  488.0 10.1 %collective-permute-start.67 = (bf16[256,768]{1,0:T(8,128)(2,1)}, bf16[256,768]{1,0:T(8,128)(2,1)S(1)}, u32[]{:S(2)}, u32[]{:S(2)}) collective-permute-start(bf16[256,768]{1,0:T(8,128)(2,1)} %get-tuple-element.641), channel_id=1, source_target_pairs={{0,4},{1,5},{2,6},{3,7},{4,0},{5,1},{6,2},{7,3},{8,12},{9,13},{10,... | collective-permute-start | bytes 1179656 | tf_op jit(solution)/shard_map/ppermute | solution.py:741
  489.1 9.0 %collective-permute-start.68 = (bf16[256,768]{1,0:T(8,128)(2,1)}, bf16[256,768]{1,0:T(8,128)(2,1)S(1)}, u32[]{:S(2)}, u32[]{:S(2)}) collective-permute-start(bf16[256,768]{1,0:T(8,128)(2,1)} %get-tuple-element.642), channel_id=1, source_target_pairs={{0,2},{1,3},{2,0},{3,1},{4,6},{5,7},{6,4},{7,5},{8,10},{9,11},{10,... | collective-permute-start | bytes 1179656 | tf_op jit(solution)/shard_map/ppermute | solution.py:741
  493.9 10.4 %all-to-all-start.1 = ((f32[32,1,576]{2,1,0:T(1,128)}), f32[32,1,576]{2,1,0:T(1,128)S(1)}, u32[]{:S(2)}, u32[]{:S(2)}) async-start(f32[32,1,576]{2,1,0:T(1,128)} %copy.73), calls=%async_computation.1 | async-start | bytes 163840 | tf_op jit(solution)/shard_map/all_to_all | solution.py:1394
  502.1 13.5 %collective-permute-start.70 = (bf16[256,768]{1,0:T(8,128)(2,1)}, bf16[256,768]{1,0:T(8,128)(2,1)S(1)}, u32[]{:S(2)}, u32[]{:S(2)}) collective-permute-start(bf16[256,768]{1,0:T(8,128)(2,1)} %get-tuple-element.660), channel_id=1, source_target_pairs={{0,8},{1,9},{2,10},{3,11},{4,12},{5,13},{6,14},{7,15},{8,0},{9,1},... | collective-permute-start | bytes 1179656 | tf_op jit(solution)/shard_map/ppermute | solution.py:741
  506.3 31.6 %collective-permute-start.73 = (f32[24,3072]{1,0:T(8,128)}, f32[24,3072]{1,0:T(8,128)S(1)}, u32[]{:S(2)}, u32[]{:S(2)}) collective-permute-start(f32[24,3072]{1,0:T(8,128)} %get-tuple-element.690), channel_id=1, source_target_pairs={{0,1},{1,0},{2,3},{3,2},{4,5},{5,4},{6,7},{7,6},{8,9},{9,8},{10,11... | collective-permute-start | bytes 884744 | tf_op jit(solution)/shard_map/ppermute | solution.py:741
  518.5 11.1 %collective-permute-start.71 = (bf16[128,768]{1,0:T(8,128)(2,1)}, bf16[128,768]{1,0:T(8,128)(2,1)S(1)}, u32[]{:S(2)}, u32[]{:S(2)}) collective-permute-start(bf16[128,768]{1,0:T(8,128)(2,1)} %get-tuple-element.669), channel_id=1, source_target_pairs={{0,16},{1,17},{2,18},{3,19},{4,20},{5,21},{6,22},{7,23},{8,24},{9,... | collective-permute-start | bytes 589832 | tf_op jit(solution)/shard_map/ppermute | solution.py:741
  524.2 13.7 %collective-permute-start.72 = (f32[24,3072]{1,0:T(8,128)}, f32[24,3072]{1,0:T(8,128)S(1)}, u32[]{:S(2)}, u32[]{:S(2)}) collective-permute-start(f32[24,3072]{1,0:T(8,128)} %get-tuple-element.682), channel_id=1, source_target_pairs={{0,1},{1,0},{2,3},{3,2},{4,5},{5,4},{6,7},{7,6},{8,9},{9,8},{10,11... | collective-permute-start | bytes 884744 | tf_op jit(solution)/shard_map/ppermute | solution.py:741
  (116 other events, 581.6 us)

commit v3 on v2

--- a/solution.py
+++ b/solution.py
@@ -128,15 +128,14 @@
 
 def attn_fwd_kernel(core, xo, xs, wq, wk, wv, small, mask, q, k, v, mo, ms, *, layer):
     half = xo.shape[0]
+    joined = jnp.concatenate([wq[...], wk[...], wv[...]], axis=1)
+    row = ROW_ATTN + 2 * layer
     for first, rows in ((0, xo), (half, xs)):
-        x = rows[...]
-        q[first : first + half, :] = (
-            dot(x, wq[...]) + small[ROW_ATTN + 2 * layer : ROW_ATTN + 2 * layer + 1, :]
-        ).astype(BF16)
-        k[first : first + half, :] = dot(x, wk[...]).astype(BF16)
-        v[first : first + half, :] = (
-            dot(x, wv[...]) + small[ROW_ATTN + 2 * layer + 1 : ROW_ATTN + 2 * layer + 2, :]
-        ).astype(BF16)
+        span = slice(first, first + half)
+        qkv = dot(rows[...], joined)
+        q[span, :] = (qkv[:, :LANES] + small[row : row + 1, :]).astype(BF16)
+        k[span, :] = qkv[:, LANES : 2 * LANES].astype(BF16)
+        v[span, :] = (qkv[:, 2 * LANES :] + small[row + 1 : row + 2, :]).astype(BF16)
     keys, values = k[...], v[...]
     low_lanes = lax.broadcasted_iota(jnp.int32, (1, LANES), 1) < HEAD_DIM
     for first, out in ((0, mo), (half, ms)):
@@ -237,12 +236,13 @@
     sums[...] = jnp.zeros_like(sums)
     sums[0:1, :] = jnp.sum(dq_s[...].astype(F32), axis=0, keepdims=True)
     sums[1:2, :] = jnp.sum(dv_s[...].astype(F32), axis=0, keepdims=True)
+    weight_grads = dot(turned[...], all_s[...]).astype(BF16)
     for part, out in enumerate((dwq, dwk, dwv)):
-        out[...] = dot(turned[...], all_s[:, part * LANES : (part + 1) * LANES]).astype(BF16)
+        out[...] = weight_grads[:, part * LANES : (part + 1) * LANES]
     out_rows = dot(mo[...], dao[...], TN) + dot(ms[...], das[...], TN)
     dwo[0] = out_rows[:, :HALF].astype(BF16)
     dwo[1] = out_rows[:, HALF:].astype(BF16)
-    total = dot(dq_s[...], wq[...], NT) + dot(dk_s[...], wk[...], NT) + dot(dv_s[...], wv[...], NT)
+    total = dot(all_s[...], jnp.concatenate([wq[...], wk[...], wv[...]], axis=1), NT)
 
     @pl.when(step == 0)
     def _():
@@ -418,7 +418,7 @@
     )(*operands)
 
 
-FF_BLOCK = 256
+FF_BLOCK = 768
 FF_STEPS = FF // CORES // FF_BLOCK
 
 
@@ -453,13 +453,13 @@
 
 def ffn_specs(tokens, col):
     return (
-        pl.BlockSpec((D, FF_BLOCK), lambda j: (0, col // FF_BLOCK + j)),
-        pl.BlockSpec((FF_BLOCK, D), lambda j: (j % DOWN_STEPS, col // D + 2 + j // DOWN_STEPS)),
+        pl.BlockSpec((D, FF_BLOCK), lambda j: (0, j)),
+        pl.BlockSpec((FF_BLOCK, D), lambda j: (j % DOWN_STEPS, col // D + j // DOWN_STEPS)),
         pl.BlockSpec((tokens, FF_BLOCK), lambda j: (0, j)),
     )
 
 
-def ffn_fwd(yo, ys, wf, col, bias, layer):
+def ffn_fwd(yo, ys, w1, w2, col, bias, layer):
     half = yo.shape[0]
     tokens = 2 * half
     width = FF // CORES
@@ -480,7 +480,7 @@
         scratch_shapes=[pltpu.VMEM((tokens, D), F32)],
         compiler_params=params(),
         cost_estimate=cost(4 * tokens * D * width, 4 * D * width + 4 * tokens * width, tokens * width),
-    )(yo, ys, wf, bias, wf)
+    )(yo, ys, w1, bias, w2)
 
 
 def ffn_bwd_kernel(dfo, dfs, w1, w2, act, slope, yo, ys, dw1, dw2, sums, po, ps, acc, du, turned):
@@ -517,7 +517,7 @@
         ps[...] = acc[half:, :].astype(BF16)
 
 
-def ffn_bwd(dfo, dfs, wf, col, act, slope, yo, ys):
+def ffn_bwd(dfo, dfs, w1, w2, col, act, slope, yo, ys):
     half = yo.shape[0]
     tokens = 2 * half
     width = FF // CORES
@@ -547,7 +547,7 @@
         ],
         compiler_params=params(),
         cost_estimate=cost(8 * tokens * D * width, 8 * D * width + 4 * tokens * width),
-    )(dfo, dfs, wf, wf, act, slope, yo, ys)
+    )(dfo, dfs, w1, w2, act, slope, yo, ys)
 
 
 def shuffle_kernel(table, *refs, moves, count):
@@ -827,6 +827,62 @@
         return [out.reshape(-1, out.shape[-1]) for out in outs]
 
 
+class LateGather(Gather):
+    def __init__(self, at, local, shapes, place, idle):
+        self.at, self.local = at, local
+        self.half = local.shape[0] // 2
+        self.shapes, self.place = shapes, place
+        self.stages = [self.first, self.second] + [self.rest] * idle
+        self.stages += [functools.partial(self.flip, step) for step in at.flips()]
+        self.spots = [0]
+        self.got = None
+
+    def first(self, got):
+        self.sent = [self.local[None, : self.half], self.local[None, self.half :]]
+        return self.near(1, self.sent[0]) + self.near(2, self.sent[1])
+
+    def rest(self, got):
+        if got:
+            self.got = got
+        return []
+
+    def flip(self, step, got):
+        if self.got is not None:
+            got = self.got
+        if len(self.spots) == 1:
+            cut = self.at.ny - 1
+            self.held = jnp.concatenate(
+                [jnp.stack([part] + list(other)).reshape((-1,) + part.shape[-3:])
+                 for part, other in zip(self.sent, (got[:cut], got[cut:]))],
+                axis=1,
+            )[None]
+        else:
+            self.held = jnp.concatenate([self.held] + list(got))
+        self.got = None
+        self.spots = self.spots + [spot ^ step for spot in self.spots]
+        return [(0, step, self.held)]
+
+    def finish(self, got):
+        at = self.at
+        rows, cols = self.local.shape[1:]
+        sources, moves, table = [], [], []
+        spots = len(self.spots) // 2
+        for number, piece in enumerate([self.held] + list(got)):
+            at_block = 0
+            for spot in self.spots[number * spots : (number + 1) * spots]:
+                for far in range(at.nx):
+                    for near in range(at.ny):
+                        for unit in range(2 * self.half):
+                            kx, ky = (near, far) if unit < self.half else (far, near)
+                            for out, step, offset, to_col, at_col, width in self.place[unit]:
+                                moves.append((out, [len(table)], to_col, number, at_block, at_col, width))
+                                table.append(at.chip_of(spot, kx, ky) * step + offset)
+                            at_block += 1
+            sources.append(piece.reshape((-1, rows, cols)))
+        outs = shuffle(jnp.stack(table), sources, [sds(shape, BF16) for shape in self.shapes], moves)
+        return [out.reshape(-1, out.shape[-1]) for out in outs]
+
+
 class Reduce:
     def __init__(self, at, first, second):
         self.at, self.halves = at, (first, second)
@@ -932,30 +988,68 @@
         return chunk.finish(self.got[self.chunks.index(chunk)])
 
 
-def blocks_kernel(scalars, *refs, count, jobs):
+def blocks_kernel(scalars, *refs, counts, loads, jobs):
+    sources, outs = refs[: counts[0]], refs[counts[0] : counts[0] + counts[1]]
+    buffers = refs[counts[0] + counts[1] : -2]
+    load_sems, out_sems = refs[-2:]
+
     def rows(place, height):
         start, slopes = place
         for number, slope in slopes:
             start = start + scalars[number] * slope
         return pl.ds(pl.multiple_of(start, 16) if slopes else start, height)
 
-    for out, to, height, terms in jobs:
-        total = None
-        for parts, place in terms:
-            values = [refs[ref][rows(place, height), :] for ref in parts]
-            value = values[0] if len(values) == 1 else jnp.concatenate(values, axis=1)
-            if len(terms) > 1:
-                value = value.astype(F32)
-            total = value if total is None else total + value
-        ref = refs[count + out]
-        ref[to : to + height, :] = total.astype(ref.dtype)
+    copies = []
+    for number, (source, place, height, buffer, row, col, width) in enumerate(loads):
+        copies.append(
+            pltpu.make_async_copy(
+                sources[source].at[rows(place, height), :],
+                buffers[buffer].at[row : row + height, col : col + width],
+                load_sems.at[number],
+            )
+        )
+    for copy in copies:
+        copy.start()
+    waited = set()
+
+    def wait(numbers):
+        for number in numbers:
+            if number not in waited:
+                waited.add(number)
+                copies[number].wait()
+
+    stores = []
+    for out, (needs, sums) in enumerate(jobs):
+        for to, height, terms in sums:
+            total = None
+            for buffer, place, numbers in terms:
+                wait(numbers)
+                value = buffers[buffer][rows(place, height), :].astype(buffers[out].dtype)
+                total = value if total is None else total + value
+            buffers[out][to : to + height, :] = total.astype(buffers[out].dtype)
+        wait(needs)
+        stores.append(pltpu.make_async_copy(buffers[out], outs[out], out_sems.at[out]))
+        stores[-1].start()
+    for store in stores:
+        store.wait()
 
 
 class Stream:
     def __init__(self, parts, first_y, rows, base=0):
         self.parts, self.first_y, self.rows, self.base = parts, first_y, rows, base
         self.age = 0
-        self.keep = self.recv = self.total = None
+        self.keep = self.recv = self.total = self.joined = None
+
+
+class Joined:
+    def __init__(self, streams):
+        self.streams, self.out, self.total = streams, None, None
+        self.rows = sum(stream.rows for stream in streams)
+        for stream in streams:
+            stream.joined = self
+
+    def start(self, stream):
+        return sum(other.rows for other in self.streams[: self.streams.index(stream)])
 
 
 class Pipe:
@@ -1015,17 +1109,8 @@
         return sent, kept
 
     def step(self, *others, extra=None):
-        arrays, shapes, jobs = [], [], []
-        heights, keeps, self.sent = {}, [], []
-
-        def number(array):
-            for i, known in enumerate(arrays):
-                if known is array:
-                    return i
-            arrays.append(array)
-            return len(arrays) - 1
-
-        todo = []
+        heights, keeps, todo, self.sent = {}, [], [], []
+        spots, self.joined = [], None
         for streams in self.groups:
             for stream in streams:
                 if stream.age > self.last:
@@ -1044,29 +1129,92 @@
             heights[2] = sum(span)
         order = list(heights)
         shapes = [sds((heights[key], D), BF16) for key in order]
+        jobs = [([], []) for _ in order]
+        arrays, loads, buffers, held = [], [], [], {}
+
+        def source(array):
+            for i, known in enumerate(arrays):
+                if known is array:
+                    return i
+            arrays.append(array)
+            return len(arrays) - 1
+
+        for stream, key, start, sent, kept, rows in todo:
+            if kept:
+                last = stream.age == self.last
+                if last and stream.joined is not None:
+                    if stream.joined.out is None:
+                        stream.joined.out = len(shapes)
+                        shapes.append(sds((stream.joined.rows, D), F32))
+                        jobs.append(([], []))
+                        self.joined = stream.joined
+                    spots.append((stream.joined.out, stream.joined.start(stream)))
+                    continue
+                keeps.append((stream, len(shapes)))
+                spots.append((len(shapes), 0))
+                shapes.append(sds((len(kept) * rows, D), F32 if last else BF16))
+                jobs.append(([], []))
+        buffers = list(shapes)
         if extra is not None:
-            jobs.append((order.index(2), span[0], span[1], [([number(extra)], (0, []))]))
+            jobs[order.index(2)][0].append(len(loads))
+            loads.append((source(extra), (0, []), span[1], order.index(2), span[0], 0, D))
+        spare = len(buffers)
+        buffers.append(None)
+        spare_rows = 0
+
+        def term(parts, place, height):
+            nonlocal spare_rows
+            if len(parts) == 1 and not any(part is parts[0] for part in stream.parts):
+                array = source(parts[0])
+                if array not in held:
+                    held[array] = (len(buffers), len(loads))
+                    loads.append((array, (0, []), parts[0].shape[0], len(buffers), 0, 0, D))
+                    buffers.append(sds(parts[0].shape, parts[0].dtype))
+                return held[array][0], place, [held[array][1]]
+            row, numbers = spare_rows, []
+            spare_rows += height
+            for number, part in enumerate(parts):
+                width = D // len(parts)
+                numbers.append(len(loads))
+                loads.append((source(part), place, height, spare, row, number * width, width))
+            return spare, (row, []), numbers
+
         for stream, key, start, sent, kept, rows in todo:
             for block, terms in enumerate(sent):
-                terms = [([number(part) for part in parts], place) for parts, place in terms]
-                jobs.append((order.index(key), start + block * rows, rows, terms))
+                out = order.index(key)
+                to = start + block * rows
+                if len(terms) == 1:
+                    ((parts, place),) = terms
+                    for number, part in enumerate(parts):
+                        width = D // len(parts)
+                        jobs[out][0].append(len(loads))
+                        loads.append((source(part), place, rows, out, to, number * width, width))
+                else:
+                    jobs[out][1].append((to, rows, [term(parts, place, rows) for parts, place in terms]))
+        spots = iter(spots)
+        for stream, key, start, sent, kept, rows in todo:
             if kept:
-                last = stream.age == self.last
-                keeps.append((stream, len(shapes)))
+                out, first = next(spots)
                 for block, terms in enumerate(kept):
-                    terms = [([number(part) for part in parts], place) for parts, place in terms]
-                    jobs.append((len(shapes), block * rows, rows, terms))
-                shapes.append(sds((len(kept) * rows, D), F32 if last else BF16))
+                    terms = [term(parts, place, rows) for parts, place in terms]
+                    jobs[out][1].append((first + block * rows, rows, terms))
+        buffers[spare] = sds((max(spare_rows, 16), D), BF16)
         outs = pl.pallas_call(
-            functools.partial(blocks_kernel, count=len(arrays), jobs=jobs),
+            functools.partial(
+                blocks_kernel, counts=(len(arrays), len(shapes)), loads=loads, jobs=jobs
+            ),
             name="blocks",
             out_shape=shapes,
             in_specs=[pl.BlockSpec(memory_space=pltpu.SMEM)]
-            + [pl.BlockSpec(memory_space=pltpu.VMEM)] * len(arrays),
-            out_specs=[pl.BlockSpec(memory_space=pltpu.VMEM)] * len(shapes),
+            + [pl.BlockSpec(memory_space=pltpu.HBM)] * len(arrays),
+            out_specs=[pl.BlockSpec(memory_space=pltpu.HBM)] * len(shapes),
+            scratch_shapes=[pltpu.VMEM(buffer.shape, buffer.dtype) for buffer in buffers]
+            + [pltpu.SemaphoreType.DMA((len(loads),)), pltpu.SemaphoreType.DMA((len(shapes),))],
             compiler_params=params(),
             cost_estimate=cost(0, sum(3 * array.size for array in arrays)),
         )(self.scalars, *arrays)
+        if self.joined is not None:
+            self.joined.total = outs[self.joined.out]
         for stream, out in keeps:
             stream.keep = outs[out]
             if stream.age == self.last:
@@ -1177,7 +1325,7 @@
         back = jnp.stack(back)
         return jnp.stack([pick(back, (page - at.y) % ny) for page in range(ny)])[:, None]
 
-    def token_facts(hidden, boxes, page_size, band_count):
+    def token_facts(hidden, out_grad, boxes, page_size, band_count):
         widths, heights = page_size[0][:, None], page_size[1][:, None]
         left = boxes[0, :, 0] * GRID // widths
         top = boxes[1, :, 0] * GRID // heights
@@ -1194,7 +1342,8 @@
         mask = jnp.where(facts_all[6:7] > 0, 0.0, DEAD).astype(F32)
         live_own = facts_own[6].astype(F32)[:, None]
         hidden_own = jnp.concatenate(to_chip(hidden[:, 0]), axis=0)
-        return index, mask, live_own, hidden_own
+        grad_own = jnp.concatenate(to_chip(out_grad[:, 0]), axis=0)
+        return index, mask, live_own, hidden_own, grad_own
 
     cut = SMALL_ROWS * rows_dev
 
@@ -1239,10 +1388,11 @@
 
     def feed(layer, state):
         y1, y1_low = state
-        (wf,) = line.result(chunks[2 + 2 * layer])
+        (w1,) = line.result(chunks[2 + 2 * layer])
+        w2, col = (w1, 2 * D) if layer == 0 else (downs[0], 0)
         y1_other = at.swap(y1_low)
-        weights[layer] += [wf, 0]
-        act, slope, part, part_other = ffn_fwd(y1_low, y1_other, wf, 0, up_bias, layer)
+        weights[layer] += [w1, w2, col]
+        act, slope, part, part_other = ffn_fwd(y1_low, y1_other, w1, w2, col, up_bias, layer)
         x, x_low, n2, r2 = add_norm(y1, part, at.swap(part_other), small, layer)
         saved[layer] += [y1_low, y1_other, act, slope, n2, r2]
         return x, x_low
@@ -1252,12 +1402,20 @@
     chunks = [Gather(at, layout_tables, table_shapes, table_place)]
     parts = [look_up]
     line.add(chunks[0])
+    down_chunk = LateGather(
+        at,
+        ffn_out[LAYERS - 1].reshape(2, chip_rows, D),
+        ((chips, chip_rows, 2 * D),),
+        ([(0, 1, 0, 0, 0, D)], [(0, 1, 0, D, 0, D)]),
+        3,
+    )
+    line.add(down_chunk)
     line.step()
     locals0 = local_weights(0)
-    token_args = (hidden, boxes, page_size, band_count)
+    token_args = (hidden, out_grad, boxes, page_size, band_count)
     small_args = (attn_bias, out_bias, norm_gain, norm_bias, ffn_out_bias, ffn_in_bias)
     locals0, token_args = line.close(locals0, token_args)
-    state = ()
+    state, downs = (), []
     running = None
     waiting = []
     for layer in range(LAYERS):
@@ -1269,24 +1427,34 @@
             layer, number = waiting.pop(0)
             if layer > 0 and number == 0:
                 local = local_weights(layer)
-            chunks.append(
-                Gather(at, local[number], (attn_shapes, ffn_shapes)[number], (attn_place, ffn_place)[number])
-            )
+            if layer > 0 and number == 1:
+                shard = jnp.stack([local[1][0], local[1][2]])
+                shapes, place = ((chips, chip_rows, 2 * D),), ([(0, 1, 0, 0, 0, D)], [(0, 1, 0, D, 0, D)])
+            else:
+                shard = local[number]
+                shapes, place = (attn_shapes, ffn_shapes)[number], (attn_place, ffn_place)[number]
+            chunks.append(Gather(at, shard, shapes, place))
             line.add(chunks[-1])
         if all(line.done(chunk) for chunk in chunks):
             state = running(state)
             break
         state = line.step(*state)
+        if line.done(down_chunk) and not downs and not line.fresh(down_chunk):
+            downs.append(line.result(down_chunk)[0])
         if running is not None:
             state = running(state)
         if len(chunks) == 2:
             tokens, small_args, late = line.close(
                 token_facts(*token_args), small_args, (attn_in, attn_out, ffn_in)
             )
-            index, mask, live_own, hidden_own = tokens
+            index, mask, live_own, hidden_own, grad_own = tokens
             attn_in, attn_out, ffn_in = late
         elif len(chunks) == 3:
+            (small_args,) = line.close(small_args)
+        elif len(chunks) == 4:
             small, up_bias = line.close(*small_params(*small_args))
+        elif downs:
+            state, downs = line.close(state, downs)
         else:
             state = line.close(*state)
         ready = [number for number, chunk in enumerate(chunks) if line.fresh(chunk)]
@@ -1296,10 +1464,10 @@
     small_grads = [None] * LAYERS
 
     def backward_ffn(layer, sources):
-        wf, col = weights[layer][3:]
+        w1, w2, col = weights[layer][3:]
         y1_low, y1_other, act, slope, n2, r2 = saved[layer][9:]
         gh2, df, sums2 = norm_bwd(sources, n2, r2, small, 2 * layer + 1)
-        dw1, dw2, up_sums, part, part_other = ffn_bwd(df, at.swap(df), wf, col, act, slope, y1_low, y1_other)
+        dw1, dw2, up_sums, part, part_other = ffn_bwd(df, at.swap(df), w1, w2, col, act, slope, y1_low, y1_other)
         small_grads[layer] = [sums2, up_sums]
         return (gh2, part, at.swap(part_other)), dw1, dw2
 
@@ -1317,7 +1485,6 @@
         dwq, dwk, dwv = dqkv
         return [dwq, dwk], [dwv, by_core(core, *dwo, 0).reshape(D, HALF)]
 
-    grad_own = jnp.concatenate(to_chip(tie(out_grad[:, 0], saved[0][0])), axis=0)
     line = Pipe(at) if tiled else Line(at)
 
     def ffn_chunk(dw1, dw2):
@@ -1344,7 +1511,7 @@
         if tiled:
             streams = [Stream([table], number < 2, table_rows) for number, table in enumerate(tables)]
             line.add(streams)
-            return streams
+            return Joined(streams)
         chunk = Reduce(at, [[table] for table in tables[:2]], [[table] for table in tables[2:]])
         line.add(chunk)
         return chunk
@@ -1352,7 +1519,7 @@
     sources, dw1, dw2 = backward_ffn(1, (grad_own, live_own))
     ffn1 = ffn_chunk(dw1, dw2)
     output = x * live_own
-    sources = line.step(*sources, extra=output[cap:] if tiled else None)
+    sources = line.step(*sources, extra=output[cap:].astype(BF16) if tiled else None)
     sources, dqkv, dwo = backward_attn(1, sources)
     sources = line.close(*sources)
     output = from_chip(output, line.extra if tiled else send_back(output))
@@ -1371,7 +1538,7 @@
     table_parts = table_grads(index, grad_low, at.swap(grad_low), chips * table_rows)
     table_parts = line.close(*table_parts)
     tab = table_chunk(table_parts)
-    line.step(extra=grad_x[cap:] if tiled else None)
+    line.step(extra=grad_x[cap:].astype(BF16) if tiled else None)
     line.close()
     input_grad = from_chip(grad_x, line.extra if tiled else send_back(grad_x))
     zeros = jnp.zeros((2, HALF), F32)
@@ -1393,17 +1560,39 @@
     )
     segments = lax.all_to_all(segments, ("page", "band"), 0, 0, tiled=True)
 
+
+    def small_outputs(segments):
+        segment = jnp.sum(segments, axis=0)
+        rows = segment[:cut].reshape(SMALL_ROWS, rows_dev)
+        return (
+            rows[ROW_ATTN:ROW_OUT].reshape(LAYERS, 2, rows_dev),
+            rows[ROW_OUT:ROW_GAIN],
+            rows[ROW_GAIN:ROW_SHIFT].reshape(LAYERS, 2, rows_dev),
+            rows[ROW_SHIFT:ROW_DOWN].reshape(LAYERS, 2, rows_dev),
+            segment[cut:].reshape(LAYERS, ff_dev),
+            rows[ROW_DOWN:SMALL_ROWS],
+        )
+
+    grads = None
     while line.busy():
         line.step()
-        line.close()
-    segments = tie(segments, tab[0].total if tiled else line.moved)
-    segment = jnp.sum(segments, axis=0)
-    rows = segment[:cut].reshape(SMALL_ROWS, rows_dev)
+        if tiled and grads is None and att0[0].total is not None:
+            results = [
+                [stream.total for stream in attn[:2] + ffn] for attn, ffn in ((att0, ffn0), (att1, ffn1))
+            ]
+            parts = []
+            for qk, vo, up_a, down_a, up_b, down_b in results:
+                mine, send = split(core_id, (qk, vo, up_a, up_b))
+                parts += [mine, at.swap(send), down_a, down_b]
+            grads = merge(core_id, parts)
+            smalls = small_outputs(tie(segments, grads[0]))
+            grads, smalls = line.close(grads, smalls)
+        else:
+            line.close()
+    if not tiled:
+        smalls = small_outputs(segments)
     if tiled:
-        grad_tables = jnp.stack([stream.total for stream in tab])
-        results = [
-            [stream.total for stream in attn[:2] + ffn] for attn, ffn in ((att0, ffn0), (att1, ffn1))
-        ]
+        grad_tables = tab.total.reshape(4, table_rows, D)
     else:
         sums = [line.result(chunk) for chunk in (att0, ffn0, att1, ffn1)]
         grad_tables = jnp.stack(line.result(tab)).reshape(4, table_rows, D)
@@ -1413,14 +1602,7 @@
             ffn = jnp.stack(ffn_sum).reshape(4, chip_rows, D)
             results.append((attn, ffn, ffn))
 
-    if tiled:
-        parts = []
-        for layer in range(LAYERS):
-            qk, vo, up_a, down_a, up_b, down_b = results[layer]
-            mine, send = split(core_id, (qk, vo, up_a, up_b))
-            parts += [mine, at.swap(send), down_a, down_b]
-        grads = merge(core_id, parts)
-    else:
+    if not tiled:
         grads = [[], [], [], []]
         for layer in range(LAYERS):
             attn_sum, up_sum, down_sum = results[layer]
@@ -1441,15 +1623,15 @@
         input_grad,
         grad_tables,
         grads[0],
-        rows[ROW_ATTN:ROW_OUT].reshape(LAYERS, 2, rows_dev),
+        smalls[0],
         grads[1],
-        rows[ROW_OUT:ROW_GAIN],
-        rows[ROW_GAIN:ROW_SHIFT].reshape(LAYERS, 2, rows_dev),
-        rows[ROW_SHIFT:ROW_DOWN].reshape(LAYERS, 2, rows_dev),
+        smalls[1],
+        smalls[2],
+        smalls[3],
         grads[2],
-        segment[cut:].reshape(LAYERS, ff_dev),
+        smalls[4],
         grads[3],
-        rows[ROW_DOWN:SMALL_ROWS],
+        smalls[5],
     )
 
 

time: 547 us -> 529 us (0.967)
  Pallas kernels: 226 us -> 207 us
  local copies, waits for them, and re-layouts: 64.6 us -> 79.6 us
  waiting for transfers between devices: 137 us -> 125 us
    ppermute x74 -> x80, waiting for transfers between devices: 131 us -> 113 us  [move(): return lax.ppermute(value, ('page', 'band'), pairs)]
    slice x15, local copies, waits for them, and re-layouts: 12.5 us -> 20.8 us  [exchange(): got[i] = moved[first:first + part.shape[0]].reshape(wants[i][2].shape)]
    pallas_call x2, Pallas kernels: 24.1 us -> 15.9 us  [ffn_fwd(): pl.pallas_call(functools.partial(ffn_fwd_kernel, layer=layer), name='ffn_...]
    pallas_call x2, Pallas kernels: 32.2 us -> 24.6 us  [ffn_bwd(): pl.pallas_call(ffn_bwd_kernel, name='ffn_bwd', out_shape=[sds((2, D, D),...]
    all_to_all x1, waiting for transfers between devices: 6.03 us -> 12.2 us  [small_params(): lax.all_to_all(jnp.broadcast_to(segment, (devices, segment.shape[0])), ('...]
    unnamed x174 -> x204, local copies, waits for them, and re-layouts: 19 us -> 25.2 us
    ppermute x74 -> x80, starting transfers between devices: 72.8 us -> 70.4 us  [move(): return lax.ppermute(value, ('page', 'band'), pairs)]
    pallas_call x5 -> x6, Pallas kernels: 20.3 us -> 21.9 us  [shuffle(): pl.pallas_call(functools.partial(shuffle_kernel, moves=moves, count=len(s...]
  transfers between devices with their start and end apart: 76 -> 82, of which waited for: 43 -> 41; matrix products, arithmetic and copies ran while one was open for 12% -> 14% of each run, Pallas kernels for 28% -> 28%
where the time goes in v3:
time: 529 us; the launch traced here: 522 us
  Pallas kernels  207 us (39%)
  waiting for transfers between devices  125 us (24%)
  local copies, waits for them, and re-layouts  79.6 us (15%)
  starting transfers between devices  77.7 us (15%)
  other arithmetic  31.1 us (6%)
    ppermute x80, waiting for transfers between devices, move(): return lax.ppermute(value, ('page', 'band'), pairs)  113 us
    ppermute x80, starting transfers between devices, move(): return lax.ppermute(value, ('page', 'band'), pairs)  70.4 us
    pallas_call x9, Pallas kernels, step(): pl.pallas_call(functools.partial(blocks_kernel, counts=(len(arrays), len(...  42.1 us
    pallas_call x2, Pallas kernels, attn_bwd(): pl.pallas_call(attn_bwd_kernel, name='attn_bwd', out_shape=[sds((D, HALF)...  34.9 us
    unnamed x204, local copies, waits for them, and re-layouts  25.2 us
    pallas_call x2, Pallas kernels, ffn_bwd(): pl.pallas_call(ffn_bwd_kernel, name='ffn_bwd', out_shape=[sds((2, D, D),...  24.6 us
    pallas_call x6, Pallas kernels, shuffle(): pl.pallas_call(functools.partial(shuffle_kernel, moves=moves, count=len(s...  21.9 us
    slice x15, local copies, waits for them, and re-layouts, exchange(): got[i] = moved[first:first + part.shape[0]].reshape(wants[i][2].shape)  20.8 us
  transfers between devices with their start and end apart: 82, of which 41 were waited for; matrix products, arithmetic and copies ran while one was open for 14% of the time, Pallas kernels for 28%

profile of v3, /device:TPU:0, one launch (start us, length us, event | category | flops | bytes accessed | tf_op | source)
XLA Modules:
  0.0 522.3 jit_solution(8013076527320101062)
XLA Ops:
  1.7 4.1 collective-permute-start
  25.8 4.0 collective-permute-done.10
  32.7 4.4 collective-permute-done.7
  54.1 4.3 collective-permute-done.16
  68.8 3.9 all-to-all-start
  75.6 12.2 %all-to-all-done = bf16[32,2,288]{2,1,0:T(2,128)(2,1)S(1)} async-done(((bf16[32,2,288]{2,1,0:T(2,128)(2,1)}), bf16[32,2,288]{2,1,0:T(2,128)(2,1)S(1)}, u32[]{:S(2)}, u32[]{:S(2)}) %all-to-all-start) | async-done | bytes 36896 | tf_op jit(solution)/shard_map/all_to_all | solution.py:1361
  107.2 3.8 shuffle.6
  111.0 5.8 %embed.1 = f32[512,768]{1,0:T(8,128)} custom-call(s32[512,8]{1,0:T(8,128)} %copy.77.idx, bf16[512,768]{1,0:T(8,128)(2,1)} %bitcast.472, bf16[512,768]{1,0:T(8,128)(2,1)} %bitcast.473, bf16[512,768]{1,0:T(8,128)(2,1)} %bitcast.474, bf16[512,768]{1,0:T(8,128)(2,1)} %bitcast.475), custom_call_target="tpu_custom_call" | custom-call | flops 1610612736 | bytes 4718592 | tf_op jit(solution)/shard_map/embed/pallas_call | solution.py:84
  120.9 8.5 %collective-permute-done.22 = bf16[768,768]{1,0:T(8,128)(2,1)} collective-permute-done((bf16[768,768]{1,0:T(8,128)(2,1)}, bf16[768,768]{1,0:T(8,128)(2,1)}, u32[]{:S(2)}, u32[]{:S(2)}) %collective-permute-start.22) | collective-permute-done | bytes 1179680 | tf_op jit(solution)/shard_map/ppermute | solution.py:741
  143.8 3.4 shuffle.7
  150.5 8.0 %attn_fwd.2 = (bf16[512,384]{1,0:T(8,128)(2,1)}, bf16[512,384]{1,0:T(8,128)(2,1)}, bf16[512,384]{1,0:T(8,128)(2,1)}, bf16[256,384]{1,0:T(8,128)(2,1)}, bf16[256,384]{1,0:T(8,128)(2,1)}) custom-call(s32[1]{0:T(128)} %bitcast.core, bf16[256,768]{1,0:T(8,128)(2,1)} %copy-done.14, bf16[256,768]{1,0:T(8,128)(2,1)} %copy-done.45, bf16[768,1536]{1,0:T(8,128)(2,1)} %bitcast.319, ...), custom_call_target="tpu_custom_call" | custom-call | flops 1711276032 | bytes 4128768 | tf_op jit(solution)/shard_map/attn_fwd/pallas_call | solution.py:163
  160.9 3.9 out_norm.2
  164.8 7.4 %collective-permute-done.28 = bf16[960,768]{1,0:T(8,128)(2,1)} collective-permute-done((bf16[960,768]{1,0:T(8,128)(2,1)}, bf16[960,768]{1,0:T(8,128)(2,1)}, u32[]{:S(2)}, u32[]{:S(2)}) %collective-permute-start.28) | collective-permute-done | bytes 1474592 | tf_op jit(solution)/shard_map/ppermute | solution.py:741
  185.6 4.8 shuffle.8
  190.4 8.0 %ffn_fwd.2 = (bf16[512,1536]{1,0:T(8,128)(2,1)}, bf16[512,1536]{1,0:T(8,128)(2,1)}, f32[256,768]{1,0:T(8,128)}, bf16[256,768]{1,0:T(8,128)(2,1)}) custom-call(bf16[256,768]{1,0:T(8,128)(2,1)} %get-tuple-element.500.yo, bf16[256,768]{1,0:T(8,128)(2,1)} %collective-permute-done.36.ys, bf16[768,3072]{1,0:T(8,128)(2,1)} %bitcast.315, f32[2,1536]{1,0:T(2,128)} %reshape.608.bias, ...), custom_call_target="tpu_custom_call" | custom-call | flops 2415919104 | bytes 7864320 | tf_op jit(solution)/shard_map/ffn_fwd/pallas_call | solution.py:467
  201.2 3.2 add_norm.2
  211.6 3.5 shuffle.9
  218.7 8.1 %attn_fwd.3 = (bf16[512,384]{1,0:T(8,128)(2,1)}, bf16[512,384]{1,0:T(8,128)(2,1)}, bf16[512,384]{1,0:T(8,128)(2,1)}, bf16[256,384]{1,0:T(8,128)(2,1)}, bf16[256,384]{1,0:T(8,128)(2,1)}) custom-call(s32[1]{0:T(128)} %bitcast.core, bf16[256,768]{1,0:T(8,128)(2,1)} %get-tuple-element.514.xo, bf16[256,768]{1,0:T(8,128)(2,1)} %copy-done.47, ...), custom_call_target="tpu_custom_call" | custom-call | flops 1711276032 | bytes 4128768 | tf_op jit(solution)/shard_map/attn_fwd/pallas_call | solution.py:163
  227.5 3.2 shuffle.10
  231.6 3.9 out_norm.3
  236.7 3.2 shuffle.11
  240.7 7.9 %ffn_fwd.3 = (bf16[512,1536]{1,0:T(8,128)(2,1)}, bf16[512,1536]{1,0:T(8,128)(2,1)}, f32[256,768]{1,0:T(8,128)}, bf16[256,768]{1,0:T(8,128)(2,1)}) custom-call(bf16[256,768]{1,0:T(8,128)(2,1)} %get-tuple-element.526.yo, bf16[256,768]{1,0:T(8,128)(2,1)} %copy-done.86, bf16[768,1536]{1,0:T(8,128)(2,1)} %bitcast.373, f32[2,1536]{1,0:T(2,128)} %reshape.608.bias, ...), custom_call_target="tpu_custom_call" | custom-call | flops 2415919104 | bytes 7864320 | tf_op jit(solution)/shard_map/ffn_fwd/pallas_call | solution.py:467
  251.4 3.1 add_norm.3
  260.2 12.2 %ffn_bwd.2 = (bf16[2,768,768]{2,1,0:T(8,128)(2,1)}, bf16[2,768,768]{2,1,0:T(8,128)(2,1)}, f32[8,1536]{1,0:T(8,128)}, f32[256,768]{1,0:T(8,128)}, bf16[256,768]{1,0:T(8,128)(2,1)}) custom-call(bf16[256,768]{1,0:T(8,128)(2,1)} %get-tuple-element.537.dfo, bf16[256,768]{1,0:T(8,128)(2,1)} %copy-done.90, bf16[768,1536]{1,0:T(8,128)(2,1)} %bitcast.374, ...), custom_call_target="tpu_custom_call" | custom-call | flops 4831838208 | bytes 12582912 | tf_op jit(solution)/shard_map/ffn_bwd/pallas_call | solution.py:525
  274.2 3.8 blocks.9
  278.8 3.3 norm_bwd.5
  284.2 17.4 %attn_bwd.2 = (bf16[768,384]{1,0:T(8,128)(2,1)}, bf16[768,384]{1,0:T(8,128)(2,1)}, bf16[768,384]{1,0:T(8,128)(2,1)}, bf16[2,384,384]{2,1,0:T(8,128)(2,1)}, f32[8...) custom-call(s32[1]{0:T(128)} %bitcast.core, bf16[256,768]{1,0:T(8,128)(2,1)} %get-tuple-element.555.dao, ...), custom_call_target="tpu_custom_call" | custom-call | flops 3825205248 | bytes 9437184 | tf_op jit(solution)/shard_map/attn_bwd/pallas_call | solution.py:269
  307.7 3.0 collective-permute-done.47.refs_3_
  312.2 5.5 %blocks.10 = (bf16[768,768]{1,0:T(8,128)(2,1)}, bf16[768,768]{1,0:T(8,128)(2,1)}, bf16[192,768]{1,0:T(8,128)(2,1)}, bf16[192,768]{1,0:T(8,128)(2,1)}, bf16[192,7...) custom-call(s32[4]{0:T(128)} %pad_add_fusion.2.scalars, bf16[1536,768]{1,0:T(8,128)(2,1)} %bitcast.336, ...), custom_call_target="tpu_custom_call" | custom-call | bytes 14450688 | tf_op jit(solution)/shard_map/blocks/pallas_call | solution.py:1202
  317.8 3.3 norm_bwd.6
  323.8 12.3 %ffn_bwd.3 = (bf16[2,768,768]{2,1,0:T(8,128)(2,1)}, bf16[2,768,768]{2,1,0:T(8,128)(2,1)}, f32[8,1536]{1,0:T(8,128)}, f32[256,768]{1,0:T(8,128)}, bf16[256,768]{1,0:T(8,128)(2,1)}) custom-call(bf16[256,768]{1,0:T(8,128)(2,1)} %get-tuple-element.581.dfo, bf16[256,768]{1,0:T(8,128)(2,1)} %copy-done.89, bf16[768,3072]{1,0:T(8,128)(2,1)} %bitcast.317, ...), custom_call_target="tpu_custom_call" | custom-call | flops 4831838208 | bytes 12582912 | tf_op jit(solution)/shard_map/ffn_bwd/pallas_call | solution.py:525
  338.1 11.6 %collective-permute-done.52.refs_1_ = bf16[768,768]{1,0:T(8,128)(2,1)S(1)} collective-permute-done((bf16[768,768]{1,0:T(8,128)(2,1)}, bf16[768,768]{1,0:T(8,128)(2,1)S(1)}, u32[]{:S(2)}, u32[]{:S(2)}) %collective-permute-start.52) | collective-permute-done | bytes 1179680 | tf_op jit(solution)/shard_map/ppermute | solution.py:741
  351.2 6.2 %blocks.11 = (bf16[384,768]{1,0:T(8,128)(2,1)}, bf16[960,768]{1,0:T(8,128)(2,1)}, bf16[960,768]{1,0:T(8,128)(2,1)}, bf16[96,768]{1,0:T(8,128)(2,1)}, bf16[96,768...) custom-call(s32[4]{0:T(128)} %pad_add_fusion.2.scalars, ...), custom_call_target="tpu_custom_call" | custom-call | bytes 15925248 | tf_op jit(solution)/shard_map/blocks/pallas_call | solution.py:1202
  360.0 3.4 norm_bwd.7
  366.2 17.4 %attn_bwd.3 = (bf16[768,384]{1,0:T(8,128)(2,1)}, bf16[768,384]{1,0:T(8,128)(2,1)}, bf16[768,384]{1,0:T(8,128)(2,1)}, bf16[2,384,384]{2,1,0:T(8,128)(2,1)}, f32[8...) custom-call(s32[1]{0:T(128)} %bitcast.core, bf16[256,768]{1,0:T(8,128)(2,1)} %get-tuple-element.609.dao, ...), custom_call_target="tpu_custom_call" | custom-call | flops 3825205248 | bytes 9437184 | tf_op jit(solution)/shard_map/attn_bwd/pallas_call | solution.py:269
  387.4 4.1 collective-permute-done.57.refs_6_
  392.6 6.5 %blocks.12 = (bf16[192,768]{1,0:T(8,128)(2,1)}, bf16[192,768]{1,0:T(8,128)(2,1)}, bf16[768,768]{1,0:T(8,128)(2,1)}, bf16[768,768]{1,0:T(8,128)(2,1)}, bf16[48,76...) custom-call(s32[4]{0:T(128)} %pad_add_fusion.2.scalars, ...), custom_call_target="tpu_custom_call" | custom-call | bytes 17694720 | tf_op jit(solution)/shard_map/blocks/pallas_call | solution.py:1202
  410.7 4.1 table_grads.1
  414.7 7.3 %collective-permute-done.62.refs_19_ = bf16[192,768]{1,0:T(8,128)(2,1)S(1)} collective-permute-done((bf16[192,768]{1,0:T(8,128)(2,1)}, bf16[192,768]{1,0:T(8,128)(2,1)S(1)}, u32[]{:S(2)}, u32[]{:S(2)}) %collective-permute-start.62) | collective-permute-done | bytes 294944 | tf_op jit(solution)/shard_map/ppermute | solution.py:741
  422.1 4.0 collective-permute-done.64.refs_5_
  427.1 6.4 %blocks.13 = (bf16[96,768]{1,0:T(8,128)(2,1)}, bf16[384,768]{1,0:T(8,128)(2,1)}, bf16[704,768]{1,0:T(8,128)(2,1)}, bf16[832,768]{1,0:T(8,128)(2,1)}, f32[48,768]...) custom-call(s32[4]{0:T(128)} %pad_add_fusion.2.scalars, ...), custom_call_target="tpu_custom_call" | custom-call | bytes 15630336 | tf_op jit(solution)/shard_map/blocks/pallas_call | solution.py:1202
  444.7 8.3 %collective-permute-done.67.refs_14_ = bf16[96,768]{1,0:T(8,128)(2,1)S(1)} collective-permute-done((bf16[96,768]{1,0:T(8,128)(2,1)}, bf16[96,768]{1,0:T(8,128)(2,1)S(1)}, u32[]{:S(2)}, u32[]{:S(2)}) %collective-permute-start.67) | collective-permute-done | bytes 147488 | tf_op jit(solution)/shard_map/ppermute | solution.py:741
  453.7 6.0 %collective-permute-done.69.refs_6_ = bf16[704,768]{1,0:T(8,128)(2,1)} collective-permute-done((bf16[704,768]{1,0:T(8,128)(2,1)}, bf16[704,768]{1,0:T(8,128)(2,1)}, u32[]{:S(2)}, u32[]{:S(2)}) %collective-permute-start.69) | collective-permute-done | bytes 1081376 | tf_op jit(solution)/shard_map/ppermute | solution.py:741
  462.8 4.9 blocks.14
  476.2 3.4 all-to-all-start.1
  482.3 3.6 blocks.15
  492.2 5.9 %collective-permute-done.75.refs_6_ = bf16[96,768]{1,0:T(8,128)(2,1)S(1)} collective-permute-done((bf16[96,768]{1,0:T(8,128)(2,1)S(1)}, bf16[96,768]{1,0:T(8,128)(2,1)S(1)}, u32[]{:S(2)}, u32[]{:S(2)}) %collective-permute-start.75) | collective-permute-done | bytes 147488 | tf_op jit(solution)/shard_map/ppermute | solution.py:741
  510.0 3.1 merge.1
  (512 shorter events, 230.4 us)
Async XLA Ops:
  1.7 13.4 %collective-permute-start = (bf16[128,768]{1,0:T(8,128)(2,1)}, bf16[128,768]{1,0:T(8,128)(2,1)S(1)}, u32[]{:S(2)}, u32[]{:S(2)}) collective-permute-start(bf16[128,768]{1,0:T(8,128)(2,1)} %bitcast.405), channel_id=1, source_target_pairs={{0,16},{1,17},{2,18},{3,19},{4,20},{5,21},{6,22},{7,23},{8,24},{9,... | collective-permute-start | bytes 589832 | tf_op jit(solution)/shard_map/ppermute | solution.py:741
  19.0 13.7 %collective-permute-start.5 = (bf16[96,768]{1,0:T(8,128)(2,1)S(1)}, bf16[96,768]{1,0:T(8,128)(2,1)S(1)}, u32[]{:S(2)}, u32[]{:S(2)}) collective-permute-start(bf16[96,768]{1,0:T(8,128)(2,1)S(1)} %bitcast.447), channel_id=1, source_target_pairs={{0,2},{1,3},{2,0},{3,1},{4,6},{5,7},{6,4},{7,5},{8,10},{9,11},{10,... | collective-permute-start | bytes 442376 | tf_op jit(solution)/shard_map/ppermute | solution.py:741
  19.4 13.2 %collective-permute-start.6 = (bf16[96,768]{1,0:T(8,128)(2,1)S(1)}, bf16[96,768]{1,0:T(8,128)(2,1)S(1)}, u32[]{:S(2)}, u32[]{:S(2)}) collective-permute-start(bf16[96,768]{1,0:T(8,128)(2,1)S(1)} %bitcast.446), channel_id=1, source_target_pairs={{0,4},{1,5},{2,6},{3,7},{4,0},{5,1},{6,2},{7,3},{8,12},{9,13},{10,... | collective-permute-start | bytes 442376 | tf_op jit(solution)/shard_map/ppermute | solution.py:741
  24.4 14.3 %collective-permute-start.4 = (bf16[256,768]{1,0:T(8,128)(2,1)S(1)}, bf16[256,768]{1,0:T(8,128)(2,1)S(1)}, u32[]{:S(2)}, u32[]{:S(2)}) collective-permute-start(bf16[256,768]{1,0:T(8,128)(2,1)S(1)} %bitcast.432), channel_id=1, source_target_pairs={{0,8},{1,9},{2,10},{3,11},{4,12},{5,13},{6,14},{7,15},{8,0},{9,1},... | collective-permute-start | bytes 1179656 | tf_op jit(solution)/shard_map/ppermute | solution.py:741
  39.0 19.4 %collective-permute-start.14 = (bf16[256,768]{1,0:T(8,128)(2,1)S(1)}, bf16[256,768]{1,0:T(8,128)(2,1)S(1)}, u32[]{:S(2)}, u32[]{:S(2)}) collective-permute-start(bf16[256,768]{1,0:T(8,128)(2,1)S(1)} %bitcast.431), channel_id=1, source_target_pairs={{0,2},{1,3},{2,0},{3,1},{4,6},{5,7},{6,4},{7,5},{8,10},{9,11},{10,... | collective-permute-start | bytes 1179656 | tf_op jit(solution)/shard_map/ppermute | solution.py:741
  40.6 17.9 %collective-permute-start.13 = (bf16[256,768]{1,0:T(8,128)(2,1)S(1)}, bf16[256,768]{1,0:T(8,128)(2,1)S(1)}, u32[]{:S(2)}, u32[]{:S(2)}) collective-permute-start(bf16[256,768]{1,0:T(8,128)(2,1)S(1)} %bitcast.430), channel_id=1, source_target_pairs={{0,4},{1,5},{2,6},{3,7},{4,0},{5,1},{6,2},{7,3},{8,12},{9,13},{10,... | collective-permute-start | bytes 1179656 | tf_op jit(solution)/shard_map/ppermute | solution.py:741
  41.2 13.0 %collective-permute-start.15 = (bf16[192,768]{1,0:T(8,128)(2,1)S(1)}, bf16[192,768]{1,0:T(8,128)(2,1)S(1)}, u32[]{:S(2)}, u32[]{:S(2)}) collective-permute-start(bf16[192,768]{1,0:T(8,128)(2,1)S(1)} %bitcast.441), channel_id=1, source_target_pairs={{0,8},{1,9},{2,10},{3,11},{4,12},{5,13},{6,14},{7,15},{8,0},{9,1},... | collective-permute-start | bytes 884744 | tf_op jit(solution)/shard_map/ppermute | solution.py:741
  43.5 15.0 %collective-permute-start.16 = (bf16[192,768]{1,0:T(8,128)(2,1)S(1)}, bf16[192,768]{1,0:T(8,128)(2,1)S(1)}, u32[]{:S(2)}, u32[]{:S(2)}) collective-permute-start(bf16[192,768]{1,0:T(8,128)(2,1)S(1)} %bitcast.387), channel_id=1, source_target_pairs={{0,16},{1,17},{2,18},{3,19},{4,20},{5,21},{6,22},{7,23},{8,24},{9,... | collective-permute-start | bytes 884744 | tf_op jit(solution)/shard_map/ppermute | solution.py:741
  62.8 27.0 %collective-permute-start.18 = (bf16[704,768]{1,0:T(8,128)(2,1)}, bf16[704,768]{1,0:T(8,128)(2,1)}, u32[]{:S(2)}, u32[]{:S(2)}) collective-permute-start(bf16[704,768]{1,0:T(8,128)(2,1)} %pad_maximum_fusion.9), channel_id=1, source_target_pairs={{0,4},{1,5},{2,6},{3,7},{4,0},{5,1},{6,2},{7,3},{8,12},{9,13},{10,... | collective-permute-start | bytes 3244040 | tf_op jit(solution)/shard_map/ppermute | solution.py:741
  65.5 27.4 %collective-permute-start.17 = (bf16[704,768]{1,0:T(8,128)(2,1)}, bf16[704,768]{1,0:T(8,128)(2,1)}, u32[]{:S(2)}, u32[]{:S(2)}) collective-permute-start(bf16[704,768]{1,0:T(8,128)(2,1)} %pad_maximum_fusion.8), channel_id=1, source_target_pairs={{0,2},{1,3},{2,0},{3,1},{4,6},{5,7},{6,4},{7,5},{8,10},{9,11},{10,... | collective-permute-start | bytes 3244040 | tf_op jit(solution)/shard_map/ppermute | solution.py:741
  66.0 30.0 %collective-permute-start.19 = (bf16[384,768]{1,0:T(8,128)(2,1)}, bf16[384,768]{1,0:T(8,128)(2,1)}, u32[]{:S(2)}, u32[]{:S(2)}) collective-permute-start(bf16[384,768]{1,0:T(8,128)(2,1)} %bitcast.73), channel_id=1, source_target_pairs={{0,8},{1,9},{2,10},{3,11},{4,12},{5,13},{6,14},{7,15},{8,0},{9,1},... | collective-permute-start | bytes 1769480 | tf_op jit(solution)/shard_map/ppermute | solution.py:741
  68.8 19.0 %all-to-all-start = ((bf16[32,2,288]{2,1,0:T(2,128)(2,1)}), bf16[32,2,288]{2,1,0:T(2,128)(2,1)S(1)}, u32[]{:S(2)}, u32[]{:S(2)}) async-start(bf16[32,2,288]{2,1,0:T(2,128)(2,1)} %reshape.697), calls=%async_computation | async-start | bytes 98304 | tf_op jit(solution)/shard_map/all_to_all | solution.py:1361
  72.7 23.3 %collective-permute-start.20 = (bf16[96,768]{1,0:T(8,128)(2,1)S(1)}, bf16[96,768]{1,0:T(8,128)(2,1)S(1)}, u32[]{:S(2)}, u32[]{:S(2)}) collective-permute-start(bf16[96,768]{1,0:T(8,128)(2,1)S(1)} %bitcast.412), channel_id=1, source_target_pairs={{0,16},{1,17},{2,18},{3,19},{4,20},{5,21},{6,22},{7,23},{8,24},{9,... | collective-permute-start | bytes 442376 | tf_op jit(solution)/shard_map/ppermute | solution.py:741
  101.2 28.3 %collective-permute-start.22 = (bf16[768,768]{1,0:T(8,128)(2,1)}, bf16[768,768]{1,0:T(8,128)(2,1)}, u32[]{:S(2)}, u32[]{:S(2)}) collective-permute-start(bf16[768,768]{1,0:T(8,128)(2,1)} %pad_maximum_fusion.4), channel_id=1, source_target_pairs={{0,4},{1,5},{2,6},{3,7},{4,0},{5,1},{6,2},{7,3},{8,12},{9,13},{10,... | collective-permute-start | bytes 3538952 | tf_op jit(solution)/shard_map/ppermute | solution.py:741
  104.0 28.0 %collective-permute-start.21 = (bf16[768,768]{1,0:T(8,128)(2,1)}, bf16[768,768]{1,0:T(8,128)(2,1)}, u32[]{:S(2)}, u32[]{:S(2)}) collective-permute-start(bf16[768,768]{1,0:T(8,128)(2,1)} %pad_maximum_fusion.3), channel_id=1, source_target_pairs={{0,2},{1,3},{2,0},{3,1},{4,6},{5,7},{6,4},{7,5},{8,10},{9,11},{10,... | collective-permute-start | bytes 3538952 | tf_op jit(solution)/shard_map/ppermute | solution.py:741
  118.4 15.8 %collective-permute-start.24 = (bf16[96,768]{1,0:T(8,128)(2,1)S(1)}, bf16[96,768]{1,0:T(8,128)(2,1)S(1)}, u32[]{:S(2)}, u32[]{:S(2)}) collective-permute-start(bf16[96,768]{1,0:T(8,128)(2,1)S(1)} %bitcast.383), channel_id=1, source_target_pairs={{0,16},{1,17},{2,18},{3,19},{4,20},{5,21},{6,22},{7,23},{8,24},{9,... | collective-permute-start | bytes 442376 | tf_op jit(solution)/shard_map/ppermute | solution.py:741
  119.0 15.1 %collective-permute-start.23 = (bf16[192,768]{1,0:T(8,128)(2,1)S(1)}, bf16[192,768]{1,0:T(8,128)(2,1)S(1)}, u32[]{:S(2)}, u32[]{:S(2)}) collective-permute-start(bf16[192,768]{1,0:T(8,128)(2,1)S(1)} %bitcast.440), channel_id=1, source_target_pairs={{0,8},{1,9},{2,10},{3,11},{4,12},{5,13},{6,14},{7,15},{8,0},{9,1},... | collective-permute-start | bytes 884744 | tf_op jit(solution)/shard_map/ppermute | solution.py:741
  138.8 33.5 %collective-permute-start.28 = (bf16[960,768]{1,0:T(8,128)(2,1)}, bf16[960,768]{1,0:T(8,128)(2,1)}, u32[]{:S(2)}, u32[]{:S(2)}) collective-permute-start(bf16[960,768]{1,0:T(8,128)(2,1)} %pad_maximum_fusion.1), channel_id=1, source_target_pairs={{0,4},{1,5},{2,6},{3,7},{4,0},{5,1},{6,2},{7,3},{8,12},{9,13},{10,... | collective-permute-start | bytes 4423688 | tf_op jit(solution)/shard_map/ppermute | solution.py:741
  141.3 34.3 %collective-permute-start.27 = (bf16[960,768]{1,0:T(8,128)(2,1)}, bf16[960,768]{1,0:T(8,128)(2,1)S(1)}, u32[]{:S(2)}, u32[]{:S(2)}) collective-permute-start(bf16[960,768]{1,0:T(8,128)(2,1)} %pad_maximum_fusion), channel_id=1, source_target_pairs={{0,2},{1,3},{2,0},{3,1},{4,6},{5,7},{6,4},{7,5},{8,10},{9,11},{10,... | collective-permute-start | bytes 4423688 | tf_op jit(solution)/shard_map/ppermute | solution.py:741
  147.2 11.4 %collective-permute-start.32 = (bf16[768,384]{1,0:T(8,128)(2,1)}, bf16[768,384]{1,0:T(8,128)(2,1)S(1)}, u32[]{:S(2)}, u32[]{:S(2)}) collective-permute-start(bf16[768,384]{1,0:T(8,128)(2,1)} %bitcast.424), channel_id=1, source_target_pairs={{0,1},{1,0},{2,3},{3,2},{4,5},{5,4},{6,7},{7,6},{8,9},{9,8},{10,11... | collective-permute-start | bytes 1769480 | tf_op jit(solution)/shard_map/ppermute | solution.py:741
  147.7 29.5 %collective-permute-start.26 = (bf16[384,768]{1,0:T(8,128)(2,1)S(1)}, bf16[384,768]{1,0:T(8,128)(2,1)}, u32[]{:S(2)}, u32[]{:S(2)}) collective-permute-start(bf16[384,768]{1,0:T(8,128)(2,1)S(1)} %bitcast.379), channel_id=1, source_target_pairs={{0,16},{1,17},{2,18},{3,19},{4,20},{5,21},{6,22},{7,23},{8,24},{9,... | collective-permute-start | bytes 1769480 | tf_op jit(solution)/shard_map/ppermute | solution.py:741
  149.7 27.4 %collective-permute-start.29 = (bf16[192,768]{1,0:T(8,128)(2,1)}, bf16[192,768]{1,0:T(8,128)(2,1)S(1)}, u32[]{:S(2)}, u32[]{:S(2)}) collective-permute-start(bf16[192,768]{1,0:T(8,128)(2,1)} %bitcast.143), channel_id=1, source_target_pairs={{0,8},{1,9},{2,10},{3,11},{4,12},{5,13},{6,14},{7,15},{8,0},{9,1},... | collective-permute-start | bytes 884744 | tf_op jit(solution)/shard_map/ppermute | solution.py:741
  180.0 30.1 %collective-permute-start.33 = (bf16[768,768]{1,0:T(8,128)(2,1)S(1)}, bf16[768,768]{1,0:T(8,128)(2,1)S(1)}, u32[]{:S(2)}, u32[]{:S(2)}) collective-permute-start(bf16[768,768]{1,0:T(8,128)(2,1)S(1)} %bitcast.361), channel_id=1, source_target_pairs={{0,8},{1,9},{2,10},{3,11},{4,12},{5,13},{6,14},{7,15},{8,0},{9,1},... | collective-permute-start | bytes 3538952 | tf_op jit(solution)/shard_map/ppermute | solution.py:741
  181.7 22.6 %collective-permute-start.35 = (bf16[576,768]{1,0:T(8,128)(2,1)}, bf16[576,768]{1,0:T(8,128)(2,1)}, u32[]{:S(2)}, u32[]{:S(2)}) collective-permute-start(bf16[576,768]{1,0:T(8,128)(2,1)} %pad_maximum_fusion.11), channel_id=1, source_target_pairs={{0,4},{1,5},{2,6},{3,7},{4,0},{5,1},{6,2},{7,3},{8,12},{9,13},{10,... | collective-permute-start | bytes 2654216 | tf_op jit(solution)/shard_map/ppermute | solution.py:741
  183.9 23.4 %collective-permute-start.34 = (bf16[576,768]{1,0:T(8,128)(2,1)}, bf16[576,768]{1,0:T(8,128)(2,1)}, u32[]{:S(2)}, u32[]{:S(2)}) collective-permute-start(bf16[576,768]{1,0:T(8,128)(2,1)} %pad_maximum_fusion.10), channel_id=1, source_target_pairs={{0,2},{1,3},{2,0},{3,1},{4,6},{5,7},{6,4},{7,5},{8,10},{9,11},{10,... | collective-permute-start | bytes 2654216 | tf_op jit(solution)/shard_map/ppermute | solution.py:741
  215.1 15.6 %collective-permute-start.42 = (bf16[768,384]{1,0:T(8,128)(2,1)}, bf16[768,384]{1,0:T(8,128)(2,1)S(1)}, u32[]{:S(2)}, u32[]{:S(2)}) collective-permute-start(bf16[768,384]{1,0:T(8,128)(2,1)} %bitcast.427), channel_id=1, source_target_pairs={{0,1},{1,0},{2,3},{3,2},{4,5},{5,4},{6,7},{7,6},{8,9},{9,8},{10,11... | collective-permute-start | bytes 1769480 | tf_op jit(solution)/shard_map/ppermute | solution.py:741
  215.4 20.1 %collective-permute-start.39 = (bf16[384,768]{1,0:T(8,128)(2,1)S(1)}, bf16[384,768]{1,0:T(8,128)(2,1)S(1)}, u32[]{:S(2)}, u32[]{:S(2)}) collective-permute-start(bf16[384,768]{1,0:T(8,128)(2,1)S(1)} %bitcast.367), channel_id=1, source_target_pairs={{0,4},{1,5},{2,6},{3,7},{4,0},{5,1},{6,2},{7,3},{8,12},{9,13},{10,... | collective-permute-start | bytes 1769480 | tf_op jit(solution)/shard_map/ppermute | solution.py:741
  216.2 19.3 %collective-permute-start.38 = (bf16[384,768]{1,0:T(8,128)(2,1)S(1)}, bf16[384,768]{1,0:T(8,128)(2,1)S(1)}, u32[]{:S(2)}, u32[]{:S(2)}) collective-permute-start(bf16[384,768]{1,0:T(8,128)(2,1)S(1)} %bitcast.365), channel_id=1, source_target_pairs={{0,2},{1,3},{2,0},{3,1},{4,6},{5,7},{6,4},{7,5},{8,10},{9,11},{10,... | collective-permute-start | bytes 1769480 | tf_op jit(solution)/shard_map/ppermute | solution.py:741
  278.1 32.7 %collective-permute-start.48 = (bf16[896,768]{1,0:T(8,128)(2,1)}, bf16[896,768]{1,0:T(8,128)(2,1)S(1)}, u32[]{:S(2)}, u32[]{:S(2)}) collective-permute-start(bf16[896,768]{1,0:T(8,128)(2,1)} %get-tuple-element.548), channel_id=1, source_target_pairs={{0,2},{1,3},{2,0},{3,1},{4,6},{5,7},{6,4},{7,5},{8,10},{9,11},{10,... | collective-permute-start | bytes 4128776 | tf_op jit(solution)/shard_map/ppermute | solution.py:741
  282.3 28.4 %collective-permute-start.47 = (bf16[768,768]{1,0:T(8,128)(2,1)}, bf16[768,768]{1,0:T(8,128)(2,1)S(1)}, u32[]{:S(2)}, u32[]{:S(2)}) collective-permute-start(bf16[768,768]{1,0:T(8,128)(2,1)} %get-tuple-element.547), channel_id=1, source_target_pairs={{0,4},{1,5},{2,6},{3,7},{4,0},{5,1},{6,2},{7,3},{8,12},{9,13},{10,... | collective-permute-start | bytes 3538952 | tf_op jit(solution)/shard_map/ppermute | solution.py:741
  321.1 28.6 %collective-permute-start.52 = (bf16[768,768]{1,0:T(8,128)(2,1)}, bf16[768,768]{1,0:T(8,128)(2,1)S(1)}, u32[]{:S(2)}, u32[]{:S(2)}) collective-permute-start(bf16[768,768]{1,0:T(8,128)(2,1)} %get-tuple-element.573), channel_id=1, source_target_pairs={{0,4},{1,5},{2,6},{3,7},{4,0},{5,1},{6,2},{7,3},{8,12},{9,13},{10,... | collective-permute-start | bytes 3538952 | tf_op jit(solution)/shard_map/ppermute | solution.py:741
  321.9 28.3 %collective-permute-start.53 = (bf16[768,768]{1,0:T(8,128)(2,1)}, bf16[768,768]{1,0:T(8,128)(2,1)S(1)}, u32[]{:S(2)}, u32[]{:S(2)}) collective-permute-start(bf16[768,768]{1,0:T(8,128)(2,1)} %get-tuple-element.574), channel_id=1, source_target_pairs={{0,2},{1,3},{2,0},{3,1},{4,6},{5,7},{6,4},{7,5},{8,10},{9,11},{10,... | collective-permute-start | bytes 3538952 | tf_op jit(solution)/shard_map/ppermute | solution.py:741
  357.4 34.1 %collective-permute-start.57 = (bf16[960,768]{1,0:T(8,128)(2,1)}, bf16[960,768]{1,0:T(8,128)(2,1)S(1)}, u32[]{:S(2)}, u32[]{:S(2)}) collective-permute-start(bf16[960,768]{1,0:T(8,128)(2,1)} %get-tuple-element.601), channel_id=1, source_target_pairs={{0,4},{1,5},{2,6},{3,7},{4,0},{5,1},{6,2},{7,3},{8,12},{9,13},{10,... | collective-permute-start | bytes 4423688 | tf_op jit(solution)/shard_map/ppermute | solution.py:741
  358.7 33.6 %collective-permute-start.58 = (bf16[960,768]{1,0:T(8,128)(2,1)}, bf16[960,768]{1,0:T(8,128)(2,1)}, u32[]{:S(2)}, u32[]{:S(2)}) collective-permute-start(bf16[960,768]{1,0:T(8,128)(2,1)} %get-tuple-element.602), channel_id=1, source_target_pairs={{0,2},{1,3},{2,0},{3,1},{4,6},{5,7},{6,4},{7,5},{8,10},{9,11},{10,... | collective-permute-start | bytes 4423688 | tf_op jit(solution)/shard_map/ppermute | solution.py:741
  363.4 23.9 %collective-permute-start.56 = (bf16[384,768]{1,0:T(8,128)(2,1)S(1)}, bf16[384,768]{1,0:T(8,128)(2,1)S(1)}, u32[]{:S(2)}, u32[]{:S(2)}) collective-permute-start(bf16[384,768]{1,0:T(8,128)(2,1)S(1)} %copy-done.85), channel_id=1, source_target_pairs={{0,8},{1,9},{2,10},{3,11},{4,12},{5,13},{6,14},{7,15},{8,0},{9,1},... | collective-permute-start | bytes 1769480 | tf_op jit(solution)/shard_map/ppermute | solution.py:741
  399.1 27.0 %collective-permute-start.64 = (bf16[768,768]{1,0:T(8,128)(2,1)}, bf16[768,768]{1,0:T(8,128)(2,1)S(1)}, u32[]{:S(2)}, u32[]{:S(2)}) collective-permute-start(bf16[768,768]{1,0:T(8,128)(2,1)} %get-tuple-element.640), channel_id=1, source_target_pairs={{0,4},{1,5},{2,6},{3,7},{4,0},{5,1},{6,2},{7,3},{8,12},{9,13},{10,... | collective-permute-start | bytes 3538952 | tf_op jit(solution)/shard_map/ppermute | solution.py:741
  400.2 26.5 %collective-permute-start.65 = (bf16[768,768]{1,0:T(8,128)(2,1)}, bf16[768,768]{1,0:T(8,128)(2,1)}, u32[]{:S(2)}, u32[]{:S(2)}) collective-permute-start(bf16[768,768]{1,0:T(8,128)(2,1)} %get-tuple-element.641), channel_id=1, source_target_pairs={{0,2},{1,3},{2,0},{3,1},{4,6},{5,7},{6,4},{7,5},{8,10},{9,11},{10,... | collective-permute-start | bytes 3538952 | tf_op jit(solution)/shard_map/ppermute | solution.py:741
  405.2 16.8 %collective-permute-start.62 = (bf16[192,768]{1,0:T(8,128)(2,1)}, bf16[192,768]{1,0:T(8,128)(2,1)S(1)}, u32[]{:S(2)}, u32[]{:S(2)}) collective-permute-start(bf16[192,768]{1,0:T(8,128)(2,1)} %get-tuple-element.638), channel_id=1, source_target_pairs={{0,16},{1,17},{2,18},{3,19},{4,20},{5,21},{6,22},{7,23},{8,24},{9,... | collective-permute-start | bytes 884744 | tf_op jit(solution)/shard_map/ppermute | solution.py:741
  406.9 15.1 %collective-permute-start.63 = (bf16[192,768]{1,0:T(8,128)(2,1)}, bf16[192,768]{1,0:T(8,128)(2,1)S(1)}, u32[]{:S(2)}, u32[]{:S(2)}) collective-permute-start(bf16[192,768]{1,0:T(8,128)(2,1)} %get-tuple-element.639), channel_id=1, source_target_pairs={{0,8},{1,9},{2,10},{3,11},{4,12},{5,13},{6,14},{7,15},{8,0},{9,1},... | collective-permute-start | bytes 884744 | tf_op jit(solution)/shard_map/ppermute | solution.py:741
  433.5 28.3 %collective-permute-start.70 = (bf16[832,768]{1,0:T(8,128)(2,1)}, bf16[832,768]{1,0:T(8,128)(2,1)S(1)}, u32[]{:S(2)}, u32[]{:S(2)}) collective-permute-start(bf16[832,768]{1,0:T(8,128)(2,1)} %get-tuple-element.670), channel_id=1, source_target_pairs={{0,2},{1,3},{2,0},{3,1},{4,6},{5,7},{6,4},{7,5},{8,10},{9,11},{10,... | collective-permute-start | bytes 3833864 | tf_op jit(solution)/shard_map/ppermute | solution.py:741
  435.7 23.9 %collective-permute-start.69 = (bf16[704,768]{1,0:T(8,128)(2,1)}, bf16[704,768]{1,0:T(8,128)(2,1)}, u32[]{:S(2)}, u32[]{:S(2)}) collective-permute-start(bf16[704,768]{1,0:T(8,128)(2,1)} %get-tuple-element.669), channel_id=1, source_target_pairs={{0,4},{1,5},{2,6},{3,7},{4,0},{5,1},{6,2},{7,3},{8,12},{9,13},{10,... | collective-permute-start | bytes 3244040 | tf_op jit(solution)/shard_map/ppermute | solution.py:741
  437.6 16.1 %collective-permute-start.68 = (bf16[384,768]{1,0:T(8,128)(2,1)}, bf16[384,768]{1,0:T(8,128)(2,1)S(1)}, u32[]{:S(2)}, u32[]{:S(2)}) collective-permute-start(bf16[384,768]{1,0:T(8,128)(2,1)} %get-tuple-element.668), channel_id=1, source_target_pairs={{0,8},{1,9},{2,10},{3,11},{4,12},{5,13},{6,14},{7,15},{8,0},{9,1},... | collective-permute-start | bytes 1769480 | tf_op jit(solution)/shard_map/ppermute | solution.py:741
  467.7 13.6 %collective-permute-start.71 = (bf16[192,768]{1,0:T(8,128)(2,1)}, bf16[192,768]{1,0:T(8,128)(2,1)S(1)}, u32[]{:S(2)}, u32[]{:S(2)}) collective-permute-start(bf16[192,768]{1,0:T(8,128)(2,1)} %get-tuple-element.688), channel_id=1, source_target_pairs={{0,16},{1,17},{2,18},{3,19},{4,20},{5,21},{6,22},{7,23},{8,24},{9,... | collective-permute-start | bytes 884744 | tf_op jit(solution)/shard_map/ppermute | solution.py:741
  469.9 11.4 %collective-permute-start.72 = (bf16[192,768]{1,0:T(8,128)(2,1)}, bf16[192,768]{1,0:T(8,128)(2,1)}, u32[]{:S(2)}, u32[]{:S(2)}) collective-permute-start(bf16[192,768]{1,0:T(8,128)(2,1)} %get-tuple-element.689), channel_id=1, source_target_pairs={{0,8},{1,9},{2,10},{3,11},{4,12},{5,13},{6,14},{7,15},{8,0},{9,1},... | collective-permute-start | bytes 884744 | tf_op jit(solution)/shard_map/ppermute | solution.py:741
  476.2 11.9 %all-to-all-start.1 = ((f32[32,1,576]{2,1,0:T(1,128)}), f32[32,1,576]{2,1,0:T(1,128)S(1)}, u32[]{:S(2)}, u32[]{:S(2)}) async-start(f32[32,1,576]{2,1,0:T(1,128)} %copy.83), calls=%async_computation.1 | async-start | bytes 163840 | tf_op jit(solution)/shard_map/all_to_all | solution.py:1561
  485.9 13.0 %collective-permute-start.76 = (bf16[256,768]{1,0:T(8,128)(2,1)}, bf16[256,768]{1,0:T(8,128)(2,1)S(1)}, u32[]{:S(2)}, u32[]{:S(2)}) collective-permute-start(bf16[256,768]{1,0:T(8,128)(2,1)} %get-tuple-element.709), channel_id=1, source_target_pairs={{0,8},{1,9},{2,10},{3,11},{4,12},{5,13},{6,14},{7,15},{8,0},{9,1},... | collective-permute-start | bytes 1179656 | tf_op jit(solution)/shard_map/ppermute | solution.py:741
  492.2 16.9 %collective-permute-start.79 = (f32[24,3072]{1,0:T(8,128)}, f32[24,3072]{1,0:T(8,128)S(1)}, u32[]{:S(2)}, u32[]{:S(2)}) collective-permute-start(f32[24,3072]{1,0:T(8,128)} %get-tuple-element.732), channel_id=1, source_target_pairs={{0,1},{1,0},{2,3},{3,2},{4,5},{5,4},{6,7},{7,6},{8,9},{9,8},{10,11... | collective-permute-start | bytes 884744 | tf_op jit(solution)/shard_map/ppermute | solution.py:741
  506.5 12.4 %collective-permute-start.77 = (bf16[128,768]{1,0:T(8,128)(2,1)S(1)}, bf16[128,768]{1,0:T(8,128)(2,1)S(1)}, u32[]{:S(2)}, u32[]{:S(2)}) collective-permute-start(bf16[128,768]{1,0:T(8,128)(2,1)S(1)} %copy-done.91), channel_id=1, source_target_pairs={{0,16},{1,17},{2,18},{3,19},{4,20},{5,21},{6,22},{7,23},{8,24},{9,... | collective-permute-start | bytes 589832 | tf_op jit(solution)/shard_map/ppermute | solution.py:741
  (135 other events, 692.3 us)

commit v4 on v3

--- a/solution.py
+++ b/solution.py
@@ -21,7 +21,7 @@
 EPS = 1e-12
 DEAD = -1000000000.0
 SCALE = HEAD_DIM ** (-0.5)
-VMEM = 60 * 1024 * 1024
+VMEM = 52 * 1024 * 1024
 F32 = jnp.float32
 BF16 = jnp.bfloat16
 
@@ -189,7 +189,7 @@
 
 def attn_bwd_kernel(
     core, dao, das, wom, wot, q, k, v, mo, ms, xo, xs, wq, wk, wv, mask,
-    dwq, dwk, dwv, dwo, sums, dxo, dxs, acc, all_s, turned,
+    dwq, dwk, dwv, dwo, dwo_sent, sums, dxo, dxs, acc, all_s, turned,
 ):
     half = xo.shape[0]
     step = pl.program_id(0)
@@ -240,8 +240,9 @@
     for part, out in enumerate((dwq, dwk, dwv)):
         out[...] = weight_grads[:, part * LANES : (part + 1) * LANES]
     out_rows = dot(mo[...], dao[...], TN) + dot(ms[...], das[...], TN)
-    dwo[0] = out_rows[:, :HALF].astype(BF16)
-    dwo[1] = out_rows[:, HALF:].astype(BF16)
+    even = core[0] == 0
+    dwo[...] = jnp.where(even, out_rows[:, :HALF], out_rows[:, HALF:]).astype(BF16)
+    dwo_sent[...] = jnp.where(even, out_rows[:, HALF:], out_rows[:, :HALF]).astype(BF16)
     total = dot(all_s[...], jnp.concatenate([wq[...], wk[...], wv[...]], axis=1), NT)
 
     @pl.when(step == 0)
@@ -271,7 +272,8 @@
         name="attn_bwd",
         out_shape=[sds((D, HALF), BF16)] * 3
         + [
-            sds((CORES, HALF, HALF), BF16),
+            sds((HALF, HALF), BF16),
+            sds((HALF, HALF), BF16),
             sds((8, HALF), F32),
             sds((half, D), F32),
             sds((half, D), BF16),
@@ -298,7 +300,8 @@
             ],
             out_specs=[weight] * 3
             + [
-                pl.BlockSpec((CORES, LANES, HALF), lambda p, core: (0, p, 0)),
+                pl.BlockSpec((LANES, HALF), lambda p, core: (p, 0)),
+                pl.BlockSpec((LANES, HALF), lambda p, core: (p, 0)),
                 pl.BlockSpec((8, LANES), col),
                 whole((half, D)),
                 whole((half, D)),
@@ -1035,9 +1038,9 @@
 
 
 class Stream:
-    def __init__(self, parts, first_y, rows, base=0):
+    def __init__(self, parts, first_y, rows, base=0, direct=False):
         self.parts, self.first_y, self.rows, self.base = parts, first_y, rows, base
-        self.age = 0
+        self.age, self.direct, self.last = 0, direct, False
         self.keep = self.recv = self.total = self.joined = None
 
 
@@ -1056,7 +1059,6 @@
     def __init__(self, at):
         self.at, self.groups = at, []
         self.bits = at.nz.bit_length() - 1
-        self.last = 2 + self.bits
         scalars = [at.x, at.y] + [at.z // (1 << bit) % 2 for bit in range(self.bits)]
         self.scalars = jnp.stack(scalars).astype(jnp.int32)
 
@@ -1088,42 +1090,61 @@
                     coords[first], coords[1 - first] = other, (far, 0)
                     sent.append([(stream.parts, chip(z, coords))])
         elif stream.age == 1:
-            ref, base = stream.recv
+            ((ref, base),) = stream.recv
             for out, side in ((sent, other), (kept, same)):
                 for z in range(nz):
                     coords = [None, None]
                     coords[first], coords[1 - first] = same, side
                     place = spot(2 * z + side[0], 1 - first, side[1], rows, base)
                     out.append([(stream.parts, chip(z, coords)), ([ref], place)])
-        elif stream.age < self.last:
+        elif stream.direct and stream.age == 2:
+            ((ref, base),) = stream.recv
+            for flip in range(nz):
+                start, slopes = 0, []
+                for bit in range(self.bits):
+                    fixed, slope = other if flip >> bit & 1 else same
+                    start += (fixed << bit) * rows
+                    slopes.append((2 + bit, (slope << bit) * rows))
+                out = sent if flip else kept
+                out.append([([stream.keep], (start, slopes)), ([ref], (base + start, slopes))])
+        elif not self.final(stream):
             bit = stream.age - 2
-            ref, base = stream.recv
+            ((ref, base),) = stream.recv
             for out, side in ((sent, other), (kept, same)):
                 for high in range(nz >> (bit + 1)):
                     fixed = 2 * high + side[0]
                     keep = spot(fixed, 2 + bit, side[1], rows)
                     out.append([([stream.keep], keep), ([ref], spot(fixed, 2 + bit, side[1], rows, base))])
         else:
-            ref, base = stream.recv
-            kept.append([([stream.keep], (0, [])), ([ref], (base, []))])
+            kept.append([([stream.keep], (0, []))] + [([ref], (base, [])) for ref, base in stream.recv])
         return sent, kept
+
+    def final(self, stream):
+        return stream.age == (3 if stream.direct else 2 + self.bits)
 
     def step(self, *others, extra=None):
         heights, keeps, todo, self.sent = {}, [], [], []
         spots, self.joined = [], None
         for streams in self.groups:
             for stream in streams:
-                if stream.age > self.last:
+                if stream.last:
                     continue
                 rows = stream.rows
                 sent, kept = self.pieces(stream, rows)
                 axis = (2, 1) if stream.first_y else (1, 2)
-                key = axis[stream.age] if stream.age < 2 else -stream.age
-                start = heights.get(key, 0)
-                if sent:
-                    heights[key] = start + len(sent) * rows
+                blocks, spans = [], []
+                if stream.age < 2:
+                    spans = [(axis[stream.age], len(sent))]
+                elif sent:
+                    spans = [(-flip, 1) for flip in range(1, len(sent) + 1)]
+                    if not stream.direct:
+                        spans = [(-(1 << (stream.age - 2)), len(sent))]
+                for key, many in spans:
+                    start = heights.get(key, 0)
+                    heights[key] = start + many * rows
                     self.sent.append((stream, key, start))
-                todo.append((stream, key, start, sent, kept, rows))
+                    blocks += [(key, start + block * rows) for block in range(many)]
+                todo.append((stream, blocks, sent, kept, rows))
         if extra is not None:
             span = (heights.get(2, 0), extra.shape[0])
             heights[2] = sum(span)
@@ -1139,9 +1160,9 @@
             arrays.append(array)
             return len(arrays) - 1
 
-        for stream, key, start, sent, kept, rows in todo:
+        for stream, blocks, sent, kept, rows in todo:
             if kept:
-                last = stream.age == self.last
+                last = self.final(stream)
                 if last and stream.joined is not None:
                     if stream.joined.out is None:
                         stream.joined.out = len(shapes)
@@ -1179,10 +1200,9 @@
                 loads.append((source(part), place, height, spare, row, number * width, width))
             return spare, (row, []), numbers
 
-        for stream, key, start, sent, kept, rows in todo:
-            for block, terms in enumerate(sent):
+        for stream, blocks, sent, kept, rows in todo:
+            for (key, to), terms in zip(blocks, sent):
                 out = order.index(key)
-                to = start + block * rows
                 if len(terms) == 1:
                     ((parts, place),) = terms
                     for number, part in enumerate(parts):
@@ -1192,7 +1212,7 @@
                 else:
                     jobs[out][1].append((to, rows, [term(parts, place, rows) for parts, place in terms]))
         spots = iter(spots)
-        for stream, key, start, sent, kept, rows in todo:
+        for stream, blocks, sent, kept, rows in todo:
             if kept:
                 out, first = next(spots)
                 for block, terms in enumerate(kept):
@@ -1217,9 +1237,10 @@
             self.joined.total = outs[self.joined.out]
         for stream, out in keeps:
             stream.keep = outs[out]
-            if stream.age == self.last:
+            if self.final(stream):
                 stream.total = outs[out]
         for stream, *_ in todo:
+            stream.last = self.final(stream)
             stream.age += 1
         payloads, others = lax.optimization_barrier((outs[: len(order)], others))
         self.moved = {}
@@ -1228,19 +1249,21 @@
             if key > 0:
                 self.moved[key] = self.at.move(payload, key, 1)
             else:
-                self.moved[key] = self.at.move(payload, 0, 1 << (-key - 2), flip=True)
+                self.moved[key] = self.at.move(payload, 0, -key, flip=True)
         return others
 
     def close(self, *others):
         self.moved, others = lax.optimization_barrier((self.moved, others))
         for stream, key, start in self.sent:
-            stream.recv = (self.moved[key], start)
+            stream.recv = []
+        for stream, key, start in self.sent:
+            stream.recv.append((self.moved[key], start))
         if self.span is not None:
             self.extra = [self.moved[2][self.span[0] : sum(self.span)]]
         return others
 
     def busy(self):
-        return any(stream.age <= self.last for streams in self.groups for stream in streams)
+        return not all(stream.last for streams in self.groups for stream in streams)
 
 
 def pick(stacked, index, axis=0):
@@ -1475,11 +1498,11 @@
         wa, wom, wot = weights[layer][:3]
         x_low, x_other, q, k, v, mix_own, mix_other, n1, r1 = saved[layer][:9]
         gh1, da, sums1 = norm_bwd(sources, n1, r1, small, 2 * layer)
-        dwq, dwk, dwv, dwo, attn_sums, part, part_other = attn_bwd(
+        dwq, dwk, dwv, dwo, dwo_sent, attn_sums, part, part_other = attn_bwd(
             core_id, da, at.swap(da), wom, wot, q, k, v, mix_own, mix_other, x_low, x_other, wa, mask
         )
         small_grads[layer] = [sums1] + small_grads[layer] + [attn_sums]
-        return (gh1, part, at.swap(part_other)), (dwq, dwk, dwv), (pick(dwo, core), at.swap(pick(dwo, 1 - core)))
+        return (gh1, part, at.swap(part_other)), (dwq, dwk, dwv), (dwo, at.swap(dwo_sent))
 
     def attn_groups(dqkv, dwo):
         dwq, dwk, dwv = dqkv
@@ -1497,10 +1520,12 @@
         line.add(chunk)
         return chunk
 
-    def attn_chunk(dqkv, dwo):
+    def attn_chunk(dqkv, dwo, direct):
         first, second = attn_groups(dqkv, dwo)
         if tiled:
-            streams = [Stream(first, True, chip_rows), Stream(second, False, chip_rows)]
+            streams = [
+                Stream(part, part is first, chip_rows, direct=direct) for part in (first, second)
+            ]
             line.add(streams)
             return streams
         chunk = Reduce(at, [first], [second])
@@ -1523,7 +1548,7 @@
     sources, dqkv, dwo = backward_attn(1, sources)
     sources = line.close(*sources)
     output = from_chip(output, line.extra if tiled else send_back(output))
-    att1 = attn_chunk(dqkv, dwo)
+    att1 = attn_chunk(dqkv, dwo, False)
     sources = line.step(*sources)
     sources, dw1, dw2 = backward_ffn(0, sources)
     sources = line.close(*sources)
@@ -1531,7 +1556,7 @@
     sources = line.step(*sources)
     sources, dqkv, dwo = backward_attn(0, sources)
     sources = line.close(*sources)
-    att0 = attn_chunk(dqkv, dwo)
+    att0 = attn_chunk(dqkv, dwo, False)
     sources = line.step(*sources)
     grad_x = sources[0] + sources[1] + sources[2].astype(F32)
     grad_low = grad_x.astype(BF16)

time: 529 us -> 515 us (0.974)
  waiting for transfers between devices: 125 us -> 150 us
  Pallas kernels: 207 us -> 184 us
  local copies, waits for them, and re-layouts: 79.6 us -> 60 us
  starting transfers between devices: 77.7 us -> 85.5 us
    ppermute x80, waiting for transfers between devices: 113 us -> 139 us  [move(): return lax.ppermute(value, ('page', 'band'), pairs)]
    ppermute x80, starting transfers between devices: 70.4 us -> 79 us  [move(): return lax.ppermute(value, ('page', 'band'), pairs)]
    slice x15, local copies, waits for them, and re-layouts: 20.8 us -> 15.3 us  [exchange(): got[i] = moved[first:first + part.shape[0]].reshape(wants[i][2].shape)]
    unnamed x204 -> x220, local copies, waits for them, and re-layouts: 25.2 us -> 25.3 us
  transfers between devices with their start and end apart: 82 -> 82, of which waited for: 41 -> 43; matrix products, arithmetic and copies ran while one was open for 14% -> 10% of each run, Pallas kernels for 28% -> 24%
where the time goes in v4:
time: 515 us; the launch traced here: 510 us
  Pallas kernels  184 us (36%)
  waiting for transfers between devices  150 us (29%)
  starting transfers between devices  85.5 us (17%)
  local copies, waits for them, and re-layouts  60 us (12%)
  other arithmetic  28.4 us (6%)
    ppermute x80, waiting for transfers between devices, move(): return lax.ppermute(value, ('page', 'band'), pairs)  139 us
    ppermute x80, starting transfers between devices, move(): return lax.ppermute(value, ('page', 'band'), pairs)  79 us
    pallas_call x9, Pallas kernels, step(): pl.pallas_call(functools.partial(blocks_kernel, counts=(len(arrays), len(...  45.1 us
    pallas_call x2, Pallas kernels, attn_bwd(): pl.pallas_call(attn_bwd_kernel, name='attn_bwd', out_shape=[sds((D, HALF)...  34 us
    unnamed x220, local copies, waits for them, and re-layouts  25.3 us
    pallas_call x2, Pallas kernels, ffn_bwd(): pl.pallas_call(ffn_bwd_kernel, name='ffn_bwd', out_shape=[sds((2, D, D),...  22.7 us
    pallas_call x6, Pallas kernels, shuffle(): pl.pallas_call(functools.partial(shuffle_kernel, moves=moves, count=len(s...  19.8 us
    pallas_call x2, Pallas kernels, attn_fwd(): pl.pallas_call(functools.partial(attn_fwd_kernel, layer=layer), name='att...  15.6 us
  transfers between devices with their start and end apart: 82, of which 43 were waited for; matrix products, arithmetic and copies ran while one was open for 10% of the time, Pallas kernels for 24%

profile of v4, /device:TPU:0, one launch (start us, length us, event | category | flops | bytes accessed | tf_op | source)
XLA Modules:
  0.0 509.6 jit_solution(10645166548556279132)
XLA Ops:
  1.7 4.1 collective-permute-start
  25.2 4.5 collective-permute-done.10
  31.9 5.1 %collective-permute-done.7 = bf16[96,768]{1,0:T(8,128)(2,1)S(1)} collective-permute-done((bf16[96,768]{1,0:T(8,128)(2,1)S(1)}, bf16[96,768]{1,0:T(8,128)(2,1)S(1)}, u32[]{:S(2)}, u32[]{:S(2)}) %collective-permute-start.7) | collective-permute-done | bytes 147488 | tf_op jit(solution)/shard_map/ppermute | solution.py:744
  47.2 7.2 %collective-permute-done.15 = bf16[192,768]{1,0:T(8,128)(2,1)S(1)} collective-permute-done((bf16[192,768]{1,0:T(8,128)(2,1)S(1)}, bf16[192,768]{1,0:T(8,128)(2,1)S(1)}, u32[]{:S(2)}, u32[]{:S(2)}) %collective-permute-start.15) | collective-permute-done | bytes 294944 | tf_op jit(solution)/shard_map/ppermute | solution.py:744
  54.4 4.0 collective-permute-done.16
  67.6 3.9 all-to-all-start
  74.4 11.2 %all-to-all-done = bf16[32,2,288]{2,1,0:T(2,128)(2,1)S(1)} async-done(((bf16[32,2,288]{2,1,0:T(2,128)(2,1)}), bf16[32,2,288]{2,1,0:T(2,128)(2,1)S(1)}, u32[]{:S(2)}, u32[]{:S(2)}) %all-to-all-start) | async-done | bytes 36896 | tf_op jit(solution)/shard_map/all_to_all | solution.py:1384
  98.6 3.3 shuffle.6
  101.9 5.1 embed.1
  109.3 3.4 collective-permute-start.24
  114.5 9.9 %collective-permute-done.22 = bf16[768,768]{1,0:T(8,128)(2,1)} collective-permute-done((bf16[768,768]{1,0:T(8,128)(2,1)}, bf16[768,768]{1,0:T(8,128)(2,1)}, u32[]{:S(2)}, u32[]{:S(2)}) %collective-permute-start.22) | collective-permute-done | bytes 1179680 | tf_op jit(solution)/shard_map/ppermute | solution.py:744
  135.7 3.0 shuffle.7
  139.2 3.4 collective-permute-start.26
  143.7 7.5 %attn_fwd.2 = (bf16[512,384]{1,0:T(8,128)(2,1)S(1)}, bf16[512,384]{1,0:T(8,128)(2,1)S(1)}, bf16[512,384]{1,0:T(8,128)(2,1)S(1)}, bf16[256,384]{1,0:T(8,128)(2,1)S(1)}, bf16[256,384]{1,0:T(8,128)(2,1)S(1)}) custom-call(s32[1]{0:T(128)} %bitcast.core, bf16[256,768]{1,0:T(8,128)(2,1)S(1)} %get-tuple-element.478.xo, bf16[256,768]{1,0:T(8,128)(2,1)} %copy-done.79, ...), custom_call_target="tpu_custom_call" | custom-call | flops 1711276032 | bytes 4128768 | tf_op jit(solution)/shard_map/attn_fwd/pallas_call | solution.py:163
  153.5 3.4 out_norm.2
  156.8 10.0 %collective-permute-done.28 = bf16[960,768]{1,0:T(8,128)(2,1)} collective-permute-done((bf16[960,768]{1,0:T(8,128)(2,1)}, bf16[960,768]{1,0:T(8,128)(2,1)}, u32[]{:S(2)}, u32[]{:S(2)}) %collective-permute-start.28) | collective-permute-done | bytes 1474592 | tf_op jit(solution)/shard_map/ppermute | solution.py:744
  177.7 4.5 shuffle.8
  182.2 7.6 %ffn_fwd.2 = (bf16[512,1536]{1,0:T(8,128)(2,1)}, bf16[512,1536]{1,0:T(8,128)(2,1)}, f32[256,768]{1,0:T(8,128)S(1)}, bf16[256,768]{1,0:T(8,128)(2,1)S(1)}) custom-call(bf16[256,768]{1,0:T(8,128)(2,1)S(1)} %get-tuple-element.502.yo, bf16[256,768]{1,0:T(8,128)(2,1)S(1)} %collective-permute-done.36.ys, bf16[768,3072]{1,0:T(8,128)(2,1)} %bitcast.344, ...), custom_call_target="tpu_custom_call" | custom-call | flops 2415919104 | bytes 7864320 | tf_op jit(solution)/shard_map/ffn_fwd/pallas_call | solution.py:470
  195.1 3.9 collective-permute-done.35
  201.4 3.3 shuffle.9
  206.6 8.1 %attn_fwd.3 = (bf16[512,384]{1,0:T(8,128)(2,1)S(1)}, bf16[512,384]{1,0:T(8,128)(2,1)S(1)}, bf16[512,384]{1,0:T(8,128)(2,1)S(1)}, bf16[256,384]{1,0:T(8,128)(2,1)S(1)}, bf16[256,384]{1,0:T(8,128)(2,1)}) custom-call(s32[1]{0:T(128)} %bitcast.core, bf16[256,768]{1,0:T(8,128)(2,1)S(1)} %get-tuple-element.516.xo, bf16[256,768]{1,0:T(8,128)(2,1)} %copy-done.80, ...), custom_call_target="tpu_custom_call" | custom-call | flops 1711276032 | bytes 4128768 | tf_op jit(solution)/shard_map/attn_fwd/pallas_call | solution.py:163
  218.9 2.9 shuffle.10
  221.8 3.6 out_norm.3
  228.9 7.7 %ffn_fwd.3 = (bf16[512,1536]{1,0:T(8,128)(2,1)}, bf16[512,1536]{1,0:T(8,128)(2,1)}, f32[256,768]{1,0:T(8,128)S(1)}, bf16[256,768]{1,0:T(8,128)(2,1)S(1)}) custom-call(bf16[256,768]{1,0:T(8,128)(2,1)S(1)} %get-tuple-element.528.yo, bf16[256,768]{1,0:T(8,128)(2,1)} %collective-permute-done.43.ys, bf16[768,1536]{1,0:T(8,128)(2,1)} %bitcast.389, ...), custom_call_target="tpu_custom_call" | custom-call | flops 2415919104 | bytes 7864320 | tf_op jit(solution)/shard_map/ffn_fwd/pallas_call | solution.py:470
  246.3 11.7 %ffn_bwd.2 = (bf16[2,768,768]{2,1,0:T(8,128)(2,1)}, bf16[2,768,768]{2,1,0:T(8,128)(2,1)}, f32[8,1536]{1,0:T(8,128)S(1)}, f32[256,768]{1,0:T(8,128)}, bf16[256,768]{1,0:T(8,128)(2,1)S(1)}) custom-call(bf16[256,768]{1,0:T(8,128)(2,1)S(1)} %get-tuple-element.539.dfo, bf16[256,768]{1,0:T(8,128)(2,1)S(1)} %collective-permute-done.45.dfs, ...), custom_call_target="tpu_custom_call" | custom-call | flops 4831838208 | bytes 12582912 | tf_op jit(solution)/shard_map/ffn_bwd/pallas_call | solution.py:528
  260.4 4.2 blocks.9
  273.4 17.1 %attn_bwd.2 = (bf16[768,384]{1,0:T(8,128)(2,1)}, bf16[768,384]{1,0:T(8,128)(2,1)}, bf16[768,384]{1,0:T(8,128)(2,1)}, bf16[384,384]{1,0:T(8,128)(2,1)S(1)}, bf16[...) custom-call(s32[1]{0:T(128)} %bitcast.core, ...), custom_call_target="tpu_custom_call" | custom-call | flops 3825205248 | bytes 9437184 | tf_op jit(solution)/shard_map/attn_bwd/pallas_call | solution.py:270
  294.4 3.0 collective-permute-done.48.refs_1_
  297.4 4.8 blocks.10
  309.3 11.0 %ffn_bwd.3 = (bf16[2,768,768]{2,1,0:T(8,128)(2,1)}, bf16[2,768,768]{2,1,0:T(8,128)(2,1)}, f32[8,1536]{1,0:T(8,128)S(1)}, f32[256,768]{1,0:T(8,128)}, bf16[256,768]{1,0:T(8,128)(2,1)S(1)}) custom-call(bf16[256,768]{1,0:T(8,128)(2,1)S(1)} %get-tuple-element.584.dfo, bf16[256,768]{1,0:T(8,128)(2,1)S(1)} %collective-permute-done.54.dfs, ...), custom_call_target="tpu_custom_call" | custom-call | flops 4831838208 | bytes 12582912 | tf_op jit(solution)/shard_map/ffn_bwd/pallas_call | solution.py:528
  322.2 12.4 %collective-permute-done.52.refs_1_ = bf16[768,768]{1,0:T(8,128)(2,1)S(1)} collective-permute-done((bf16[768,768]{1,0:T(8,128)(2,1)S(1)}, bf16[768,768]{1,0:T(8,128)(2,1)S(1)}, u32[]{:S(2)}, u32[]{:S(2)}) %collective-permute-start.52) | collective-permute-done | bytes 1179680 | tf_op jit(solution)/shard_map/ppermute | solution.py:744
  336.9 5.7 %blocks.11 = (bf16[384,768]{1,0:T(8,128)(2,1)}, bf16[960,768]{1,0:T(8,128)(2,1)}, bf16[960,768]{1,0:T(8,128)(2,1)}, bf16[96,768]{1,0:T(8,128)(2,1)S(1)}, bf16[96...) custom-call(s32[4]{0:T(128)S(1)} %pad_add_fusion.2.scalars, ...), custom_call_target="tpu_custom_call" | custom-call | bytes 15925248 | tf_op jit(solution)/shard_map/blocks/pallas_call | solution.py:1222
  351.2 16.9 %attn_bwd.3 = (bf16[768,384]{1,0:T(8,128)(2,1)}, bf16[768,384]{1,0:T(8,128)(2,1)}, bf16[768,384]{1,0:T(8,128)(2,1)}, bf16[384,384]{1,0:T(8,128)(2,1)S(1)}, bf16[...) custom-call(s32[1]{0:T(128)} %bitcast.core, ...), custom_call_target="tpu_custom_call" | custom-call | flops 3825205248 | bytes 9437184 | tf_op jit(solution)/shard_map/attn_bwd/pallas_call | solution.py:270
  370.7 7.3 %collective-permute-done.57.refs_6_ = bf16[960,768]{1,0:T(8,128)(2,1)S(1)} collective-permute-done((bf16[960,768]{1,0:T(8,128)(2,1)}, bf16[960,768]{1,0:T(8,128)(2,1)S(1)}, u32[]{:S(2)}, u32[]{:S(2)}) %collective-permute-start.57) | collective-permute-done | bytes 1474592 | tf_op jit(solution)/shard_map/ppermute | solution.py:744
  379.7 6.8 %blocks.12 = (bf16[192,768]{1,0:T(8,128)(2,1)S(1)}, bf16[192,768]{1,0:T(8,128)(2,1)S(1)}, bf16[768,768]{1,0:T(8,128)(2,1)}, bf16[768,768]{1,0:T(8,128)(2,1)}, bf...) custom-call(s32[4]{0:T(128)S(1)} %pad_add_fusion.2.scalars, ...), custom_call_target="tpu_custom_call" | custom-call | bytes 17694720 | tf_op jit(solution)/shard_map/blocks/pallas_call | solution.py:1222
  394.0 3.4 collective-permute-start.62
  399.3 2.9 table_grads.1
  403.1 8.5 %collective-permute-done.62.refs_19_ = bf16[192,768]{1,0:T(8,128)(2,1)S(1)} collective-permute-done((bf16[192,768]{1,0:T(8,128)(2,1)S(1)}, bf16[192,768]{1,0:T(8,128)(2,1)S(1)}, u32[]{:S(2)}, u32[]{:S(2)}) %collective-permute-start.62) | collective-permute-done | bytes 294944 | tf_op jit(solution)/shard_map/ppermute | solution.py:744
  414.2 7.6 %blocks.13 = (bf16[96,768]{1,0:T(8,128)(2,1)S(1)}, bf16[384,768]{1,0:T(8,128)(2,1)}, bf16[704,768]{1,0:T(8,128)(2,1)}, bf16[832,768]{1,0:T(8,128)(2,1)}, f32[48,...) custom-call(s32[4]{0:T(128)S(1)} %pad_add_fusion.2.scalars, ...), custom_call_target="tpu_custom_call" | custom-call | bytes 15630336 | tf_op jit(solution)/shard_map/blocks/pallas_call | solution.py:1222
  428.0 2.9 collective-permute-start.67
  430.9 9.7 %collective-permute-done.67.refs_14_ = bf16[96,768]{1,0:T(8,128)(2,1)S(1)} collective-permute-done((bf16[96,768]{1,0:T(8,128)(2,1)S(1)}, bf16[96,768]{1,0:T(8,128)(2,1)S(1)}, u32[]{:S(2)}, u32[]{:S(2)}) %collective-permute-start.67) | collective-permute-done | bytes 147488 | tf_op jit(solution)/shard_map/ppermute | solution.py:744
  441.4 5.1 collective-permute-done.69.refs_6_
  446.5 3.7 collective-permute-done.70.refs_8_
  450.2 6.9 %blocks.14 = (bf16[192,768]{1,0:T(8,128)(2,1)}, bf16[192,768]{1,0:T(8,128)(2,1)}, bf16[256,768]{1,0:T(8,128)(2,1)}, bf16[256,768]{1,0:T(8,128)(2,1)}, f32[48,768...) custom-call(s32[4]{0:T(128)S(1)} %pad_add_fusion.2.scalars, ...), custom_call_target="tpu_custom_call" | custom-call | bytes 11354112 | tf_op jit(solution)/shard_map/blocks/pallas_call | solution.py:1222
  467.9 3.4 collective-permute-done.71.refs_10_
  472.7 4.4 blocks.15
  482.9 5.0 collective-permute-done.75.refs_6_
  502.0 5.5 %collective-permute-done.77.refs_1_ = bf16[128,768]{1,0:T(8,128)(2,1)S(1)} collective-permute-done((bf16[128,768]{1,0:T(8,128)(2,1)S(1)}, bf16[128,768]{1,0:T(8,128)(2,1)S(1)}, u32[]{:S(2)}, u32[]{:S(2)}) %collective-permute-start.77) | collective-permute-done | bytes 196640 | tf_op jit(solution)/shard_map/ppermute | solution.py:744
  (526 shorter events, 206.9 us)
Async XLA Ops:
  1.7 13.4 %collective-permute-start = (bf16[128,768]{1,0:T(8,128)(2,1)}, bf16[128,768]{1,0:T(8,128)(2,1)S(1)}, u32[]{:S(2)}, u32[]{:S(2)}) collective-permute-start(bf16[128,768]{1,0:T(8,128)(2,1)} %bitcast.417), channel_id=1, source_target_pairs={{0,16},{1,17},{2,18},{3,19},{4,20},{5,21},{6,22},{7,23},{8,24},{9,... | collective-permute-start | bytes 589832 | tf_op jit(solution)/shard_map/ppermute | solution.py:744
  19.0 12.9 %collective-permute-start.5 = (bf16[96,768]{1,0:T(8,128)(2,1)S(1)}, bf16[96,768]{1,0:T(8,128)(2,1)S(1)}, u32[]{:S(2)}, u32[]{:S(2)}) collective-permute-start(bf16[96,768]{1,0:T(8,128)(2,1)S(1)} %bitcast.447), channel_id=1, source_target_pairs={{0,2},{1,3},{2,0},{3,1},{4,6},{5,7},{6,4},{7,5},{8,10},{9,11},{10,... | collective-permute-start | bytes 442376 | tf_op jit(solution)/shard_map/ppermute | solution.py:744
  19.4 12.5 %collective-permute-start.6 = (bf16[96,768]{1,0:T(8,128)(2,1)S(1)}, bf16[96,768]{1,0:T(8,128)(2,1)S(1)}, u32[]{:S(2)}, u32[]{:S(2)}) collective-permute-start(bf16[96,768]{1,0:T(8,128)(2,1)S(1)} %bitcast.446), channel_id=1, source_target_pairs={{0,4},{1,5},{2,6},{3,7},{4,0},{5,1},{6,2},{7,3},{8,12},{9,13},{10,... | collective-permute-start | bytes 442376 | tf_op jit(solution)/shard_map/ppermute | solution.py:744
  24.4 14.3 %collective-permute-start.4 = (bf16[256,768]{1,0:T(8,128)(2,1)S(1)}, bf16[256,768]{1,0:T(8,128)(2,1)S(1)}, u32[]{:S(2)}, u32[]{:S(2)}) collective-permute-start(bf16[256,768]{1,0:T(8,128)(2,1)S(1)} %bitcast.431), channel_id=1, source_target_pairs={{0,8},{1,9},{2,10},{3,11},{4,12},{5,13},{6,14},{7,15},{8,0},{9,1},... | collective-permute-start | bytes 1179656 | tf_op jit(solution)/shard_map/ppermute | solution.py:744
  39.0 19.4 %collective-permute-start.14 = (bf16[256,768]{1,0:T(8,128)(2,1)S(1)}, bf16[256,768]{1,0:T(8,128)(2,1)S(1)}, u32[]{:S(2)}, u32[]{:S(2)}) collective-permute-start(bf16[256,768]{1,0:T(8,128)(2,1)S(1)} %bitcast.430), channel_id=1, source_target_pairs={{0,2},{1,3},{2,0},{3,1},{4,6},{5,7},{6,4},{7,5},{8,10},{9,11},{10,... | collective-permute-start | bytes 1179656 | tf_op jit(solution)/shard_map/ppermute | solution.py:744
  40.6 17.9 %collective-permute-start.13 = (bf16[256,768]{1,0:T(8,128)(2,1)S(1)}, bf16[256,768]{1,0:T(8,128)(2,1)S(1)}, u32[]{:S(2)}, u32[]{:S(2)}) collective-permute-start(bf16[256,768]{1,0:T(8,128)(2,1)S(1)} %bitcast.429), channel_id=1, source_target_pairs={{0,4},{1,5},{2,6},{3,7},{4,0},{5,1},{6,2},{7,3},{8,12},{9,13},{10,... | collective-permute-start | bytes 1179656 | tf_op jit(solution)/shard_map/ppermute | solution.py:744
  41.1 13.3 %collective-permute-start.15 = (bf16[192,768]{1,0:T(8,128)(2,1)S(1)}, bf16[192,768]{1,0:T(8,128)(2,1)S(1)}, u32[]{:S(2)}, u32[]{:S(2)}) collective-permute-start(bf16[192,768]{1,0:T(8,128)(2,1)S(1)} %bitcast.440), channel_id=1, source_target_pairs={{0,8},{1,9},{2,10},{3,11},{4,12},{5,13},{6,14},{7,15},{8,0},{9,1},... | collective-permute-start | bytes 884744 | tf_op jit(solution)/shard_map/ppermute | solution.py:744
  43.4 15.0 %collective-permute-start.16 = (bf16[192,768]{1,0:T(8,128)(2,1)S(1)}, bf16[192,768]{1,0:T(8,128)(2,1)S(1)}, u32[]{:S(2)}, u32[]{:S(2)}) collective-permute-start(bf16[192,768]{1,0:T(8,128)(2,1)S(1)} %bitcast.327), channel_id=1, source_target_pairs={{0,16},{1,17},{2,18},{3,19},{4,20},{5,21},{6,22},{7,23},{8,24},{9,... | collective-permute-start | bytes 884744 | tf_op jit(solution)/shard_map/ppermute | solution.py:744
  61.7 24.7 %collective-permute-start.18 = (bf16[704,768]{1,0:T(8,128)(2,1)}, bf16[704,768]{1,0:T(8,128)(2,1)}, u32[]{:S(2)}, u32[]{:S(2)}) collective-permute-start(bf16[704,768]{1,0:T(8,128)(2,1)} %pad_maximum_fusion.9), channel_id=1, source_target_pairs={{0,4},{1,5},{2,6},{3,7},{4,0},{5,1},{6,2},{7,3},{8,12},{9,13},{10,... | collective-permute-start | bytes 3244040 | tf_op jit(solution)/shard_map/ppermute | solution.py:744
  64.3 25.2 %collective-permute-start.17 = (bf16[704,768]{1,0:T(8,128)(2,1)}, bf16[704,768]{1,0:T(8,128)(2,1)S(1)}, u32[]{:S(2)}, u32[]{:S(2)}) collective-permute-start(bf16[704,768]{1,0:T(8,128)(2,1)} %pad_maximum_fusion.8), channel_id=1, source_target_pairs={{0,2},{1,3},{2,0},{3,1},{4,6},{5,7},{6,4},{7,5},{8,10},{9,11},{10,... | collective-permute-start | bytes 3244040 | tf_op jit(solution)/shard_map/ppermute | solution.py:744
  64.8 25.7 %collective-permute-start.19 = (bf16[384,768]{1,0:T(8,128)(2,1)}, bf16[384,768]{1,0:T(8,128)(2,1)}, u32[]{:S(2)}, u32[]{:S(2)}) collective-permute-start(bf16[384,768]{1,0:T(8,128)(2,1)} %bitcast.73), channel_id=1, source_target_pairs={{0,8},{1,9},{2,10},{3,11},{4,12},{5,13},{6,14},{7,15},{8,0},{9,1},... | collective-permute-start | bytes 1769480 | tf_op jit(solution)/shard_map/ppermute | solution.py:744
  67.6 17.9 %all-to-all-start = ((bf16[32,2,288]{2,1,0:T(2,128)(2,1)}), bf16[32,2,288]{2,1,0:T(2,128)(2,1)S(1)}, u32[]{:S(2)}, u32[]{:S(2)}) async-start(bf16[32,2,288]{2,1,0:T(2,128)(2,1)} %reshape.697), calls=%async_computation | async-start | bytes 98304 | tf_op jit(solution)/shard_map/all_to_all | solution.py:1384
  71.5 19.0 %collective-permute-start.20 = (bf16[96,768]{1,0:T(8,128)(2,1)S(1)}, bf16[96,768]{1,0:T(8,128)(2,1)S(1)}, u32[]{:S(2)}, u32[]{:S(2)}) collective-permute-start(bf16[96,768]{1,0:T(8,128)(2,1)S(1)} %bitcast.330), channel_id=1, source_target_pairs={{0,16},{1,17},{2,18},{3,19},{4,20},{5,21},{6,22},{7,23},{8,24},{9,... | collective-permute-start | bytes 442376 | tf_op jit(solution)/shard_map/ppermute | solution.py:744
  96.2 28.3 %collective-permute-start.22 = (bf16[768,768]{1,0:T(8,128)(2,1)}, bf16[768,768]{1,0:T(8,128)(2,1)}, u32[]{:S(2)}, u32[]{:S(2)}) collective-permute-start(bf16[768,768]{1,0:T(8,128)(2,1)} %pad_maximum_fusion.4), channel_id=1, source_target_pairs={{0,4},{1,5},{2,6},{3,7},{4,0},{5,1},{6,2},{7,3},{8,12},{9,13},{10,... | collective-permute-start | bytes 3538952 | tf_op jit(solution)/shard_map/ppermute | solution.py:744
  97.8 28.7 %collective-permute-start.21 = (bf16[768,768]{1,0:T(8,128)(2,1)}, bf16[768,768]{1,0:T(8,128)(2,1)}, u32[]{:S(2)}, u32[]{:S(2)}) collective-permute-start(bf16[768,768]{1,0:T(8,128)(2,1)} %pad_maximum_fusion.3), channel_id=1, source_target_pairs={{0,2},{1,3},{2,0},{3,1},{4,6},{5,7},{6,4},{7,5},{8,10},{9,11},{10,... | collective-permute-start | bytes 3538952 | tf_op jit(solution)/shard_map/ppermute | solution.py:744
  109.3 18.6 %collective-permute-start.24 = (bf16[96,768]{1,0:T(8,128)(2,1)S(1)}, bf16[96,768]{1,0:T(8,128)(2,1)S(1)}, u32[]{:S(2)}, u32[]{:S(2)}) collective-permute-start(bf16[96,768]{1,0:T(8,128)(2,1)S(1)} %bitcast.397), channel_id=1, source_target_pairs={{0,16},{1,17},{2,18},{3,19},{4,20},{5,21},{6,22},{7,23},{8,24},{9,... | collective-permute-start | bytes 442376 | tf_op jit(solution)/shard_map/ppermute | solution.py:744
  112.7 15.2 %collective-permute-start.23 = (bf16[192,768]{1,0:T(8,128)(2,1)S(1)}, bf16[192,768]{1,0:T(8,128)(2,1)S(1)}, u32[]{:S(2)}, u32[]{:S(2)}) collective-permute-start(bf16[192,768]{1,0:T(8,128)(2,1)S(1)} %bitcast.439), channel_id=1, source_target_pairs={{0,8},{1,9},{2,10},{3,11},{4,12},{5,13},{6,14},{7,15},{8,0},{9,1},... | collective-permute-start | bytes 884744 | tf_op jit(solution)/shard_map/ppermute | solution.py:744
  133.1 33.8 %collective-permute-start.28 = (bf16[960,768]{1,0:T(8,128)(2,1)}, bf16[960,768]{1,0:T(8,128)(2,1)}, u32[]{:S(2)}, u32[]{:S(2)}) collective-permute-start(bf16[960,768]{1,0:T(8,128)(2,1)} %pad_maximum_fusion.1), channel_id=1, source_target_pairs={{0,4},{1,5},{2,6},{3,7},{4,0},{5,1},{6,2},{7,3},{8,12},{9,13},{10,... | collective-permute-start | bytes 4423688 | tf_op jit(solution)/shard_map/ppermute | solution.py:744
  135.0 35.2 %collective-permute-start.27 = (bf16[960,768]{1,0:T(8,128)(2,1)}, bf16[960,768]{1,0:T(8,128)(2,1)}, u32[]{:S(2)}, u32[]{:S(2)}) collective-permute-start(bf16[960,768]{1,0:T(8,128)(2,1)} %pad_maximum_fusion), channel_id=1, source_target_pairs={{0,2},{1,3},{2,0},{3,1},{4,6},{5,7},{6,4},{7,5},{8,10},{9,11},{10,... | collective-permute-start | bytes 4423688 | tf_op jit(solution)/shard_map/ppermute | solution.py:744
  138.7 13.2 %collective-permute-start.32 = (bf16[768,384]{1,0:T(8,128)(2,1)S(1)}, bf16[768,384]{1,0:T(8,128)(2,1)S(1)}, u32[]{:S(2)}, u32[]{:S(2)}) collective-permute-start(bf16[768,384]{1,0:T(8,128)(2,1)S(1)} %bitcast.336), channel_id=1, source_target_pairs={{0,1},{1,0},{2,3},{3,2},{4,5},{5,4},{6,7},{7,6},{8,9},{9,8},{10,11... | collective-permute-start | bytes 1769480 | tf_op jit(solution)/shard_map/ppermute | solution.py:744
  139.2 34.4 %collective-permute-start.26 = (bf16[384,768]{1,0:T(8,128)(2,1)S(1)}, bf16[384,768]{1,0:T(8,128)(2,1)S(1)}, u32[]{:S(2)}, u32[]{:S(2)}) collective-permute-start(bf16[384,768]{1,0:T(8,128)(2,1)S(1)} %bitcast.394), channel_id=1, source_target_pairs={{0,16},{1,17},{2,18},{3,19},{4,20},{5,21},{6,22},{7,23},{8,24},{9,... | collective-permute-start | bytes 1769480 | tf_op jit(solution)/shard_map/ppermute | solution.py:744
  142.6 31.0 %collective-permute-start.29 = (bf16[192,768]{1,0:T(8,128)(2,1)}, bf16[192,768]{1,0:T(8,128)(2,1)S(1)}, u32[]{:S(2)}, u32[]{:S(2)}) collective-permute-start(bf16[192,768]{1,0:T(8,128)(2,1)} %bitcast.143), channel_id=1, source_target_pairs={{0,8},{1,9},{2,10},{3,11},{4,12},{5,13},{6,14},{7,15},{8,0},{9,1},... | collective-permute-start | bytes 884744 | tf_op jit(solution)/shard_map/ppermute | solution.py:744
  174.9 26.3 %collective-permute-start.33 = (bf16[768,768]{1,0:T(8,128)(2,1)S(1)}, bf16[768,768]{1,0:T(8,128)(2,1)S(1)}, u32[]{:S(2)}, u32[]{:S(2)}) collective-permute-start(bf16[768,768]{1,0:T(8,128)(2,1)S(1)} %bitcast.319), channel_id=1, source_target_pairs={{0,8},{1,9},{2,10},{3,11},{4,12},{5,13},{6,14},{7,15},{8,0},{9,1},... | collective-permute-start | bytes 3538952 | tf_op jit(solution)/shard_map/ppermute | solution.py:744
  176.8 22.1 %collective-permute-start.35 = (bf16[576,768]{1,0:T(8,128)(2,1)S(1)}, bf16[576,768]{1,0:T(8,128)(2,1)S(1)}, u32[]{:S(2)}, u32[]{:S(2)}) collective-permute-start(bf16[576,768]{1,0:T(8,128)(2,1)S(1)} %pad_maximum_fusion.11), channel_id=1, source_target_pairs={{0,4},{1,5},{2,6},{3,7},{4,0},{5,1},{6,2},{7,3},{8,12},{9,13},{10,... | collective-permute-start | bytes 2654216 | tf_op jit(solution)/shard_map/ppermute | solution.py:744
  177.3 22.5 %collective-permute-start.34 = (bf16[576,768]{1,0:T(8,128)(2,1)S(1)}, bf16[576,768]{1,0:T(8,128)(2,1)S(1)}, u32[]{:S(2)}, u32[]{:S(2)}) collective-permute-start(bf16[576,768]{1,0:T(8,128)(2,1)S(1)} %pad_maximum_fusion.10), channel_id=1, source_target_pairs={{0,2},{1,3},{2,0},{3,1},{4,6},{5,7},{6,4},{7,5},{8,10},{9,11},{10,... | collective-permute-start | bytes 2654216 | tf_op jit(solution)/shard_map/ppermute | solution.py:744
  204.7 17.1 %collective-permute-start.42 = (bf16[768,384]{1,0:T(8,128)(2,1)}, bf16[768,384]{1,0:T(8,128)(2,1)}, u32[]{:S(2)}, u32[]{:S(2)}) collective-permute-start(bf16[768,384]{1,0:T(8,128)(2,1)} %bitcast.183.wom), channel_id=1, source_target_pairs={{0,1},{1,0},{2,3},{3,2},{4,5},{5,4},{6,7},{7,6},{8,9},{9,8},{10,11... | collective-permute-start | bytes 1769480 | tf_op jit(solution)/shard_map/ppermute | solution.py:744
  205.0 20.4 %collective-permute-start.39 = (bf16[384,768]{1,0:T(8,128)(2,1)S(1)}, bf16[384,768]{1,0:T(8,128)(2,1)}, u32[]{:S(2)}, u32[]{:S(2)}) collective-permute-start(bf16[384,768]{1,0:T(8,128)(2,1)S(1)} %bitcast.323), channel_id=1, source_target_pairs={{0,4},{1,5},{2,6},{3,7},{4,0},{5,1},{6,2},{7,3},{8,12},{9,13},{10,... | collective-permute-start | bytes 1769480 | tf_op jit(solution)/shard_map/ppermute | solution.py:744
  205.4 20.1 %collective-permute-start.38 = (bf16[384,768]{1,0:T(8,128)(2,1)S(1)}, bf16[384,768]{1,0:T(8,128)(2,1)}, u32[]{:S(2)}, u32[]{:S(2)}) collective-permute-start(bf16[384,768]{1,0:T(8,128)(2,1)S(1)} %bitcast.321), channel_id=1, source_target_pairs={{0,2},{1,3},{2,0},{3,1},{4,6},{5,7},{6,4},{7,5},{8,10},{9,11},{10,... | collective-permute-start | bytes 1769480 | tf_op jit(solution)/shard_map/ppermute | solution.py:744
  264.5 32.8 %collective-permute-start.48 = (bf16[896,768]{1,0:T(8,128)(2,1)}, bf16[896,768]{1,0:T(8,128)(2,1)}, u32[]{:S(2)}, u32[]{:S(2)}) collective-permute-start(bf16[896,768]{1,0:T(8,128)(2,1)} %get-tuple-element.550), channel_id=1, source_target_pairs={{0,2},{1,3},{2,0},{3,1},{4,6},{5,7},{6,4},{7,5},{8,10},{9,11},{10,... | collective-permute-start | bytes 4128776 | tf_op jit(solution)/shard_map/ppermute | solution.py:744
  266.1 28.3 %collective-permute-start.47 = (bf16[768,768]{1,0:T(8,128)(2,1)}, bf16[768,768]{1,0:T(8,128)(2,1)}, u32[]{:S(2)}, u32[]{:S(2)}) collective-permute-start(bf16[768,768]{1,0:T(8,128)(2,1)} %get-tuple-element.549), channel_id=1, source_target_pairs={{0,4},{1,5},{2,6},{3,7},{4,0},{5,1},{6,2},{7,3},{8,12},{9,13},{10,... | collective-permute-start | bytes 3538952 | tf_op jit(solution)/shard_map/ppermute | solution.py:744
  306.2 28.4 %collective-permute-start.52 = (bf16[768,768]{1,0:T(8,128)(2,1)S(1)}, bf16[768,768]{1,0:T(8,128)(2,1)S(1)}, u32[]{:S(2)}, u32[]{:S(2)}) collective-permute-start(bf16[768,768]{1,0:T(8,128)(2,1)S(1)} %copy-done.97), channel_id=1, source_target_pairs={{0,4},{1,5},{2,6},{3,7},{4,0},{5,1},{6,2},{7,3},{8,12},{9,13},{10,... | collective-permute-start | bytes 3538952 | tf_op jit(solution)/shard_map/ppermute | solution.py:744
  307.8 28.1 %collective-permute-start.53 = (bf16[768,768]{1,0:T(8,128)(2,1)S(1)}, bf16[768,768]{1,0:T(8,128)(2,1)S(1)}, u32[]{:S(2)}, u32[]{:S(2)}) collective-permute-start(bf16[768,768]{1,0:T(8,128)(2,1)S(1)} %copy-done.96), channel_id=1, source_target_pairs={{0,2},{1,3},{2,0},{3,1},{4,6},{5,7},{6,4},{7,5},{8,10},{9,11},{10,... | collective-permute-start | bytes 3538952 | tf_op jit(solution)/shard_map/ppermute | solution.py:744
  344.1 33.8 %collective-permute-start.57 = (bf16[960,768]{1,0:T(8,128)(2,1)}, bf16[960,768]{1,0:T(8,128)(2,1)S(1)}, u32[]{:S(2)}, u32[]{:S(2)}) collective-permute-start(bf16[960,768]{1,0:T(8,128)(2,1)} %get-tuple-element.604), channel_id=1, source_target_pairs={{0,4},{1,5},{2,6},{3,7},{4,0},{5,1},{6,2},{7,3},{8,12},{9,13},{10,... | collective-permute-start | bytes 4423688 | tf_op jit(solution)/shard_map/ppermute | solution.py:744
  344.8 33.8 %collective-permute-start.58 = (bf16[960,768]{1,0:T(8,128)(2,1)}, bf16[960,768]{1,0:T(8,128)(2,1)S(1)}, u32[]{:S(2)}, u32[]{:S(2)}) collective-permute-start(bf16[960,768]{1,0:T(8,128)(2,1)} %get-tuple-element.605), channel_id=1, source_target_pairs={{0,2},{1,3},{2,0},{3,1},{4,6},{5,7},{6,4},{7,5},{8,10},{9,11},{10,... | collective-permute-start | bytes 4423688 | tf_op jit(solution)/shard_map/ppermute | solution.py:744
  348.6 22.0 %collective-permute-start.56 = (bf16[384,768]{1,0:T(8,128)(2,1)S(1)}, bf16[384,768]{1,0:T(8,128)(2,1)S(1)}, u32[]{:S(2)}, u32[]{:S(2)}) collective-permute-start(bf16[384,768]{1,0:T(8,128)(2,1)S(1)} %copy-done.98), channel_id=1, source_target_pairs={{0,8},{1,9},{2,10},{3,11},{4,12},{5,13},{6,14},{7,15},{8,0},{9,1},... | collective-permute-start | bytes 1769480 | tf_op jit(solution)/shard_map/ppermute | solution.py:744
  386.6 26.8 %collective-permute-start.64 = (bf16[768,768]{1,0:T(8,128)(2,1)}, bf16[768,768]{1,0:T(8,128)(2,1)}, u32[]{:S(2)}, u32[]{:S(2)}) collective-permute-start(bf16[768,768]{1,0:T(8,128)(2,1)} %get-tuple-element.644), channel_id=1, source_target_pairs={{0,4},{1,5},{2,6},{3,7},{4,0},{5,1},{6,2},{7,3},{8,12},{9,13},{10,... | collective-permute-start | bytes 3538952 | tf_op jit(solution)/shard_map/ppermute | solution.py:744
  387.7 26.5 %collective-permute-start.65 = (bf16[768,768]{1,0:T(8,128)(2,1)}, bf16[768,768]{1,0:T(8,128)(2,1)}, u32[]{:S(2)}, u32[]{:S(2)}) collective-permute-start(bf16[768,768]{1,0:T(8,128)(2,1)} %get-tuple-element.645), channel_id=1, source_target_pairs={{0,2},{1,3},{2,0},{3,1},{4,6},{5,7},{6,4},{7,5},{8,10},{9,11},{10,... | collective-permute-start | bytes 3538952 | tf_op jit(solution)/shard_map/ppermute | solution.py:744
  394.0 17.5 %collective-permute-start.62 = (bf16[192,768]{1,0:T(8,128)(2,1)S(1)}, bf16[192,768]{1,0:T(8,128)(2,1)S(1)}, u32[]{:S(2)}, u32[]{:S(2)}) collective-permute-start(bf16[192,768]{1,0:T(8,128)(2,1)S(1)} %get-tuple-element.642), channel_id=1, source_target_pairs={{0,16},{1,17},{2,18},{3,19},{4,20},{5,21},{6,22},{7,23},{8,24},{9,... | collective-permute-start | bytes 884744 | tf_op jit(solution)/shard_map/ppermute | solution.py:744
  397.5 14.7 %collective-permute-start.63 = (bf16[192,768]{1,0:T(8,128)(2,1)S(1)}, bf16[192,768]{1,0:T(8,128)(2,1)S(1)}, u32[]{:S(2)}, u32[]{:S(2)}) collective-permute-start(bf16[192,768]{1,0:T(8,128)(2,1)S(1)} %get-tuple-element.643), channel_id=1, source_target_pairs={{0,8},{1,9},{2,10},{3,11},{4,12},{5,13},{6,14},{7,15},{8,0},{9,1},... | collective-permute-start | bytes 884744 | tf_op jit(solution)/shard_map/ppermute | solution.py:744
  421.7 28.4 %collective-permute-start.70 = (bf16[832,768]{1,0:T(8,128)(2,1)}, bf16[832,768]{1,0:T(8,128)(2,1)}, u32[]{:S(2)}, u32[]{:S(2)}) collective-permute-start(bf16[832,768]{1,0:T(8,128)(2,1)} %get-tuple-element.674), channel_id=1, source_target_pairs={{0,2},{1,3},{2,0},{3,1},{4,6},{5,7},{6,4},{7,5},{8,10},{9,11},{10,... | collective-permute-start | bytes 3833864 | tf_op jit(solution)/shard_map/ppermute | solution.py:744
  423.3 23.2 %collective-permute-start.69 = (bf16[704,768]{1,0:T(8,128)(2,1)}, bf16[704,768]{1,0:T(8,128)(2,1)}, u32[]{:S(2)}, u32[]{:S(2)}) collective-permute-start(bf16[704,768]{1,0:T(8,128)(2,1)} %get-tuple-element.673), channel_id=1, source_target_pairs={{0,4},{1,5},{2,6},{3,7},{4,0},{5,1},{6,2},{7,3},{8,12},{9,13},{10,... | collective-permute-start | bytes 3244040 | tf_op jit(solution)/shard_map/ppermute | solution.py:744
  426.0 15.4 %collective-permute-start.68 = (bf16[384,768]{1,0:T(8,128)(2,1)}, bf16[384,768]{1,0:T(8,128)(2,1)S(1)}, u32[]{:S(2)}, u32[]{:S(2)}) collective-permute-start(bf16[384,768]{1,0:T(8,128)(2,1)} %get-tuple-element.672), channel_id=1, source_target_pairs={{0,8},{1,9},{2,10},{3,11},{4,12},{5,13},{6,14},{7,15},{8,0},{9,1},... | collective-permute-start | bytes 1769480 | tf_op jit(solution)/shard_map/ppermute | solution.py:744
  428.0 12.6 %collective-permute-start.67 = (bf16[96,768]{1,0:T(8,128)(2,1)S(1)}, bf16[96,768]{1,0:T(8,128)(2,1)S(1)}, u32[]{:S(2)}, u32[]{:S(2)}) collective-permute-start(bf16[96,768]{1,0:T(8,128)(2,1)S(1)} %get-tuple-element.671), channel_id=1, source_target_pairs={{0,16},{1,17},{2,18},{3,19},{4,20},{5,21},{6,22},{7,23},{8,24},{9,... | collective-permute-start | bytes 442376 | tf_op jit(solution)/shard_map/ppermute | solution.py:744
  457.7 13.6 %collective-permute-start.71 = (bf16[192,768]{1,0:T(8,128)(2,1)}, bf16[192,768]{1,0:T(8,128)(2,1)S(1)}, u32[]{:S(2)}, u32[]{:S(2)}) collective-permute-start(bf16[192,768]{1,0:T(8,128)(2,1)} %get-tuple-element.692), channel_id=1, source_target_pairs={{0,16},{1,17},{2,18},{3,19},{4,20},{5,21},{6,22},{7,23},{8,24},{9,... | collective-permute-start | bytes 884744 | tf_op jit(solution)/shard_map/ppermute | solution.py:744
  465.3 14.1 %all-to-all-start.1 = ((f32[32,1,576]{2,1,0:T(1,128)}), f32[32,1,576]{2,1,0:T(1,128)S(1)}, u32[]{:S(2)}, u32[]{:S(2)}) async-start(f32[32,1,576]{2,1,0:T(1,128)} %copy.83), calls=%async_computation.1 | async-start | bytes 163840 | tf_op jit(solution)/shard_map/all_to_all | solution.py:1586
  477.2 12.9 %collective-permute-start.76 = (bf16[256,768]{1,0:T(8,128)(2,1)}, bf16[256,768]{1,0:T(8,128)(2,1)S(1)}, u32[]{:S(2)}, u32[]{:S(2)}) collective-permute-start(bf16[256,768]{1,0:T(8,128)(2,1)} %get-tuple-element.713), channel_id=1, source_target_pairs={{0,8},{1,9},{2,10},{3,11},{4,12},{5,13},{6,14},{7,15},{8,0},{9,1},... | collective-permute-start | bytes 1179656 | tf_op jit(solution)/shard_map/ppermute | solution.py:744
  482.8 13.4 %collective-permute-start.79 = (f32[24,3072]{1,0:T(8,128)S(1)}, f32[24,3072]{1,0:T(8,128)S(1)}, u32[]{:S(2)}, u32[]{:S(2)}) collective-permute-start(f32[24,3072]{1,0:T(8,128)S(1)} %get-tuple-element.736), channel_id=1, source_target_pairs={{0,1},{1,0},{2,3},{3,2},{4,5},{5,4},{6,7},{7,6},{8,9},{9,8},{10,11... | collective-permute-start | bytes 884744 | tf_op jit(solution)/shard_map/ppermute | solution.py:744
  495.0 12.4 %collective-permute-start.77 = (bf16[128,768]{1,0:T(8,128)(2,1)S(1)}, bf16[128,768]{1,0:T(8,128)(2,1)S(1)}, u32[]{:S(2)}, u32[]{:S(2)}) collective-permute-start(bf16[128,768]{1,0:T(8,128)(2,1)S(1)} %get-tuple-element.722), channel_id=1, source_target_pairs={{0,16},{1,17},{2,18},{3,19},{4,20},{5,21},{6,22},{7,23},{8,24},{9,... | collective-permute-start | bytes 589832 | tf_op jit(solution)/shard_map/ppermute | solution.py:744
  (143 other events, 682.9 us)

commit v5 on v4

--- a/solution.py
+++ b/solution.py
@@ -1,4 +1,5 @@
 import functools
+import math
 
 import jax
 import jax.numpy as jnp
@@ -557,7 +558,10 @@
     for out, to, to_col, source, at, at_col, width in moves:
         to = table[to[0]] if isinstance(to, list) else to
         at = table[at[0]] if isinstance(at, list) else at
-        refs[count + out][to, :, to_col : to_col + width] = refs[source][at, :, at_col : at_col + width]
+        ref, cols = refs[source], slice(at_col, at_col + width)
+        rows = refs[count + out].shape[1]
+        block = ref[at : at + rows, cols] if len(ref.shape) == 2 else ref[at, :, cols]
+        refs[count + out][to, :, to_col : to_col + width] = block
 
 
 def shuffle(table, sources, shapes, moves):
@@ -743,21 +747,20 @@
             pairs.append((device, ((place[0] * nx + place[1]) * ny + place[2]) * nc + place[3]))
         return lax.ppermute(value, ("page", "band"), pairs)
 
-    def exchange(self, wants):
+    def payloads(self, wants):
         keys = []
         for axis, step, _ in wants:
-            key = (axis, step if axis == 0 else step % self.sizes[axis])
-            keys.append(key)
-        got = [None] * len(wants)
+            keys.append((axis, step if axis == 0 else step % self.sizes[axis]))
+        merged, places = {}, [None] * len(wants)
         for key in dict.fromkeys(keys):
             numbers = [i for i, other in enumerate(keys) if other == key]
             flat = [wants[i][2].reshape(-1, wants[i][2].shape[-1]) for i in numbers]
-            moved = self.move(jnp.concatenate(flat) if len(flat) > 1 else flat[0], *key, flip=key[0] == 0)
+            merged[key] = jnp.concatenate(flat) if len(flat) > 1 else flat[0]
             first = 0
             for i, part in zip(numbers, flat):
-                got[i] = moved[first : first + part.shape[0]].reshape(wants[i][2].shape)
+                places[i] = (key, first, wants[i][2].shape)
                 first += part.shape[0]
-        return got
+        return merged, places
 
     def swap(self, value):
         return self.move(value, 3, 1)
@@ -803,29 +806,26 @@
         self.sent = [jnp.stack([part] + got) for part, got in zip(self.sent, (got[:cut], got[cut:]))]
         return self.near(2, self.sent[0]) + self.near(1, self.sent[1])
 
-    def finish(self, got):
+    def finish(self, got, mine):
         at = self.at
-        rows, cols = self.local.shape[1:]
+        rows = self.local.shape[1]
         sources, moves, table = [], [], []
         cut = at.ny - 1
-        for axes, part, other, start in (
-            ((1, 2), self.sent[0], got[:cut], 0),
-            ((2, 1), self.sent[1], got[cut:], self.half),
+        for axes, pieces, start in (
+            ((1, 2), mine[:1] + got[:cut], 0),
+            ((2, 1), mine[cut : cut + 1] + got[cut:], self.half),
         ):
-            for far, piece in enumerate([part] + list(other)):
-                number = 0
+            for far, piece in enumerate(pieces):
+                source, spot, stride = piece.source(sources, rows)
                 for near in range(at.sizes[axes[0]]):
                     kx, ky = (near, far) if axes[0] == 1 else (far, near)
                     for kz in self.spots:
                         chip = at.chip_of(kz, kx, ky)
                         for unit in range(start, start + self.half):
                             for out, step, offset, to_col, at_col, width in self.place[unit]:
-                                moves.append(
-                                    (out, [len(table)], to_col, len(sources), number, at_col, width)
-                                )
+                                moves.append((out, [len(table)], to_col, source, spot, at_col, width))
                                 table.append(chip * step + offset)
-                            number += 1
-                sources.append(piece.reshape((-1, rows, cols)))
+                            spot += stride
         outs = shuffle(jnp.stack(table), sources, [sds(shape, BF16) for shape in self.shapes], moves)
         return [out.reshape(-1, out.shape[-1]) for out in outs]
 
@@ -865,23 +865,22 @@
         self.spots = self.spots + [spot ^ step for spot in self.spots]
         return [(0, step, self.held)]
 
-    def finish(self, got):
+    def finish(self, got, mine):
         at = self.at
-        rows, cols = self.local.shape[1:]
+        rows = self.local.shape[1]
         sources, moves, table = [], [], []
         spots = len(self.spots) // 2
-        for number, piece in enumerate([self.held] + list(got)):
-            at_block = 0
+        for number, piece in enumerate((mine[0], got[0])):
+            source, block, stride = piece.source(sources, rows)
             for spot in self.spots[number * spots : (number + 1) * spots]:
                 for far in range(at.nx):
                     for near in range(at.ny):
                         for unit in range(2 * self.half):
                             kx, ky = (near, far) if unit < self.half else (far, near)
                             for out, step, offset, to_col, at_col, width in self.place[unit]:
-                                moves.append((out, [len(table)], to_col, number, at_block, at_col, width))
+                                moves.append((out, [len(table)], to_col, source, block, at_col, width))
                                 table.append(at.chip_of(spot, kx, ky) * step + offset)
-                            at_block += 1
-            sources.append(piece.reshape((-1, rows, cols)))
+                            block += stride
         outs = shuffle(jnp.stack(table), sources, [sds(shape, BF16) for shape in self.shapes], moves)
         return [out.reshape(-1, out.shape[-1]) for out in outs]
 
@@ -949,32 +948,56 @@
         return total[: self.cut], total[self.cut :]
 
 
+class Piece:
+    def __init__(self, array, first, shape):
+        self.array, self.first, self.shape = array, first, shape
+
+    def value(self):
+        rows = math.prod(self.shape[:-1])
+        return self.array[self.first : self.first + rows].reshape(self.shape)
+
+    def source(self, sources, rows):
+        if rows % 16:
+            sources.append(self.value().reshape(-1, rows, self.shape[-1]))
+            return len(sources) - 1, 0, 1
+        for number, array in enumerate(sources):
+            if array is self.array:
+                return number, self.first, rows
+        sources.append(self.array)
+        return len(sources) - 1, self.first, rows
+
+
 class Line:
     def __init__(self, at):
-        self.at, self.chunks, self.age, self.got = at, [], [], []
+        self.at, self.chunks, self.age, self.got, self.mine = at, [], [], [], []
 
     def add(self, chunk):
         self.chunks.append(chunk)
         self.age.append(0)
         self.got.append([])
+        self.mine.append([])
 
     def step(self, *others, extra=None):
         wants, spans = [], []
         for number, chunk in enumerate(self.chunks):
             if self.age[number] < len(chunk.stages):
-                new = chunk.stages[self.age[number]](self.got[number])
+                new = chunk.stages[self.age[number]]([piece.value() for piece in self.got[number]])
                 spans.append((number, len(wants), len(wants) + len(new)))
                 wants += new
                 self.age[number] += 1
-        values, others = lax.optimization_barrier(([want[2] for want in wants], others))
-        wants = [want[:2] + (value,) for want, value in zip(wants, values)]
-        self.spans, self.moved = spans, self.at.exchange(wants)
+        merged, self.places = self.at.payloads(wants)
+        values, others = lax.optimization_barrier((list(merged.values()), others))
+        merged = dict(zip(merged, values))
+        self.moved = {key: self.at.move(value, *key, flip=key[0] == 0) for key, value in merged.items()}
+        self.spans = spans
+        for number, start, stop in spans:
+            self.mine[number] = [Piece(merged[key], *place) for key, *place in self.places[start:stop]]
         return others
 
     def close(self, *others):
         self.moved, others = lax.optimization_barrier((self.moved, others))
         for number, start, stop in self.spans:
-            self.got[number] = self.moved[start:stop]
+            self.got[number] = [Piece(self.moved[key], *place) for key, *place in self.places[start:stop]]
         return others
 
     def busy(self):
@@ -988,7 +1011,10 @@
         return self.done(chunk) and any(span[0] == self.chunks.index(chunk) for span in self.spans)
 
     def result(self, chunk):
-        return chunk.finish(self.got[self.chunks.index(chunk)])
+        number = self.chunks.index(chunk)
+        if isinstance(chunk, Gather):
+            return chunk.finish(self.got[number], self.mine[number])
+        return chunk.finish([piece.value() for piece in self.got[number]])
 
 
 def blocks_kernel(scalars, *refs, counts, loads, jobs):

time: 515 us -> 501 us (0.973)
  waiting for transfers between devices: 150 us -> 169 us
  starting transfers between devices: 85.5 us -> 66.9 us
  local copies, waits for them, and re-layouts: 60 us -> 47.9 us
    ppermute x80, starting transfers between devices: 79 us -> 59.4 us  [move(): return lax.ppermute(value, ('page', 'band'), pairs)]
    ppermute x80, waiting for transfers between devices: 139 us -> 156 us  [move(): return lax.ppermute(value, ('page', 'band'), pairs)]
    slice x15 -> x8, local copies, waits for them, and re-layouts: 15.3 us -> 6.28 us  [value(): return self.array[self.first:self.first + rows].reshape(self.shape)]
    unnamed x220 -> x216, local copies, waits for them, and re-layouts: 25.3 us -> 23.4 us
  transfers between devices with their start and end apart: 82 -> 82, of which waited for: 43 -> 50; matrix products, arithmetic and copies ran while one was open for 10% -> 6% of each run, Pallas kernels for 24% -> 25%
where the time goes in v5:
time: 501 us; the launch traced here: 496 us
  Pallas kernels  184 us (37%)
  waiting for transfers between devices  169 us (34%)
  starting transfers between devices  66.9 us (13%)
  local copies, waits for them, and re-layouts  47.9 us (10%)
  other arithmetic  25.3 us (5%)
    ppermute x80, waiting for transfers between devices, move(): return lax.ppermute(value, ('page', 'band'), pairs)  156 us
    ppermute x80, starting transfers between devices, move(): return lax.ppermute(value, ('page', 'band'), pairs)  59.4 us
    pallas_call x9, Pallas kernels, step(): pl.pallas_call(functools.partial(blocks_kernel, counts=(len(arrays), len(...  44.7 us
    pallas_call x2, Pallas kernels, attn_bwd(): pl.pallas_call(attn_bwd_kernel, name='attn_bwd', out_shape=[sds((D, HALF)...  34.6 us
    unnamed x216, local copies, waits for them, and re-layouts  23.4 us
    pallas_call x2, Pallas kernels, ffn_bwd(): pl.pallas_call(ffn_bwd_kernel, name='ffn_bwd', out_shape=[sds((2, D, D),...  22.1 us
    pallas_call x6, Pallas kernels, shuffle(): pl.pallas_call(functools.partial(shuffle_kernel, moves=moves, count=len(s...  21.4 us
    pallas_call x2, Pallas kernels, attn_fwd(): pl.pallas_call(functools.partial(attn_fwd_kernel, layer=layer), name='att...  15.6 us
  transfers between devices with their start and end apart: 82, of which 50 were waited for; matrix products, arithmetic and copies ran while one was open for 6% of the time, Pallas kernels for 25%

profile of v5, /device:TPU:0, one launch (start us, length us, event | category | flops | bytes accessed | tf_op | source)
XLA Modules:
  0.0 495.9 jit_solution(9187809840006359905)
XLA Ops:
  1.7 4.1 collective-permute-start
  23.8 4.0 collective-permute-start.4
  30.1 3.6 collective-permute-done.7
  33.7 3.7 collective-permute-done.4
  42.3 8.6 %collective-permute-done.13 = bf16[192,768]{1,0:T(8,128)(2,1)S(1)} collective-permute-done((bf16[192,768]{1,0:T(8,128)(2,1)S(1)}, bf16[192,768]{1,0:T(8,128)(2,1)S(1)}, u32[]{:S(2)}, u32[]{:S(2)}) %collective-permute-start.13) | collective-permute-done | bytes 294944 | tf_op jit(solution)/shard_map/ppermute | solution.py:748
  50.8 4.4 collective-permute-done.14
  64.3 3.1 all-to-all-start
  71.0 13.0 %all-to-all-done = bf16[32,2,288]{2,1,0:T(2,128)(2,1)S(1)} async-done(((bf16[32,2,288]{2,1,0:T(2,128)(2,1)}), bf16[32,2,288]{2,1,0:T(2,128)(2,1)S(1)}, u32[]{:S(2)}, u32[]{:S(2)}) %all-to-all-start) | async-done | bytes 36896 | tf_op jit(solution)/shard_map/all_to_all | solution.py:1410
  94.0 3.6 shuffle.6
  97.5 5.0 %embed.1 = f32[512,768]{1,0:T(8,128)} custom-call(s32[512,8]{1,0:T(8,128)S(1)} %copy.80.idx, bf16[512,768]{1,0:T(8,128)(2,1)S(1)} %bitcast.285, bf16[512,768]{1,0:T(8,128)(2,1)S(1)} %bitcast.286, bf16[512,768]{1,0:T(8,128)(2,1)} %bitcast.404, bf16[512,768]{1,0:T(8,128)(2,1)} %bitcast.405), custom_call_target="tpu_custom_call" | custom-call | flops 1610612736 | bytes 4718592 | tf_op jit(solution)/shard_map/embed/pallas_call | solution.py:85
  107.0 7.5 %collective-permute-done.22 = bf16[96,768]{1,0:T(8,128)(2,1)S(1)} collective-permute-done((bf16[96,768]{1,0:T(8,128)(2,1)S(1)}, bf16[96,768]{1,0:T(8,128)(2,1)S(1)}, u32[]{:S(2)}, u32[]{:S(2)}) %collective-permute-start.22) | collective-permute-done | bytes 147488 | tf_op jit(solution)/shard_map/ppermute | solution.py:748
  116.7 3.3 collective-permute-done.23.refs_3_
  129.8 3.8 shuffle.7
  136.9 7.5 %attn_fwd.2 = (bf16[512,384]{1,0:T(8,128)(2,1)S(1)}, bf16[512,384]{1,0:T(8,128)(2,1)S(1)}, bf16[512,384]{1,0:T(8,128)(2,1)S(1)}, bf16[256,384]{1,0:T(8,128)(2,1)S(1)}, bf16[256,384]{1,0:T(8,128)(2,1)S(1)}) custom-call(s32[1]{0:T(128)} %bitcast.core, bf16[256,768]{1,0:T(8,128)(2,1)S(1)} %get-tuple-element.454.xo, bf16[256,768]{1,0:T(8,128)(2,1)} %copy-done.76, ...), custom_call_target="tpu_custom_call" | custom-call | flops 1711276032 | bytes 4128768 | tf_op jit(solution)/shard_map/attn_fwd/pallas_call | solution.py:164
  146.0 3.4 out_norm.2
  149.4 4.1 collective-permute-done.26
  153.5 6.9 %collective-permute-done.27 = bf16[384,768]{1,0:T(8,128)(2,1)S(1)} collective-permute-done((bf16[384,768]{1,0:T(8,128)(2,1)S(1)}, bf16[384,768]{1,0:T(8,128)(2,1)S(1)}, u32[]{:S(2)}, u32[]{:S(2)}) %collective-permute-start.27) | collective-permute-done | bytes 589856 | tf_op jit(solution)/shard_map/ppermute | solution.py:748
  167.2 4.7 shuffle.8
  171.9 7.6 %ffn_fwd.2 = (bf16[512,1536]{1,0:T(8,128)(2,1)}, bf16[512,1536]{1,0:T(8,128)(2,1)}, f32[256,768]{1,0:T(8,128)S(1)}, bf16[256,768]{1,0:T(8,128)(2,1)S(1)}) custom-call(bf16[256,768]{1,0:T(8,128)(2,1)S(1)} %get-tuple-element.474.yo, bf16[256,768]{1,0:T(8,128)(2,1)S(1)} %collective-permute-done.36.ys, bf16[768,3072]{1,0:T(8,128)(2,1)} %bitcast.287, ...), custom_call_target="tpu_custom_call" | custom-call | flops 2415919104 | bytes 7864320 | tf_op jit(solution)/shard_map/ffn_fwd/pallas_call | solution.py:471
  187.9 4.0 collective-permute-done.33.refs_1_
  192.2 3.6 shuffle.9
  198.8 8.1 %attn_fwd.3 = (bf16[512,384]{1,0:T(8,128)(2,1)S(1)}, bf16[512,384]{1,0:T(8,128)(2,1)S(1)}, bf16[512,384]{1,0:T(8,128)(2,1)S(1)}, bf16[256,384]{1,0:T(8,128)(2,1)S(1)}, bf16[256,384]{1,0:T(8,128)(2,1)}) custom-call(s32[1]{0:T(128)} %bitcast.core, bf16[256,768]{1,0:T(8,128)(2,1)S(1)} %get-tuple-element.486.xo, bf16[256,768]{1,0:T(8,128)(2,1)} %copy-done.77, ...), custom_call_target="tpu_custom_call" | custom-call | flops 1711276032 | bytes 4128768 | tf_op jit(solution)/shard_map/attn_fwd/pallas_call | solution.py:164
  212.1 3.6 out_norm.3
  219.3 7.2 %ffn_fwd.3 = (bf16[512,1536]{1,0:T(8,128)(2,1)}, bf16[512,1536]{1,0:T(8,128)(2,1)}, f32[256,768]{1,0:T(8,128)S(1)}, bf16[256,768]{1,0:T(8,128)(2,1)S(1)}) custom-call(bf16[256,768]{1,0:T(8,128)(2,1)S(1)} %get-tuple-element.496.yo, bf16[256,768]{1,0:T(8,128)(2,1)S(1)} %collective-permute-done.43.ys, bf16[768,1536]{1,0:T(8,128)(2,1)} %bitcast.323, ...), custom_call_target="tpu_custom_call" | custom-call | flops 2415919104 | bytes 7864320 | tf_op jit(solution)/shard_map/ffn_fwd/pallas_call | solution.py:471
  236.3 10.9 %ffn_bwd.2 = (bf16[2,768,768]{2,1,0:T(8,128)(2,1)}, bf16[2,768,768]{2,1,0:T(8,128)(2,1)}, f32[8,1536]{1,0:T(8,128)S(1)}, f32[256,768]{1,0:T(8,128)}, bf16[256,768]{1,0:T(8,128)(2,1)S(1)}) custom-call(bf16[256,768]{1,0:T(8,128)(2,1)S(1)} %get-tuple-element.507.dfo, bf16[256,768]{1,0:T(8,128)(2,1)S(1)} %collective-permute-done.45.dfs, ...), custom_call_target="tpu_custom_call" | custom-call | flops 4831838208 | bytes 12582912 | tf_op jit(solution)/shard_map/ffn_bwd/pallas_call | solution.py:529
  249.5 3.9 blocks.9
  261.3 17.2 %attn_bwd.2 = (bf16[768,384]{1,0:T(8,128)(2,1)}, bf16[768,384]{1,0:T(8,128)(2,1)}, bf16[768,384]{1,0:T(8,128)(2,1)}, bf16[384,384]{1,0:T(8,128)(2,1)S(1)}, bf16[...) custom-call(s32[1]{0:T(128)} %bitcast.core, ...), custom_call_target="tpu_custom_call" | custom-call | flops 3825205248 | bytes 9437184 | tf_op jit(solution)/shard_map/attn_bwd/pallas_call | solution.py:271
  282.5 3.8 collective-permute-done.48.refs_1_
  286.3 4.9 blocks.10
  297.3 11.1 %ffn_bwd.3 = (bf16[2,768,768]{2,1,0:T(8,128)(2,1)}, bf16[2,768,768]{2,1,0:T(8,128)(2,1)}, f32[8,1536]{1,0:T(8,128)S(1)}, f32[256,768]{1,0:T(8,128)}, bf16[256,768]{1,0:T(8,128)(2,1)S(1)}) custom-call(bf16[256,768]{1,0:T(8,128)(2,1)S(1)} %get-tuple-element.552.dfo, bf16[256,768]{1,0:T(8,128)(2,1)S(1)} %collective-permute-done.54.dfs, ...), custom_call_target="tpu_custom_call" | custom-call | flops 4831838208 | bytes 12582912 | tf_op jit(solution)/shard_map/ffn_bwd/pallas_call | solution.py:529
  310.2 13.3 %collective-permute-done.52.refs_1_ = bf16[768,768]{1,0:T(8,128)(2,1)S(1)} collective-permute-done((bf16[768,768]{1,0:T(8,128)(2,1)S(1)}, bf16[768,768]{1,0:T(8,128)(2,1)S(1)}, u32[]{:S(2)}, u32[]{:S(2)}) %collective-permute-start.52) | collective-permute-done | bytes 1179680 | tf_op jit(solution)/shard_map/ppermute | solution.py:748
  324.9 5.6 %blocks.11 = (bf16[384,768]{1,0:T(8,128)(2,1)}, bf16[960,768]{1,0:T(8,128)(2,1)}, bf16[960,768]{1,0:T(8,128)(2,1)}, bf16[96,768]{1,0:T(8,128)(2,1)S(1)}, bf16[96...) custom-call(s32[4]{0:T(128)S(1)} %pad_add_fusion.2.scalars, ...), custom_call_target="tpu_custom_call" | custom-call | bytes 15925248 | tf_op jit(solution)/shard_map/blocks/pallas_call | solution.py:1248
  339.0 17.3 %attn_bwd.3 = (bf16[768,384]{1,0:T(8,128)(2,1)}, bf16[768,384]{1,0:T(8,128)(2,1)}, bf16[768,384]{1,0:T(8,128)(2,1)}, bf16[384,384]{1,0:T(8,128)(2,1)S(1)}, bf16[...) custom-call(s32[1]{0:T(128)} %bitcast.core, ...), custom_call_target="tpu_custom_call" | custom-call | flops 3825205248 | bytes 9437184 | tf_op jit(solution)/shard_map/attn_bwd/pallas_call | solution.py:271
  358.9 7.2 %collective-permute-done.57.refs_6_ = bf16[960,768]{1,0:T(8,128)(2,1)S(1)} collective-permute-done((bf16[960,768]{1,0:T(8,128)(2,1)}, bf16[960,768]{1,0:T(8,128)(2,1)S(1)}, u32[]{:S(2)}, u32[]{:S(2)}) %collective-permute-start.57) | collective-permute-done | bytes 1474592 | tf_op jit(solution)/shard_map/ppermute | solution.py:748
  368.0 6.8 %blocks.12 = (bf16[192,768]{1,0:T(8,128)(2,1)S(1)}, bf16[192,768]{1,0:T(8,128)(2,1)S(1)}, bf16[768,768]{1,0:T(8,128)(2,1)}, bf16[768,768]{1,0:T(8,128)(2,1)}, bf...) custom-call(s32[4]{0:T(128)S(1)} %pad_add_fusion.2.scalars, ...), custom_call_target="tpu_custom_call" | custom-call | bytes 17694720 | tf_op jit(solution)/shard_map/blocks/pallas_call | solution.py:1248
  383.7 2.9 table_grads.1
  387.5 10.5 %collective-permute-done.62.refs_19_ = bf16[192,768]{1,0:T(8,128)(2,1)S(1)} collective-permute-done((bf16[192,768]{1,0:T(8,128)(2,1)S(1)}, bf16[192,768]{1,0:T(8,128)(2,1)S(1)}, u32[]{:S(2)}, u32[]{:S(2)}) %collective-permute-start.62) | collective-permute-done | bytes 294944 | tf_op jit(solution)/shard_map/ppermute | solution.py:748
  398.0 4.2 collective-permute-done.64.refs_5_
  402.9 7.6 %blocks.13 = (bf16[96,768]{1,0:T(8,128)(2,1)S(1)}, bf16[384,768]{1,0:T(8,128)(2,1)}, bf16[704,768]{1,0:T(8,128)(2,1)}, bf16[832,768]{1,0:T(8,128)(2,1)}, f32[48,...) custom-call(s32[4]{0:T(128)S(1)} %pad_add_fusion.2.scalars, ...), custom_call_target="tpu_custom_call" | custom-call | bytes 15630336 | tf_op jit(solution)/shard_map/blocks/pallas_call | solution.py:1248
  416.1 11.4 %collective-permute-done.67.refs_14_ = bf16[96,768]{1,0:T(8,128)(2,1)S(1)} collective-permute-done((bf16[96,768]{1,0:T(8,128)(2,1)S(1)}, bf16[96,768]{1,0:T(8,128)(2,1)S(1)}, u32[]{:S(2)}, u32[]{:S(2)}) %collective-permute-start.67) | collective-permute-done | bytes 147488 | tf_op jit(solution)/shard_map/ppermute | solution.py:748
  429.9 5.0 %collective-permute-done.69.refs_6_ = bf16[704,768]{1,0:T(8,128)(2,1)} collective-permute-done((bf16[704,768]{1,0:T(8,128)(2,1)}, bf16[704,768]{1,0:T(8,128)(2,1)}, u32[]{:S(2)}, u32[]{:S(2)}) %collective-permute-start.69) | collective-permute-done | bytes 1081376 | tf_op jit(solution)/shard_map/ppermute | solution.py:748
  434.9 3.3 collective-permute-done.70.refs_8_
  438.2 6.7 %blocks.14 = (bf16[192,768]{1,0:T(8,128)(2,1)}, bf16[192,768]{1,0:T(8,128)(2,1)}, bf16[256,768]{1,0:T(8,128)(2,1)}, bf16[256,768]{1,0:T(8,128)(2,1)}, f32[48,768...) custom-call(s32[4]{0:T(128)S(1)} %pad_add_fusion.2.scalars, ...), custom_call_target="tpu_custom_call" | custom-call | bytes 11354112 | tf_op jit(solution)/shard_map/blocks/pallas_call | solution.py:1248
  450.4 4.3 all-to-all-start.1
  454.8 3.3 collective-permute-done.71.refs_10_
  459.0 4.4 blocks.15
  467.8 6.4 %collective-permute-done.75.refs_6_ = bf16[96,768]{1,0:T(8,128)(2,1)S(1)} collective-permute-done((bf16[96,768]{1,0:T(8,128)(2,1)S(1)}, bf16[96,768]{1,0:T(8,128)(2,1)S(1)}, u32[]{:S(2)}, u32[]{:S(2)}) %collective-permute-start.75) | collective-permute-done | bytes 147488 | tf_op jit(solution)/shard_map/ppermute | solution.py:748
  488.3 5.5 %collective-permute-done.77.refs_1_ = bf16[128,768]{1,0:T(8,128)(2,1)S(1)} collective-permute-done((bf16[128,768]{1,0:T(8,128)(2,1)S(1)}, bf16[128,768]{1,0:T(8,128)(2,1)S(1)}, u32[]{:S(2)}, u32[]{:S(2)}) %collective-permute-start.77) | collective-permute-done | bytes 196640 | tf_op jit(solution)/shard_map/ppermute | solution.py:748
  (515 shorter events, 187.3 us)
Async XLA Ops:
  1.7 13.4 %collective-permute-start = (bf16[128,768]{1,0:T(8,128)(2,1)}, bf16[128,768]{1,0:T(8,128)(2,1)S(1)}, u32[]{:S(2)}, u32[]{:S(2)}) collective-permute-start(bf16[128,768]{1,0:T(8,128)(2,1)} %bitcast.349), channel_id=1, source_target_pairs={{0,16},{1,17},{2,18},{3,19},{4,20},{5,21},{6,22},{7,23},{8,24},{9,... | collective-permute-start | bytes 589832 | tf_op jit(solution)/shard_map/ppermute | solution.py:748
  19.0 11.1 %collective-permute-start.5 = (bf16[96,768]{1,0:T(8,128)(2,1)S(1)}, bf16[96,768]{1,0:T(8,128)(2,1)S(1)}, u32[]{:S(2)}, u32[]{:S(2)}) collective-permute-start(bf16[96,768]{1,0:T(8,128)(2,1)S(1)} %bitcast.276), channel_id=1, source_target_pairs={{0,16},{1,17},{2,18},{3,19},{4,20},{5,21},{6,22},{7,23},{8,24},{9,... | collective-permute-start | bytes 442376 | tf_op jit(solution)/shard_map/ppermute | solution.py:748
  19.0 11.1 %collective-permute-start.6 = (bf16[96,768]{1,0:T(8,128)(2,1)S(1)}, bf16[96,768]{1,0:T(8,128)(2,1)S(1)}, u32[]{:S(2)}, u32[]{:S(2)}) collective-permute-start(bf16[96,768]{1,0:T(8,128)(2,1)S(1)} %bitcast.382), channel_id=1, source_target_pairs={{0,4},{1,5},{2,6},{3,7},{4,0},{5,1},{6,2},{7,3},{8,12},{9,13},{10,... | collective-permute-start | bytes 442376 | tf_op jit(solution)/shard_map/ppermute | solution.py:748
  23.8 13.5 %collective-permute-start.4 = (bf16[256,768]{1,0:T(8,128)(2,1)S(1)}, bf16[256,768]{1,0:T(8,128)(2,1)S(1)}, u32[]{:S(2)}, u32[]{:S(2)}) collective-permute-start(bf16[256,768]{1,0:T(8,128)(2,1)S(1)} %bitcast.364), channel_id=1, source_target_pairs={{0,8},{1,9},{2,10},{3,11},{4,12},{5,13},{6,14},{7,15},{8,0},{9,1},... | collective-permute-start | bytes 1179656 | tf_op jit(solution)/shard_map/ppermute | solution.py:748
  37.7 17.5 %collective-permute-start.15 = (bf16[256,768]{1,0:T(8,128)(2,1)S(1)}, bf16[256,768]{1,0:T(8,128)(2,1)S(1)}, u32[]{:S(2)}, u32[]{:S(2)}) collective-permute-start(bf16[256,768]{1,0:T(8,128)(2,1)S(1)} %bitcast.363), channel_id=1, source_target_pairs={{0,4},{1,5},{2,6},{3,7},{4,0},{5,1},{6,2},{7,3},{8,12},{9,13},{10,... | collective-permute-start | bytes 1179656 | tf_op jit(solution)/shard_map/ppermute | solution.py:748
  38.3 16.9 %collective-permute-start.16 = (bf16[256,768]{1,0:T(8,128)(2,1)S(1)}, bf16[256,768]{1,0:T(8,128)(2,1)S(1)}, u32[]{:S(2)}, u32[]{:S(2)}) collective-permute-start(bf16[256,768]{1,0:T(8,128)(2,1)S(1)} %bitcast.362), channel_id=1, source_target_pairs={{0,2},{1,3},{2,0},{3,1},{4,6},{5,7},{6,4},{7,5},{8,10},{9,11},{10,... | collective-permute-start | bytes 1179656 | tf_op jit(solution)/shard_map/ppermute | solution.py:748
  38.8 12.0 %collective-permute-start.13 = (bf16[192,768]{1,0:T(8,128)(2,1)S(1)}, bf16[192,768]{1,0:T(8,128)(2,1)S(1)}, u32[]{:S(2)}, u32[]{:S(2)}) collective-permute-start(bf16[192,768]{1,0:T(8,128)(2,1)S(1)} %bitcast.374), channel_id=1, source_target_pairs={{0,8},{1,9},{2,10},{3,11},{4,12},{5,13},{6,14},{7,15},{8,0},{9,1},... | collective-permute-start | bytes 884744 | tf_op jit(solution)/shard_map/ppermute | solution.py:748
  40.5 14.7 %collective-permute-start.14 = (bf16[192,768]{1,0:T(8,128)(2,1)S(1)}, bf16[192,768]{1,0:T(8,128)(2,1)S(1)}, u32[]{:S(2)}, u32[]{:S(2)}) collective-permute-start(bf16[192,768]{1,0:T(8,128)(2,1)S(1)} %bitcast.270), channel_id=1, source_target_pairs={{0,16},{1,17},{2,18},{3,19},{4,20},{5,21},{6,22},{7,23},{8,24},{9,... | collective-permute-start | bytes 884744 | tf_op jit(solution)/shard_map/ppermute | solution.py:748
  58.4 26.4 %collective-permute-start.19 = (bf16[704,768]{1,0:T(8,128)(2,1)}, bf16[704,768]{1,0:T(8,128)(2,1)}, u32[]{:S(2)}, u32[]{:S(2)}) collective-permute-start(bf16[704,768]{1,0:T(8,128)(2,1)} %pad_maximum_fusion.9.refs_2_), channel_id=1, source_target_pairs={{0,4},{1,5},{2,6},{3,7},{4,0},{5,1},{6,2},{7,3},{8,12},{9,13},{10,... | collective-permute-start | bytes 3244040 | tf_op jit(solution)/shard_map/ppermute | solution.py:748
  59.9 24.9 %collective-permute-start.20 = (bf16[704,768]{1,0:T(8,128)(2,1)S(1)}, bf16[704,768]{1,0:T(8,128)(2,1)}, u32[]{:S(2)}, u32[]{:S(2)}) collective-permute-start(bf16[704,768]{1,0:T(8,128)(2,1)S(1)} %pad_maximum_fusion.8.refs_0_), channel_id=1, source_target_pairs={{0,2},{1,3},{2,0},{3,1},{4,6},{5,7},{6,4},{7,5},{8,10},{9,11},{10,... | collective-permute-start | bytes 3244040 | tf_op jit(solution)/shard_map/ppermute | solution.py:748
  61.4 23.4 %collective-permute-start.17 = (bf16[384,768]{1,0:T(8,128)(2,1)}, bf16[384,768]{1,0:T(8,128)(2,1)}, u32[]{:S(2)}, u32[]{:S(2)}) collective-permute-start(bf16[384,768]{1,0:T(8,128)(2,1)} %bitcast.60), channel_id=1, source_target_pairs={{0,8},{1,9},{2,10},{3,11},{4,12},{5,13},{6,14},{7,15},{8,0},{9,1},... | collective-permute-start | bytes 1769480 | tf_op jit(solution)/shard_map/ppermute | solution.py:748
  64.3 19.7 %all-to-all-start = ((bf16[32,2,288]{2,1,0:T(2,128)(2,1)}), bf16[32,2,288]{2,1,0:T(2,128)(2,1)S(1)}, u32[]{:S(2)}, u32[]{:S(2)}) async-start(bf16[32,2,288]{2,1,0:T(2,128)(2,1)} %reshape.477), calls=%async_computation | async-start | bytes 98304 | tf_op jit(solution)/shard_map/all_to_all | solution.py:1410
  67.4 17.4 %collective-permute-start.18 = (bf16[96,768]{1,0:T(8,128)(2,1)S(1)}, bf16[96,768]{1,0:T(8,128)(2,1)S(1)}, u32[]{:S(2)}, u32[]{:S(2)}) collective-permute-start(bf16[96,768]{1,0:T(8,128)(2,1)S(1)} %bitcast.273), channel_id=1, source_target_pairs={{0,16},{1,17},{2,18},{3,19},{4,20},{5,21},{6,22},{7,23},{8,24},{9,... | collective-permute-start | bytes 442376 | tf_op jit(solution)/shard_map/ppermute | solution.py:748
  91.6 28.4 %collective-permute-start.23 = (bf16[768,768]{1,0:T(8,128)(2,1)}, bf16[768,768]{1,0:T(8,128)(2,1)}, u32[]{:S(2)}, u32[]{:S(2)}) collective-permute-start(bf16[768,768]{1,0:T(8,128)(2,1)} %pad_maximum_fusion.4.refs_2_), channel_id=1, source_target_pairs={{0,4},{1,5},{2,6},{3,7},{4,0},{5,1},{6,2},{7,3},{8,12},{9,13},{10,... | collective-permute-start | bytes 3538952 | tf_op jit(solution)/shard_map/ppermute | solution.py:748
  93.0 27.8 %collective-permute-start.24 = (bf16[768,768]{1,0:T(8,128)(2,1)S(1)}, bf16[768,768]{1,0:T(8,128)(2,1)}, u32[]{:S(2)}, u32[]{:S(2)}) collective-permute-start(bf16[768,768]{1,0:T(8,128)(2,1)S(1)} %pad_maximum_fusion.3.refs_0_), channel_id=1, source_target_pairs={{0,2},{1,3},{2,0},{3,1},{4,6},{5,7},{6,4},{7,5},{8,10},{9,11},{10,... | collective-permute-start | bytes 3538952 | tf_op jit(solution)/shard_map/ppermute | solution.py:748
  104.1 12.6 %collective-permute-start.21 = (bf16[192,768]{1,0:T(8,128)(2,1)S(1)}, bf16[192,768]{1,0:T(8,128)(2,1)S(1)}, u32[]{:S(2)}, u32[]{:S(2)}) collective-permute-start(bf16[192,768]{1,0:T(8,128)(2,1)S(1)} %bitcast.372), channel_id=1, source_target_pairs={{0,8},{1,9},{2,10},{3,11},{4,12},{5,13},{6,14},{7,15},{8,0},{9,1},... | collective-permute-start | bytes 884744 | tf_op jit(solution)/shard_map/ppermute | solution.py:748
  127.4 33.5 %collective-permute-start.28 = (bf16[960,768]{1,0:T(8,128)(2,1)}, bf16[960,768]{1,0:T(8,128)(2,1)}, u32[]{:S(2)}, u32[]{:S(2)}) collective-permute-start(bf16[960,768]{1,0:T(8,128)(2,1)} %pad_maximum_fusion.1.refs_2_), channel_id=1, source_target_pairs={{0,4},{1,5},{2,6},{3,7},{4,0},{5,1},{6,2},{7,3},{8,12},{9,13},{10,... | collective-permute-start | bytes 4423688 | tf_op jit(solution)/shard_map/ppermute | solution.py:748
  128.1 33.1 %collective-permute-start.29 = (bf16[960,768]{1,0:T(8,128)(2,1)S(1)}, bf16[960,768]{1,0:T(8,128)(2,1)}, u32[]{:S(2)}, u32[]{:S(2)}) collective-permute-start(bf16[960,768]{1,0:T(8,128)(2,1)S(1)} %pad_maximum_fusion.refs_0_), channel_id=1, source_target_pairs={{0,2},{1,3},{2,0},{3,1},{4,6},{5,7},{6,4},{7,5},{8,10},{9,11},{10,... | collective-permute-start | bytes 4423688 | tf_op jit(solution)/shard_map/ppermute | solution.py:748
  134.1 26.3 %collective-permute-start.27 = (bf16[384,768]{1,0:T(8,128)(2,1)S(1)}, bf16[384,768]{1,0:T(8,128)(2,1)S(1)}, u32[]{:S(2)}, u32[]{:S(2)}) collective-permute-start(bf16[384,768]{1,0:T(8,128)(2,1)S(1)} %bitcast.354), channel_id=1, source_target_pairs={{0,16},{1,17},{2,18},{3,19},{4,20},{5,21},{6,22},{7,23},{8,24},{9,... | collective-permute-start | bytes 1769480 | tf_op jit(solution)/shard_map/ppermute | solution.py:748
  136.1 17.3 %collective-permute-start.26 = (bf16[192,768]{1,0:T(8,128)(2,1)S(1)}, bf16[192,768]{1,0:T(8,128)(2,1)S(1)}, u32[]{:S(2)}, u32[]{:S(2)}) collective-permute-start(bf16[192,768]{1,0:T(8,128)(2,1)S(1)} %bitcast.373), channel_id=1, source_target_pairs={{0,8},{1,9},{2,10},{3,11},{4,12},{5,13},{6,14},{7,15},{8,0},{9,1},... | collective-permute-start | bytes 884744 | tf_op jit(solution)/shard_map/ppermute | solution.py:748
  164.8 27.2 %collective-permute-start.33 = (bf16[768,768]{1,0:T(8,128)(2,1)S(1)}, bf16[768,768]{1,0:T(8,128)(2,1)S(1)}, u32[]{:S(2)}, u32[]{:S(2)}) collective-permute-start(bf16[768,768]{1,0:T(8,128)(2,1)S(1)} %bitcast.264), channel_id=1, source_target_pairs={{0,8},{1,9},{2,10},{3,11},{4,12},{5,13},{6,14},{7,15},{8,0},{9,1},... | collective-permute-start | bytes 3538952 | tf_op jit(solution)/shard_map/ppermute | solution.py:748
  164.9 22.1 %collective-permute-start.34 = (bf16[576,768]{1,0:T(8,128)(2,1)S(1)}, bf16[576,768]{1,0:T(8,128)(2,1)S(1)}, u32[]{:S(2)}, u32[]{:S(2)}) collective-permute-start(bf16[576,768]{1,0:T(8,128)(2,1)S(1)} %pad_maximum_fusion.11.refs_2_), channel_id=1, source_target_pairs={{0,4},{1,5},{2,6},{3,7},{4,0},{5,1},{6,2},{7,3},{8,12},{9,13},{10,... | collective-permute-start | bytes 2654216 | tf_op jit(solution)/shard_map/ppermute | solution.py:748
  166.2 21.7 %collective-permute-start.35 = (bf16[576,768]{1,0:T(8,128)(2,1)S(1)}, bf16[576,768]{1,0:T(8,128)(2,1)S(1)}, u32[]{:S(2)}, u32[]{:S(2)}) collective-permute-start(bf16[576,768]{1,0:T(8,128)(2,1)S(1)} %pad_maximum_fusion.10.refs_0_), channel_id=1, source_target_pairs={{0,2},{1,3},{2,0},{3,1},{4,6},{5,7},{6,4},{7,5},{8,10},{9,11},{10,... | collective-permute-start | bytes 2654216 | tf_op jit(solution)/shard_map/ppermute | solution.py:748
  195.8 16.3 %collective-permute-start.42 = (bf16[768,384]{1,0:T(8,128)(2,1)}, bf16[768,384]{1,0:T(8,128)(2,1)}, u32[]{:S(2)}, u32[]{:S(2)}) collective-permute-start(bf16[768,384]{1,0:T(8,128)(2,1)} %bitcast.140.wom), channel_id=1, source_target_pairs={{0,1},{1,0},{2,3},{3,2},{4,5},{5,4},{6,7},{7,6},{8,9},{9,8},{10,11... | collective-permute-start | bytes 1769480 | tf_op jit(solution)/shard_map/ppermute | solution.py:748
  196.2 19.6 %collective-permute-start.38 = (bf16[384,768]{1,0:T(8,128)(2,1)S(1)}, bf16[384,768]{1,0:T(8,128)(2,1)}, u32[]{:S(2)}, u32[]{:S(2)}) collective-permute-start(bf16[384,768]{1,0:T(8,128)(2,1)S(1)} %bitcast.268), channel_id=1, source_target_pairs={{0,4},{1,5},{2,6},{3,7},{4,0},{5,1},{6,2},{7,3},{8,12},{9,13},{10,... | collective-permute-start | bytes 1769480 | tf_op jit(solution)/shard_map/ppermute | solution.py:748
  196.7 19.0 %collective-permute-start.39 = (bf16[384,768]{1,0:T(8,128)(2,1)S(1)}, bf16[384,768]{1,0:T(8,128)(2,1)}, u32[]{:S(2)}, u32[]{:S(2)}) collective-permute-start(bf16[384,768]{1,0:T(8,128)(2,1)S(1)} %bitcast.266), channel_id=1, source_target_pairs={{0,2},{1,3},{2,0},{3,1},{4,6},{5,7},{6,4},{7,5},{8,10},{9,11},{10,... | collective-permute-start | bytes 1769480 | tf_op jit(solution)/shard_map/ppermute | solution.py:748
  253.5 32.8 %collective-permute-start.48 = (bf16[896,768]{1,0:T(8,128)(2,1)}, bf16[896,768]{1,0:T(8,128)(2,1)}, u32[]{:S(2)}, u32[]{:S(2)}) collective-permute-start(bf16[896,768]{1,0:T(8,128)(2,1)} %get-tuple-element.518), channel_id=1, source_target_pairs={{0,2},{1,3},{2,0},{3,1},{4,6},{5,7},{6,4},{7,5},{8,10},{9,11},{10,... | collective-permute-start | bytes 4128776 | tf_op jit(solution)/shard_map/ppermute | solution.py:748
  254.2 28.3 %collective-permute-start.47 = (bf16[768,768]{1,0:T(8,128)(2,1)}, bf16[768,768]{1,0:T(8,128)(2,1)}, u32[]{:S(2)}, u32[]{:S(2)}) collective-permute-start(bf16[768,768]{1,0:T(8,128)(2,1)} %get-tuple-element.517), channel_id=1, source_target_pairs={{0,4},{1,5},{2,6},{3,7},{4,0},{5,1},{6,2},{7,3},{8,12},{9,13},{10,... | collective-permute-start | bytes 3538952 | tf_op jit(solution)/shard_map/ppermute | solution.py:748
  295.2 28.4 %collective-permute-start.52 = (bf16[768,768]{1,0:T(8,128)(2,1)S(1)}, bf16[768,768]{1,0:T(8,128)(2,1)S(1)}, u32[]{:S(2)}, u32[]{:S(2)}) collective-permute-start(bf16[768,768]{1,0:T(8,128)(2,1)S(1)} %copy-done.95), channel_id=1, source_target_pairs={{0,4},{1,5},{2,6},{3,7},{4,0},{5,1},{6,2},{7,3},{8,12},{9,13},{10,... | collective-permute-start | bytes 3538952 | tf_op jit(solution)/shard_map/ppermute | solution.py:748
  295.8 28.1 %collective-permute-start.53 = (bf16[768,768]{1,0:T(8,128)(2,1)S(1)}, bf16[768,768]{1,0:T(8,128)(2,1)S(1)}, u32[]{:S(2)}, u32[]{:S(2)}) collective-permute-start(bf16[768,768]{1,0:T(8,128)(2,1)S(1)} %copy-done.94), channel_id=1, source_target_pairs={{0,2},{1,3},{2,0},{3,1},{4,6},{5,7},{6,4},{7,5},{8,10},{9,11},{10,... | collective-permute-start | bytes 3538952 | tf_op jit(solution)/shard_map/ppermute | solution.py:748
  332.0 34.1 %collective-permute-start.57 = (bf16[960,768]{1,0:T(8,128)(2,1)}, bf16[960,768]{1,0:T(8,128)(2,1)S(1)}, u32[]{:S(2)}, u32[]{:S(2)}) collective-permute-start(bf16[960,768]{1,0:T(8,128)(2,1)} %get-tuple-element.572), channel_id=1, source_target_pairs={{0,4},{1,5},{2,6},{3,7},{4,0},{5,1},{6,2},{7,3},{8,12},{9,13},{10,... | collective-permute-start | bytes 4423688 | tf_op jit(solution)/shard_map/ppermute | solution.py:748
  333.4 33.5 %collective-permute-start.58 = (bf16[960,768]{1,0:T(8,128)(2,1)}, bf16[960,768]{1,0:T(8,128)(2,1)S(1)}, u32[]{:S(2)}, u32[]{:S(2)}) collective-permute-start(bf16[960,768]{1,0:T(8,128)(2,1)} %get-tuple-element.573), channel_id=1, source_target_pairs={{0,2},{1,3},{2,0},{3,1},{4,6},{5,7},{6,4},{7,5},{8,10},{9,11},{10,... | collective-permute-start | bytes 4423688 | tf_op jit(solution)/shard_map/ppermute | solution.py:748
  336.5 22.4 %collective-permute-start.56 = (bf16[384,768]{1,0:T(8,128)(2,1)S(1)}, bf16[384,768]{1,0:T(8,128)(2,1)S(1)}, u32[]{:S(2)}, u32[]{:S(2)}) collective-permute-start(bf16[384,768]{1,0:T(8,128)(2,1)S(1)} %copy-done.96), channel_id=1, source_target_pairs={{0,8},{1,9},{2,10},{3,11},{4,12},{5,13},{6,14},{7,15},{8,0},{9,1},... | collective-permute-start | bytes 1769480 | tf_op jit(solution)/shard_map/ppermute | solution.py:748
  375.5 26.7 %collective-permute-start.64 = (bf16[768,768]{1,0:T(8,128)(2,1)}, bf16[768,768]{1,0:T(8,128)(2,1)}, u32[]{:S(2)}, u32[]{:S(2)}) collective-permute-start(bf16[768,768]{1,0:T(8,128)(2,1)} %get-tuple-element.612), channel_id=1, source_target_pairs={{0,4},{1,5},{2,6},{3,7},{4,0},{5,1},{6,2},{7,3},{8,12},{9,13},{10,... | collective-permute-start | bytes 3538952 | tf_op jit(solution)/shard_map/ppermute | solution.py:748
  376.5 26.4 %collective-permute-start.65 = (bf16[768,768]{1,0:T(8,128)(2,1)}, bf16[768,768]{1,0:T(8,128)(2,1)}, u32[]{:S(2)}, u32[]{:S(2)}) collective-permute-start(bf16[768,768]{1,0:T(8,128)(2,1)} %get-tuple-element.613), channel_id=1, source_target_pairs={{0,2},{1,3},{2,0},{3,1},{4,6},{5,7},{6,4},{7,5},{8,10},{9,11},{10,... | collective-permute-start | bytes 3538952 | tf_op jit(solution)/shard_map/ppermute | solution.py:748
  381.6 16.4 %collective-permute-start.62 = (bf16[192,768]{1,0:T(8,128)(2,1)S(1)}, bf16[192,768]{1,0:T(8,128)(2,1)S(1)}, u32[]{:S(2)}, u32[]{:S(2)}) collective-permute-start(bf16[192,768]{1,0:T(8,128)(2,1)S(1)} %get-tuple-element.610), channel_id=1, source_target_pairs={{0,16},{1,17},{2,18},{3,19},{4,20},{5,21},{6,22},{7,23},{8,24},{9,... | collective-permute-start | bytes 884744 | tf_op jit(solution)/shard_map/ppermute | solution.py:748
  381.7 16.3 %collective-permute-start.63 = (bf16[192,768]{1,0:T(8,128)(2,1)S(1)}, bf16[192,768]{1,0:T(8,128)(2,1)S(1)}, u32[]{:S(2)}, u32[]{:S(2)}) collective-permute-start(bf16[192,768]{1,0:T(8,128)(2,1)S(1)} %get-tuple-element.611), channel_id=1, source_target_pairs={{0,8},{1,9},{2,10},{3,11},{4,12},{5,13},{6,14},{7,15},{8,0},{9,1},... | collective-permute-start | bytes 884744 | tf_op jit(solution)/shard_map/ppermute | solution.py:748
  410.5 27.7 %collective-permute-start.70 = (bf16[832,768]{1,0:T(8,128)(2,1)}, bf16[832,768]{1,0:T(8,128)(2,1)}, u32[]{:S(2)}, u32[]{:S(2)}) collective-permute-start(bf16[832,768]{1,0:T(8,128)(2,1)} %get-tuple-element.642), channel_id=1, source_target_pairs={{0,2},{1,3},{2,0},{3,1},{4,6},{5,7},{6,4},{7,5},{8,10},{9,11},{10,... | collective-permute-start | bytes 3833864 | tf_op jit(solution)/shard_map/ppermute | solution.py:748
  411.8 23.1 %collective-permute-start.69 = (bf16[704,768]{1,0:T(8,128)(2,1)}, bf16[704,768]{1,0:T(8,128)(2,1)}, u32[]{:S(2)}, u32[]{:S(2)}) collective-permute-start(bf16[704,768]{1,0:T(8,128)(2,1)} %get-tuple-element.641), channel_id=1, source_target_pairs={{0,4},{1,5},{2,6},{3,7},{4,0},{5,1},{6,2},{7,3},{8,12},{9,13},{10,... | collective-permute-start | bytes 3244040 | tf_op jit(solution)/shard_map/ppermute | solution.py:748
  414.4 15.5 %collective-permute-start.68 = (bf16[384,768]{1,0:T(8,128)(2,1)}, bf16[384,768]{1,0:T(8,128)(2,1)}, u32[]{:S(2)}, u32[]{:S(2)}) collective-permute-start(bf16[384,768]{1,0:T(8,128)(2,1)} %get-tuple-element.640), channel_id=1, source_target_pairs={{0,8},{1,9},{2,10},{3,11},{4,12},{5,13},{6,14},{7,15},{8,0},{9,1},... | collective-permute-start | bytes 1769480 | tf_op jit(solution)/shard_map/ppermute | solution.py:748
  415.0 12.6 %collective-permute-start.67 = (bf16[96,768]{1,0:T(8,128)(2,1)S(1)}, bf16[96,768]{1,0:T(8,128)(2,1)S(1)}, u32[]{:S(2)}, u32[]{:S(2)}) collective-permute-start(bf16[96,768]{1,0:T(8,128)(2,1)S(1)} %get-tuple-element.639), channel_id=1, source_target_pairs={{0,16},{1,17},{2,18},{3,19},{4,20},{5,21},{6,22},{7,23},{8,24},{9,... | collective-permute-start | bytes 442376 | tf_op jit(solution)/shard_map/ppermute | solution.py:748
  445.6 12.5 %collective-permute-start.71 = (bf16[192,768]{1,0:T(8,128)(2,1)}, bf16[192,768]{1,0:T(8,128)(2,1)S(1)}, u32[]{:S(2)}, u32[]{:S(2)}) collective-permute-start(bf16[192,768]{1,0:T(8,128)(2,1)} %get-tuple-element.660), channel_id=1, source_target_pairs={{0,16},{1,17},{2,18},{3,19},{4,20},{5,21},{6,22},{7,23},{8,24},{9,... | collective-permute-start | bytes 884744 | tf_op jit(solution)/shard_map/ppermute | solution.py:748
  445.6 12.5 %collective-permute-start.72 = (bf16[192,768]{1,0:T(8,128)(2,1)}, bf16[192,768]{1,0:T(8,128)(2,1)S(1)}, u32[]{:S(2)}, u32[]{:S(2)}) collective-permute-start(bf16[192,768]{1,0:T(8,128)(2,1)} %get-tuple-element.661), channel_id=1, source_target_pairs={{0,8},{1,9},{2,10},{3,11},{4,12},{5,13},{6,14},{7,15},{8,0},{9,1},... | collective-permute-start | bytes 884744 | tf_op jit(solution)/shard_map/ppermute | solution.py:748
  446.9 11.1 %collective-permute-start.73 = (bf16[256,768]{1,0:T(8,128)(2,1)}, bf16[256,768]{1,0:T(8,128)(2,1)S(1)}, u32[]{:S(2)}, u32[]{:S(2)}) collective-permute-start(bf16[256,768]{1,0:T(8,128)(2,1)} %get-tuple-element.662), channel_id=1, source_target_pairs={{0,4},{1,5},{2,6},{3,7},{4,0},{5,1},{6,2},{7,3},{8,12},{9,13},{10,... | collective-permute-start | bytes 1179656 | tf_op jit(solution)/shard_map/ppermute | solution.py:748
  450.4 14.3 %all-to-all-start.1 = ((f32[32,1,576]{2,1,0:T(1,128)}), f32[32,1,576]{2,1,0:T(1,128)S(1)}, u32[]{:S(2)}, u32[]{:S(2)}) async-start(f32[32,1,576]{2,1,0:T(1,128)} %copy.86), calls=%async_computation.1 | async-start | bytes 163840 | tf_op jit(solution)/shard_map/all_to_all | solution.py:1612
  463.5 12.9 %collective-permute-start.76 = (bf16[256,768]{1,0:T(8,128)(2,1)}, bf16[256,768]{1,0:T(8,128)(2,1)S(1)}, u32[]{:S(2)}, u32[]{:S(2)}) collective-permute-start(bf16[256,768]{1,0:T(8,128)(2,1)} %get-tuple-element.681), channel_id=1, source_target_pairs={{0,8},{1,9},{2,10},{3,11},{4,12},{5,13},{6,14},{7,15},{8,0},{9,1},... | collective-permute-start | bytes 1179656 | tf_op jit(solution)/shard_map/ppermute | solution.py:748
  467.7 14.8 %collective-permute-start.79 = (f32[24,3072]{1,0:T(8,128)S(1)}, f32[24,3072]{1,0:T(8,128)S(1)}, u32[]{:S(2)}, u32[]{:S(2)}) collective-permute-start(f32[24,3072]{1,0:T(8,128)S(1)} %get-tuple-element.704), channel_id=1, source_target_pairs={{0,1},{1,0},{2,3},{3,2},{4,5},{5,4},{6,7},{7,6},{8,9},{9,8},{10,11... | collective-permute-start | bytes 884744 | tf_op jit(solution)/shard_map/ppermute | solution.py:748
  481.3 12.4 %collective-permute-start.77 = (bf16[128,768]{1,0:T(8,128)(2,1)S(1)}, bf16[128,768]{1,0:T(8,128)(2,1)S(1)}, u32[]{:S(2)}, u32[]{:S(2)}) collective-permute-start(bf16[128,768]{1,0:T(8,128)(2,1)S(1)} %get-tuple-element.690), channel_id=1, source_target_pairs={{0,16},{1,17},{2,18},{3,19},{4,20},{5,21},{6,22},{7,23},{8,24},{9,... | collective-permute-start | bytes 589832 | tf_op jit(solution)/shard_map/ppermute | solution.py:748
  (140 other events, 722.2 us)

commit v6 on v5

--- a/solution.py
+++ b/solution.py
@@ -256,7 +256,7 @@
 
     @pl.when(step == PAIRS - 1)
     def _():
-        dxo[...] = acc[:half, :]
+        dxo[...] = acc[:half, :].astype(BF16)
         dxs[...] = acc[half:, :].astype(BF16)
 
 
@@ -276,7 +276,7 @@
             sds((HALF, HALF), BF16),
             sds((HALF, HALF), BF16),
             sds((8, HALF), F32),
-            sds((half, D), F32),
+            sds((half, D), BF16),
             sds((half, D), BF16),
         ],
         grid_spec=pltpu.PrefetchScalarGridSpec(
@@ -366,7 +366,7 @@
 
 
 def add_norm_kernel(base, part, recv, small, y, yb, n, rstd, *, layer):
-    h = base[...] + part[...] + recv[...].astype(F32) + small[ROW_DOWN + layer : ROW_DOWN + layer + 1, :]
+    h = base[...] + part[...].astype(F32) + recv[...].astype(F32) + small[ROW_DOWN + layer : ROW_DOWN + layer + 1, :]
     row = 2 * layer + 1
     norm_rows(
         h, small[ROW_GAIN + row : ROW_GAIN + row + 1, :], small[ROW_SHIFT + row : ROW_SHIFT + row + 1, :],
@@ -390,7 +390,7 @@
 def norm_bwd_kernel(*refs, row, summed):
     if summed:
         base, part, recv, n, rstd, small, gh, ghb, sums = refs
-        gz = base[...] + part[...] + recv[...].astype(F32)
+        gz = base[...] + part[...].astype(F32) + recv[...].astype(F32)
     else:
         base, live, n, rstd, small, gh, ghb, sums = refs
         gz = base[...].astype(F32) * live[...]
@@ -448,7 +448,7 @@
 
     @pl.when(j == FF_STEPS - 1)
     def _():
-        po[...] = acc[:half, :]
+        po[...] = acc[:half, :].astype(BF16)
         ps[...] = acc[half:, :].astype(BF16)
 
 
@@ -471,7 +471,7 @@
     return pl.pallas_call(
         functools.partial(ffn_fwd_kernel, layer=layer),
         name="ffn_fwd",
-        out_shape=[sds((tokens, width), BF16)] * 2 + [sds((half, D), F32), sds((half, D), BF16)],
+        out_shape=[sds((tokens, width), BF16)] * 2 + [sds((half, D), BF16)] * 2,
         grid=(FF_STEPS,),
         in_specs=[
             whole((half, D)),
@@ -517,7 +517,7 @@
 
     @pl.when(j == FF_STEPS - 1)
     def _():
-        po[...] = acc[:half, :]
+        po[...] = acc[:half, :].astype(BF16)
         ps[...] = acc[half:, :].astype(BF16)
 
 
@@ -533,7 +533,7 @@
             sds((2, D, D), BF16),
             sds((2, D, D), BF16),
             sds((8, width), F32),
-            sds((half, D), F32),
+            sds((half, D), BF16),
             sds((half, D), BF16),
         ],
         grid=(FF_STEPS,),
@@ -1584,7 +1584,7 @@
     sources = line.close(*sources)
     att0 = attn_chunk(dqkv, dwo, False)
     sources = line.step(*sources)
-    grad_x = sources[0] + sources[1] + sources[2].astype(F32)
+    grad_x = sources[0] + sources[1].astype(F32) + sources[2].astype(F32)
     grad_low = grad_x.astype(BF16)
     table_parts = table_grads(index, grad_low, at.swap(grad_low), chips * table_rows)
     table_parts = line.close(*table_parts)

time: 501 us -> 501 us (level)
    unnamed x216 -> x210, local copies, waits for them, and re-layouts: 23.4 us -> 19.3 us
  transfers between devices with their start and end apart: 82 -> 82, of which waited for: 50 -> 50; matrix products, arithmetic and copies ran while one was open for 6% -> 6% of each run, Pallas kernels for 25% -> 26%
where the time goes in v6:
time: 501 us; the launch traced here: 495 us
  Pallas kernels  187 us (37%)
  waiting for transfers between devices  170 us (34%)
  starting transfers between devices  67.1 us (13%)
  local copies, waits for them, and re-layouts  42.9 us (9%)
  other arithmetic  25.7 us (5%)
    ppermute x80, waiting for transfers between devices, move(): return lax.ppermute(value, ('page', 'band'), pairs)  157 us
    ppermute x80, starting transfers between devices, move(): return lax.ppermute(value, ('page', 'band'), pairs)  60 us
    pallas_call x9, Pallas kernels, step(): pl.pallas_call(functools.partial(blocks_kernel, counts=(len(arrays), len(...  45.2 us
    pallas_call x2, Pallas kernels, attn_bwd(): pl.pallas_call(attn_bwd_kernel, name='attn_bwd', out_shape=[sds((D, HALF)...  33.6 us
    pallas_call x2, Pallas kernels, ffn_bwd(): pl.pallas_call(ffn_bwd_kernel, name='ffn_bwd', out_shape=[sds((2, D, D),...  23 us
    pallas_call x6, Pallas kernels, shuffle(): pl.pallas_call(functools.partial(shuffle_kernel, moves=moves, count=len(s...  21.2 us
    unnamed x210, local copies, waits for them, and re-layouts  19.3 us
    pallas_call x2, Pallas kernels, attn_fwd(): pl.pallas_call(functools.partial(attn_fwd_kernel, layer=layer), name='att...  15.6 us
  transfers between devices with their start and end apart: 82, of which 50 were waited for; matrix products, arithmetic and copies ran while one was open for 6% of the time, Pallas kernels for 26%

profile of v6, /device:TPU:0, one launch (start us, length us, event | category | flops | bytes accessed | tf_op | source)
XLA Modules:
  0.0 495.0 jit_solution(6469777403292697764)
XLA Ops:
  1.7 4.1 collective-permute-start
  23.8 4.0 collective-permute-start.4
  30.0 3.6 collective-permute-done.7
  33.7 3.7 collective-permute-done.4
  42.2 8.6 %collective-permute-done.13 = bf16[192,768]{1,0:T(8,128)(2,1)S(1)} collective-permute-done((bf16[192,768]{1,0:T(8,128)(2,1)S(1)}, bf16[192,768]{1,0:T(8,128)(2,1)S(1)}, u32[]{:S(2)}, u32[]{:S(2)}) %collective-permute-start.13) | collective-permute-done | bytes 294944 | tf_op jit(solution)/shard_map/ppermute | solution.py:748
  50.8 4.4 collective-permute-done.14
  64.3 3.1 all-to-all-start
  71.0 13.0 %all-to-all-done = bf16[32,2,288]{2,1,0:T(2,128)(2,1)S(1)} async-done(((bf16[32,2,288]{2,1,0:T(2,128)(2,1)}), bf16[32,2,288]{2,1,0:T(2,128)(2,1)S(1)}, u32[]{:S(2)}, u32[]{:S(2)}) %all-to-all-start) | async-done | bytes 36896 | tf_op jit(solution)/shard_map/all_to_all | solution.py:1410
  94.0 3.6 shuffle.6
  97.6 5.1 %embed.1 = f32[512,768]{1,0:T(8,128)} custom-call(s32[512,8]{1,0:T(8,128)S(1)} %copy.80.idx, bf16[512,768]{1,0:T(8,128)(2,1)S(1)} %bitcast.285, bf16[512,768]{1,0:T(8,128)(2,1)S(1)} %bitcast.286, bf16[512,768]{1,0:T(8,128)(2,1)} %bitcast.404, bf16[512,768]{1,0:T(8,128)(2,1)} %bitcast.405), custom_call_target="tpu_custom_call" | custom-call | flops 1610612736 | bytes 4718592 | tf_op jit(solution)/shard_map/embed/pallas_call | solution.py:85
  107.1 7.5 %collective-permute-done.22 = bf16[96,768]{1,0:T(8,128)(2,1)S(1)} collective-permute-done((bf16[96,768]{1,0:T(8,128)(2,1)S(1)}, bf16[96,768]{1,0:T(8,128)(2,1)S(1)}, u32[]{:S(2)}, u32[]{:S(2)}) %collective-permute-start.22) | collective-permute-done | bytes 147488 | tf_op jit(solution)/shard_map/ppermute | solution.py:748
  116.7 3.2 collective-permute-done.23.refs_3_
  129.8 3.8 shuffle.7
  136.9 7.5 %attn_fwd.2 = (bf16[512,384]{1,0:T(8,128)(2,1)S(1)}, bf16[512,384]{1,0:T(8,128)(2,1)S(1)}, bf16[512,384]{1,0:T(8,128)(2,1)S(1)}, bf16[256,384]{1,0:T(8,128)(2,1)S(1)}, bf16[256,384]{1,0:T(8,128)(2,1)S(1)}) custom-call(s32[1]{0:T(128)} %bitcast.core, bf16[256,768]{1,0:T(8,128)(2,1)S(1)} %get-tuple-element.454.xo, bf16[256,768]{1,0:T(8,128)(2,1)} %copy-done.72, ...), custom_call_target="tpu_custom_call" | custom-call | flops 1711276032 | bytes 4128768 | tf_op jit(solution)/shard_map/attn_fwd/pallas_call | solution.py:164
  146.0 3.4 out_norm.2
  149.4 4.1 collective-permute-done.26
  153.5 6.9 %collective-permute-done.27 = bf16[384,768]{1,0:T(8,128)(2,1)S(1)} collective-permute-done((bf16[384,768]{1,0:T(8,128)(2,1)S(1)}, bf16[384,768]{1,0:T(8,128)(2,1)S(1)}, u32[]{:S(2)}, u32[]{:S(2)}) %collective-permute-start.27) | collective-permute-done | bytes 589856 | tf_op jit(solution)/shard_map/ppermute | solution.py:748
  167.2 4.7 shuffle.8
  172.0 7.5 %ffn_fwd.2 = (bf16[512,1536]{1,0:T(8,128)(2,1)}, bf16[512,1536]{1,0:T(8,128)(2,1)}, bf16[256,768]{1,0:T(8,128)(2,1)S(1)}, bf16[256,768]{1,0:T(8,128)(2,1)S(1)}) custom-call(bf16[256,768]{1,0:T(8,128)(2,1)S(1)} %get-tuple-element.474.yo, bf16[256,768]{1,0:T(8,128)(2,1)S(1)} %collective-permute-done.36.ys, bf16[768,3072]{1,0:T(8,128)(2,1)} %bitcast.287, ...), custom_call_target="tpu_custom_call" | custom-call | flops 2415919104 | bytes 7864320 | tf_op jit(solution)/shard_map/ffn_fwd/pallas_call | solution.py:471
  188.0 4.0 collective-permute-done.33.refs_1_
  193.0 3.5 shuffle.9
  199.6 8.1 %attn_fwd.3 = (bf16[512,384]{1,0:T(8,128)(2,1)S(1)}, bf16[512,384]{1,0:T(8,128)(2,1)S(1)}, bf16[512,384]{1,0:T(8,128)(2,1)S(1)}, bf16[256,384]{1,0:T(8,128)(2,1)S(1)}, bf16[256,384]{1,0:T(8,128)(2,1)}) custom-call(s32[1]{0:T(128)} %bitcast.core, bf16[256,768]{1,0:T(8,128)(2,1)S(1)} %get-tuple-element.486.xo, bf16[256,768]{1,0:T(8,128)(2,1)} %copy-done.73, ...), custom_call_target="tpu_custom_call" | custom-call | flops 1711276032 | bytes 4128768 | tf_op jit(solution)/shard_map/attn_fwd/pallas_call | solution.py:164
  212.9 3.6 out_norm.3
  220.1 7.5 %ffn_fwd.3 = (bf16[512,1536]{1,0:T(8,128)(2,1)}, bf16[512,1536]{1,0:T(8,128)(2,1)}, bf16[256,768]{1,0:T(8,128)(2,1)S(1)}, bf16[256,768]{1,0:T(8,128)(2,1)}) custom-call(bf16[256,768]{1,0:T(8,128)(2,1)S(1)} %get-tuple-element.496.yo, bf16[256,768]{1,0:T(8,128)(2,1)S(1)} %collective-permute-done.43.ys, bf16[768,1536]{1,0:T(8,128)(2,1)} %bitcast.323, ...), custom_call_target="tpu_custom_call" | custom-call | flops 2415919104 | bytes 7864320 | tf_op jit(solution)/shard_map/ffn_fwd/pallas_call | solution.py:471
  236.7 11.5 %ffn_bwd.2 = (bf16[2,768,768]{2,1,0:T(8,128)(2,1)}, bf16[2,768,768]{2,1,0:T(8,128)(2,1)}, f32[8,1536]{1,0:T(8,128)S(1)}, bf16[256,768]{1,0:T(8,128)(2,1)S(1)}, bf16[256,768]{1,0:T(8,128)(2,1)S(1)}) custom-call(bf16[256,768]{1,0:T(8,128)(2,1)S(1)} %get-tuple-element.507.dfo, bf16[256,768]{1,0:T(8,128)(2,1)S(1)} %collective-permute-done.45.dfs, ...), custom_call_target="tpu_custom_call" | custom-call | flops 4831838208 | bytes 12582912 | tf_op jit(solution)/shard_map/ffn_bwd/pallas_call | solution.py:529
  249.7 4.1 blocks.9
  261.4 16.8 %attn_bwd.2 = (bf16[768,384]{1,0:T(8,128)(2,1)}, bf16[768,384]{1,0:T(8,128)(2,1)}, bf16[768,384]{1,0:T(8,128)(2,1)}, bf16[384,384]{1,0:T(8,128)(2,1)S(1)}, bf16[...) custom-call(s32[1]{0:T(128)} %bitcast.core, ...), custom_call_target="tpu_custom_call" | custom-call | flops 3825205248 | bytes 9437184 | tf_op jit(solution)/shard_map/attn_bwd/pallas_call | solution.py:271
  282.8 3.8 collective-permute-done.48.refs_1_
  286.6 5.0 %blocks.10 = (bf16[768,768]{1,0:T(8,128)(2,1)}, bf16[768,768]{1,0:T(8,128)(2,1)}, bf16[192,768]{1,0:T(8,128)(2,1)S(1)}, bf16[192,768]{1,0:T(8,128)(2,1)S(1)}, bf...) custom-call(s32[4]{0:T(128)S(1)} %pad_add_fusion.2.scalars, bf16[1536,768]{1,0:T(8,128)(2,1)} %bitcast.304, ...), custom_call_target="tpu_custom_call" | custom-call | bytes 14450688 | tf_op jit(solution)/shard_map/blocks/pallas_call | solution.py:1248
  291.7 3.1 norm_bwd.6
  296.9 11.6 %ffn_bwd.3 = (bf16[2,768,768]{2,1,0:T(8,128)(2,1)}, bf16[2,768,768]{2,1,0:T(8,128)(2,1)}, f32[8,1536]{1,0:T(8,128)S(1)}, bf16[256,768]{1,0:T(8,128)(2,1)S(1)}, bf16[256,768]{1,0:T(8,128)(2,1)S(1)}) custom-call(bf16[256,768]{1,0:T(8,128)(2,1)S(1)} %get-tuple-element.552.dfo, bf16[256,768]{1,0:T(8,128)(2,1)S(1)} %collective-permute-done.54.dfs, ...), custom_call_target="tpu_custom_call" | custom-call | flops 4831838208 | bytes 12582912 | tf_op jit(solution)/shard_map/ffn_bwd/pallas_call | solution.py:529
  310.3 12.8 %collective-permute-done.52.refs_1_ = bf16[768,768]{1,0:T(8,128)(2,1)S(1)} collective-permute-done((bf16[768,768]{1,0:T(8,128)(2,1)S(1)}, bf16[768,768]{1,0:T(8,128)(2,1)S(1)}, u32[]{:S(2)}, u32[]{:S(2)}) %collective-permute-start.52) | collective-permute-done | bytes 1179680 | tf_op jit(solution)/shard_map/ppermute | solution.py:748
  324.6 5.7 %blocks.11 = (bf16[384,768]{1,0:T(8,128)(2,1)}, bf16[960,768]{1,0:T(8,128)(2,1)}, bf16[960,768]{1,0:T(8,128)(2,1)}, bf16[96,768]{1,0:T(8,128)(2,1)S(1)}, bf16[96...) custom-call(s32[4]{0:T(128)S(1)} %pad_add_fusion.2.scalars, ...), custom_call_target="tpu_custom_call" | custom-call | bytes 15925248 | tf_op jit(solution)/shard_map/blocks/pallas_call | solution.py:1248
  338.6 16.8 %attn_bwd.3 = (bf16[768,384]{1,0:T(8,128)(2,1)}, bf16[768,384]{1,0:T(8,128)(2,1)}, bf16[768,384]{1,0:T(8,128)(2,1)}, bf16[384,384]{1,0:T(8,128)(2,1)S(1)}, bf16[...) custom-call(s32[1]{0:T(128)} %bitcast.core, ...), custom_call_target="tpu_custom_call" | custom-call | flops 3825205248 | bytes 9437184 | tf_op jit(solution)/shard_map/attn_bwd/pallas_call | solution.py:271
  358.1 7.2 %collective-permute-done.57.refs_6_ = bf16[960,768]{1,0:T(8,128)(2,1)S(1)} collective-permute-done((bf16[960,768]{1,0:T(8,128)(2,1)}, bf16[960,768]{1,0:T(8,128)(2,1)S(1)}, u32[]{:S(2)}, u32[]{:S(2)}) %collective-permute-start.57) | collective-permute-done | bytes 1474592 | tf_op jit(solution)/shard_map/ppermute | solution.py:748
  367.1 6.8 %blocks.12 = (bf16[192,768]{1,0:T(8,128)(2,1)S(1)}, bf16[192,768]{1,0:T(8,128)(2,1)S(1)}, bf16[768,768]{1,0:T(8,128)(2,1)}, bf16[768,768]{1,0:T(8,128)(2,1)}, bf...) custom-call(s32[4]{0:T(128)S(1)} %pad_add_fusion.2.scalars, ...), custom_call_target="tpu_custom_call" | custom-call | bytes 17694720 | tf_op jit(solution)/shard_map/blocks/pallas_call | solution.py:1248
  386.8 10.5 %collective-permute-done.62.refs_19_ = bf16[192,768]{1,0:T(8,128)(2,1)S(1)} collective-permute-done((bf16[192,768]{1,0:T(8,128)(2,1)S(1)}, bf16[192,768]{1,0:T(8,128)(2,1)S(1)}, u32[]{:S(2)}, u32[]{:S(2)}) %collective-permute-start.62) | collective-permute-done | bytes 294944 | tf_op jit(solution)/shard_map/ppermute | solution.py:748
  397.3 4.0 collective-permute-done.64.refs_5_
  402.0 7.6 %blocks.13 = (bf16[96,768]{1,0:T(8,128)(2,1)S(1)}, bf16[384,768]{1,0:T(8,128)(2,1)}, bf16[704,768]{1,0:T(8,128)(2,1)}, bf16[832,768]{1,0:T(8,128)(2,1)}, f32[48,...) custom-call(s32[4]{0:T(128)S(1)} %pad_add_fusion.2.scalars, ...), custom_call_target="tpu_custom_call" | custom-call | bytes 15630336 | tf_op jit(solution)/shard_map/blocks/pallas_call | solution.py:1248
  415.3 11.4 %collective-permute-done.67.refs_14_ = bf16[96,768]{1,0:T(8,128)(2,1)S(1)} collective-permute-done((bf16[96,768]{1,0:T(8,128)(2,1)S(1)}, bf16[96,768]{1,0:T(8,128)(2,1)S(1)}, u32[]{:S(2)}, u32[]{:S(2)}) %collective-permute-start.67) | collective-permute-done | bytes 147488 | tf_op jit(solution)/shard_map/ppermute | solution.py:748
  429.1 5.1 %collective-permute-done.69.refs_6_ = bf16[704,768]{1,0:T(8,128)(2,1)} collective-permute-done((bf16[704,768]{1,0:T(8,128)(2,1)}, bf16[704,768]{1,0:T(8,128)(2,1)}, u32[]{:S(2)}, u32[]{:S(2)}) %collective-permute-start.69) | collective-permute-done | bytes 1081376 | tf_op jit(solution)/shard_map/ppermute | solution.py:748
  434.1 3.0 collective-permute-done.70.refs_8_
  437.2 6.9 %blocks.14 = (bf16[192,768]{1,0:T(8,128)(2,1)}, bf16[192,768]{1,0:T(8,128)(2,1)}, bf16[256,768]{1,0:T(8,128)(2,1)}, bf16[256,768]{1,0:T(8,128)(2,1)}, f32[48,768...) custom-call(s32[4]{0:T(128)S(1)} %pad_add_fusion.2.scalars, ...), custom_call_target="tpu_custom_call" | custom-call | bytes 11354112 | tf_op jit(solution)/shard_map/blocks/pallas_call | solution.py:1248
  449.8 4.0 all-to-all-start.1
  453.8 3.4 collective-permute-done.71.refs_10_
  458.2 4.4 blocks.15
  467.1 6.1 %collective-permute-done.75.refs_6_ = bf16[96,768]{1,0:T(8,128)(2,1)S(1)} collective-permute-done((bf16[96,768]{1,0:T(8,128)(2,1)S(1)}, bf16[96,768]{1,0:T(8,128)(2,1)S(1)}, u32[]{:S(2)}, u32[]{:S(2)}) %collective-permute-start.75) | collective-permute-done | bytes 147488 | tf_op jit(solution)/shard_map/ppermute | solution.py:748
  487.4 5.5 %collective-permute-done.77.refs_1_ = bf16[128,768]{1,0:T(8,128)(2,1)S(1)} collective-permute-done((bf16[128,768]{1,0:T(8,128)(2,1)S(1)}, bf16[128,768]{1,0:T(8,128)(2,1)S(1)}, u32[]{:S(2)}, u32[]{:S(2)}) %collective-permute-start.77) | collective-permute-done | bytes 196640 | tf_op jit(solution)/shard_map/ppermute | solution.py:748
  (509 shorter events, 186.9 us)
Async XLA Ops:
  1.7 13.4 %collective-permute-start = (bf16[128,768]{1,0:T(8,128)(2,1)}, bf16[128,768]{1,0:T(8,128)(2,1)S(1)}, u32[]{:S(2)}, u32[]{:S(2)}) collective-permute-start(bf16[128,768]{1,0:T(8,128)(2,1)} %bitcast.349), channel_id=1, source_target_pairs={{0,16},{1,17},{2,18},{3,19},{4,20},{5,21},{6,22},{7,23},{8,24},{9,... | collective-permute-start | bytes 589832 | tf_op jit(solution)/shard_map/ppermute | solution.py:748
  18.9 11.1 %collective-permute-start.5 = (bf16[96,768]{1,0:T(8,128)(2,1)S(1)}, bf16[96,768]{1,0:T(8,128)(2,1)S(1)}, u32[]{:S(2)}, u32[]{:S(2)}) collective-permute-start(bf16[96,768]{1,0:T(8,128)(2,1)S(1)} %bitcast.276), channel_id=1, source_target_pairs={{0,16},{1,17},{2,18},{3,19},{4,20},{5,21},{6,22},{7,23},{8,24},{9,... | collective-permute-start | bytes 442376 | tf_op jit(solution)/shard_map/ppermute | solution.py:748
  18.9 11.1 %collective-permute-start.6 = (bf16[96,768]{1,0:T(8,128)(2,1)S(1)}, bf16[96,768]{1,0:T(8,128)(2,1)S(1)}, u32[]{:S(2)}, u32[]{:S(2)}) collective-permute-start(bf16[96,768]{1,0:T(8,128)(2,1)S(1)} %bitcast.382), channel_id=1, source_target_pairs={{0,4},{1,5},{2,6},{3,7},{4,0},{5,1},{6,2},{7,3},{8,12},{9,13},{10,... | collective-permute-start | bytes 442376 | tf_op jit(solution)/shard_map/ppermute | solution.py:748
  23.8 13.5 %collective-permute-start.4 = (bf16[256,768]{1,0:T(8,128)(2,1)S(1)}, bf16[256,768]{1,0:T(8,128)(2,1)S(1)}, u32[]{:S(2)}, u32[]{:S(2)}) collective-permute-start(bf16[256,768]{1,0:T(8,128)(2,1)S(1)} %bitcast.364), channel_id=1, source_target_pairs={{0,8},{1,9},{2,10},{3,11},{4,12},{5,13},{6,14},{7,15},{8,0},{9,1},... | collective-permute-start | bytes 1179656 | tf_op jit(solution)/shard_map/ppermute | solution.py:748
  37.7 17.5 %collective-permute-start.15 = (bf16[256,768]{1,0:T(8,128)(2,1)S(1)}, bf16[256,768]{1,0:T(8,128)(2,1)S(1)}, u32[]{:S(2)}, u32[]{:S(2)}) collective-permute-start(bf16[256,768]{1,0:T(8,128)(2,1)S(1)} %bitcast.363), channel_id=1, source_target_pairs={{0,4},{1,5},{2,6},{3,7},{4,0},{5,1},{6,2},{7,3},{8,12},{9,13},{10,... | collective-permute-start | bytes 1179656 | tf_op jit(solution)/shard_map/ppermute | solution.py:748
  38.3 16.9 %collective-permute-start.16 = (bf16[256,768]{1,0:T(8,128)(2,1)S(1)}, bf16[256,768]{1,0:T(8,128)(2,1)S(1)}, u32[]{:S(2)}, u32[]{:S(2)}) collective-permute-start(bf16[256,768]{1,0:T(8,128)(2,1)S(1)} %bitcast.362), channel_id=1, source_target_pairs={{0,2},{1,3},{2,0},{3,1},{4,6},{5,7},{6,4},{7,5},{8,10},{9,11},{10,... | collective-permute-start | bytes 1179656 | tf_op jit(solution)/shard_map/ppermute | solution.py:748
  38.8 12.0 %collective-permute-start.13 = (bf16[192,768]{1,0:T(8,128)(2,1)S(1)}, bf16[192,768]{1,0:T(8,128)(2,1)S(1)}, u32[]{:S(2)}, u32[]{:S(2)}) collective-permute-start(bf16[192,768]{1,0:T(8,128)(2,1)S(1)} %bitcast.374), channel_id=1, source_target_pairs={{0,8},{1,9},{2,10},{3,11},{4,12},{5,13},{6,14},{7,15},{8,0},{9,1},... | collective-permute-start | bytes 884744 | tf_op jit(solution)/shard_map/ppermute | solution.py:748
  40.5 14.7 %collective-permute-start.14 = (bf16[192,768]{1,0:T(8,128)(2,1)S(1)}, bf16[192,768]{1,0:T(8,128)(2,1)S(1)}, u32[]{:S(2)}, u32[]{:S(2)}) collective-permute-start(bf16[192,768]{1,0:T(8,128)(2,1)S(1)} %bitcast.270), channel_id=1, source_target_pairs={{0,16},{1,17},{2,18},{3,19},{4,20},{5,21},{6,22},{7,23},{8,24},{9,... | collective-permute-start | bytes 884744 | tf_op jit(solution)/shard_map/ppermute | solution.py:748
  58.5 26.4 %collective-permute-start.19 = (bf16[704,768]{1,0:T(8,128)(2,1)}, bf16[704,768]{1,0:T(8,128)(2,1)}, u32[]{:S(2)}, u32[]{:S(2)}) collective-permute-start(bf16[704,768]{1,0:T(8,128)(2,1)} %pad_maximum_fusion.9.refs_2_), channel_id=1, source_target_pairs={{0,4},{1,5},{2,6},{3,7},{4,0},{5,1},{6,2},{7,3},{8,12},{9,13},{10,... | collective-permute-start | bytes 3244040 | tf_op jit(solution)/shard_map/ppermute | solution.py:748
  60.0 24.9 %collective-permute-start.20 = (bf16[704,768]{1,0:T(8,128)(2,1)S(1)}, bf16[704,768]{1,0:T(8,128)(2,1)}, u32[]{:S(2)}, u32[]{:S(2)}) collective-permute-start(bf16[704,768]{1,0:T(8,128)(2,1)S(1)} %pad_maximum_fusion.8.refs_0_), channel_id=1, source_target_pairs={{0,2},{1,3},{2,0},{3,1},{4,6},{5,7},{6,4},{7,5},{8,10},{9,11},{10,... | collective-permute-start | bytes 3244040 | tf_op jit(solution)/shard_map/ppermute | solution.py:748
  61.5 23.4 %collective-permute-start.17 = (bf16[384,768]{1,0:T(8,128)(2,1)}, bf16[384,768]{1,0:T(8,128)(2,1)}, u32[]{:S(2)}, u32[]{:S(2)}) collective-permute-start(bf16[384,768]{1,0:T(8,128)(2,1)} %bitcast.60), channel_id=1, source_target_pairs={{0,8},{1,9},{2,10},{3,11},{4,12},{5,13},{6,14},{7,15},{8,0},{9,1},... | collective-permute-start | bytes 1769480 | tf_op jit(solution)/shard_map/ppermute | solution.py:748
  64.3 19.7 %all-to-all-start = ((bf16[32,2,288]{2,1,0:T(2,128)(2,1)}), bf16[32,2,288]{2,1,0:T(2,128)(2,1)S(1)}, u32[]{:S(2)}, u32[]{:S(2)}) async-start(bf16[32,2,288]{2,1,0:T(2,128)(2,1)} %reshape.477), calls=%async_computation | async-start | bytes 98304 | tf_op jit(solution)/shard_map/all_to_all | solution.py:1410
  67.4 17.4 %collective-permute-start.18 = (bf16[96,768]{1,0:T(8,128)(2,1)S(1)}, bf16[96,768]{1,0:T(8,128)(2,1)S(1)}, u32[]{:S(2)}, u32[]{:S(2)}) collective-permute-start(bf16[96,768]{1,0:T(8,128)(2,1)S(1)} %bitcast.273), channel_id=1, source_target_pairs={{0,16},{1,17},{2,18},{3,19},{4,20},{5,21},{6,22},{7,23},{8,24},{9,... | collective-permute-start | bytes 442376 | tf_op jit(solution)/shard_map/ppermute | solution.py:748
  91.6 28.4 %collective-permute-start.23 = (bf16[768,768]{1,0:T(8,128)(2,1)}, bf16[768,768]{1,0:T(8,128)(2,1)}, u32[]{:S(2)}, u32[]{:S(2)}) collective-permute-start(bf16[768,768]{1,0:T(8,128)(2,1)} %pad_maximum_fusion.4.refs_2_), channel_id=1, source_target_pairs={{0,4},{1,5},{2,6},{3,7},{4,0},{5,1},{6,2},{7,3},{8,12},{9,13},{10,... | collective-permute-start | bytes 3538952 | tf_op jit(solution)/shard_map/ppermute | solution.py:748
  93.0 27.8 %collective-permute-start.24 = (bf16[768,768]{1,0:T(8,128)(2,1)S(1)}, bf16[768,768]{1,0:T(8,128)(2,1)}, u32[]{:S(2)}, u32[]{:S(2)}) collective-permute-start(bf16[768,768]{1,0:T(8,128)(2,1)S(1)} %pad_maximum_fusion.3.refs_0_), channel_id=1, source_target_pairs={{0,2},{1,3},{2,0},{3,1},{4,6},{5,7},{6,4},{7,5},{8,10},{9,11},{10,... | collective-permute-start | bytes 3538952 | tf_op jit(solution)/shard_map/ppermute | solution.py:748
  104.1 12.6 %collective-permute-start.21 = (bf16[192,768]{1,0:T(8,128)(2,1)S(1)}, bf16[192,768]{1,0:T(8,128)(2,1)S(1)}, u32[]{:S(2)}, u32[]{:S(2)}) collective-permute-start(bf16[192,768]{1,0:T(8,128)(2,1)S(1)} %bitcast.372), channel_id=1, source_target_pairs={{0,8},{1,9},{2,10},{3,11},{4,12},{5,13},{6,14},{7,15},{8,0},{9,1},... | collective-permute-start | bytes 884744 | tf_op jit(solution)/shard_map/ppermute | solution.py:748
  127.4 33.5 %collective-permute-start.28 = (bf16[960,768]{1,0:T(8,128)(2,1)}, bf16[960,768]{1,0:T(8,128)(2,1)}, u32[]{:S(2)}, u32[]{:S(2)}) collective-permute-start(bf16[960,768]{1,0:T(8,128)(2,1)} %pad_maximum_fusion.1.refs_2_), channel_id=1, source_target_pairs={{0,4},{1,5},{2,6},{3,7},{4,0},{5,1},{6,2},{7,3},{8,12},{9,13},{10,... | collective-permute-start | bytes 4423688 | tf_op jit(solution)/shard_map/ppermute | solution.py:748
  128.1 33.1 %collective-permute-start.29 = (bf16[960,768]{1,0:T(8,128)(2,1)S(1)}, bf16[960,768]{1,0:T(8,128)(2,1)}, u32[]{:S(2)}, u32[]{:S(2)}) collective-permute-start(bf16[960,768]{1,0:T(8,128)(2,1)S(1)} %pad_maximum_fusion.refs_0_), channel_id=1, source_target_pairs={{0,2},{1,3},{2,0},{3,1},{4,6},{5,7},{6,4},{7,5},{8,10},{9,11},{10,... | collective-permute-start | bytes 4423688 | tf_op jit(solution)/shard_map/ppermute | solution.py:748
  134.1 26.3 %collective-permute-start.27 = (bf16[384,768]{1,0:T(8,128)(2,1)S(1)}, bf16[384,768]{1,0:T(8,128)(2,1)S(1)}, u32[]{:S(2)}, u32[]{:S(2)}) collective-permute-start(bf16[384,768]{1,0:T(8,128)(2,1)S(1)} %bitcast.354), channel_id=1, source_target_pairs={{0,16},{1,17},{2,18},{3,19},{4,20},{5,21},{6,22},{7,23},{8,24},{9,... | collective-permute-start | bytes 1769480 | tf_op jit(solution)/shard_map/ppermute | solution.py:748
  136.2 17.3 %collective-permute-start.26 = (bf16[192,768]{1,0:T(8,128)(2,1)S(1)}, bf16[192,768]{1,0:T(8,128)(2,1)S(1)}, u32[]{:S(2)}, u32[]{:S(2)}) collective-permute-start(bf16[192,768]{1,0:T(8,128)(2,1)S(1)} %bitcast.373), channel_id=1, source_target_pairs={{0,8},{1,9},{2,10},{3,11},{4,12},{5,13},{6,14},{7,15},{8,0},{9,1},... | collective-permute-start | bytes 884744 | tf_op jit(solution)/shard_map/ppermute | solution.py:748
  164.8 27.2 %collective-permute-start.33 = (bf16[768,768]{1,0:T(8,128)(2,1)S(1)}, bf16[768,768]{1,0:T(8,128)(2,1)S(1)}, u32[]{:S(2)}, u32[]{:S(2)}) collective-permute-start(bf16[768,768]{1,0:T(8,128)(2,1)S(1)} %bitcast.264), channel_id=1, source_target_pairs={{0,8},{1,9},{2,10},{3,11},{4,12},{5,13},{6,14},{7,15},{8,0},{9,1},... | collective-permute-start | bytes 3538952 | tf_op jit(solution)/shard_map/ppermute | solution.py:748
  164.9 22.1 %collective-permute-start.34 = (bf16[576,768]{1,0:T(8,128)(2,1)S(1)}, bf16[576,768]{1,0:T(8,128)(2,1)S(1)}, u32[]{:S(2)}, u32[]{:S(2)}) collective-permute-start(bf16[576,768]{1,0:T(8,128)(2,1)S(1)} %pad_maximum_fusion.11.refs_2_), channel_id=1, source_target_pairs={{0,4},{1,5},{2,6},{3,7},{4,0},{5,1},{6,2},{7,3},{8,12},{9,13},{10,... | collective-permute-start | bytes 2654216 | tf_op jit(solution)/shard_map/ppermute | solution.py:748
  166.2 21.7 %collective-permute-start.35 = (bf16[576,768]{1,0:T(8,128)(2,1)S(1)}, bf16[576,768]{1,0:T(8,128)(2,1)S(1)}, u32[]{:S(2)}, u32[]{:S(2)}) collective-permute-start(bf16[576,768]{1,0:T(8,128)(2,1)S(1)} %pad_maximum_fusion.10.refs_0_), channel_id=1, source_target_pairs={{0,2},{1,3},{2,0},{3,1},{4,6},{5,7},{6,4},{7,5},{8,10},{9,11},{10,... | collective-permute-start | bytes 2654216 | tf_op jit(solution)/shard_map/ppermute | solution.py:748
  196.5 16.4 %collective-permute-start.42 = (bf16[768,384]{1,0:T(8,128)(2,1)}, bf16[768,384]{1,0:T(8,128)(2,1)}, u32[]{:S(2)}, u32[]{:S(2)}) collective-permute-start(bf16[768,384]{1,0:T(8,128)(2,1)} %bitcast.140.wom), channel_id=1, source_target_pairs={{0,1},{1,0},{2,3},{3,2},{4,5},{5,4},{6,7},{7,6},{8,9},{9,8},{10,11... | collective-permute-start | bytes 1769480 | tf_op jit(solution)/shard_map/ppermute | solution.py:748
  197.0 19.5 %collective-permute-start.38 = (bf16[384,768]{1,0:T(8,128)(2,1)S(1)}, bf16[384,768]{1,0:T(8,128)(2,1)}, u32[]{:S(2)}, u32[]{:S(2)}) collective-permute-start(bf16[384,768]{1,0:T(8,128)(2,1)S(1)} %bitcast.268), channel_id=1, source_target_pairs={{0,4},{1,5},{2,6},{3,7},{4,0},{5,1},{6,2},{7,3},{8,12},{9,13},{10,... | collective-permute-start | bytes 1769480 | tf_op jit(solution)/shard_map/ppermute | solution.py:748
  197.5 19.0 %collective-permute-start.39 = (bf16[384,768]{1,0:T(8,128)(2,1)S(1)}, bf16[384,768]{1,0:T(8,128)(2,1)}, u32[]{:S(2)}, u32[]{:S(2)}) collective-permute-start(bf16[384,768]{1,0:T(8,128)(2,1)S(1)} %bitcast.266), channel_id=1, source_target_pairs={{0,2},{1,3},{2,0},{3,1},{4,6},{5,7},{6,4},{7,5},{8,10},{9,11},{10,... | collective-permute-start | bytes 1769480 | tf_op jit(solution)/shard_map/ppermute | solution.py:748
  253.8 32.9 %collective-permute-start.48 = (bf16[896,768]{1,0:T(8,128)(2,1)}, bf16[896,768]{1,0:T(8,128)(2,1)}, u32[]{:S(2)}, u32[]{:S(2)}) collective-permute-start(bf16[896,768]{1,0:T(8,128)(2,1)} %get-tuple-element.518), channel_id=1, source_target_pairs={{0,2},{1,3},{2,0},{3,1},{4,6},{5,7},{6,4},{7,5},{8,10},{9,11},{10,... | collective-permute-start | bytes 4128776 | tf_op jit(solution)/shard_map/ppermute | solution.py:748
  254.6 28.3 %collective-permute-start.47 = (bf16[768,768]{1,0:T(8,128)(2,1)}, bf16[768,768]{1,0:T(8,128)(2,1)}, u32[]{:S(2)}, u32[]{:S(2)}) collective-permute-start(bf16[768,768]{1,0:T(8,128)(2,1)} %get-tuple-element.517), channel_id=1, source_target_pairs={{0,4},{1,5},{2,6},{3,7},{4,0},{5,1},{6,2},{7,3},{8,12},{9,13},{10,... | collective-permute-start | bytes 3538952 | tf_op jit(solution)/shard_map/ppermute | solution.py:748
  294.7 28.4 %collective-permute-start.52 = (bf16[768,768]{1,0:T(8,128)(2,1)S(1)}, bf16[768,768]{1,0:T(8,128)(2,1)S(1)}, u32[]{:S(2)}, u32[]{:S(2)}) collective-permute-start(bf16[768,768]{1,0:T(8,128)(2,1)S(1)} %copy-done.92), channel_id=1, source_target_pairs={{0,4},{1,5},{2,6},{3,7},{4,0},{5,1},{6,2},{7,3},{8,12},{9,13},{10,... | collective-permute-start | bytes 3538952 | tf_op jit(solution)/shard_map/ppermute | solution.py:748
  295.5 28.1 %collective-permute-start.53 = (bf16[768,768]{1,0:T(8,128)(2,1)S(1)}, bf16[768,768]{1,0:T(8,128)(2,1)S(1)}, u32[]{:S(2)}, u32[]{:S(2)}) collective-permute-start(bf16[768,768]{1,0:T(8,128)(2,1)S(1)} %copy-done.91), channel_id=1, source_target_pairs={{0,2},{1,3},{2,0},{3,1},{4,6},{5,7},{6,4},{7,5},{8,10},{9,11},{10,... | collective-permute-start | bytes 3538952 | tf_op jit(solution)/shard_map/ppermute | solution.py:748
  331.1 34.1 %collective-permute-start.57 = (bf16[960,768]{1,0:T(8,128)(2,1)}, bf16[960,768]{1,0:T(8,128)(2,1)S(1)}, u32[]{:S(2)}, u32[]{:S(2)}) collective-permute-start(bf16[960,768]{1,0:T(8,128)(2,1)} %get-tuple-element.572), channel_id=1, source_target_pairs={{0,4},{1,5},{2,6},{3,7},{4,0},{5,1},{6,2},{7,3},{8,12},{9,13},{10,... | collective-permute-start | bytes 4423688 | tf_op jit(solution)/shard_map/ppermute | solution.py:748
  332.4 33.5 %collective-permute-start.58 = (bf16[960,768]{1,0:T(8,128)(2,1)}, bf16[960,768]{1,0:T(8,128)(2,1)S(1)}, u32[]{:S(2)}, u32[]{:S(2)}) collective-permute-start(bf16[960,768]{1,0:T(8,128)(2,1)} %get-tuple-element.573), channel_id=1, source_target_pairs={{0,2},{1,3},{2,0},{3,1},{4,6},{5,7},{6,4},{7,5},{8,10},{9,11},{10,... | collective-permute-start | bytes 4423688 | tf_op jit(solution)/shard_map/ppermute | solution.py:748
  336.2 21.9 %collective-permute-start.56 = (bf16[384,768]{1,0:T(8,128)(2,1)S(1)}, bf16[384,768]{1,0:T(8,128)(2,1)S(1)}, u32[]{:S(2)}, u32[]{:S(2)}) collective-permute-start(bf16[384,768]{1,0:T(8,128)(2,1)S(1)} %copy-done.93), channel_id=1, source_target_pairs={{0,8},{1,9},{2,10},{3,11},{4,12},{5,13},{6,14},{7,15},{8,0},{9,1},... | collective-permute-start | bytes 1769480 | tf_op jit(solution)/shard_map/ppermute | solution.py:748
  374.6 26.7 %collective-permute-start.64 = (bf16[768,768]{1,0:T(8,128)(2,1)}, bf16[768,768]{1,0:T(8,128)(2,1)}, u32[]{:S(2)}, u32[]{:S(2)}) collective-permute-start(bf16[768,768]{1,0:T(8,128)(2,1)} %get-tuple-element.612), channel_id=1, source_target_pairs={{0,4},{1,5},{2,6},{3,7},{4,0},{5,1},{6,2},{7,3},{8,12},{9,13},{10,... | collective-permute-start | bytes 3538952 | tf_op jit(solution)/shard_map/ppermute | solution.py:748
  375.6 26.4 %collective-permute-start.65 = (bf16[768,768]{1,0:T(8,128)(2,1)}, bf16[768,768]{1,0:T(8,128)(2,1)}, u32[]{:S(2)}, u32[]{:S(2)}) collective-permute-start(bf16[768,768]{1,0:T(8,128)(2,1)} %get-tuple-element.613), channel_id=1, source_target_pairs={{0,2},{1,3},{2,0},{3,1},{4,6},{5,7},{6,4},{7,5},{8,10},{9,11},{10,... | collective-permute-start | bytes 3538952 | tf_op jit(solution)/shard_map/ppermute | solution.py:748
  380.9 16.4 %collective-permute-start.62 = (bf16[192,768]{1,0:T(8,128)(2,1)S(1)}, bf16[192,768]{1,0:T(8,128)(2,1)S(1)}, u32[]{:S(2)}, u32[]{:S(2)}) collective-permute-start(bf16[192,768]{1,0:T(8,128)(2,1)S(1)} %get-tuple-element.610), channel_id=1, source_target_pairs={{0,16},{1,17},{2,18},{3,19},{4,20},{5,21},{6,22},{7,23},{8,24},{9,... | collective-permute-start | bytes 884744 | tf_op jit(solution)/shard_map/ppermute | solution.py:748
  381.0 16.3 %collective-permute-start.63 = (bf16[192,768]{1,0:T(8,128)(2,1)S(1)}, bf16[192,768]{1,0:T(8,128)(2,1)S(1)}, u32[]{:S(2)}, u32[]{:S(2)}) collective-permute-start(bf16[192,768]{1,0:T(8,128)(2,1)S(1)} %get-tuple-element.611), channel_id=1, source_target_pairs={{0,8},{1,9},{2,10},{3,11},{4,12},{5,13},{6,14},{7,15},{8,0},{9,1},... | collective-permute-start | bytes 884744 | tf_op jit(solution)/shard_map/ppermute | solution.py:748
  409.6 27.6 %collective-permute-start.70 = (bf16[832,768]{1,0:T(8,128)(2,1)}, bf16[832,768]{1,0:T(8,128)(2,1)}, u32[]{:S(2)}, u32[]{:S(2)}) collective-permute-start(bf16[832,768]{1,0:T(8,128)(2,1)} %get-tuple-element.642), channel_id=1, source_target_pairs={{0,2},{1,3},{2,0},{3,1},{4,6},{5,7},{6,4},{7,5},{8,10},{9,11},{10,... | collective-permute-start | bytes 3833864 | tf_op jit(solution)/shard_map/ppermute | solution.py:748
  411.0 23.2 %collective-permute-start.69 = (bf16[704,768]{1,0:T(8,128)(2,1)}, bf16[704,768]{1,0:T(8,128)(2,1)}, u32[]{:S(2)}, u32[]{:S(2)}) collective-permute-start(bf16[704,768]{1,0:T(8,128)(2,1)} %get-tuple-element.641), channel_id=1, source_target_pairs={{0,4},{1,5},{2,6},{3,7},{4,0},{5,1},{6,2},{7,3},{8,12},{9,13},{10,... | collective-permute-start | bytes 3244040 | tf_op jit(solution)/shard_map/ppermute | solution.py:748
  413.6 15.5 %collective-permute-start.68 = (bf16[384,768]{1,0:T(8,128)(2,1)}, bf16[384,768]{1,0:T(8,128)(2,1)}, u32[]{:S(2)}, u32[]{:S(2)}) collective-permute-start(bf16[384,768]{1,0:T(8,128)(2,1)} %get-tuple-element.640), channel_id=1, source_target_pairs={{0,8},{1,9},{2,10},{3,11},{4,12},{5,13},{6,14},{7,15},{8,0},{9,1},... | collective-permute-start | bytes 1769480 | tf_op jit(solution)/shard_map/ppermute | solution.py:748
  414.2 12.6 %collective-permute-start.67 = (bf16[96,768]{1,0:T(8,128)(2,1)S(1)}, bf16[96,768]{1,0:T(8,128)(2,1)S(1)}, u32[]{:S(2)}, u32[]{:S(2)}) collective-permute-start(bf16[96,768]{1,0:T(8,128)(2,1)S(1)} %get-tuple-element.639), channel_id=1, source_target_pairs={{0,16},{1,17},{2,18},{3,19},{4,20},{5,21},{6,22},{7,23},{8,24},{9,... | collective-permute-start | bytes 442376 | tf_op jit(solution)/shard_map/ppermute | solution.py:748
  444.8 12.4 %collective-permute-start.71 = (bf16[192,768]{1,0:T(8,128)(2,1)}, bf16[192,768]{1,0:T(8,128)(2,1)S(1)}, u32[]{:S(2)}, u32[]{:S(2)}) collective-permute-start(bf16[192,768]{1,0:T(8,128)(2,1)} %get-tuple-element.660), channel_id=1, source_target_pairs={{0,16},{1,17},{2,18},{3,19},{4,20},{5,21},{6,22},{7,23},{8,24},{9,... | collective-permute-start | bytes 884744 | tf_op jit(solution)/shard_map/ppermute | solution.py:748
  444.8 12.5 %collective-permute-start.72 = (bf16[192,768]{1,0:T(8,128)(2,1)}, bf16[192,768]{1,0:T(8,128)(2,1)}, u32[]{:S(2)}, u32[]{:S(2)}) collective-permute-start(bf16[192,768]{1,0:T(8,128)(2,1)} %get-tuple-element.661), channel_id=1, source_target_pairs={{0,8},{1,9},{2,10},{3,11},{4,12},{5,13},{6,14},{7,15},{8,0},{9,1},... | collective-permute-start | bytes 884744 | tf_op jit(solution)/shard_map/ppermute | solution.py:748
  446.2 11.1 %collective-permute-start.73 = (bf16[256,768]{1,0:T(8,128)(2,1)}, bf16[256,768]{1,0:T(8,128)(2,1)S(1)}, u32[]{:S(2)}, u32[]{:S(2)}) collective-permute-start(bf16[256,768]{1,0:T(8,128)(2,1)} %get-tuple-element.662), channel_id=1, source_target_pairs={{0,4},{1,5},{2,6},{3,7},{4,0},{5,1},{6,2},{7,3},{8,12},{9,13},{10,... | collective-permute-start | bytes 1179656 | tf_op jit(solution)/shard_map/ppermute | solution.py:748
  449.8 14.1 %all-to-all-start.1 = ((f32[32,1,576]{2,1,0:T(1,128)}), f32[32,1,576]{2,1,0:T(1,128)S(1)}, u32[]{:S(2)}, u32[]{:S(2)}) async-start(f32[32,1,576]{2,1,0:T(1,128)} %copy.86), calls=%async_computation.1 | async-start | bytes 163840 | tf_op jit(solution)/shard_map/all_to_all | solution.py:1612
  462.7 12.8 %collective-permute-start.76 = (bf16[256,768]{1,0:T(8,128)(2,1)}, bf16[256,768]{1,0:T(8,128)(2,1)S(1)}, u32[]{:S(2)}, u32[]{:S(2)}) collective-permute-start(bf16[256,768]{1,0:T(8,128)(2,1)} %get-tuple-element.681), channel_id=1, source_target_pairs={{0,8},{1,9},{2,10},{3,11},{4,12},{5,13},{6,14},{7,15},{8,0},{9,1},... | collective-permute-start | bytes 1179656 | tf_op jit(solution)/shard_map/ppermute | solution.py:748
  467.0 14.6 %collective-permute-start.79 = (f32[24,3072]{1,0:T(8,128)S(1)}, f32[24,3072]{1,0:T(8,128)S(1)}, u32[]{:S(2)}, u32[]{:S(2)}) collective-permute-start(f32[24,3072]{1,0:T(8,128)S(1)} %get-tuple-element.704), channel_id=1, source_target_pairs={{0,1},{1,0},{2,3},{3,2},{4,5},{5,4},{6,7},{7,6},{8,9},{9,8},{10,11... | collective-permute-start | bytes 884744 | tf_op jit(solution)/shard_map/ppermute | solution.py:748
  480.4 12.4 %collective-permute-start.77 = (bf16[128,768]{1,0:T(8,128)(2,1)S(1)}, bf16[128,768]{1,0:T(8,128)(2,1)S(1)}, u32[]{:S(2)}, u32[]{:S(2)}) collective-permute-start(bf16[128,768]{1,0:T(8,128)(2,1)S(1)} %get-tuple-element.690), channel_id=1, source_target_pairs={{0,16},{1,17},{2,18},{3,19},{4,20},{5,21},{6,22},{7,23},{8,24},{9,... | collective-permute-start | bytes 589832 | tf_op jit(solution)/shard_map/ppermute | solution.py:748
  (137 other events, 765.3 us)
